TPU v7x, 128 devices: a whole 4x4x4 slice. The times are simulated.
128 devices in a mesh: expert: 32 (over y, z, core), tensor: 4 (over x).
Axes of the slice: x: 4, y: 4, z: 4, core: 2. Of those that a mesh axis runs over, the one named last changes fastest.
Arguments:
- tokens: bfloat16 [8192, 2048], P('expert', 'tensor'), may hold values from -6 to 6
- out_grad: bfloat16 [8192, 2048], P('expert', 'tensor'), may hold values from -6 to 6
- seq_lengths: int32 [32, 3], P('expert'), may hold values from 1 to 128, 256 in all within a row
- dest_index: int32 [8192], P('expert'), may hold values from 0 to 8191, as said below
- routes: int32 [8192, 8], P('expert'), may hold values from 0 to 63, all different within a row; in each aligned block of 256 rows (0 to 255, 256 to 511, ...) at most 48 rows name the same one
- pair_order: int32 [32, 2048], P('expert'), may hold values from 0 to 2047, each once within a row
- norm1_gain: bfloat16 [2048], replicated, may hold values from 0.25 to 1.75
- w_query: bfloat16 [2048, 2048], P(None, 'tensor'), may hold values from -0.125 to 0.125
- w_key: bfloat16 [2048, 2048], P(None, 'tensor'), may hold values from -0.125 to 0.125
- w_value: bfloat16 [2048, 2048], P(None, 'tensor'), may hold values from -0.125 to 0.125
- q_gain: bfloat16 [128], replicated, may hold values from 0.25 to 1.75
- k_gain: bfloat16 [128], replicated, may hold values from 0.25 to 1.75
- w_output: bfloat16 [2048, 2048], P('tensor'), may hold values from -1 to 1
- norm2_gain: bfloat16 [2048], replicated, may hold values from 0.25 to 1.75
- w_router: bfloat16 [2048, 64], replicated, may hold values from -0.0625 to 0.0625
- expert_w: bfloat16 [64, 2048, 3, 1024], P('expert', None, None, 'tensor'), may hold values from -3 to 3
Outputs:
- block_out: bfloat16 [8192, 2048], P('expert', 'tensor')
- grad_tokens: bfloat16 [8192, 2048], P('expert', 'tensor')
- grad_norm1: float32 [2048], replicated
- grad_query: float32 [2048, 2048], P(None, 'tensor')
- grad_key: float32 [2048, 2048], P(None, 'tensor')
- grad_value: float32 [2048, 2048], P(None, 'tensor')
- grad_qgain: float32 [128], replicated
- grad_kgain: float32 [128], replicated
- grad_output: float32 [2048, 2048], P('tensor')
- grad_norm2: float32 [2048], replicated
- grad_router: float32 [2048, 64], replicated
- grad_experts: float32 [64, 2048, 3, 1024], P('expert', None, None, 'tensor')
Inputs may be any that keep to these rules, and one draw needn't show every extreme that they name: `dest_index`: a permutation of the balanced positions; the arriving rows of each group go to exactly 8 positions of every group's range of 256 positions. `routes`: each row names 8 different experts; within the rows of one group no expert is named more than 48 times. `pair_order`: each row is a permutation. `seq_lengths`: each row sums to 256 and its largest entry is 128.
All inputs are finite; a program needn't handle non-finite values.
Results may differ from a plain program's by a relative error of at most 0.035.
Values may be sent and summed in bfloat16 or wider, within the bound.
A program may use at most 256 MiB of HBM per device.

v0:
```python
import math

import jax
import jax.numpy as jnp
from jax import lax
from jax.sharding import PartitionSpec as P

norm_eps = 1e-06
rope_base = 10000.0
mask_fill = -1e30


def prefix(part, axis, combine, identity):
    place = lax.axis_index(axis)
    gathered = lax.all_gather(part, axis)
    state = jnp.zeros_like(part) + jnp.asarray(identity, part.dtype)

    def one(step, state):
        return combine(state, lax.dynamic_index_in_dim(gathered, step, 0, False))

    return lax.fori_loop(0, place, one, state)


def rms_apply(values, gain_vec):
    inverse = lax.rsqrt(jnp.mean(values * values, axis=-1, keepdims=True) + norm_eps)
    return values * inverse * gain_vec


def rope_tables(positions, width):
    half_width = width // 2
    steps_idx = jnp.arange(half_width, dtype=jnp.float32)
    freqs = jnp.exp(steps_idx * (-2.0 * math.log(rope_base) / width))
    angles = positions.astype(jnp.float32)[:, None] * freqs[None, :]
    return (jnp.cos(angles), jnp.sin(angles))


def head_prep(raw, gain_vec, cos_tab, sin_tab, heads):
    token_count = raw.shape[0]
    shaped = rms_apply(raw.reshape(token_count, heads, -1), gain_vec)
    half_width = shaped.shape[-1] // 2
    lower_half = shaped[..., :half_width]
    upper_half = shaped[..., half_width:]
    cos_rows = cos_tab[:, None, :]
    sin_rows = sin_tab[:, None, :]
    return jnp.concatenate(
        [
            lower_half * cos_rows - upper_half * sin_rows,
            upper_half * cos_rows + lower_half * sin_rows,
        ],
        axis=-1,
    )


def sequence_layout(lengths_row, count):
    seq_ends = jnp.cumsum(lengths_row)
    places = jnp.arange(count, dtype=jnp.int32)
    passed = (places[:, None] >= seq_ends[None, :]).astype(jnp.int32)
    seq_ids = jnp.sum(passed, axis=1)
    starts = jnp.sum(passed * lengths_row[None, :], axis=1)
    return (seq_ids, places - starts)


def pair_ranks(pair_expert, order_keys, expert_hot, expert_axis):
    pair_total = pair_expert.shape[0]
    keyed = pair_expert * pair_total + order_keys
    sorter = jnp.argsort(keyed)
    sorted_ids = pair_expert[sorter]
    counts = jnp.sum(expert_hot.astype(jnp.int32), axis=0)
    starts = jnp.cumsum(counts) - counts
    start_of = jnp.sum(
        jnp.where(sorted_ids[:, None] == expert_axis[None, :], starts[None, :], 0), axis=1
    )
    positions = jnp.arange(pair_total, dtype=jnp.int32) - start_of
    ranks = jnp.zeros((pair_total,), jnp.int32).at[sorter].set(positions)
    return (ranks, counts)


def add_counts(earlier, later):
    return earlier + later


def expert_work(rows_in, grads_in, weights):
    gate_up = jnp.einsum("rd,dcf->rcf", rows_in, weights[:, :2], preferred_element_type=jnp.float32)
    gate_pre = gate_up[:, 0]
    up_pre = gate_up[:, 1]
    sigmoid_gate = jax.nn.sigmoid(gate_pre)
    silu_gate = gate_pre * sigmoid_gate
    active = (silu_gate * up_pre).astype(jnp.bfloat16)
    partial_out = jnp.einsum("rf,df->rd", active, weights[:, 2], preferred_element_type=jnp.float32)
    d_active = jnp.einsum("rd,df->rf", grads_in, weights[:, 2], preferred_element_type=jnp.float32)
    d_gate = d_active * up_pre * sigmoid_gate * (1.0 + gate_pre * (1.0 - sigmoid_gate))
    d_up = d_active * silu_gate
    d_pair = jnp.stack([d_gate, d_up], axis=1).astype(jnp.bfloat16)
    d_rows = jnp.einsum("rcf,dcf->rd", d_pair, weights[:, :2], preferred_element_type=jnp.float32)
    grad_in = jnp.einsum("rd,rcf->dcf", rows_in, d_pair, preferred_element_type=jnp.float32)
    grad_down = jnp.einsum("rd,rf->df", grads_in, active, preferred_element_type=jnp.float32)
    grad_all = jnp.concatenate([grad_in, grad_down[:, None, :]], axis=1)
    return (partial_out.astype(jnp.bfloat16), d_rows.astype(jnp.bfloat16), grad_all)


def body(
    tokens,
    out_grad,
    seq_lengths,
    dest_index,
    routes,
    pair_order,
    norm1_gain,
    w_query,
    w_key,
    w_value,
    q_gain,
    k_gain,
    w_output,
    norm2_gain,
    w_router,
    expert_w,
):
    groups = lax.axis_size("expert")
    tensor_count = lax.axis_size("tensor")
    group_id = lax.axis_index("expert")
    tensor_id = lax.axis_index("tensor")
    tok_count, col_count = tokens.shape
    width = col_count * tensor_count
    move_rows = tok_count // groups
    dest_all = lax.all_gather(dest_index, "expert", axis=0, tiled=True)
    sorter = jnp.argsort(dest_index)
    got_x, got_dy = (
        lax.all_to_all(
            tokens[sorter].reshape(groups, move_rows, col_count),
            "expert",
            split_axis=0,
            concat_axis=0,
            tiled=True,
        ),
        lax.all_to_all(
            out_grad[sorter].reshape(groups, move_rows, col_count),
            "expert",
            split_axis=0,
            concat_axis=0,
            tiled=True,
        ),
    )
    sorted_all = jnp.sort(dest_all.reshape(groups, tok_count), axis=1)
    mine = (
        lax.dynamic_slice_in_dim(sorted_all, group_id * move_rows, move_rows, 1)
        - group_id * tok_count
    )
    mine_flat = mine.reshape(-1)
    local_x = (
        jnp.zeros((tok_count, col_count), jnp.bfloat16)
        .at[mine_flat]
        .set(got_x.reshape(-1, col_count))
    )
    local_dy = (
        jnp.zeros((tok_count, col_count), jnp.bfloat16)
        .at[mine_flat]
        .set(got_dy.reshape(-1, col_count))
    )
    full_x, full_dy = (
        lax.all_gather(local_x, "tensor", axis=1, tiled=True),
        lax.all_gather(local_dy, "tensor", axis=1, tiled=True),
    )
    x_float = full_x.astype(jnp.float32)
    dy_float = full_dy.astype(jnp.float32)
    seq_ids, positions = sequence_layout(seq_lengths[0], tok_count)
    same_seq = seq_ids[:, None] == seq_ids[None, :]
    head_dim = q_gain.shape[0]
    heads_local = w_query.shape[1] // head_dim
    scale_attn = 1.0 / math.sqrt(head_dim)
    cos_tab, sin_tab = rope_tables(positions, head_dim)
    gain_one = norm1_gain.astype(jnp.float32)
    normed_float, norm_one_back = jax.vjp(rms_apply, x_float, gain_one)
    normed = normed_float.astype(jnp.bfloat16)
    q_raw = jnp.dot(normed, w_query, preferred_element_type=jnp.float32)
    k_raw = jnp.dot(normed, w_key, preferred_element_type=jnp.float32)
    v_raw = jnp.dot(normed, w_value, preferred_element_type=jnp.float32)

    def prep_pair(query_in, key_in, qgain_in, kgain_in):
        return (
            head_prep(query_in, qgain_in, cos_tab, sin_tab, heads_local),
            head_prep(key_in, kgain_in, cos_tab, sin_tab, heads_local),
        )

    rotated, prep_back = jax.vjp(
        prep_pair, q_raw, k_raw, q_gain.astype(jnp.float32), k_gain.astype(jnp.float32)
    )
    query_b = rotated[0].astype(jnp.bfloat16)
    key_b = rotated[1].astype(jnp.bfloat16)
    value_b = v_raw.reshape(tok_count, heads_local, head_dim).astype(jnp.bfloat16)
    scores = (
        jnp.einsum("qhd,khd->hqk", query_b, key_b, preferred_element_type=jnp.float32) * scale_attn
    )
    scores = jnp.where(same_seq[None], scores, mask_fill)
    peak = jnp.max(scores, axis=-1, keepdims=True)
    log_total = peak + jnp.log(jnp.sum(jnp.exp(scores - peak), axis=-1, keepdims=True))
    probs_b = jnp.exp(scores - log_total).astype(jnp.bfloat16)
    attended = (
        jnp.einsum("hqk,khd->qhd", probs_b, value_b, preferred_element_type=jnp.float32)
        .reshape(tok_count, heads_local * head_dim)
        .astype(jnp.bfloat16)
    )
    attn_part = jnp.dot(attended, w_output, preferred_element_type=jnp.float32)
    attn_full = lax.psum(attn_part, "tensor")
    resid = x_float + attn_full
    gain_two = norm2_gain.astype(jnp.float32)
    mixed_float, norm_two_back = jax.vjp(rms_apply, resid, gain_two)
    mixed_b = mixed_float.astype(jnp.bfloat16)
    logits = jnp.dot(mixed_b, w_router, preferred_element_type=jnp.float32)
    expert_count = w_router.shape[1]
    top_count = routes.shape[1]
    expert_axis = jnp.arange(expert_count, dtype=jnp.int32)
    route_hot = routes[:, :, None] == expert_axis[None, None, :]
    chosen = jnp.sum(jnp.where(route_hot, logits[:, None, :], 0.0), axis=-1)
    chosen_peak = jnp.max(chosen, axis=-1, keepdims=True)
    chosen_exp = jnp.exp(chosen - chosen_peak)
    gates = chosen_exp / jnp.sum(chosen_exp, axis=-1, keepdims=True)
    pair_expert = routes.reshape(-1)
    pair_total = tok_count * top_count
    expert_hot = pair_expert[:, None] == expert_axis[None, :]
    ranks, counts = pair_ranks(pair_expert, pair_order[0], expert_hot, expert_axis)
    offsets = prefix(counts, "expert", add_counts, jnp.zeros_like(counts))
    capacity = 5 * tok_count * groups * top_count // (4 * expert_count)
    most_rows = 3 * tok_count * top_count // (2 * expert_count)
    slot_global = (
        jnp.sum(jnp.where(expert_hot, offsets[None, :], 0), axis=1).astype(jnp.int32) + ranks
    )
    kept = slot_global < capacity
    keep_mask = kept.reshape(tok_count, top_count).astype(jnp.float32)
    gate_eff = gates * keep_mask
    slot_index = pair_expert * most_rows + ranks
    target = jnp.where(kept, slot_index, expert_count * most_rows)
    slot_source = (
        jnp.full((expert_count * most_rows,), pair_total, jnp.int32)
        .at[target]
        .set(jnp.arange(pair_total, dtype=jnp.int32), mode="drop")
    )
    filled = slot_source < pair_total
    safe_source = jnp.minimum(slot_source, pair_total - 1)
    slot_token = safe_source // top_count
    slot_gate = jnp.where(filled, gate_eff.reshape(-1)[safe_source], 0.0)
    send_rows = jnp.where(
        filled[:, None], mixed_b[slot_token], jnp.zeros((), jnp.bfloat16)
    ).reshape(expert_count, most_rows, width)
    send_grads = (
        (slot_gate[:, None] * dy_float[slot_token])
        .astype(jnp.bfloat16)
        .reshape(expert_count, most_rows, width)
    )
    recv_rows, recv_grads = (
        lax.all_to_all(send_rows, "expert", split_axis=0, concat_axis=1, tiled=True),
        lax.all_to_all(send_grads, "expert", split_axis=0, concat_axis=1, tiled=True),
    )
    back_out, back_rows, expert_grad = jax.vmap(expert_work)(recv_rows, recv_grads, expert_w)
    safe_slot = jnp.where(kept, slot_index, 0)
    kept_float = kept.astype(jnp.float32)[:, None]
    ret_out, ret_rows = (
        lax.all_to_all(back_out, "expert", split_axis=1, concat_axis=0, tiled=True),
        lax.all_to_all(back_rows, "expert", split_axis=1, concat_axis=0, tiled=True),
    )
    pair_out = (ret_out.reshape(-1, width)[safe_slot].astype(jnp.float32) * kept_float).reshape(
        tok_count, top_count, width
    )
    pair_rows = (ret_rows.reshape(-1, width)[safe_slot].astype(jnp.float32) * kept_float).reshape(
        tok_count, top_count, width
    )
    moe_part = jnp.einsum("pk,pkd->pd", gate_eff, pair_out)
    mixed_part = jnp.sum(pair_rows, axis=1)
    dgate_part = jnp.einsum("pd,pkd->pk", dy_float, pair_out)
    moe_full, mixed_experts, dgate_full = (
        lax.psum(moe_part.astype(jnp.bfloat16), "tensor").astype(jnp.float32),
        lax.psum(mixed_part.astype(jnp.bfloat16), "tensor").astype(jnp.float32),
        lax.psum(dgate_part.astype(jnp.bfloat16), "tensor").astype(jnp.float32),
    )
    out_full = resid + moe_full
    out_slice = lax.dynamic_slice_in_dim(out_full, tensor_id * col_count, col_count, 1).astype(
        jnp.bfloat16
    )
    d_gates = dgate_full * keep_mask
    d_chosen = gates * (d_gates - jnp.sum(gates * d_gates, axis=1, keepdims=True))
    d_logits = jnp.sum(jnp.where(route_hot, d_chosen[:, :, None], 0.0), axis=1).astype(jnp.bfloat16)
    router_grad = jnp.einsum("pd,pe->de", mixed_b, d_logits, preferred_element_type=jnp.float32)
    d_mixed = mixed_experts + jnp.einsum(
        "pe,de->pd", d_logits, w_router, preferred_element_type=jnp.float32
    )
    d_resid_norm, gain_two_grad = norm_two_back(d_mixed)
    d_resid = dy_float + d_resid_norm
    d_resid_b = d_resid.astype(jnp.bfloat16)
    out_proj_grad = jnp.einsum("pa,pd->ad", attended, d_resid_b, preferred_element_type=jnp.float32)
    d_att = (
        jnp.einsum("pd,ad->pa", d_resid_b, w_output, preferred_element_type=jnp.float32)
        .astype(jnp.bfloat16)
        .reshape(tok_count, heads_local, head_dim)
    )
    scores_again = (
        jnp.einsum("qhd,khd->hqk", query_b, key_b, preferred_element_type=jnp.float32) * scale_attn
    )
    scores_again = jnp.where(same_seq[None], scores_again, mask_fill)
    probs_again = jnp.exp(scores_again - log_total)
    probs_again_b = probs_again.astype(jnp.bfloat16)
    d_probs = jnp.einsum("qhd,khd->hqk", d_att, value_b, preferred_element_type=jnp.float32)
    delta = jnp.sum(probs_again * d_probs, axis=-1, keepdims=True)
    d_scores = (probs_again * (d_probs - delta)).astype(jnp.bfloat16)
    d_query = (
        jnp.einsum("hqk,khd->qhd", d_scores, key_b, preferred_element_type=jnp.float32) * scale_attn
    )
    d_key = (
        jnp.einsum("hqk,qhd->khd", d_scores, query_b, preferred_element_type=jnp.float32)
        * scale_attn
    )
    d_value = (
        jnp.einsum("hqk,qhd->khd", probs_again_b, d_att, preferred_element_type=jnp.float32)
        .reshape(tok_count, -1)
        .astype(jnp.bfloat16)
    )
    d_qraw, d_kraw, qgain_part, kgain_part = prep_back((d_query, d_key))
    d_qraw_b = d_qraw.astype(jnp.bfloat16)
    d_kraw_b = d_kraw.astype(jnp.bfloat16)
    d_normed = jnp.einsum("pa,da->pd", d_qraw_b, w_query, preferred_element_type=jnp.float32)
    d_normed = d_normed + jnp.einsum(
        "pa,da->pd", d_kraw_b, w_key, preferred_element_type=jnp.float32
    )
    d_normed = d_normed + jnp.einsum(
        "pa,da->pd", d_value, w_value, preferred_element_type=jnp.float32
    )
    query_grad = jnp.einsum("pd,pa->da", normed, d_qraw_b, preferred_element_type=jnp.float32)
    key_grad = jnp.einsum("pd,pa->da", normed, d_kraw_b, preferred_element_type=jnp.float32)
    value_grad = jnp.einsum("pd,pa->da", normed, d_value, preferred_element_type=jnp.float32)
    d_normed_full, qgain_sum, kgain_sum = (
        lax.psum(d_normed.astype(jnp.bfloat16), "tensor").astype(jnp.float32),
        lax.psum(qgain_part.astype(jnp.bfloat16), "tensor").astype(jnp.float32),
        lax.psum(kgain_part.astype(jnp.bfloat16), "tensor").astype(jnp.float32),
    )
    d_x_norm, gain_one_grad = norm_one_back(d_normed_full)
    d_tokens = d_resid + d_x_norm
    summed = (
        lax.psum(query_grad.astype(jnp.bfloat16), "expert").astype(jnp.float32),
        lax.psum(key_grad.astype(jnp.bfloat16), "expert").astype(jnp.float32),
        lax.psum(value_grad.astype(jnp.bfloat16), "expert").astype(jnp.float32),
        lax.psum(out_proj_grad.astype(jnp.bfloat16), "expert").astype(jnp.float32),
        lax.psum(router_grad.astype(jnp.bfloat16), "expert").astype(jnp.float32),
        lax.psum(gain_one_grad.astype(jnp.bfloat16), "expert").astype(jnp.float32),
        lax.psum(gain_two_grad.astype(jnp.bfloat16), "expert").astype(jnp.float32),
        lax.psum(qgain_sum.astype(jnp.bfloat16), "expert").astype(jnp.float32),
        lax.psum(kgain_sum.astype(jnp.bfloat16), "expert").astype(jnp.float32),
    )
    dx_slice = lax.dynamic_slice_in_dim(d_tokens, tensor_id * col_count, col_count, 1).astype(
        jnp.bfloat16
    )
    back_x, back_dx = (
        lax.all_to_all(
            out_slice[mine_flat].reshape(groups, move_rows, col_count),
            "expert",
            split_axis=0,
            concat_axis=0,
            tiled=True,
        ),
        lax.all_to_all(
            dx_slice[mine_flat].reshape(groups, move_rows, col_count),
            "expert",
            split_axis=0,
            concat_axis=0,
            tiled=True,
        ),
    )
    block_out = (
        jnp.zeros((tok_count, col_count), jnp.bfloat16)
        .at[sorter]
        .set(back_x.reshape(-1, col_count))
    )
    grad_tokens = (
        jnp.zeros((tok_count, col_count), jnp.bfloat16)
        .at[sorter]
        .set(back_dx.reshape(-1, col_count))
    )
    return (
        block_out,
        grad_tokens,
        summed[5],
        summed[0],
        summed[1],
        summed[2],
        summed[7],
        summed[8],
        summed[3],
        summed[6],
        summed[4],
        expert_grad,
    )


def solution(mesh):
    in_specs = (
        P("expert", "tensor"),
        P("expert", "tensor"),
        P("expert", None),
        P("expert"),
        P("expert", None),
        P("expert", None),
        P(),
        P(None, "tensor"),
        P(None, "tensor"),
        P(None, "tensor"),
        P(),
        P(),
        P("tensor", None),
        P(),
        P(),
        P("expert", None, None, "tensor"),
    )
    out_specs = (
        P("expert", "tensor"),
        P("expert", "tensor"),
        P(),
        P(None, "tensor"),
        P(None, "tensor"),
        P(None, "tensor"),
        P(),
        P(),
        P("tensor", None),
        P(),
        P(),
        P("expert", None, None, "tensor"),
    )
    return jax.shard_map(body, mesh=mesh, in_specs=in_specs, out_specs=out_specs, check_vma=False)
```

profile of v0, /device:TPU:1, one launch (start us, length us, event | category | flops | bytes accessed | tf_op | source)
XLA Modules:
  0.0 1445.9 jit_solution(9418103351728467371)
XLA Ops:
  7.3 27.1 %all-gather.1 = s32[32,1,256]{2,1,0:T(1,128)S(1)} all-gather(s32[1,1,256]{2,1,0:T(1,128)} %bitcast.239), channel_id=1, replica_groups=mesh['expert'=32,'tensor'=4] {'expert'}, dimensions={0}, use_global_device_ids=true | all-gather | bytes 33792 | tf_op jit(solution)/shard_map/all_gather | solution.py:126
  64.2 11.8 gather_fusion.1
  77.6 10.9 all-reduce.4
  138.3 41.4 %all-reduce.14.cloned.1.call-done = f32[256,2048]{1,0:T(8,128)} async-done(((f32[256,2048]{1,0:T(8,128)}), f32[256,2048]{1,0:T(8,128)}) %all-reduce.14.cloned.1.call-update) | async-done | bytes 2097168 | tf_op jit(solution)/shard_map/psum | solution.py:204
  183.3 15.7 %gather_fusion.2 = bf16[3072,2048]{1,0:T(8,128)(2,1)} fusion(bf16[256,2048]{1,0:T(8,128)(2,1)S(1)} %multiply_convert_fusion.4, s32[3072]{0:T(1024)S(1)} %get-tuple-element.93), kind=kCustom, calls=%fused_computation.2 | custom fusion | bytes 25178112 | tf_op jit(solution)/shard_map/gather | solution.py:243
  199.0 10.7 broadcast_select_fusion
  219.6 172.7 %all-to-all-done.1 = bf16[64,48,2048]{2,1,0:T(8,128)(2,1)} async-done(((bf16[64,48,2048]{2,1,0:T(8,128)(2,1)}), bf16[64,48,2048]{2,1,0:T(8,128)(2,1)}, u32[]{:S(2)}, u32[]{:S(2)}) %all-to-all-start.1) | async-done | bytes 12582944 | tf_op jit(solution)/shard_map/all_to_all | solution.py:251
  392.3 30.1 %all-to-all-start.4 = ((bf16[32,8,512]{2,1,0:T(8,128)(2,1)}), bf16[32,8,512]{2,1,0:T(8,128)(2,1)S(1)}, u32[]{:S(2)}, u32[]{:S(2)}) async-start(bf16[32,8,512]{2,1,0:T(8,128)(2,1)} %bitcast.235), calls=%async_computation.4 | async-start | bytes 524288 | tf_op jit(solution)/shard_map/all_to_all | solution.py:136
  429.0 10.1 fusion.77
  451.3 23.6 %copy.228 = bf16[2,1536,2048]{2,0,1:T(2,128)(2,1)} copy(bf16[2,1536,2048]{2,1,0:T(8,128)(2,1)} %convolution_convert_fusion) | data formatting | bytes 25165824 | tf_op jit(solution)/shard_map/vmap()/convert_element_type | solution.py:98
  485.9 21.9 %all-gather.7.cloned.1.call-done = bf16[256,2048]{1,0:T(8,128)(2,1)} async-done(((bf16[256,512]{1,0:T(8,128)(2,1)}), bf16[256,2048]{1,0:T(8,128)(2,1)}) %all-gather.7.cloned.1.call-update) | async-done | bytes 1048592 | tf_op jit(solution)/shard_map/all_gather | solution.py:162
  510.6 25.9 %gather_fusion.7 = f32[3072,2048]{1,0:T(8,128)} fusion(f32[256,2048]{1,0:T(8,128)} %convert_element_type.232, s32[3072]{0:T(1024)} %copy-done.51), kind=kCustom, calls=%fused_computation.7 | custom fusion | bytes 50343936 | tf_op jit(solution)/shard_map/gather | solution.py:246
  537.6 119.5 %all-to-all-done.2 = bf16[2,1536,2048]{2,0,1:T(2,128)(2,1)} async-done(((bf16[2,1536,2048]{2,0,1:T(2,128)(2,1)}), bf16[2,1536,2048]{2,0,1:T(2,128)(2,1)}, u32[]{:S(2)}, u32[]{:S(2)}) %all-to-all-start.2) | async-done | bytes 12582944 | tf_op jit(solution)/shard_map/all_to_all | solution.py:258
  657.1 13.3 copy.229
  670.4 22.6 %gather_fusion.3 = bf16[2048,2048]{1,0:T(8,128)(2,1)} fusion(bf16[3072,2048]{1,0:T(8,128)(2,1)} %bitcast.210, s32[2048]{0:T(1024)S(1)} %copy-done.54), kind=kCustom, calls=%fused_computation.3 | custom fusion | bytes 16785408 | tf_op jit(solution)/shard_map/gather | solution.py:261
  693.0 10.1 fusion.1
  715.6 30.7 %gather_fusion.6 = f32[3072]{0:T(1024)} fusion(f32[2048]{0:T(1024)S(1)} %broadcast_select_fusion.2, s32[3072]{0:T(1024)} %get-tuple-element.92), kind=kCustom, calls=%fused_computation.6 | custom fusion | bytes 36864 | tf_op jit(solution)/shard_map/gather | solution.py:241
  749.0 9.3 multiply_convert_fusion
  758.3 172.4 %all_to_all.86 = bf16[64,48,2048]{2,1,0:T(8,128)(2,1)S(1)} all-to-all(bf16[64,48,2048]{2,1,0:T(8,128)(2,1)S(1)} %multiply_convert_fusion), channel_id=1, replica_groups=mesh['expert'=32,'tensor'=4] {'expert'}, dimensions={0} | all-to-all | bytes 25165824 | tf_op jit(solution)/shard_map/all_to_all | solution.py:252
  935.8 11.2 fusion.21
  947.0 12.6 bitcast_convert_fusion
  959.6 21.2 %copy.233 = bf16[2,1536,2048]{2,0,1:T(2,128)(2,1)S(1)} copy(bf16[2,1536,2048]{2,1,0:T(8,128)(2,1)} %bitcast_convert_fusion) | data formatting | bytes 25165824 | tf_op jit(solution)/shard_map/vmap()/convert_element_type | solution.py:98
  980.8 144.7 %all_to_all.87 = bf16[2,1536,2048]{2,0,1:T(2,128)(2,1)S(1)} all-to-all(bf16[2,1536,2048]{2,0,1:T(2,128)(2,1)S(1)} %copy.233), channel_id=1, replica_groups=mesh['expert'=32,'tensor'=4] {'expert'}, dimensions={1} | all-to-all | bytes 25165824 | tf_op jit(solution)/shard_map/all_to_all | solution.py:259
  1133.4 22.5 %gather_fusion.8 = bf16[2048,2048]{1,0:T(8,128)(2,1)} fusion(bf16[3072,2048]{1,0:T(8,128)(2,1)} %bitcast.211, s32[2048]{0:T(1024)S(1)} %copy-done.55), kind=kCustom, calls=%fused_computation.8 | custom fusion | bytes 16785408 | tf_op jit(solution)/shard_map/gather | solution.py:264
  1156.0 12.3 fusion
  1177.1 31.4 %all-reduce.16.cloned.1.call-done = bf16[256,2048]{1,0:T(8,128)(2,1)} async-done(((bf16[256,2048]{1,0:T(8,128)(2,1)}), bf16[256,2048]{1,0:T(8,128)(2,1)}) %all-reduce.16.cloned.1.call-update) | async-done | bytes 1048592 | tf_op jit(solution)/shard_map/psum | solution.py:272
  1250.2 12.2 convolution_bitcast_fusion
  1262.4 12.9 fusion.8
  1275.3 21.2 %all-reduce.20.cloned.1.call-done = (bf16[256,2048]{1,0:T(8,128)(2,1)}, bf16[256,2048]{1,0:T(8,128)(2,1)}) async-done(((bf16[256,2048]{1,0:T(8,128)(2,1)}, bf16[256,2048]{1,0:T(8,128)(2,1)}), (bf16[256,2048]{1,0:T(8,128)(2,1)}, bf16[256,2048]{1,0:T(8,128)(2,1)})) %all-reduce.20.cloned.1.call-update) | async-done | bytes 2097168 | tf_op jit(solution)/shard_map/psum | solution.py:271
  1320.9 11.5 pad_maximum_fusion
  1339.2 65.7 %all-reduce.5 = (bf16[2048]{0:T(1024)(128)(2,1)S(1)}, bf16[128]{0:T(256)(128)(2,1)S(1)}, bf16[128]{0:T(256)(128)(2,1)S(1)}, bf16[2048]{0:T(1024)(128)(2,1)S(1)}) all-reduce(bf16[2048]{0:T(1024)(128)(2,1)S(1)} %get-tuple-element.42, bf16[128]{0:T(256)(128)(2,1)S(1)} %get-tuple-element.67, ...), channel_id=1, replica_groups=mesh['expert'=32,'tensor'=4] {'expert'}, use_global_device_ids=true, to_apply=%region_41.42 | all-reduce | flops 4352 | bytes 17408 | tf_op jit(solution)/shard_map/psum | solution.py:342
  1411.7 14.0 all-reduce.18.cloned.1.call-done
  (366 shorter events, 257.1 us)
Async XLA Ops:
  7.2 109.9 %copy-start = (bf16[512,2048]{1,0:T(8,128)(2,1)S(1)}, bf16[512,2048]{1,0:T(8,128)(2,1)}, u32[]{:S(2)}) copy-start(bf16[512,2048]{1,0:T(8,128)(2,1)} %param.30) | copy-start | bytes 6291460
  7.2 39.7 %copy-start.83 = (bf16[2048]{0:T(1024)(128)(2,1)S(1)}, bf16[2048]{0:T(1024)(128)(2,1)}, u32[]{:S(2)}) copy-start(bf16[2048]{0:T(1024)(128)(2,1)} %param.24) | copy-start | bytes 12292
  7.2 39.7 %copy-start.90 = (bf16[128]{0:T(256)(128)(2,1)S(1)}, bf16[128]{0:T(256)(128)(2,1)}, u32[]{:S(2)}) copy-start(bf16[128]{0:T(256)(128)(2,1)} %param.28) | copy-start | bytes 772
  7.2 40.2 %copy-start.91 = (bf16[128]{0:T(256)(128)(2,1)S(1)}, bf16[128]{0:T(256)(128)(2,1)}, u32[]{:S(2)}) copy-start(bf16[128]{0:T(256)(128)(2,1)} %param.29) | copy-start | bytes 772
  7.2 40.8 %copy-start.89 = (s32[1,3]{1,0:T(1,128)S(1)}, s32[1,3]{1,0:T(1,128)}, u32[]{:S(2)}) copy-start(s32[1,3]{1,0:T(1,128)} %param.20) | copy-start | bytes 40
  7.2 41.0 %copy-start.56 = (s32[256,8]{0,1:T(8,128)S(1)}, s32[256,8]{0,1:T(8,128)}, u32[]{:S(2)}) copy-start(s32[256,8]{0,1:T(8,128)} %param.22) | copy-start | bytes 24580
  7.2 41.3 %sort.46.cloned.1.call-start = ((), (), s32[]{:S(2)}) async-start(), calls=%async_computation.14 | async-start | bytes 98336 | tf_op jit(solution)/shard_map/jit(sort)/sort | solution.py:144
  41.8 14.0 all-to-all-start
  46.8 45.1 %all-gather.5.cloned.1.call-start = ((), (), s32[]{:S(2)}) async-start(), calls=%async_computation.8 | async-start | bytes 1310720 | tf_op jit(solution)/shard_map/all_gather | solution.py:161
  46.9 66.5 %copy-start.46 = (f32[2048]{0:T(1024)}, f32[2048]{0:T(1024)S(1)}, u32[]{:S(2)}) copy-start(f32[2048]{0:T(1024)S(1)} %convert_element_type.210) | copy-start | bytes 24580
  49.4 26.6 %copy-start.87 = (s32[256,1]{0,1:T(1,128)}, s32[256,1]{0,1:T(1,128)S(1)}, u32[]{:S(2)}) copy-start(s32[256,1]{0,1:T(1,128)S(1)} %compare_select_fusion.4) | copy-start | bytes 3076
  58.0 121.7 %all-reduce.14.cloned.1.call-start = ((), (), s32[]{:S(2)}) async-start(), calls=%async_computation.9 | async-start | bytes 4194304 | tf_op jit(solution)/shard_map/psum | solution.py:204
  129.5 355.5 %copy-start.71 = (pred[2048]{0:T(1024)(128)(4,1)}, pred[2048]{0:T(1024)(128)(4,1)S(1)}, u32[]{:S(2)}) copy-start(pred[2048]{0:T(1024)(128)(4,1)S(1)} %get-tuple-element.74) | copy-start | bytes 6148
  137.6 44.1 %copy-start.48 = (s32[3072]{0:T(1024)}, s32[3072]{0:T(1024)S(1)}, u32[]{:S(2)}) copy-start(s32[3072]{0:T(1024)S(1)} %scatter_custom_fusion.2) | copy-start | bytes 36868
  138.3 45.0 %copy-start.51 = (s32[3072]{0:T(1024)}, s32[3072]{0:T(1024)S(1)}, u32[]{:S(2)}) copy-start(s32[3072]{0:T(1024)S(1)} %get-tuple-element.93) | copy-start | bytes 36868
  138.3 44.7 %copy-start.49 = (f32[2048]{0:T(1024)S(1)}, f32[2048]{0:T(1024)}, u32[]{:S(2)}) copy-start(f32[2048]{0:T(1024)} %convert_element_type.223) | copy-start | bytes 24580
  183.3 353.1 %copy-start.1 = (bf16[256,2048]{1,0:T(8,128)(2,1)}, bf16[256,2048]{1,0:T(8,128)(2,1)S(1)}, u32[]{:S(2)}) copy-start(bf16[256,2048]{1,0:T(8,128)(2,1)S(1)} %multiply_convert_fusion.4) | copy-start | bytes 3145732
  209.7 182.5 %all-to-all-start.1 = ((bf16[64,48,2048]{2,1,0:T(8,128)(2,1)}), bf16[64,48,2048]{2,1,0:T(8,128)(2,1)}, u32[]{:S(2)}, u32[]{:S(2)}) async-start(bf16[64,48,2048]{2,1,0:T(8,128)(2,1)} %broadcast_select_fusion), calls=%async_computation.1 | async-start | bytes 25165824 | tf_op jit(solution)/shard_map/all_to_all | solution.py:251
  392.3 82.7 %all-to-all-start.4 = ((bf16[32,8,512]{2,1,0:T(8,128)(2,1)}), bf16[32,8,512]{2,1,0:T(8,128)(2,1)S(1)}, u32[]{:S(2)}, u32[]{:S(2)}) async-start(bf16[32,8,512]{2,1,0:T(8,128)(2,1)} %bitcast.235), calls=%async_computation.4 | async-start | bytes 524288 | tf_op jit(solution)/shard_map/all_to_all | solution.py:136
  475.0 182.1 %all-to-all-start.2 = ((bf16[2,1536,2048]{2,0,1:T(2,128)(2,1)}), bf16[2,1536,2048]{2,0,1:T(2,128)(2,1)}, u32[]{:S(2)}, u32[]{:S(2)}) async-start(bf16[2,1536,2048]{2,0,1:T(2,128)(2,1)} %copy.228), calls=%async_computation.2 | async-start | bytes 25165824 | tf_op jit(solution)/shard_map/all_to_all | solution.py:258
  482.5 25.3 %all-gather.7.cloned.1.call-start = ((), (), s32[]{:S(2)}) async-start(), calls=%async_computation.10 | async-start | bytes 1310720 | tf_op jit(solution)/shard_map/all_gather | solution.py:162
  484.8 723.6 %all-reduce.16.cloned.1.call-start = ((), (), s32[]{:S(2)}) async-start(), calls=%async_computation.11 | async-start | bytes 2097152 | tf_op jit(solution)/shard_map/psum | solution.py:272
  510.6 26.3 %copy-start.57 = (s32[256,8]{0,1:T(8,128)S(1)}, s32[256,8]{0,1:T(8,128)}, u32[]{:S(2)}) copy-start(s32[256,8]{0,1:T(8,128)} %param.22) | copy-start | bytes 24580
  537.0 133.4 %copy-start.77 = (f32[256]{0:T(256)}, f32[256]{0:T(256)S(1)}, u32[]{:S(2)}) copy-start(f32[256]{0:T(256)S(1)} %reduce_max.19) | copy-start | bytes 3076
  758.3 177.5 %slice-start = ((s8[6291456]{0:T(1024)(128)(4,1)}), s8[4194304]{0:T(1024)(128)(4,1)S(1)}, s32[]{:S(2)}) async-start(s8[6291456]{0:T(1024)(128)(4,1)} %bitcast.220), calls=%async_computation.16 | async-start | bytes 8388608
  1168.2 128.3 %all-reduce.20.cloned.1.call-start = ((), (), s32[]{:S(2)}) async-start(), calls=%async_computation.13 | async-start | bytes 4194304 | tf_op jit(solution)/shard_map/psum | solution.py:271
  1175.4 33.1 %copy-start.50 = (f32[2048]{0:T(1024)S(1)}, f32[2048]{0:T(1024)}, u32[]{:S(2)}) copy-start(f32[2048]{0:T(1024)} %convert_element_type.223) | copy-start | bytes 24580
  1175.4 33.1 %copy-start.73 = (f32[256]{0:T(256)S(1)}, f32[256]{0:T(256)}, u32[]{:S(2)}) copy-start(f32[256]{0:T(256)} %copy-done.72) | copy-start | bytes 3076
  1177.1 34.3 %copy-start.79 = (f32[256]{0:T(256)S(1)}, f32[256]{0:T(256)}, u32[]{:S(2)}) copy-start(f32[256]{0:T(256)} %copy-done.78) | copy-start | bytes 3076
  1235.3 190.4 %all-reduce.18.cloned.1.call-start = ((), (), s32[]{:S(2)}) async-start(), calls=%async_computation.12 | async-start | bytes 17301504 | tf_op jit(solution)/shard_map/psum | solution.py:337
  1299.5 17.7 %all-to-all-start.3 = ((bf16[32,8,512]{2,1,0:T(8,128)(2,1)}), bf16[32,8,512]{2,1,0:T(8,128)(2,1)S(1)}, u32[]{:S(2)}, u32[]{:S(2)}) async-start(bf16[32,8,512]{2,1,0:T(8,128)(2,1)} %bitcast.234), calls=%async_computation.3 | async-start | bytes 524288 | tf_op jit(solution)/shard_map/all_to_all | solution.py:351
  1317.3 92.1 %all-to-all-start.7 = ((bf16[32,8,512]{2,1,0:T(8,128)(2,1)}), bf16[32,8,512]{2,1,0:T(8,128)(2,1)S(1)}, u32[]{:S(2)}, u32[]{:S(2)}) async-start(bf16[32,8,512]{2,1,0:T(8,128)(2,1)} %bitcast.51), calls=%async_computation.7 | async-start | bytes 524288 | tf_op jit(solution)/shard_map/all_to_all | solution.py:358
  (77 other events, 402.2 us)
Sparse Core Ops, SparseCore 0:
  35.2 3.2 sort.48.cloned.1.call-done
  58.1 20.2 all-gather.4
  119.2 60.4 all-reduce.13
  485.2 22.5 all-gather.6
  1168.4 40.0 all-reduce.15
  1235.4 61.0 all-reduce.19
  1300.6 125.0 all-reduce.17
  (1 shorter events, 0.0 us)
where the time goes:
time: 1450 us
  blocking collectives  435 us (30%)
  waiting for transfers between devices  433 us (30%)
  local copies, waits for them, and re-layouts  272 us (19%)
  matrix products  122 us (8%)
  other arithmetic  105 us (7%)
  starting transfers between devices  62.6 us (4%)
  between operations  16.5 us (1%)
    all_to_all x1, waiting for transfers between devices, body(): lax.all_to_all(send_rows, 'expert', split_axis=0, concat_axis=1, tiled=True)  173 us
    all_to_all x1, blocking collectives, body(): lax.all_to_all(send_grads, 'expert', split_axis=0, concat_axis=1, tiled=T...  172 us
    all_to_all x1, blocking collectives, body(): lax.all_to_all(back_rows, 'expert', split_axis=1, concat_axis=0, tiled=True)  145 us
    all_to_all x1, waiting for transfers between devices, body(): lax.all_to_all(back_out, 'expert', split_axis=1, concat_axis=0, tiled=True)  120 us
    psum x1, blocking collectives, body(): lax.psum(gain_one_grad.astype(jnp.bfloat16), 'expert').astype(jnp.float32)  65.7 us
    psum x1, waiting for transfers between devices, body(): attn_full = lax.psum(attn_part, 'tensor')  41.4 us
    psum x1, waiting for transfers between devices, body(): lax.psum(mixed_part.astype(jnp.bfloat16), 'tensor').astype(jnp.float32)  31.4 us
    gather x1, local copies, waits for them, and re-layouts, body(): slot_gate = jnp.where(filled, gate_eff.reshape(-1)[safe_source], 0.0)  30.7 us
  transfers between devices with their start and end apart: 12, of which 9 were waited for; matrix products, arithmetic and copies ran while one was open for 14% of the time, Pallas kernels for 0%

commit v1 on v0

v1 whole, which is shorter than its diff:
```python
import functools
import math

import jax
import jax.numpy as jnp
from jax import lax
from jax.experimental import pallas as pl
from jax.experimental.pallas import tpu as pltpu
from jax.sharding import PartitionSpec as P

norm_eps = 1e-06
rope_base = 10000.0
mask_fill = -1e30


def rms_apply(values, gain_vec):
    inverse = lax.rsqrt(jnp.mean(values * values, axis=-1, keepdims=True) + norm_eps)
    return values * inverse * gain_vec


def rope_tables(positions, width):
    half_width = width // 2
    steps_idx = jnp.arange(half_width, dtype=jnp.float32)
    freqs = jnp.exp(steps_idx * (-2.0 * math.log(rope_base) / width))
    angles = positions.astype(jnp.float32)[:, None] * freqs[None, :]
    return (jnp.cos(angles), jnp.sin(angles))


def head_prep(raw, gain_vec, cos_tab, sin_tab, heads):
    token_count = raw.shape[0]
    shaped = rms_apply(raw.reshape(token_count, heads, -1), gain_vec)
    half_width = shaped.shape[-1] // 2
    lower_half = shaped[..., :half_width]
    upper_half = shaped[..., half_width:]
    cos_rows = cos_tab[:, None, :]
    sin_rows = sin_tab[:, None, :]
    return jnp.concatenate(
        [
            lower_half * cos_rows - upper_half * sin_rows,
            upper_half * cos_rows + lower_half * sin_rows,
        ],
        axis=-1,
    )


def sequence_layout(lengths_row, count):
    seq_ends = jnp.cumsum(lengths_row)
    places = jnp.arange(count, dtype=jnp.int32)
    passed = (places[:, None] >= seq_ends[None, :]).astype(jnp.int32)
    seq_ids = jnp.sum(passed, axis=1)
    starts = jnp.sum(passed * lengths_row[None, :], axis=1)
    return (seq_ids, places - starts)


BF = jnp.bfloat16
F32 = jnp.float32


def dot(left, right, left_dim=1, right_dim=0):
    return lax.dot_general(
        left, right, (((left_dim,), (right_dim,)), ((), ())), preferred_element_type=F32
    )


def expert_kernel(side, per, rows_ref, grads_ref, w_ref, *rest):
    if side:
        y_in, dx_in = rest[:2]
        rest = rest[2:]
    y_ref, dx_ref, grad_ref, rows, rows_t, dys, dys_t, y_acc, dx_acc = rest
    step = pl.program_id(0)
    count = rows.shape[0]
    both = rows_ref.shape[0]

    def selector(shape, row_dim):
        place = lax.broadcasted_iota(jnp.int32, shape, row_dim)
        source = lax.broadcasted_iota(jnp.int32, shape, 1 - row_dim)
        return (place + (place // per + side) * per == source).astype(F32).astype(BF)

    @pl.when(step == 0)
    def _():
        pick = selector((count, both), 0)
        rows[...] = dot(pick, rows_ref[...]).astype(BF)
        dys[...] = dot(pick, grads_ref[...]).astype(BF)
        rows_t[...] = rows[...].T
        dys_t[...] = dys[...].T
        y_acc[...] = jnp.zeros_like(y_acc)
        dx_acc[...] = jnp.zeros_like(dx_acc)

    w_gate, w_up, w_down = w_ref[0, 0], w_ref[0, 1], w_ref[0, 2]
    gate = dot(rows[...], w_gate)
    up = dot(rows[...], w_up)
    d_act = dot(dys[...], w_down)
    sig = 1.0 / (1.0 + jnp.exp(-gate))
    silu = gate * sig
    act = (silu * up).astype(BF)
    d_gate = (d_act * up * sig * (1.0 + gate * (1.0 - sig))).astype(BF)
    d_up = (d_act * silu).astype(BF)
    y_acc[...] += dot(act, w_down, 1, 1)
    dx_acc[...] += dot(d_gate, w_gate, 1, 1) + dot(d_up, w_up, 1, 1)
    grad_ref[0, 0] = dot(rows_t[...], d_gate).astype(BF)
    grad_ref[0, 1] = dot(rows_t[...], d_up).astype(BF)
    grad_ref[0, 2] = dot(dys_t[...], act).astype(BF)

    @pl.when(step == pl.num_programs(0) - 1)
    def _():
        spread = selector((both, count), 1)
        y_all = dot(spread, y_acc[...].astype(BF)).astype(BF)
        dx_all = dot(spread, dx_acc[...].astype(BF)).astype(BF)
        if side:
            y_all = y_all + y_in[...]
            dx_all = dx_all + dx_in[...]
        y_ref[...] = y_all
        dx_ref[...] = dx_all


def expert_call(side, per, rows, grads, weights, earlier):
    quarters, _, width, hidden = weights.shape
    both = rows.shape[0]
    count = both // 2
    whole = pl.BlockSpec((both, width), lambda q: (0, 0), pipeline_mode=pl.Buffered(1))
    block = pl.BlockSpec((1, 3, width, hidden), lambda q: (q, 0, 0, 0))
    flops = 2 * 9 * count * width * hidden * quarters
    moved = 2 * (2 * weights.size + 4 * rows.size)
    return pl.pallas_call(
        functools.partial(expert_kernel, side, per),
        grid=(quarters,),
        out_shape=(
            jax.ShapeDtypeStruct((both, width), BF),
            jax.ShapeDtypeStruct((both, width), BF),
            jax.ShapeDtypeStruct(weights.shape, BF),
        ),
        in_specs=[whole, whole, block] + [whole] * len(earlier),
        out_specs=(whole, whole, block),
        scratch_shapes=[
            pltpu.VMEM((count, width), BF),
            pltpu.VMEM((width, count), BF),
            pltpu.VMEM((count, width), BF),
            pltpu.VMEM((width, count), BF),
            pltpu.VMEM((count, width), F32),
            pltpu.VMEM((count, width), F32),
        ],
        compiler_params=pltpu.CompilerParams(vmem_limit_bytes=60 * 1024 * 1024),
        cost_estimate=pl.CostEstimate(
            flops=flops, bytes_accessed=moved, transcendentals=count * hidden * quarters
        ),
        name=f"expert{side}",
    )(rows, grads, weights, *earlier)


def exchange(value, axis):
    return lax.all_to_all(value, axis, split_axis=0, concat_axis=0, tiled=True)


def gather_blocks(value, axis):
    return exchange(jnp.broadcast_to(value[None], (lax.axis_size(axis),) + value.shape), axis)


def side_by_side(blocks):
    return jnp.concatenate([blocks[t] for t in range(blocks.shape[0])], axis=1)


def column_blocks(value, count):
    return jnp.stack(jnp.split(value, count, axis=1))


def body(
    tokens,
    out_grad,
    seq_lengths,
    dest_index,
    routes,
    pair_order,
    norm1_gain,
    w_query,
    w_key,
    w_value,
    q_gain,
    k_gain,
    w_output,
    norm2_gain,
    w_router,
    expert_w,
):
    groups = lax.axis_size("expert")
    tensor_count = lax.axis_size("tensor")
    group_id = lax.axis_index("expert")
    tensor_id = lax.axis_index("tensor")
    tok_count, col_count = tokens.shape
    width = col_count * tensor_count
    move_rows = tok_count // groups
    expert_count = w_router.shape[1]
    top_count = routes.shape[1]
    local_experts = expert_w.shape[0]

    w_stored = jnp.transpose(expert_w, (0, 2, 1, 3))
    w_all = [lax.all_gather(w_stored[e], "tensor", axis=0) for e in range(local_experts)]

    routes_t = routes.T
    order_t = pair_order[0].reshape(tok_count, top_count).T
    pair_expert = routes_t.reshape(-1)
    pair_total = tok_count * top_count
    base = pair_expert * pair_total
    keyed = base + order_t.reshape(-1)
    before = (keyed[None, :] < keyed[:, None]) & (keyed[None, :] >= base[:, None])
    ranks = jnp.sum(before.astype(jnp.int32), axis=1).reshape(top_count, tok_count)
    expert_axis = jnp.arange(expert_count, dtype=jnp.int32)
    route_hot = routes_t[:, None, :] == expert_axis[None, :, None]
    counts = jnp.sum(route_hot.astype(F32), axis=(0, 2))

    places = jnp.arange(tok_count, dtype=jnp.int32)
    arrival_rank = jnp.sum((dest_index[None, :] < dest_index[:, None]).astype(jnp.int32), axis=1)
    by_rank = (arrival_rank[None, :] == places[:, None]).astype(BF)
    inner = jnp.broadcast_to((dest_index % tok_count).astype(BF)[:, None], (tok_count, 64))
    facts = jnp.broadcast_to(counts.astype(BF)[None, :], (tok_count, expert_count))
    outgoing = dot(by_rank, jnp.concatenate([tokens, out_grad, inner, facts], axis=1)).astype(BF)
    got = exchange(outgoing.reshape(groups, move_rows, -1), "expert")
    all_counts = got[:, 0, 2 * col_count + 64 :].astype(jnp.int32)
    lower = jnp.arange(groups, dtype=jnp.int32) < group_id
    offsets = jnp.sum(jnp.where(lower[:, None], all_counts, 0), axis=0)
    mine = got[:, :, 2 * col_count].astype(jnp.int32).reshape(-1)
    put = (mine[None, :] == places[:, None]).astype(BF)
    local = dot(put, got.reshape(tok_count, -1)[:, : 2 * col_count]).astype(BF)
    blocks = gather_blocks(local, "tensor")
    full_x = side_by_side(blocks[:, :, :col_count])
    full_dy = side_by_side(blocks[:, :, col_count:])
    x_float = full_x.astype(jnp.float32)
    dy_float = full_dy.astype(jnp.float32)
    seq_ids, positions = sequence_layout(seq_lengths[0], tok_count)
    same_seq = seq_ids[:, None] == seq_ids[None, :]
    head_dim = q_gain.shape[0]
    heads_local = w_query.shape[1] // head_dim
    scale_attn = 1.0 / math.sqrt(head_dim)
    cos_tab, sin_tab = rope_tables(positions, head_dim)
    gain_one = norm1_gain.astype(jnp.float32)
    normed_float, norm_one_back = jax.vjp(rms_apply, x_float, gain_one)
    normed = normed_float.astype(jnp.bfloat16)
    q_raw = jnp.dot(normed, w_query, preferred_element_type=jnp.float32)
    k_raw = jnp.dot(normed, w_key, preferred_element_type=jnp.float32)
    v_raw = jnp.dot(normed, w_value, preferred_element_type=jnp.float32)

    def prep_pair(query_in, key_in, qgain_in, kgain_in):
        return (
            head_prep(query_in, qgain_in, cos_tab, sin_tab, heads_local),
            head_prep(key_in, kgain_in, cos_tab, sin_tab, heads_local),
        )

    rotated, prep_back = jax.vjp(
        prep_pair, q_raw, k_raw, q_gain.astype(jnp.float32), k_gain.astype(jnp.float32)
    )
    query_b = rotated[0].astype(jnp.bfloat16)
    key_b = rotated[1].astype(jnp.bfloat16)
    value_b = v_raw.reshape(tok_count, heads_local, head_dim).astype(jnp.bfloat16)
    scores = (
        jnp.einsum("qhd,khd->hqk", query_b, key_b, preferred_element_type=jnp.float32) * scale_attn
    )
    scores = jnp.where(same_seq[None], scores, mask_fill)
    peak = jnp.max(scores, axis=-1, keepdims=True)
    log_total = peak + jnp.log(jnp.sum(jnp.exp(scores - peak), axis=-1, keepdims=True))
    probs_b = jnp.exp(scores - log_total).astype(jnp.bfloat16)
    attended = (
        jnp.einsum("hqk,khd->qhd", probs_b, value_b, preferred_element_type=jnp.float32)
        .reshape(tok_count, heads_local * head_dim)
        .astype(jnp.bfloat16)
    )
    attn_part = jnp.dot(attended, w_output, preferred_element_type=jnp.float32)
    attn_got = exchange(column_blocks(attn_part.astype(BF), tensor_count), "tensor")
    attn_sum = jnp.sum(attn_got.astype(F32), axis=0).astype(BF)
    attn_full = side_by_side(gather_blocks(attn_sum, "tensor")).astype(F32)
    resid = x_float + attn_full
    gain_two = norm2_gain.astype(jnp.float32)
    mixed_float, norm_two_back = jax.vjp(rms_apply, resid, gain_two)
    mixed_b = mixed_float.astype(jnp.bfloat16)
    logits_t = dot(w_router, mixed_b, 0, 1)
    chosen = jnp.sum(jnp.where(route_hot, logits_t[None], 0.0), axis=1)
    chosen_exp = jnp.exp(chosen - jnp.max(chosen, axis=0, keepdims=True))
    gates = chosen_exp / jnp.sum(chosen_exp, axis=0, keepdims=True)
    capacity = 5 * tok_count * groups * top_count // (4 * expert_count)
    most_rows = 3 * tok_count * top_count // (2 * expert_count)
    per = most_rows // tensor_count
    slot_global = jnp.sum(jnp.where(route_hot, offsets[None, :, None], 0), axis=1) + ranks
    kept = slot_global < capacity
    keep_mask = kept.astype(F32)
    gate_eff = gates * keep_mask

    slots = expert_count * per
    here = kept & (ranks % tensor_count == tensor_id)
    slot_of = jnp.where(here, routes_t * per + ranks // tensor_count, -1)
    slot_axis = jnp.arange(slots, dtype=jnp.int32)
    slot_hot = slot_of[:, None, :] == slot_axis[None, :, None]
    slot_pick = jnp.sum(slot_hot.astype(F32), axis=0).astype(BF)
    slot_weight = jnp.sum(jnp.where(slot_hot, gate_eff[:, None, :], 0.0), axis=0)
    slot_gate = jnp.sum(slot_weight, axis=1)
    send_rows = dot(slot_pick, mixed_b).astype(BF)
    slot_dy = dot(slot_pick, full_dy)
    send_grads = (slot_gate[:, None] * slot_dy).astype(BF)
    recv_rows, recv_grads = (
        exchange(value.reshape(groups, -1, width), "expert").reshape(slots, width)
        for value in (send_rows, send_grads)
    )
    earlier = ()
    expert_grads = []
    for e in range(local_experts):
        *earlier, partial = expert_call(e, per, recv_rows, recv_grads, w_all[e], earlier)
        expert_grads.append(lax.psum_scatter(partial, "tensor", scatter_dimension=0, tiled=False))
    ret_rows = exchange(earlier[1].reshape(groups, -1, width), "expert").reshape(slots, width)
    ret_out = exchange(earlier[0].reshape(groups, -1, width), "expert").reshape(slots, width)
    mixed_part = dot(slot_pick, ret_rows, 0, 0)
    weight_hi = slot_weight.astype(BF)
    weight_lo = (slot_weight - weight_hi.astype(F32)).astype(BF)
    moe_part = dot(weight_hi, ret_out, 0, 0) + dot(weight_lo, ret_out, 0, 0)
    dgate_slot = jnp.sum(slot_dy * ret_out.astype(F32), axis=1)
    dgate_part = jnp.sum(jnp.where(slot_hot, dgate_slot[None, :, None], 0.0), axis=1)
    dgate_block = jnp.pad(dgate_part.T.astype(BF), ((0, 0), (0, 128 - top_count)))
    leaving = jnp.concatenate(
        [
            column_blocks(moe_part.astype(BF), tensor_count),
            column_blocks(mixed_part.astype(BF), tensor_count),
            jnp.broadcast_to(dgate_block[None], (tensor_count,) + dgate_block.shape),
        ],
        axis=2,
    )
    summed_t = jnp.sum(exchange(leaving, "tensor").astype(F32), axis=0)
    moe_slice = summed_t[:, :col_count]
    mixed_slice = summed_t[:, col_count : 2 * col_count].astype(BF)
    dgate_full = summed_t[:, 2 * col_count : 2 * col_count + top_count].T
    mixed_experts = side_by_side(gather_blocks(mixed_slice, "tensor")).astype(F32)
    resid_slice = lax.dynamic_slice_in_dim(resid, tensor_id * col_count, col_count, 1)
    out_slice = (resid_slice + moe_slice).astype(BF)
    d_gates = dgate_full * keep_mask
    d_chosen = gates * (d_gates - jnp.sum(gates * d_gates, axis=0, keepdims=True))
    d_logits = jnp.sum(jnp.where(route_hot, d_chosen[:, None, :], 0.0), axis=0).astype(BF)
    router_grad = dot(mixed_b, d_logits, 0, 1)
    d_mixed = mixed_experts + dot(d_logits, w_router, 0, 1)
    d_resid_norm, gain_two_grad = norm_two_back(d_mixed)
    d_resid = dy_float + d_resid_norm
    d_resid_b = d_resid.astype(jnp.bfloat16)
    out_proj_grad = jnp.einsum("pa,pd->ad", attended, d_resid_b, preferred_element_type=jnp.float32)
    d_att = (
        jnp.einsum("pd,ad->pa", d_resid_b, w_output, preferred_element_type=jnp.float32)
        .astype(jnp.bfloat16)
        .reshape(tok_count, heads_local, head_dim)
    )
    scores_again = (
        jnp.einsum("qhd,khd->hqk", query_b, key_b, preferred_element_type=jnp.float32) * scale_attn
    )
    scores_again = jnp.where(same_seq[None], scores_again, mask_fill)
    probs_again = jnp.exp(scores_again - log_total)
    probs_again_b = probs_again.astype(jnp.bfloat16)
    d_probs = jnp.einsum("qhd,khd->hqk", d_att, value_b, preferred_element_type=jnp.float32)
    delta = jnp.sum(probs_again * d_probs, axis=-1, keepdims=True)
    d_scores = (probs_again * (d_probs - delta)).astype(jnp.bfloat16)
    d_query = (
        jnp.einsum("hqk,khd->qhd", d_scores, key_b, preferred_element_type=jnp.float32) * scale_attn
    )
    d_key = (
        jnp.einsum("hqk,qhd->khd", d_scores, query_b, preferred_element_type=jnp.float32)
        * scale_attn
    )
    d_value = (
        jnp.einsum("hqk,qhd->khd", probs_again_b, d_att, preferred_element_type=jnp.float32)
        .reshape(tok_count, -1)
        .astype(jnp.bfloat16)
    )
    d_qraw, d_kraw, qgain_part, kgain_part = prep_back((d_query, d_key))
    d_qraw_b = d_qraw.astype(jnp.bfloat16)
    d_kraw_b = d_kraw.astype(jnp.bfloat16)
    d_normed = jnp.einsum("pa,da->pd", d_qraw_b, w_query, preferred_element_type=jnp.float32)
    d_normed = d_normed + jnp.einsum(
        "pa,da->pd", d_kraw_b, w_key, preferred_element_type=jnp.float32
    )
    d_normed = d_normed + jnp.einsum(
        "pa,da->pd", d_value, w_value, preferred_element_type=jnp.float32
    )
    query_grad = jnp.einsum("pd,pa->da", normed, d_qraw_b, preferred_element_type=jnp.float32)
    key_grad = jnp.einsum("pd,pa->da", normed, d_kraw_b, preferred_element_type=jnp.float32)
    value_grad = jnp.einsum("pd,pa->da", normed, d_value, preferred_element_type=jnp.float32)
    normed_got = exchange(column_blocks(d_normed.astype(BF), tensor_count), "tensor")
    normed_sum = jnp.sum(normed_got.astype(F32), axis=0).astype(BF)
    d_normed_full = side_by_side(gather_blocks(normed_sum, "tensor")).astype(F32)
    d_x_norm, gain_one_grad = norm_one_back(d_normed_full)
    d_tokens = d_resid + d_x_norm
    summed = tuple(
        lax.psum(value.astype(BF), axes).astype(F32)
        for value, axes in (
            (query_grad, "expert"),
            (key_grad, "expert"),
            (value_grad, "expert"),
            (out_proj_grad, "expert"),
            (router_grad, "expert"),
            (gain_one_grad, "expert"),
            (gain_two_grad, "expert"),
            (qgain_part, ("expert", "tensor")),
            (kgain_part, ("expert", "tensor")),
        )
    )
    dx_slice = lax.dynamic_slice_in_dim(d_tokens, tensor_id * col_count, col_count, 1).astype(BF)
    going = dot(put, jnp.concatenate([out_slice, dx_slice], axis=1), 0, 0).astype(BF)
    back = exchange(going.reshape(groups, move_rows, -1), "expert").reshape(tok_count, -1)
    back = dot(by_rank, back, 0, 0).astype(BF)
    block_out = back[:, :col_count]
    grad_tokens = back[:, col_count:]
    expert_grad = jnp.transpose(jnp.stack(expert_grads).astype(F32), (0, 2, 1, 3))
    return (
        block_out,
        grad_tokens,
        summed[5],
        summed[0],
        summed[1],
        summed[2],
        summed[7],
        summed[8],
        summed[3],
        summed[6],
        summed[4],
        expert_grad,
    )


def solution(mesh):
    in_specs = (
        P("expert", "tensor"),
        P("expert", "tensor"),
        P("expert", None),
        P("expert"),
        P("expert", None),
        P("expert", None),
        P(),
        P(None, "tensor"),
        P(None, "tensor"),
        P(None, "tensor"),
        P(),
        P(),
        P("tensor", None),
        P(),
        P(),
        P("expert", None, None, "tensor"),
    )
    out_specs = (
        P("expert", "tensor"),
        P("expert", "tensor"),
        P(),
        P(None, "tensor"),
        P(None, "tensor"),
        P(None, "tensor"),
        P(),
        P(),
        P("tensor", None),
        P(),
        P(),
        P("expert", None, None, "tensor"),
    )
    return jax.shard_map(body, mesh=mesh, in_specs=in_specs, out_specs=out_specs, check_vma=False)
```

time: 1450 us -> 911 us (0.63)
  local copies, waits for them, and re-layouts: 272 us -> 41.2 us
  blocking collectives: 435 us -> 287 us
  waiting for transfers between devices: 433 us -> 326 us
  matrix products: 122 us -> 45.6 us
  Pallas kernels: 0 us -> 65.1 us
  other arithmetic: 105 us -> 72.1 us
    all_to_all x2 -> x5, blocking collectives: 317 us -> 157 us  [exchange(): return lax.all_to_all(value, axis, split_axis=0, concat_axis=0, tiled=True)]
    reduce_scatter x0 -> x2, waiting for transfers between devices: none -> 156 us  [body(): lax.psum_scatter(partial, 'tensor', scatter_dimension=0, tiled=False)]
    gather x10 -> x0, local copies, waits for them, and re-layouts: 138 us -> none  [the longest x1 30.7 us: body(): slot_gate = jnp.where(filled, gate_eff.reshape(-1)[safe_source], 0.0)]
    all_to_all x6 -> x8, waiting for transfers between devices: 303 us -> 168 us  [exchange(): return lax.all_to_all(value, axis, split_axis=0, concat_axis=0, tiled=True)]
    psum x4 -> x1, waiting for transfers between devices: 108 us -> 0.01 us  [body(): lax.psum(value.astype(BF), axes).astype(F32)]
    dot_general x11 -> x12, matrix products: 88.2 us -> 21.2 us  [dot(): lax.dot_general(left, right, (((left_dim,), (right_dim,)), ((), ())), pre...]
    pallas_call x0 -> x2, Pallas kernels: none -> 65.1 us  [expert_call(): pl.pallas_call(functools.partial(expert_kernel, side, per), grid=(quarter...]
    psum x3 -> x2, blocking collectives: 79.6 us -> 130 us  [body(): lax.psum(value.astype(BF), axes).astype(F32)]
  transfers between devices with their start and end apart: 12 -> 13, of which waited for: 9 -> 9; matrix products, arithmetic and copies ran while one was open for 14% -> 11% of each run, Pallas kernels for 0% -> 3%
where the time goes in v1:
time: 911 us; the launch traced here: 901 us
  waiting for transfers between devices  326 us (36%)
  blocking collectives  287 us (32%)
  other arithmetic  72.1 us (8%)
  Pallas kernels  65.1 us (7%)
  starting transfers between devices  48.2 us (5%)
  matrix products  45.6 us (5%)
  local copies, waits for them, and re-layouts  41.2 us (5%)
  between operations  16 us (2%)
    all_to_all x8, waiting for transfers between devices, exchange(): return lax.all_to_all(value, axis, split_axis=0, concat_axis=0, tiled=True)  168 us
    all_to_all x5, blocking collectives, exchange(): return lax.all_to_all(value, axis, split_axis=0, concat_axis=0, tiled=True)  157 us
    reduce_scatter x2, waiting for transfers between devices, body(): lax.psum_scatter(partial, 'tensor', scatter_dimension=0, tiled=False)  156 us
    psum x2, blocking collectives, body(): lax.psum(value.astype(BF), axes).astype(F32)  130 us
    pallas_call x2, Pallas kernels, expert_call(): pl.pallas_call(functools.partial(expert_kernel, side, per), grid=(quarter...  65.1 us
    all_to_all x8, starting transfers between devices, exchange(): return lax.all_to_all(value, axis, split_axis=0, concat_axis=0, tiled=True)  48 us
    dot_general x12, matrix products, dot(): lax.dot_general(left, right, (((left_dim,), (right_dim,)), ((), ())), pre...  21.2 us
  transfers between devices with their start and end apart: 13, of which 9 were waited for; matrix products, arithmetic and copies ran while one was open for 11% of the time, Pallas kernels for 3%

profile of v1, /device:TPU:1, one launch (start us, length us, event | category | flops | bytes accessed | tf_op | source)
XLA Modules:
  0.0 900.8 jit_solution(7463007341162177451)
XLA Ops:
  7.2 6.1 fusion.69
  15.3 21.7 %all_to_all.65 = bf16[32,8,1152]{2,1,0:T(8,128)(2,1)S(1)} all-to-all(bf16[32,8,1152]{2,1,0:T(8,128)(2,1)S(1)} %fusion.2), channel_id=1, replica_groups=mesh['expert'=32,'tensor'=4] {'expert'}, dimensions={0} | all-to-all | bytes 1179648 | tf_op jit(solution)/shard_map/all_to_all | solution.py:151
  39.7 4.6 all-to-all-start.1
  47.6 46.0 %all-to-all-done.1 = bf16[4,256,1024]{2,1,0:T(8,128)(2,1)} async-done(((bf16[4,256,1024]{2,1,0:T(8,128)(2,1)}), bf16[4,256,1024]{2,1,0:T(8,128)(2,1)}, u32[]{:S(2)}, u32[]{:S(2)}) %all-to-all-start.1) | async-done | bytes 2097184 | tf_op jit(solution)/shard_map/all_to_all | solution.py:151
  117.1 4.3 all-to-all-start.2
  126.8 4.6 convert_reduce_fusion
  131.4 16.5 %all-to-all-done.2 = bf16[4,256,512]{2,1,0:T(8,128)(2,1)} async-done(((bf16[4,256,512]{2,1,0:T(8,128)(2,1)}), bf16[4,256,512]{2,1,0:T(8,128)(2,1)}, u32[]{:S(2)}, u32[]{:S(2)}) %all-to-all-start.2) | async-done | bytes 1048608 | tf_op jit(solution)/shard_map/all_to_all | solution.py:151
  152.1 4.6 all-to-all-start.3
  158.0 21.3 %all-to-all-done.3 = bf16[4,256,512]{2,1,0:T(8,128)(2,1)} async-done(((bf16[4,256,512]{2,1,0:T(8,128)(2,1)}), bf16[4,256,512]{2,1,0:T(8,128)(2,1)}, u32[]{:S(2)}, u32[]{:S(2)}) %all-to-all-start.3) | async-done | bytes 1048608 | tf_op jit(solution)/shard_map/all_to_all | solution.py:151
  190.6 8.1 all-to-all-start.4
  198.8 6.2 multiply_convert_fusion
  204.9 33.6 %all-to-all-done.4 = bf16[32,24,2048]{2,1,0:T(8,128)(2,1)} async-done(((bf16[32,24,2048]{2,1,0:T(8,128)(2,1)}), bf16[32,24,2048]{2,1,0:T(8,128)(2,1)}, u32[]{:S(2)}, u32[]{:S(2)}) %all-to-all-start.4) | async-done | bytes 3145760 | tf_op jit(solution)/shard_map/all_to_all | solution.py:151
  238.6 44.5 %all_to_all.66 = bf16[32,24,2048]{2,1,0:T(8,128)(2,1)} all-to-all(bf16[32,24,2048]{2,1,0:T(8,128)(2,1)} %bitcast.213), channel_id=1, replica_groups=mesh['expert'=32,'tensor'=4] {'expert'}, dimensions={0} | all-to-all | bytes 6291456 | tf_op jit(solution)/shard_map/all_to_all | solution.py:151
  283.0 31.4 %expert0.1 = (bf16[768,2048]{1,0:T(8,128)(2,1)}, bf16[768,2048]{1,0:T(8,128)(2,1)}, bf16[4,3,2048,256]{3,2,1,0:T(8,128)(2,1)}) custom-call(bf16[768,2048]{1,0:T(8,128)(2,1)} %bitcast.24.rows_ref, bf16[768,2048]{1,0:T(8,128)(2,1)} %bitcast.216, bf16[4,3,2048,256]{3,2,1,0:T(8,128)(2,1)} %all-gather.5.cloned.1.call-done.w_ref), custom_call_target="tpu_custom_call" | custom-call | flops 14495514624 | bytes 37748736 | tf_op jit(solution)/shard_map/expert0/pallas_call | solution.py:124
  314.5 33.6 %expert1.1 = (bf16[768,2048]{1,0:T(8,128)(2,1)}, bf16[768,2048]{1,0:T(8,128)(2,1)}, bf16[4,3,2048,256]{3,2,1,0:T(8,128)(2,1)}) custom-call(bf16[768,2048]{1,0:T(8,128)(2,1)} %bitcast.24.rows_ref, bf16[768,2048]{1,0:T(8,128)(2,1)} %bitcast.217, bf16[4,3,2048,256]{3,2,1,0:T(8,128)(2,1)} %all-gather.3.cloned.1.call-done.w_ref, ...), custom_call_target="tpu_custom_call" | custom-call | flops 14495514624 | bytes 37748736 | tf_op jit(solution)/shard_map/expert1/pallas_call | solution.py:124
  348.1 44.1 %all_to_all.67 = bf16[32,24,2048]{2,1,0:T(8,128)(2,1)} all-to-all(bf16[32,24,2048]{2,1,0:T(8,128)(2,1)} %bitcast.218), channel_id=1, replica_groups=mesh['expert'=32,'tensor'=4] {'expert'}, dimensions={0} | all-to-all | bytes 6291456 | tf_op jit(solution)/shard_map/all_to_all | solution.py:151
  392.2 4.9 all-to-all-start.7
  397.1 4.4 multiply_reduce_fusion
  402.5 34.4 %all-to-all-done.7 = bf16[32,24,2048]{2,1,0:T(8,128)(2,1)} async-done(((bf16[32,24,2048]{2,1,0:T(8,128)(2,1)}), bf16[32,24,2048]{2,1,0:T(8,128)(2,1)}, u32[]{:S(2)}, u32[]{:S(2)}) %all-to-all-start.7) | async-done | bytes 3145760 | tf_op jit(solution)/shard_map/all_to_all | solution.py:151
  443.6 31.4 %all_to_all.68 = bf16[4,256,1152]{2,1,0:T(8,128)(2,1)S(1)} all-to-all(bf16[4,256,1152]{2,1,0:T(8,128)(2,1)S(1)} %pad_maximum_fusion), channel_id=1, replica_groups=mesh['expert'=32,'tensor'=4] {'tensor'}, dimensions={0} | all-to-all | bytes 4718592 | tf_op jit(solution)/shard_map/all_to_all | solution.py:151
  477.6 4.3 all-to-all-start.9
  486.3 8.8 all-to-all-done.9
  531.8 15.1 %all_to_all.69 = bf16[4,256,512]{2,1,0:T(8,128)(2,1)} all-to-all(bf16[4,256,512]{2,1,0:T(8,128)(2,1)S(1)} %pad_maximum_fusion.4), channel_id=1, replica_groups=mesh['expert'=32,'tensor'=4] {'tensor'}, dimensions={0} | all-to-all | bytes 2097152 | tf_op jit(solution)/shard_map/all_to_all | solution.py:151
  549.4 4.6 all-to-all-start.11
  557.4 7.3 all-to-all-done.11
  569.9 12.6 %all-to-all-start.12 = ((bf16[32,8,1024]{2,1,0:T(8,128)(2,1)}), bf16[32,8,1024]{2,1,0:T(8,128)(2,1)S(1)}, u32[]{:S(2)}, u32[]{:S(2)}) async-start(bf16[32,8,1024]{2,1,0:T(8,128)(2,1)} %fusion.6), calls=%async_computation.12 | async-start | bytes 1048576 | tf_op jit(solution)/shard_map/all_to_all | solution.py:151
  582.6 66.0 %all-reduce.5 = (bf16[128]{0:T(256)(128)(2,1)S(1)}, bf16[128]{0:T(256)(128)(2,1)S(1)}) all-reduce(bf16[128]{0:T(256)(128)(2,1)S(1)} %get-tuple-element.30, bf16[128]{0:T(256)(128)(2,1)S(1)} %get-tuple-element.28), channel_id=1, replica_groups=mesh['expert'=32,'tensor'=4] {'expert','tensor'}, use_global_device_ids=true, to_apply=%region_38.39 | all-reduce | flops 256 | bytes 1024 | tf_op jit(solution)/shard_map/psum | solution.py:383
  649.6 64.0 %all-reduce.6 = (bf16[2048]{0:T(1024)(128)(2,1)S(1)}, bf16[2048]{0:T(1024)(128)(2,1)S(1)}) all-reduce(bf16[2048]{0:T(1024)(128)(2,1)S(1)} %get-tuple-element.26, bf16[2048]{0:T(1024)(128)(2,1)S(1)} %get-tuple-element.24), channel_id=1, replica_groups=mesh['expert'=32,'tensor'=4] {'expert'}, use_global_device_ids=true, to_apply=%region_33.34 | all-reduce | flops 4096 | bytes 16384 | tf_op jit(solution)/shard_map/psum | solution.py:383
  716.0 4.6 convert_element_type.323
  729.2 38.8 %reduce-scatter.5.cloned.1.call-done = bf16[1,3,2048,256]{3,2,1,0:T(8,128)(2,1)} async-done(((bf16[4,3,2048,256]{3,2,1,0:T(8,128)(2,1)}), bf16[1,3,2048,256]{3,2,1,0:T(8,128)(2,1)}) %reduce-scatter.5.cloned.1.call-update) | async-done | bytes 3145744 | tf_op jit(solution)/shard_map/reduce_scatter | solution.py:304
  768.1 117.3 %reduce-scatter.3.cloned.1.call-done = bf16[1,3,2048,256]{3,2,1,0:T(8,128)(2,1)} async-done(((bf16[4,3,2048,256]{3,2,1,0:T(8,128)(2,1)}), bf16[1,3,2048,256]{3,2,1,0:T(8,128)(2,1)}) %reduce-scatter.3.cloned.1.call-update) | async-done | bytes 3145744 | tf_op jit(solution)/shard_map/reduce_scatter | solution.py:304
  885.4 8.4 convert_bitcast_fusion
  (383 shorter events, 126.6 us)
Async XLA Ops:
  7.2 107.9 %copy-start = (bf16[512,2048]{1,0:T(8,128)(2,1)S(1)}, bf16[512,2048]{1,0:T(8,128)(2,1)}, u32[]{:S(2)}) copy-start(bf16[512,2048]{1,0:T(8,128)(2,1)} %param.28) | copy-start | bytes 6291460
  7.2 275.9 %all-gather.5.cloned.1.call-start = ((), (), s32[]{:S(2)}) async-start(), calls=%async_computation.16 | async-start | bytes 15728640 | tf_op jit(solution)/shard_map/all_gather | solution.py:196
  13.4 301.1 %all-gather.3.cloned.1.call-start = ((), (), s32[]{:S(2)}) async-start(), calls=%async_computation.15 | async-start | bytes 15728640 | tf_op jit(solution)/shard_map/all_gather | solution.py:196
  14.3 23.7 %copy-start.100 = (s32[256]{0:T(256)}, s32[256]{0:T(256)S(1)}, u32[]{:S(2)}) copy-start(s32[256]{0:T(256)S(1)} %convert_reduce_fusion.4) | copy-start | bytes 3076
  39.7 5.7 copy-start.112
  39.7 53.9 %all-to-all-start.1 = ((bf16[4,256,1024]{2,1,0:T(8,128)(2,1)}), bf16[4,256,1024]{2,1,0:T(8,128)(2,1)}, u32[]{:S(2)}, u32[]{:S(2)}) async-start(bf16[4,256,1024]{2,1,0:T(8,128)(2,1)} %broadcast_in_dim.102), calls=%async_computation.1 | async-start | bytes 4194304 | tf_op jit(solution)/shard_map/all_to_all | solution.py:151
  44.3 57.4 %copy-start.87 = (f32[2048]{0:T(1024)}, f32[2048]{0:T(1024)S(1)}, u32[]{:S(2)}) copy-start(f32[2048]{0:T(1024)S(1)} %convert_element_type.269) | copy-start | bytes 24580
  47.6 63.6 %copy-start.58 = (f32[256,64]{1,0:T(8,128)}, f32[256,64]{1,0:T(8,128)S(1)}, u32[]{:S(2)}) copy-start(f32[256,64]{1,0:T(8,128)S(1)} %get-tuple-element.103) | copy-start | bytes 196612
  101.7 8.3 copy-start.85
  116.0 6.6 copy-start.104
  117.1 30.8 %all-to-all-start.2 = ((bf16[4,256,512]{2,1,0:T(8,128)(2,1)}), bf16[4,256,512]{2,1,0:T(8,128)(2,1)}, u32[]{:S(2)}, u32[]{:S(2)}) async-start(bf16[4,256,512]{2,1,0:T(8,128)(2,1)} %pad_maximum_fusion.2), calls=%async_computation.2 | async-start | bytes 2097152 | tf_op jit(solution)/shard_map/all_to_all | solution.py:151
  121.4 59.7 %copy-start.77 = (f32[2048]{0:T(1024)}, f32[2048]{0:T(1024)S(1)}, u32[]{:S(2)}) copy-start(f32[2048]{0:T(1024)S(1)} %convert_element_type.286) | copy-start | bytes 24580
  152.1 27.2 %all-to-all-start.3 = ((bf16[4,256,512]{2,1,0:T(8,128)(2,1)}), bf16[4,256,512]{2,1,0:T(8,128)(2,1)}, u32[]{:S(2)}, u32[]{:S(2)}) async-start(bf16[4,256,512]{2,1,0:T(8,128)(2,1)} %broadcast_in_dim.109), calls=%async_computation.3 | async-start | bytes 2097152 | tf_op jit(solution)/shard_map/all_to_all | solution.py:151
  158.0 26.6 %copy-start.90 = (pred[8,256]{1,0:T(8,128)(4,1)}, pred[8,256]{1,0:T(8,128)(4,1)S(1)}, u32[]{:S(2)}) copy-start(pred[8,256]{1,0:T(8,128)(4,1)S(1)} %get-tuple-element.47) | copy-start | bytes 6148
  184.5 6.1 copy-start.91
  184.5 6.1 copy-start.92
  190.6 48.0 %all-to-all-start.4 = ((bf16[32,24,2048]{2,1,0:T(8,128)(2,1)}), bf16[32,24,2048]{2,1,0:T(8,128)(2,1)}, u32[]{:S(2)}, u32[]{:S(2)}) async-start(bf16[32,24,2048]{2,1,0:T(8,128)(2,1)} %bitcast.212), calls=%async_computation.4 | async-start | bytes 6291456 | tf_op jit(solution)/shard_map/all_to_all | solution.py:151
  392.2 44.7 %all-to-all-start.7 = ((bf16[32,24,2048]{2,1,0:T(8,128)(2,1)}), bf16[32,24,2048]{2,1,0:T(8,128)(2,1)}, u32[]{:S(2)}, u32[]{:S(2)}) async-start(bf16[32,24,2048]{2,1,0:T(8,128)(2,1)} %bitcast.215), calls=%async_computation.7 | async-start | bytes 6291456 | tf_op jit(solution)/shard_map/all_to_all | solution.py:151
  477.6 17.5 %all-to-all-start.9 = ((bf16[4,256,512]{2,1,0:T(8,128)(2,1)}), bf16[4,256,512]{2,1,0:T(8,128)(2,1)}, u32[]{:S(2)}, u32[]{:S(2)}) async-start(bf16[4,256,512]{2,1,0:T(8,128)(2,1)} %broadcast_in_dim.120), calls=%async_computation.9 | async-start | bytes 2097152 | tf_op jit(solution)/shard_map/all_to_all | solution.py:151
  481.8 234.2 %all-reduce.10.cloned.1.call-start = ((), (), s32[]{:S(2)}) async-start(), calls=%async_computation.19 | async-start | bytes 17301504 | tf_op jit(solution)/shard_map/psum | solution.py:383
  482.6 14.0 %copy-start.78 = (f32[2048]{0:T(1024)S(1)}, f32[2048]{0:T(1024)}, u32[]{:S(2)}) copy-start(f32[2048]{0:T(1024)} %copy-done.77) | copy-start | bytes 24580
  482.6 14.0 %copy-start.103 = (f32[256]{0:T(256)S(1)}, f32[256]{0:T(256)}, u32[]{:S(2)}) copy-start(f32[256]{0:T(256)} %copy-done.102) | copy-start | bytes 3076
  512.4 6.4 copy-start.9
  512.5 6.4 copy-start.14
  512.5 6.4 copy-start.19
  512.5 6.3 copy-start.89
  512.5 6.3 copy-start.95
  525.4 242.6 %reduce-scatter.5.cloned.1.call-start = ((), (), s32[]{:S(2)}) async-start(), calls=%async_computation.18 | async-start | bytes 15728640 | tf_op jit(solution)/shard_map/reduce_scatter | solution.py:304
  526.0 359.4 %reduce-scatter.3.cloned.1.call-start = ((), (), s32[]{:S(2)}) async-start(), calls=%async_computation.17 | async-start | bytes 15728640 | tf_op jit(solution)/shard_map/reduce_scatter | solution.py:304
  549.4 15.3 %all-to-all-start.11 = ((bf16[4,256,512]{2,1,0:T(8,128)(2,1)}), bf16[4,256,512]{2,1,0:T(8,128)(2,1)}, u32[]{:S(2)}, u32[]{:S(2)}) async-start(bf16[4,256,512]{2,1,0:T(8,128)(2,1)} %broadcast_in_dim.129), calls=%async_computation.11 | async-start | bytes 2097152 | tf_op jit(solution)/shard_map/all_to_all | solution.py:151
  567.4 147.5 %copy-start.101 = (s32[256]{0:T(256)S(1)}, s32[256]{0:T(256)}, u32[]{:S(2)}) copy-start(s32[256]{0:T(256)} %copy-done.100) | copy-start | bytes 3076
  569.9 144.9 %all-to-all-start.12 = ((bf16[32,8,1024]{2,1,0:T(8,128)(2,1)}), bf16[32,8,1024]{2,1,0:T(8,128)(2,1)S(1)}, u32[]{:S(2)}, u32[]{:S(2)}) async-start(bf16[32,8,1024]{2,1,0:T(8,128)(2,1)} %fusion.6), calls=%async_computation.12 | async-start | bytes 1048576 | tf_op jit(solution)/shard_map/all_to_all | solution.py:151
  (97 other events, 214.6 us)
Sparse Core Ops, SparseCore 0:
  13.5 163.9 all-gather.4
  179.7 122.3 all-gather.2
  525.5 125.4 all-reduce.9
  653.5 114.4 reduce-scatter.4
  771.1 114.2 reduce-scatter.2

commit v2 on v1

v2 whole, which is shorter than its diff:
```python
import functools
import math

import jax
import jax.numpy as jnp
from jax import lax
from jax.experimental import pallas as pl
from jax.experimental.pallas import tpu as pltpu
from jax.sharding import PartitionSpec as P

norm_eps = 1e-06
rope_base = 10000.0
mask_fill = -1e30


def rope_tables(positions, width):
    half_width = width // 2
    steps_idx = jnp.arange(half_width, dtype=jnp.float32)
    freqs = jnp.exp(steps_idx * (-2.0 * math.log(rope_base) / width))
    angles = positions.astype(jnp.float32)[:, None] * freqs[None, :]
    return (jnp.cos(angles), jnp.sin(angles))


def sequence_layout(lengths_row, count):
    seq_ends = jnp.cumsum(lengths_row)
    places = jnp.arange(count, dtype=jnp.int32)
    passed = (places[:, None] >= seq_ends[None, :]).astype(jnp.int32)
    seq_ids = jnp.sum(passed, axis=1)
    starts = jnp.sum(passed * lengths_row[None, :], axis=1)
    return (seq_ids, places - starts)


BF = jnp.bfloat16
F32 = jnp.float32


def dot(left, right, left_dim=1, right_dim=0):
    return lax.dot_general(
        left, right, (((left_dim,), (right_dim,)), ((), ())), preferred_element_type=F32
    )


def exchange(value, axis):
    return lax.all_to_all(value, axis, split_axis=0, concat_axis=0, tiled=True)


def gather_blocks(value, axis):
    return exchange(jnp.broadcast_to(value[None], (lax.axis_size(axis),) + value.shape), axis)


def column_blocks(value, count):
    return jnp.stack(jnp.split(value, count, axis=1))


MESH = pl.DeviceIdType.MESH


def tensor_peers():
    me = lax.axis_index("tensor")
    count = lax.axis_size("tensor")
    return me, [(me + d) % count for d in range(1, count)]


def greet(axis, peers):
    barrier = pltpu.get_barrier_semaphore()
    for peer in peers:
        pl.semaphore_signal(barrier, inc=1, device_id={axis: peer}, device_id_type=MESH)
    return lambda: pl.semaphore_wait(barrier, len(peers))


class Post:
    def __init__(self, axis, send_sem, recv_sem):
        self.axis, self.send_sem, self.recv_sem = axis, send_sem, recv_sem
        self.started = []
        self.used = 0

    def push(self, source, target, peer):
        slot = self.used
        self.used += 1
        copy = pltpu.make_async_remote_copy(
            src_ref=source,
            dst_ref=target,
            send_sem=self.send_sem.at[slot],
            recv_sem=self.recv_sem.at[slot],
            device_id={self.axis: peer},
            device_id_type=MESH,
        )
        copy.start()
        self.started.append(copy)
        return copy

    def finish(self):
        for copy in self.started:
            copy.wait_send()
        self.started = []


def arrive(copies):
    for copy in copies:
        copy.wait_recv()


def fetch(pairs, sem):
    copies = [
        pltpu.make_async_copy(source, target, sem.at[n]) for n, (source, target) in enumerate(pairs)
    ]
    for copy in copies:
        copy.start()
    return copies


def turn(value, cos_rows, sin_rows):
    return value * cos_rows + pltpu.roll(value, value.shape[-1] // 2, 1) * sin_rows


def inverse_rms(total, width):
    return lax.rsqrt(total * (1.0 / width) + norm_eps)


def row_sum(value):
    return jnp.sum(value, axis=1, keepdims=True)


def softmax_rows(query, key, bias, scale):
    scores = dot(query, key, 1, 1) * scale + bias
    grown = jnp.exp(scores - jnp.max(scores, axis=1, keepdims=True))
    return grown / row_sum(grown)


def front_kernel(
    local, bias, cos_rows, sin_rows, gain1, gain2, q_gain, k_gain, router_t, routes, slot_of, keep,
    wq_hbm, wk_hbm, wv_hbm, wo_hbm,
    x_out, dy_out, an_out, resid_out, mixed_out, q_out, k_out, qh_out, kh_out, vh_out, ob_out,
    gates_out, send_out, send_dy_out, pick_out,
    wq, wk, wv, wo, x_all, dy_all, parts, box, total, load_sem, send_sem, recv_sem,
):
    me, peers = tensor_peers()
    ready = greet("tensor", peers)
    loads = fetch([(wq_hbm, wq), (wk_hbm, wk), (wv_hbm, wv), (wo_hbm, wo)], load_sem)
    blocks, tok, col = x_all.shape
    width = blocks * col
    x_all[me] = local[:, :col]
    dy_all[me] = local[:, col:]
    ready()
    post = Post("tensor", send_sem, recv_sem)
    x_in = [post.push(x_all.at[me], x_all.at[me], peer) for peer in peers]
    dy_in = [post.push(dy_all.at[me], dy_all.at[me], peer) for peer in peers]
    arrive(x_in)
    square = jnp.zeros((tok, 1), F32)
    for t in range(blocks):
        value = x_all[t].astype(F32)
        square = square + row_sum(value * value)
    r1 = inverse_rms(square, width)
    for t in range(blocks):
        an_out[t] = (x_all[t].astype(F32) * r1 * gain1[t : t + 1, :]).astype(BF)
    x_out[...] = x_all[...]

    for copy in loads:
        copy.wait()

    def project(weight):
        value = dot(an_out[0], weight[0:col, :])
        for t in range(1, blocks):
            value = value + dot(an_out[t], weight[t * col : (t + 1) * col, :])
        return value

    q_out[...] = project(wq)
    k_out[...] = project(wk)
    vh_out[...] = project(wv).astype(BF)
    head = q_gain.shape[1]
    scale = 1.0 / math.sqrt(head)
    for h in range(col // head):
        lanes = slice(h * head, (h + 1) * head)
        for raw, gain, rotated in ((q_out, q_gain, qh_out), (k_out, k_gain, kh_out)):
            value = raw[:, lanes]
            value = value * inverse_rms(row_sum(value * value), head) * gain[...]
            rotated[:, lanes] = turn(value, cos_rows[...], sin_rows[...]).astype(BF)
        probs = softmax_rows(qh_out[:, lanes], kh_out[:, lanes], bias[...], scale).astype(BF)
        ob_out[:, lanes] = dot(probs, vh_out[:, lanes]).astype(BF)
    for t in range(blocks):
        parts[t] = dot(ob_out[...], wo[:, t * col : (t + 1) * col]).astype(BF)
    arrive([post.push(parts.at[peer], box.at[d], peer) for d, peer in enumerate(peers)])
    summed = parts[me].astype(F32)
    for d in range(blocks - 1):
        summed = summed + box[d].astype(F32)
    total[me] = summed.astype(BF)
    arrive([post.push(total.at[me], total.at[me], peer) for peer in peers])
    square = jnp.zeros((tok, 1), F32)
    for t in range(blocks):
        value = x_all[t].astype(F32) + total[t].astype(F32)
        resid_out[t] = value
        square = square + row_sum(value * value)
    r2 = inverse_rms(square, width)
    logits = jnp.zeros((router_t.shape[0], tok), F32)
    for t in range(blocks):
        mixed_out[t] = (resid_out[t] * r2 * gain2[t : t + 1, :]).astype(BF)
        logits = logits + dot(router_t[:, t * col : (t + 1) * col], mixed_out[t], 1, 1)
    expert = lax.broadcasted_iota(jnp.int32, logits.shape, 0)
    top = routes.shape[0]
    chosen = [
        jnp.sum(jnp.where(routes[k : k + 1, :] == expert, logits, 0.0), axis=0, keepdims=True)
        for k in range(top)
    ]
    peak = functools.reduce(jnp.maximum, chosen)
    grown = [jnp.exp(value - peak) for value in chosen]
    whole = functools.reduce(jnp.add, grown)
    slots = send_out.shape[0]
    slot = lax.broadcasted_iota(jnp.int32, (slots, tok), 0)
    pick = jnp.zeros((slots, tok), F32)
    weight = jnp.zeros((slots, tok), F32)
    for k in range(top):
        gate = grown[k] / whole
        gates_out[k : k + 1, :] = gate
        hot = slot_of[k : k + 1, :] == slot
        pick = jnp.where(hot, 1.0, pick)
        weight = jnp.where(hot, gate * keep[k : k + 1, :], weight)
    pick_out[...] = pick.T.astype(BF)
    pick = pick.astype(BF)
    for t in range(blocks):
        send_out[:, t * col : (t + 1) * col] = dot(pick, mixed_out[t]).astype(BF)
    gate = row_sum(weight)
    first = gate.astype(BF)
    second = (gate - first.astype(F32)).astype(BF)
    third = (gate - first.astype(F32) - second.astype(F32)).astype(BF)
    lane = lax.broadcasted_iota(jnp.int32, (slots, 128), 1)
    facts = jnp.zeros((slots, 128), F32)
    for n, piece in enumerate((first, second, third)):
        facts = jnp.where(lane == n, piece.astype(F32), facts)
    send_out[:, width:] = facts.astype(BF)
    arrive(dy_in)
    dy_out[...] = dy_all[...]
    for t in range(blocks):
        send_dy_out[:, t * col : (t + 1) * col] = dot(pick, dy_all[t]).astype(BF)
    post.finish()


def front_call(local, bias, cos_rows, sin_rows, gain1, gain2, q_gain, k_gain, router_t, routes,
               slot_of, keep, weights, slots):
    tok, both = local.shape
    col = both // 2
    blocks = gain1.shape[0]
    width = col * blocks
    shape = jax.ShapeDtypeStruct
    vmem = pl.BlockSpec(memory_space=pltpu.VMEM)
    tiles = (blocks, tok, col)
    top = routes.shape[0]
    return pl.pallas_call(
        front_kernel,
        out_shape=(
            shape(tiles, BF), shape(tiles, BF), shape(tiles, BF), shape(tiles, F32),
            shape(tiles, BF), shape((tok, col), F32), shape((tok, col), F32),
            shape((tok, col), BF), shape((tok, col), BF), shape((tok, col), BF),
            shape((tok, col), BF), shape((top, tok), F32), shape((slots, width + 128), BF),
            shape((slots, width), BF), shape((tok, slots), BF),
        ),
        in_specs=[vmem] * 12 + [pl.BlockSpec(memory_space=pl.ANY)] * 4,
        out_specs=(vmem,) * 15,
        scratch_shapes=[
            pltpu.VMEM((width, col), BF), pltpu.VMEM((width, col), BF), pltpu.VMEM((width, col), BF),
            pltpu.VMEM((col, width), BF),
            pltpu.VMEM(tiles, BF), pltpu.VMEM(tiles, BF), pltpu.VMEM(tiles, BF),
            pltpu.VMEM((blocks - 1, tok, col), BF), pltpu.VMEM(tiles, BF),
            pltpu.SemaphoreType.DMA((4,)),
            pltpu.SemaphoreType.DMA((12,)), pltpu.SemaphoreType.DMA((12,)),
        ],
        compiler_params=pltpu.CompilerParams(
            collective_id=1, has_side_effects=True, vmem_limit_bytes=56 * 1024 * 1024
        ),
        name="front",
    )(local, bias, cos_rows, sin_rows, gain1, gain2, q_gain, k_gain, router_t, routes, slot_of,
      keep, *weights)


def back_kernel(
    pick_t, ret, slot_of, keep, gates, routes, bias, cos_rows, sin_rows, gain1, gain2, q_gain,
    k_gain, router, resid, dy_all, x_all, mixed, qh, kh, vh, ob,
    q_hbm, k_hbm, an_hbm, wq_hbm, wk_hbm, wv_hbm, wo_hbm,
    grads, dx_out, small_out,
    q_raw, k_raw, an, wq, wk, wv, wo, parts, box, total, dm, dr, d_qkv, d_att,
    dg_mine, dg_box, note, load_sem, send_sem, recv_sem,
):
    me, peers = tensor_peers()
    ready = greet("tensor", peers)
    loads = fetch(
        [(wo_hbm, wo), (q_hbm, q_raw), (k_hbm, k_raw), (wq_hbm, wq), (wk_hbm, wk), (wv_hbm, wv),
         (an_hbm, an)],
        load_sem,
    )
    blocks, tok, col = parts.shape
    width = blocks * col
    post = Post("tensor", send_sem, recv_sem)
    for t in range(blocks):
        parts[t] = dot(pick_t[...], ret[:, t * col : (t + 1) * col]).astype(BF)
    ready()
    part_in = [post.push(parts.at[peer], box.at[d], peer) for d, peer in enumerate(peers)]
    slots = ret.shape[0]
    dgate = row_sum(ret[:, width : width + 128].astype(F32))
    slot = lax.broadcasted_iota(jnp.int32, (slots, tok), 0)
    top = routes.shape[0]
    for k in range(top):
        hot = slot_of[k : k + 1, :] == slot
        dg_mine[k : k + 1, :] = jnp.sum(jnp.where(hot, dgate, 0.0), axis=0, keepdims=True)
    dg_in = [post.push(dg_mine, dg_box.at[d], peer) for d, peer in enumerate(peers)]
    arrive(part_in)
    summed = parts[me].astype(F32)
    for d in range(blocks - 1):
        summed = summed + box[d].astype(F32)
    total[me] = summed.astype(BF)
    total_in = [post.push(total.at[me], total.at[me], peer) for peer in peers]

    arrive(dg_in)
    d_gates = dg_mine[...]
    for d in range(blocks - 1):
        d_gates = d_gates + dg_box[d]
    d_gates = d_gates * keep[...]
    gate = gates[...]
    d_chosen = gate * (d_gates - jnp.sum(gate * d_gates, axis=0, keepdims=True))
    expert = lax.broadcasted_iota(jnp.int32, (router.shape[1], tok), 0)
    d_logits_t = jnp.zeros(expert.shape, F32)
    for k in range(top):
        hot = routes[k : k + 1, :] == expert
        d_logits_t = jnp.where(hot, d_chosen[k : k + 1, :], d_logits_t)
    d_logits = d_logits_t.T.astype(BF)
    square = jnp.zeros((tok, 1), F32)
    for t in range(blocks):
        rows = slice(t * col, (t + 1) * col)
        grads[rows, 4 * col :] = dot(mixed[t].T, d_logits).astype(BF)
        dm[t] = dot(d_logits, router[rows, :], 1, 1)
        square = square + row_sum(resid[t] * resid[t])
    r2 = inverse_rms(square, width)
    arrive(total_in)
    cross = jnp.zeros((tok, 1), F32)
    for t in range(blocks):
        dm[t] = dm[t] + total[t].astype(F32)
        cross = cross + row_sum(resid[t] * gain2[t : t + 1, :] * dm[t])
    cross = cross * (1.0 / width) * r2 * r2 * r2
    for t in range(blocks):
        d_mixed = dm[t]
        small_out[4 + t : 5 + t, :] = jnp.sum(d_mixed * resid[t] * r2, axis=0, keepdims=True)
        d_resid = dy_all[t].astype(F32) + r2 * gain2[t : t + 1, :] * d_mixed - resid[t] * cross
        dm[t] = d_resid
        dr[t] = d_resid.astype(BF)
    for copy in loads:
        copy.wait()
    value = dot(dr[0], wo[:, 0:col], 1, 1)
    for t in range(1, blocks):
        value = value + dot(dr[t], wo[:, t * col : (t + 1) * col], 1, 1)
    d_att[...] = value.astype(BF)

    head = q_gain.shape[1]
    scale = 1.0 / math.sqrt(head)
    q_part = jnp.zeros((1, head), F32)
    k_part = jnp.zeros((1, head), F32)

    def unturn(grown, raw, gain):
        d_unit = grown * cos_rows[...] - pltpu.roll(grown, head // 2, 1) * sin_rows[...]
        inverse = inverse_rms(row_sum(raw * raw), head)
        unit = raw * inverse
        gain_part = jnp.sum(d_unit * unit, axis=0, keepdims=True)
        d_unit = d_unit * gain[...]
        d_raw = inverse * (d_unit - unit * (row_sum(unit * d_unit) * (1.0 / head)))
        return d_raw.astype(BF), gain_part

    for h in range(col // head):
        lanes = slice(h * head, (h + 1) * head)
        probs = softmax_rows(qh[:, lanes], kh[:, lanes], bias[...], scale)
        d_head = d_att[:, lanes]
        d_probs = dot(d_head, vh[:, lanes], 1, 1)
        d_scores = probs * (d_probs - row_sum(probs * d_probs))
        d_qkv[:, 2 * col + h * head : 2 * col + (h + 1) * head] = dot(
            probs.T.astype(BF), d_head
        ).astype(BF)
        d_q, part = unturn(dot(d_scores.astype(BF), kh[:, lanes]) * scale, q_raw[:, lanes], q_gain)
        q_part = q_part + part
        d_qkv[:, lanes] = d_q
        d_k, part = unturn(dot(d_scores.T.astype(BF), qh[:, lanes]) * scale, k_raw[:, lanes], k_gain)
        k_part = k_part + part
        d_qkv[:, col + h * head : col + (h + 1) * head] = d_k
    post.finish()
    for t in range(blocks):
        rows = slice(t * col, (t + 1) * col)
        parts[t] = (
            dot(d_qkv[:, 0:col], wq[rows, :], 1, 1)
            + dot(d_qkv[:, col : 2 * col], wk[rows, :], 1, 1)
            + dot(d_qkv[:, 2 * col : 3 * col], wv[rows, :], 1, 1)
        ).astype(BF)
    again = [post.push(parts.at[peer], box.at[blocks - 1 + d], peer) for d, peer in enumerate(peers)]
    for t in range(blocks):
        rows = slice(t * col, (t + 1) * col)
        grads[rows, : 3 * col] = dot(an[t].T, d_qkv[...]).astype(BF)
        grads[rows, 3 * col : 4 * col] = dot(dr[t].T, ob[...]).astype(BF)
    square = jnp.zeros((tok, 1), F32)
    for t in range(blocks):
        value = x_all[t].astype(F32)
        square = square + row_sum(value * value)
    r1 = inverse_rms(square, width)
    arrive(again)
    d_an = parts[me].astype(F32)
    for d in range(blocks - 1):
        d_an = d_an + box[blocks - 1 + d].astype(F32)
    x_mine = x_all[me].astype(F32)
    grown = gain1[pl.ds(me, 1), :] * d_an
    mean_part = row_sum(x_mine * grown)
    note[me, 0:8, :] = jnp.broadcast_to(
        jnp.sum(d_an * x_mine * r1, axis=0, keepdims=True), (8, col)
    )
    note[me, 8:16, 0:tok] = jnp.broadcast_to(mean_part, (tok, 128)).T[0:8, :]
    note[me, 8:16, tok : tok + head] = jnp.broadcast_to(q_part, (8, head))
    note[me, 8:16, tok + head : tok + 2 * head] = jnp.broadcast_to(k_part, (8, head))
    arrive([post.push(note.at[me], note.at[me], peer) for peer in peers])
    facts = note[0, 8:16, :]
    for t in range(1, blocks):
        facts = facts + note[t, 8:16, :]
    for t in range(blocks):
        small_out[t : t + 1, :] = note[t, 0:1, :]
    small_out[8:16, :] = facts
    mean = jnp.broadcast_to(facts[0:1, 0:tok], (128, tok)).T[:, 0:1] * (1.0 / width)
    dx_out[...] = (dm[me] + r1 * grown - x_mine * (r1 * r1 * r1 * mean)).astype(BF)
    post.finish()


def back_call(pick_t, ret, slot_of, keep, gates, routes, bias, cos_rows, sin_rows, gain1, gain2,
              q_gain, k_gain, router, resid, dy_all, x_all, mixed, qh, kh, vh, ob, q_raw, k_raw,
              an, weights):
    blocks, tok, col = x_all.shape
    width = blocks * col
    tiles = (blocks, tok, col)
    shape = jax.ShapeDtypeStruct
    vmem = pl.BlockSpec(memory_space=pltpu.VMEM)
    top = routes.shape[0]
    count = 5 * (blocks - 1)
    return pl.pallas_call(
        back_kernel,
        out_shape=(
            shape((width, 4 * col + 128), BF), shape((tok, col), BF), shape((16, col), F32),
        ),
        in_specs=[vmem] * 22 + [pl.BlockSpec(memory_space=pl.ANY)] * 7,
        out_specs=(vmem,) * 3,
        scratch_shapes=[
            pltpu.VMEM((tok, col), F32), pltpu.VMEM((tok, col), F32), pltpu.VMEM(tiles, BF),
            pltpu.VMEM((width, col), BF), pltpu.VMEM((width, col), BF), pltpu.VMEM((width, col), BF),
            pltpu.VMEM((col, width), BF),
            pltpu.VMEM(tiles, BF), pltpu.VMEM((2 * (blocks - 1), tok, col), BF),
            pltpu.VMEM(tiles, BF), pltpu.VMEM(tiles, F32), pltpu.VMEM(tiles, BF),
            pltpu.VMEM((tok, 3 * col), BF), pltpu.VMEM((tok, col), BF),
            pltpu.VMEM((top, tok), F32), pltpu.VMEM((blocks - 1, top, tok), F32),
            pltpu.VMEM((blocks, 16, col), F32),
            pltpu.SemaphoreType.DMA((7,)),
            pltpu.SemaphoreType.DMA((count,)), pltpu.SemaphoreType.DMA((count,)),
        ],
        compiler_params=pltpu.CompilerParams(
            collective_id=2, has_side_effects=True, vmem_limit_bytes=60 * 1024 * 1024
        ),
        name="back",
    )(pick_t, ret, slot_of, keep, gates, routes, bias, cos_rows, sin_rows, gain1, gain2, q_gain,
      k_gain, router, resid, dy_all, x_all, mixed, qh, kh, vh, ob, q_raw, k_raw, an, *weights)


def expert_kernel(side, per, rows_ref, grads_ref, w_ref, *rest):
    if side:
        y_in, dx_in = rest[:2]
        rest = rest[2:]
    y_ref, dx_ref, grad_ref, rows, rows_t, dys, dys_t, y_acc, dx_acc, gate_of, dgate = rest
    step = pl.program_id(0)
    count = rows.shape[0]
    both = rows_ref.shape[0]

    def selector(shape, row_dim):
        place = lax.broadcasted_iota(jnp.int32, shape, row_dim)
        source = lax.broadcasted_iota(jnp.int32, shape, 1 - row_dim)
        return (place + (place // per + side) * per == source).astype(F32).astype(BF)

    @pl.when(step == 0)
    def _():
        pick = selector((count, both), 0)
        width = rows.shape[1]
        rows[...] = dot(pick, rows_ref[:, :width]).astype(BF)
        gate_of[...] = row_sum(dot(pick, rows_ref[:, width:]))
        dy_rows = dot(pick, grads_ref[...])
        dys[...] = dy_rows.astype(BF)
        rows_t[...] = rows[...].T
        dys_t[...] = (dy_rows * gate_of[...]).astype(BF).T
        dgate[...] = jnp.zeros_like(dgate)
        y_acc[...] = jnp.zeros_like(y_acc)
        dx_acc[...] = jnp.zeros_like(dx_acc)

    w_gate, w_up, w_down = w_ref[0, 0], w_ref[0, 1], w_ref[0, 2]
    gate = dot(rows[...], w_gate)
    up = dot(rows[...], w_up)
    d_raw = dot(dys[...], w_down)
    d_act = d_raw * gate_of[...]
    sig = 1.0 / (1.0 + jnp.exp(-gate))
    silu = gate * sig
    act = (silu * up).astype(BF)
    dgate[...] += row_sum(act.astype(F32) * d_raw)
    d_gate = (d_act * up * sig * (1.0 + gate * (1.0 - sig))).astype(BF)
    d_up = (d_act * silu).astype(BF)
    y_acc[...] += dot(act, w_down, 1, 1)
    dx_acc[...] += dot(d_gate, w_gate, 1, 1) + dot(d_up, w_up, 1, 1)
    grad_ref[0, 0] = dot(rows_t[...], d_gate).astype(BF)
    grad_ref[0, 1] = dot(rows_t[...], d_up).astype(BF)
    grad_ref[0, 2] = dot(dys_t[...], act).astype(BF)

    @pl.when(step == pl.num_programs(0) - 1)
    def _():
        spread = selector((both, count), 1)
        width = rows.shape[1]
        first = dgate[...].astype(BF).astype(F32)
        lane = lax.broadcasted_iota(jnp.int32, (count, 128), 1)
        facts = jnp.where(lane == 0, first, jnp.where(lane == 1, dgate[...] - first, 0.0))
        y_all = dot(spread, (y_acc[...] * gate_of[...]).astype(BF)).astype(BF)
        dx_all = dot(spread, dx_acc[...].astype(BF)).astype(BF)
        facts = dot(spread, facts.astype(BF)).astype(BF)
        if side:
            y_all = y_all + y_in[...]
            dx_all = dx_all + dx_in[:, :width]
            facts = facts + dx_in[:, width:]
        y_ref[...] = y_all
        dx_ref[:, :width] = dx_all
        dx_ref[:, width:] = facts


def expert_call(side, per, rows, grads, weights, earlier):
    quarters, _, width, hidden = weights.shape
    both = rows.shape[0]
    count = both // 2
    whole = pl.BlockSpec((both, width), lambda q: (0, 0), pipeline_mode=pl.Buffered(1))
    wider = pl.BlockSpec((both, width + 128), lambda q: (0, 0), pipeline_mode=pl.Buffered(1))
    block = pl.BlockSpec((1, 3, width, hidden), lambda q: (q, 0, 0, 0))
    flops = 2 * 9 * count * width * hidden * quarters
    moved = 2 * (2 * weights.size + 4 * rows.size)
    return pl.pallas_call(
        functools.partial(expert_kernel, side, per),
        grid=(quarters,),
        out_shape=(
            jax.ShapeDtypeStruct((both, width), BF),
            jax.ShapeDtypeStruct((both, width + 128), BF),
            jax.ShapeDtypeStruct(weights.shape, BF),
        ),
        in_specs=[wider, whole, block] + [whole, wider][: len(earlier)],
        out_specs=(whole, wider, block),
        scratch_shapes=[
            pltpu.VMEM((count, width), BF),
            pltpu.VMEM((width, count), BF),
            pltpu.VMEM((count, width), BF),
            pltpu.VMEM((width, count), BF),
            pltpu.VMEM((count, width), F32),
            pltpu.VMEM((count, width), F32),
            pltpu.VMEM((count, 1), F32),
            pltpu.VMEM((count, 1), F32),
        ],
        compiler_params=pltpu.CompilerParams(vmem_limit_bytes=60 * 1024 * 1024),
        cost_estimate=pl.CostEstimate(
            flops=flops, bytes_accessed=moved, transcendentals=count * hidden * quarters
        ),
        name=f"expert{side}",
    )(rows, grads, weights, *earlier)


def plane():
    me = lax.axis_index("expert")
    core, z, y = me % 2, (me // 2) % 4, me // 8
    return [
        (core, me + 1 - 2 * core),
        ((y + y // 2) % 2, me + 8 * (1 - 2 * (y % 2))),
        (y // 2, me + 8 * (3 - 2 * y)),
        ((z + z // 2) % 2, me + 2 * (1 - 2 * (z % 2))),
        (z // 2, me + 2 * (3 - 2 * z)),
    ]

ORDERS = ((1, 3, 2, 4), (3, 2, 4, 1), (2, 4, 1, 3), (4, 1, 3, 2))

def reduce_kernel(part, out, buf, box, got, load_sem, out_sem, send_sem, recv_sem):
    dims = plane()
    barrier = pltpu.get_barrier_semaphore()
    for _, partner in dims:
        pl.semaphore_signal(barrier, inc=1, device_id={"expert": partner}, device_id_type=MESH)
    load = pltpu.make_async_copy(part, buf, load_sem)
    load.start()
    pl.semaphore_wait(barrier, len(dims))
    load.wait()
    core = dims[0][0]
    sends = []

    def push(slot, source, target, partner):
        copy = pltpu.make_async_remote_copy(
            src_ref=source, dst_ref=target, send_sem=send_sem.at[slot], recv_sem=recv_sem.at[slot],
            device_id={"expert": partner}, device_id_type=MESH)
        copy.start()
        sends.append(copy)
        return copy

    def add(target, target_at, place, first, count):
        def one(i, _):
            total = buf[place + i].astype(F32) + box[first + i].astype(F32)
            target[target_at + i] = total.astype(BF)
            return 0
        lax.fori_loop(0, count, one, 0)

    copies = []
    for s in range(4):
        copies.append(push(s, buf.at[pl.ds((1 - core) * 64 + s * 16, 16)], box.at[pl.ds(31 * s, 16)], dims[0][1]))
    place = [core * 64 + s * 16 for s in range(4)]
    for s in range(4):
        copies[s].wait_recv()
        add(buf, place[s], place[s], 31 * s, 16)
        bit, partner = dims[ORDERS[s][0]]
        copies[s] = push(4 + s, buf.at[pl.ds(place[s] + (1 - bit) * 8, 8)], box.at[pl.ds(31 * s + 16, 8)], partner)
        place[s] = place[s] + bit * 8
    size, first = 8, 16
    for k in range(1, 5):
        for s in range(4):
            copies[s].wait_recv()
            if k < 4:
                add(buf, place[s], place[s], 31 * s + first, size)
                bit, partner = dims[ORDERS[s][k]]
                half = size // 2
                copies[s] = push(4 * (k + 1) + s, buf.at[pl.ds(place[s] + (1 - bit) * half, half)],
                                 box.at[pl.ds(31 * s + first + size, half)], partner)
                place[s] = place[s] + bit * half
            else:
                add(got, place[s], place[s], 31 * s + first, 1)
                bit, partner = dims[ORDERS[s][3]]
                here = got.at[pl.ds(place[s], 1)]
                copies[s] = push(20 + s, here, here, partner)
        first, size = first + size, size // 2
    size = 1
    for k in range(3, -1, -1):
        for s in range(4):
            copies[s].wait_recv()
            bit, _ = dims[ORDERS[s][k]]
            place[s] = place[s] - bit * size
            if k:
                _, partner = dims[ORDERS[s][k - 1]]
            else:
                partner = dims[0][1]
            here = got.at[pl.ds(place[s], 2 * size)]
            copies[s] = push(20 + 4 * (4 - k) + s, here, here, partner)
        size *= 2
    for s in range(4):
        copies[s].wait_recv()
    store = pltpu.make_async_copy(got, out, out_sem)
    store.start()
    for copy in sends:
        copy.wait_send()
    store.wait()

def reduce_call(part):
    chunks, rows, cols = part.shape
    return pl.pallas_call(
        reduce_kernel,
        out_shape=jax.ShapeDtypeStruct(part.shape, BF),
        in_specs=[pl.BlockSpec(memory_space=pl.ANY)],
        out_specs=pl.BlockSpec(memory_space=pl.ANY),
        scratch_shapes=[
            pltpu.VMEM(part.shape, BF),
            pltpu.VMEM((124, rows, cols), BF),
            pltpu.VMEM(part.shape, BF),
            pltpu.SemaphoreType.DMA, pltpu.SemaphoreType.DMA,
            pltpu.SemaphoreType.DMA((40,)), pltpu.SemaphoreType.DMA((40,)),
        ],
        compiler_params=pltpu.CompilerParams(collective_id=3, has_side_effects=True, vmem_limit_bytes=48*1024*1024),
        name="reduce",
    )(part)


def body(
    tokens,
    out_grad,
    seq_lengths,
    dest_index,
    routes,
    pair_order,
    norm1_gain,
    w_query,
    w_key,
    w_value,
    q_gain,
    k_gain,
    w_output,
    norm2_gain,
    w_router,
    expert_w,
):
    groups = lax.axis_size("expert")
    tensor_count = lax.axis_size("tensor")
    group_id = lax.axis_index("expert")
    tensor_id = lax.axis_index("tensor")
    tok_count, col_count = tokens.shape
    width = col_count * tensor_count
    move_rows = tok_count // groups
    expert_count = w_router.shape[1]
    top_count = routes.shape[1]
    local_experts = expert_w.shape[0]

    w_stored = jnp.transpose(expert_w, (0, 2, 1, 3))
    w_all = [lax.all_gather(w_stored[e], "tensor", axis=0) for e in range(local_experts)]

    routes_t = routes.T
    order_t = pair_order[0].reshape(tok_count, top_count).T
    pair_expert = routes_t.reshape(-1)
    pair_total = tok_count * top_count
    base = pair_expert * pair_total
    keyed = base + order_t.reshape(-1)
    before = (keyed[None, :] < keyed[:, None]) & (keyed[None, :] >= base[:, None])
    ranks = jnp.sum(before.astype(jnp.int32), axis=1).reshape(top_count, tok_count)
    expert_axis = jnp.arange(expert_count, dtype=jnp.int32)
    route_hot = routes_t[:, None, :] == expert_axis[None, :, None]
    counts = jnp.sum(route_hot.astype(F32), axis=(0, 2))

    places = jnp.arange(tok_count, dtype=jnp.int32)
    arrival_rank = jnp.sum((dest_index[None, :] < dest_index[:, None]).astype(jnp.int32), axis=1)
    by_rank = (arrival_rank[None, :] == places[:, None]).astype(BF)
    inner = jnp.broadcast_to((dest_index % tok_count).astype(BF)[:, None], (tok_count, 64))
    facts = jnp.broadcast_to(counts.astype(BF)[None, :], (tok_count, expert_count))
    outgoing = dot(by_rank, jnp.concatenate([tokens, out_grad, inner, facts], axis=1)).astype(BF)
    got = exchange(outgoing.reshape(groups, move_rows, -1), "expert")
    all_counts = got[:, 0, 2 * col_count + 64 :].astype(jnp.int32)
    lower = jnp.arange(groups, dtype=jnp.int32) < group_id
    offsets = jnp.sum(jnp.where(lower[:, None], all_counts, 0), axis=0)
    mine = got[:, :, 2 * col_count].astype(jnp.int32).reshape(-1)
    put = (mine[None, :] == places[:, None]).astype(BF)
    local = dot(put, got.reshape(tok_count, -1)[:, : 2 * col_count]).astype(BF)
    capacity = 5 * tok_count * groups * top_count // (4 * expert_count)
    most_rows = 3 * tok_count * top_count // (2 * expert_count)
    per = most_rows // tensor_count
    slots = expert_count * per
    slot_global = jnp.sum(jnp.where(route_hot, offsets[None, :, None], 0), axis=1) + ranks
    kept = slot_global < capacity
    keep_mask = kept.astype(F32)
    here = kept & (ranks % tensor_count == tensor_id)
    slot_of = jnp.where(here, routes_t * per + ranks // tensor_count, -1)

    seq_ids, positions = sequence_layout(seq_lengths[0], tok_count)
    bias = jnp.where(seq_ids[:, None] == seq_ids[None, :], 0.0, mask_fill)
    cos_tab, sin_tab = rope_tables(positions, q_gain.shape[0])
    cos_rows = jnp.concatenate([cos_tab, cos_tab], axis=1)
    sin_rows = jnp.concatenate([-sin_tab, sin_tab], axis=1)
    gain1 = norm1_gain.astype(F32).reshape(tensor_count, col_count)
    gain2 = norm2_gain.astype(F32).reshape(tensor_count, col_count)
    head_gains = (q_gain.astype(F32)[None], k_gain.astype(F32)[None])
    router = jnp.pad(w_router, ((0, 0), (0, 128 - expert_count)))
    weights = (w_query, w_key, w_value, w_output)
    (
        x_all, dy_all, normed, resid, mixed, q_raw, k_raw, qh, kh, vh, attended, gates, send_rows,
        send_dy, pick_t,
    ) = front_call(
        local, bias, cos_rows, sin_rows, gain1, gain2, *head_gains, router.T, routes_t, slot_of,
        keep_mask, weights, slots,
    )
    recv_rows = exchange(send_rows.reshape(groups, -1, width + 128), "expert")
    recv_dy = exchange(send_dy.reshape(groups, -1, width), "expert")
    earlier = ()
    expert_grads = []
    for e in range(local_experts):
        *earlier, partial = expert_call(
            e, per, recv_rows.reshape(slots, -1), recv_dy.reshape(slots, -1), w_all[e], earlier
        )
        expert_grads.append(lax.psum_scatter(partial, "tensor", scatter_dimension=0, tiled=False))
    out_rows, d_rows = earlier
    ret_rows = exchange(d_rows.reshape(groups, -1, width + 128), "expert")
    ret_rows, out_rows = lax.optimization_barrier((ret_rows, out_rows))
    ret_out = exchange(out_rows.reshape(groups, -1, width), "expert")
    grads, dx_slice, small = back_call(
        pick_t, ret_rows.reshape(slots, -1), slot_of, keep_mask, gates, routes_t, bias, cos_rows,
        sin_rows, gain1, gain2, *head_gains, router, resid, dy_all, x_all, mixed, qh, kh, vh,
        attended, q_raw, k_raw, normed, weights,
    )
    moe_part = dot(pick_t, ret_out.reshape(slots, -1)).astype(BF)
    moe_got = exchange(column_blocks(moe_part, tensor_count), "tensor")
    moe_slice = jnp.sum(moe_got.astype(F32), axis=0)
    resid_slice = lax.dynamic_index_in_dim(resid, tensor_id, 0, False)
    out_slice = (resid_slice + moe_slice).astype(BF)
    summed = reduce_call(grads.reshape(4 * groups, -1, grads.shape[1])).reshape(grads.shape)

    going = dot(put, jnp.concatenate([out_slice, dx_slice], axis=1), 0, 0).astype(BF)
    small = small[:9].astype(BF).reshape(move_rows, -1)
    small = jnp.pad(small, ((0, 0), (0, -small.shape[1] % 128)))
    small = jnp.broadcast_to(small[None], (groups,) + small.shape)
    back = exchange(jnp.concatenate([going.reshape(groups, move_rows, -1), small], axis=2), "expert")
    small = jnp.sum(back[:, :, 2 * col_count :].astype(F32), axis=0)[:, : 9 * col_count // move_rows]
    small = small.reshape(-1)
    back = dot(by_rank, back.reshape(tok_count, -1)[:, : 2 * col_count], 0, 0).astype(BF)
    expert_grad = jnp.transpose(jnp.stack(expert_grads).astype(F32), (0, 2, 1, 3))
    wide = [summed[:, n * col_count : (n + 1) * col_count] for n in range(4)]
    gain_at = 2 * width + tok_count
    head = q_gain.shape[0]
    return (
        back[:, :col_count],
        back[:, col_count:],
        small[:width],
        wide[0].astype(F32),
        wide[1].astype(F32),
        wide[2].astype(F32),
        small[gain_at : gain_at + head],
        small[gain_at + head : gain_at + 2 * head],
        wide[3].T.astype(F32),
        small[width : 2 * width],
        summed[:, width : width + expert_count].astype(F32),
        expert_grad,
    )


def solution(mesh):
    in_specs = (
        P("expert", "tensor"),
        P("expert", "tensor"),
        P("expert", None),
        P("expert"),
        P("expert", None),
        P("expert", None),
        P(),
        P(None, "tensor"),
        P(None, "tensor"),
        P(None, "tensor"),
        P(),
        P(),
        P("tensor", None),
        P(),
        P(),
        P("expert", None, None, "tensor"),
    )
    out_specs = (
        P("expert", "tensor"),
        P("expert", "tensor"),
        P(),
        P(None, "tensor"),
        P(None, "tensor"),
        P(None, "tensor"),
        P(),
        P(),
        P("tensor", None),
        P(),
        P(),
        P("expert", None, None, "tensor"),
    )
    return jax.shard_map(body, mesh=mesh, in_specs=in_specs, out_specs=out_specs, check_vma=False)
```

time: 911 us -> 664 us (0.73)
  waiting for transfers between devices: 326 us -> 28.2 us
  Pallas kernels: 65.1 us -> 347 us
  blocking collectives: 287 us -> 186 us
  matrix products: 45.6 us -> 3.98 us
  other arithmetic: 72.1 us -> 34.3 us
  starting transfers between devices: 48.2 us -> 19.8 us
  local copies, waits for them, and re-layouts: 41.2 us -> 19.3 us
    pallas_call x0 -> x3, Pallas kernels: none -> 280 us  [the longest x1 109 us: front_call(): pl.pallas_call(front_kernel, out_shape=(shape(tiles, BF), shape(tiles, BF...]
    all_to_all x8 -> x3, waiting for transfers between devices: 168 us -> 0.9 us  [exchange(): return lax.all_to_all(value, axis, split_axis=0, concat_axis=0, tiled=True)]
    reduce_scatter x2, waiting for transfers between devices: 156 us -> 0.01 us  [body(): lax.psum_scatter(partial, 'tensor', scatter_dimension=0, tiled=False)]
    psum x2 -> x0, blocking collectives: 130 us -> none  [body(): lax.psum(value.astype(BF), axes).astype(F32)]
    all_to_all x5 -> x4, blocking collectives: 157 us -> 186 us  [exchange(): return lax.all_to_all(value, axis, split_axis=0, concat_axis=0, tiled=True)]
    all_to_all x8 -> x3, starting transfers between devices: 48 us -> 19.7 us  [exchange(): return lax.all_to_all(value, axis, split_axis=0, concat_axis=0, tiled=True)]
    all_gather x2, waiting for transfers between devices: 0.01 us -> 26.1 us  [body(): lax.all_gather(w_stored[e], 'tensor', axis=0)]
    dot_general x18 -> x0, matrix products: 24.4 us -> none  [the longest x1 3.17 us: body(): k_raw = jnp.dot(normed, w_key, preferred_element_type=jnp.float32)]
  transfers between devices with their start and end apart: 13 -> 7, of which waited for: 9 -> 2; matrix products, arithmetic and copies ran while one was open for 11% -> 6% of each run, Pallas kernels for 3% -> 48%
where the time goes in v2:
time: 664 us; the launch traced here: 653 us
  Pallas kernels  347 us (52%)
  blocking collectives  186 us (28%)
  other arithmetic  34.3 us (5%)
  waiting for transfers between devices  28.2 us (4%)
  starting transfers between devices  19.8 us (3%)
  local copies, waits for them, and re-layouts  19.3 us (3%)
  between operations  14.6 us (2%)
    all_to_all x4, blocking collectives, exchange(): return lax.all_to_all(value, axis, split_axis=0, concat_axis=0, tiled=True)  186 us
    pallas_call x1, Pallas kernels, front_call(): pl.pallas_call(front_kernel, out_shape=(shape(tiles, BF), shape(tiles, BF...  109 us
    pallas_call x1, Pallas kernels, back_call(): pl.pallas_call(back_kernel, out_shape=(shape((width, 4 * col + 128), BF),...  90.1 us
    pallas_call x1, Pallas kernels, reduce_call(): pl.pallas_call(reduce_kernel, out_shape=jax.ShapeDtypeStruct(part.shape,...  81.2 us
    pallas_call x2, Pallas kernels, expert_call(): pl.pallas_call(functools.partial(expert_kernel, side, per), grid=(quarter...  66.7 us
    all_gather x2, waiting for transfers between devices, body(): lax.all_gather(w_stored[e], 'tensor', axis=0)  26.1 us
    all_to_all x3, starting transfers between devices, exchange(): return lax.all_to_all(value, axis, split_axis=0, concat_axis=0, tiled=True)  19.7 us
  transfers between devices with their start and end apart: 7, of which 2 were waited for; matrix products, arithmetic and copies ran while one was open for 6% of the time, Pallas kernels for 48%

profile of v2, /device:TPU:1, one launch (start us, length us, event | category | flops | bytes accessed | tf_op | source)
XLA Modules:
  0.0 653.2 jit_solution(13122758365839303801)
XLA Ops:
  7.2 6.0 fusion.24
  14.8 1.2 fusion
  15.9 9.7 %all-to-all-start = ((bf16[32,8,1152]{2,1,0:T(8,128)(2,1)}), bf16[32,8,1152]{2,1,0:T(8,128)(2,1)S(1)}, u32[]{:S(2)}, u32[]{:S(2)}) async-start(bf16[32,8,1152]{2,1,0:T(8,128)(2,1)} %fusion), calls=%async_computation | async-start | bytes 1179648 | tf_op jit(solution)/shard_map/all_to_all | solution.py:44
  28.5 3.4 convert_reduce_fusion
  32.3 1.0 fusion.26
  33.2 1.0 copy.50.router_t
  34.9 0.8 pad_maximum_fusion.2
  37.1 0.9 all-to-all-done
  40.3 1.1 convolution_convert_fusion.4.local
  41.3 108.8 %front.1 = (bf16[4,256,512]{2,1,0:T(8,128)(2,1)}, bf16[4,256,512]{2,1,0:T(8,128)(2,1)}, bf16[4,256,512]{2,1,0:T(8,128)(2,1)}, f32[4,256,512]{2,1,0:T(8,128)}, bf...) custom-call(bf16[256,1024]{1,0:T(8,128)(2,1)} %convolution_convert_f, ...), custom_call_target="tpu_custom_call" | custom-call | tf_op jit(solution)/shard_map/front/pallas_call | solution.py:247
  150.2 47.3 %all_to_all.35 = bf16[32,24,2048]{2,1,0:T(8,128)(2,1)} all-to-all(bf16[32,24,2048]{2,1,0:T(8,128)(2,1)} %bitcast.71), channel_id=1, replica_groups=mesh['expert'=32,'tensor'=4] {'expert'}, dimensions={0} | all-to-all | bytes 6291456 | tf_op jit(solution)/shard_map/all_to_all | solution.py:44
  197.5 46.0 %all_to_all.36 = bf16[32,24,2176]{2,1,0:T(8,128)(2,1)} all-to-all(bf16[32,24,2176]{2,1,0:T(8,128)(2,1)S(1)} %bitcast.67), channel_id=1, replica_groups=mesh['expert'=32,'tensor'=4] {'expert'}, dimensions={0} | all-to-all | bytes 6684672 | tf_op jit(solution)/shard_map/all_to_all | solution.py:44
  243.4 32.4 %expert0.1 = (bf16[768,2048]{1,0:T(8,128)(2,1)}, bf16[768,2176]{1,0:T(8,128)(2,1)}, bf16[4,3,2048,256]{3,2,1,0:T(8,128)(2,1)}) custom-call(bf16[768,2176]{1,0:T(8,128)(2,1)} %bitcast.65, bf16[768,2048]{1,0:T(8,128)(2,1)} %bitcast.69, bf16[4,3,2048,256]{3,2,1,0:T(8,128)(2,1)} %all-gather.5.cloned.1.call-done.w_ref), custom_call_target="tpu_custom_call" | custom-call | flops 14495514624 | bytes 38535168 | tf_op jit(solution)/shard_map/expert0/pallas_call | solution.py:532
  275.9 26.1 %all-gather.3.cloned.1.call-done.w_ref = bf16[4,3,2048,256]{3,2,1,0:T(8,128)(2,1)} async-done(((bf16[1,3,2048,256]{3,2,1,0:T(8,128)(2,1)}), bf16[4,3,2048,256]{3,2,1,0:T(8,128)(2,1)}) %all-gather.3.cloned.1.call-update) | async-done | bytes 12582928 | tf_op jit(solution)/shard_map/all_gather | solution.py:697
  302.0 34.3 %expert1.1 = (bf16[768,2048]{1,0:T(8,128)(2,1)}, bf16[768,2176]{1,0:T(8,128)(2,1)}, bf16[4,3,2048,256]{3,2,1,0:T(8,128)(2,1)}) custom-call(bf16[768,2176]{1,0:T(8,128)(2,1)} %bitcast.66, bf16[768,2048]{1,0:T(8,128)(2,1)} %bitcast.70, bf16[4,3,2048,256]{3,2,1,0:T(8,128)(2,1)} %all-gather.3.cloned.1.call-done.w_ref, ...), custom_call_target="tpu_custom_call" | custom-call | flops 14495514624 | bytes 38535168 | tf_op jit(solution)/shard_map/expert1/pallas_call | solution.py:532
  336.8 1.4 copy-done
  338.3 49.9 %all_to_all.37 = bf16[32,24,2176]{2,1,0:T(8,128)(2,1)} all-to-all(bf16[32,24,2176]{2,1,0:T(8,128)(2,1)S(1)} %bitcast.64), channel_id=1, replica_groups=mesh['expert'=32,'tensor'=4] {'expert'}, dimensions={0} | all-to-all | bytes 6684672 | tf_op jit(solution)/shard_map/all_to_all | solution.py:44
  388.2 43.0 %all_to_all.38 = bf16[32,24,2048]{2,1,0:T(8,128)(2,1)S(1)} all-to-all(bf16[32,24,2048]{2,1,0:T(8,128)(2,1)S(1)} %bitcast.68), channel_id=1, replica_groups=mesh['expert'=32,'tensor'=4] {'expert'}, dimensions={0} | all-to-all | bytes 6291456 | tf_op jit(solution)/shard_map/all_to_all | solution.py:44
  431.2 1.0 convolution_convert_fusion.1
  432.3 1.1 pad_maximum_fusion
  433.4 3.9 all-to-all-start.5
  437.3 90.1 %back.1 = (bf16[2048,2176]{1,0:T(8,128)(2,1)}, bf16[256,512]{1,0:T(8,128)(2,1)}, f32[16,512]{1,0:T(8,128)}) custom-call(bf16[256,768]{1,0:T(8,128)(2,1)} %get-tuple-element.39.pick_t, bf16[768,2176]{1,0:T(8,128)(2,1)} %bitcast.60, s32[8,256]{1,0:T(8,128)} %fusion.15.slot_of, f32[8,256]{1,0:T(8,128)} %get-tuple-element.66.keep, ...), custom_call_target="tpu_custom_call" | custom-call | tf_op jit(solution)/shard_map/back/pallas_call | solution.py:432
  528.3 81.2 %reduce.7 = bf16[128,16,2176]{2,1,0:T(8,128)(2,1)} custom-call(bf16[128,16,2176]{2,1,0:T(8,128)(2,1)} %bitcast.61), custom_call_target="tpu_custom_call" | custom-call | tf_op jit(solution)/shard_map/reduce/pallas_call | solution.py:650
  609.7 1.1 fusion.7
  611.2 1.0 pad_maximum_fusion.1
  612.2 6.1 all-to-all-start.6
  618.3 9.4 %fusion.23 = (bf16[2048,512]{1,0:T(8,128)(2,1)}, f32[2048,512]{1,0:T(8,128)}, f32[2048,512]{1,0:T(8,128)}, f32[2048,512]{1,0:T(8,128)}) fusion(bf16[2048,2176]{1,0:T(8,128)(2,1)} %bitcast.58), kind=kLoop, calls=%fused_computation.78 | loop fusion | flops 3145728 | bytes 23068672 | tf_op jit(solution)/shard_map/slice | solution.py:785
  627.7 1.1 slice.100
  629.0 0.8 convert_element_type.127
  629.8 2.9 copy.53
  632.8 2.5 convert_bitcast_fusion.1
  637.8 8.4 %convert_bitcast_fusion = f32[2,2048,3,256]{3,1,2,0:T(8,128)} fusion(bf16[1,3,2048,256]{3,2,1,0:T(8,128)(2,1)} %reduce-scatter.5.cloned.1.call-done, bf16[1,3,2048,256]{3,2,1,0:T(8,128)(2,1)} %reduce-scatter.3.cloned.1.call-done), kind=kLoop, calls=%fused_computation.1 | loop fusion | flops 6291456 | bytes 18874368 | tf_op jit(solution)/shard_map/transpose | solution.py:784
  (91 shorter events, 13.5 us)
Async XLA Ops:
  7.2 236.3 %all-gather.5.cloned.1.call-start = ((), (), s32[]{:S(2)}) async-start(), calls=%async_computation.10 | async-start | bytes 15728640 | tf_op jit(solution)/shard_map/all_gather | solution.py:697
  13.2 0.8 copy-start.4
  13.2 1.0 copy-start.11
  13.2 1.1 copy-start.5
  13.2 1.1 copy-start.6
  13.2 288.8 %all-gather.3.cloned.1.call-start = ((), (), s32[]{:S(2)}) async-start(), calls=%async_computation.9 | async-start | bytes 15728640 | tf_op jit(solution)/shard_map/all_gather | solution.py:697
  13.3 12.5 %copy-start.9 = (bf16[2048]{0:T(1024)(128)(2,1)S(1)}, bf16[2048]{0:T(1024)(128)(2,1)}, u32[]{:S(2)}) copy-start(bf16[2048]{0:T(1024)(128)(2,1)} %param.22) | copy-start | bytes 12292
  13.3 13.1 %copy-start.10 = (bf16[2048]{0:T(1024)(128)(2,1)S(1)}, bf16[2048]{0:T(1024)(128)(2,1)}, u32[]{:S(2)}) copy-start(bf16[2048]{0:T(1024)(128)(2,1)} %param.29) | copy-start | bytes 12292
  13.3 13.7 %copy-start.12 = (s32[1,3]{1,0:T(1,128)S(1)}, s32[1,3]{1,0:T(1,128)}, u32[]{:S(2)}) copy-start(s32[1,3]{1,0:T(1,128)} %param.18) | copy-start | bytes 40
  13.3 14.4 %copy-start.8 = (s32[1,2048]{1,0:T(1,128)S(1)}, s32[1,2048]{1,0:T(1,128)}, u32[]{:S(2)}) copy-start(s32[1,2048]{1,0:T(1,128)} %param.21) | copy-start | bytes 24580
  13.3 18.7 %copy-start.7 = (bf16[2048,64]{0,1:T(8,128)(2,1)S(1)}, bf16[2048,64]{0,1:T(8,128)(2,1)}, u32[]{:S(2)}) copy-start(bf16[2048,64]{0,1:T(8,128)(2,1)} %param.30) | copy-start | bytes 786436
  15.9 19.8 %copy-start.13 = (bf16[128]{0:T(256)(128)(2,1)S(1)}, bf16[128]{0:T(256)(128)(2,1)}, u32[]{:S(2)}) copy-start(bf16[128]{0:T(256)(128)(2,1)} %param.27) | copy-start | bytes 772
  15.9 19.8 %copy-start.14 = (bf16[128]{0:T(256)(128)(2,1)S(1)}, bf16[128]{0:T(256)(128)(2,1)}, u32[]{:S(2)}) copy-start(bf16[128]{0:T(256)(128)(2,1)} %param.26) | copy-start | bytes 772
  15.9 22.0 %all-to-all-start = ((bf16[32,8,1152]{2,1,0:T(8,128)(2,1)}), bf16[32,8,1152]{2,1,0:T(8,128)(2,1)S(1)}, u32[]{:S(2)}, u32[]{:S(2)}) async-start(bf16[32,8,1152]{2,1,0:T(8,128)(2,1)} %fusion), calls=%async_computation | async-start | bytes 1179648 | tf_op jit(solution)/shard_map/all_to_all | solution.py:44
  25.7 612.1 %reduce-scatter.5.cloned.1.call-start = ((), (), s32[]{:S(2)}) async-start(), calls=%async_computation.12 | async-start | bytes 15728640 | tf_op jit(solution)/shard_map/reduce_scatter | solution.py:759
  150.2 47.3 %copy-start.1 = (bf16[768,2176]{1,0:T(8,128)(2,1)S(1)}, bf16[768,2176]{1,0:T(8,128)(2,1)}, u32[]{:S(2)}) copy-start(bf16[768,2176]{1,0:T(8,128)(2,1)} %get-tuple-element.40) | copy-start | bytes 10027012
  336.3 301.5 %reduce-scatter.3.cloned.1.call-start = ((), (), s32[]{:S(2)}) async-start(), calls=%async_computation.11 | async-start | bytes 15728640 | tf_op jit(solution)/shard_map/reduce_scatter | solution.py:759
  336.3 1.9 copy-start
  338.3 49.9 %copy-start.2 = (bf16[768,2048]{1,0:T(8,128)(2,1)S(1)}, bf16[768,2048]{1,0:T(8,128)(2,1)}, u32[]{:S(2)}) copy-start(bf16[768,2048]{1,0:T(8,128)(2,1)} %get-tuple-element.46) | copy-start | bytes 9437188
  388.2 43.0 %copy-start.3 = (bf16[256,768]{1,0:T(8,128)(2,1)S(1)}, bf16[256,768]{1,0:T(8,128)(2,1)}, u32[]{:S(2)}) copy-start(bf16[256,768]{1,0:T(8,128)(2,1)} %get-tuple-element.39.pick_t) | copy-start | bytes 1179652
  433.4 176.1 %all-to-all-start.5 = ((bf16[4,256,512]{2,1,0:T(8,128)(2,1)}), bf16[4,256,512]{2,1,0:T(8,128)(2,1)S(1)}, u32[]{:S(2)}, u32[]{:S(2)}) async-start(bf16[4,256,512]{2,1,0:T(8,128)(2,1)} %pad_maximum_fusion), calls=%async_computation.5 | async-start | bytes 2097152 | tf_op jit(solution)/shard_map/all_to_all | solution.py:44
  528.3 82.5 %copy-start.15 = (bf16[256,512]{1,0:T(8,128)(2,1)S(1)}, bf16[256,512]{1,0:T(8,128)(2,1)}, u32[]{:S(2)}) copy-start(bf16[256,512]{1,0:T(8,128)(2,1)} %get-tuple-element.59) | copy-start | bytes 786436
  612.2 23.1 %all-to-all-start.6 = ((bf16[32,8,1664]{2,1,0:T(8,128)(2,1)}), bf16[32,8,1664]{2,1,0:T(8,128)(2,1)S(1)}, u32[]{:S(2)}, u32[]{:S(2)}) async-start(bf16[32,8,1664]{2,1,0:T(8,128)(2,1)} %pad_maximum_fusion.1), calls=%async_computation.6 | async-start | bytes 1703936 | tf_op jit(solution)/shard_map/all_to_all | solution.py:44
Sparse Core Ops, SparseCore 0:
  13.3 166.7 all-gather.4
  182.4 119.5 all-gather.2
  336.4 131.1 reduce-scatter.4
  470.5 133.2 reduce-scatter.2

commit v3 on v2

--- a/solution.py
+++ b/solution.py
@@ -32,6 +32,8 @@
 
 BF = jnp.bfloat16
 F32 = jnp.float32
+COSTE = pl.CostEstimate(flops=20000000000, bytes_accessed=1, transcendentals=0)
+COST = pl.CostEstimate(flops=1, bytes_accessed=1, transcendentals=0)
 
 
 def dot(left, right, left_dim=1, right_dim=0):
@@ -100,6 +102,53 @@
         copy.wait_recv()
 
 
+def ring(me):
+    count = lax.axis_size("tensor")
+    return (me + 1) % count, (me + count - 1) % count
+
+
+def gather_start(post, ref, me):
+    right, left = ring(me)
+    return [post.push(ref.at[me], ref.at[me], peer) for peer in (right, left)]
+
+
+def gather_relay(post, ref, me, first):
+    right, left = ring(me)
+    half = ref.shape[1] // 2
+    first[0].wait_recv()
+    here = ref.at[left, pl.ds(0, half)]
+    one = post.push(here, here, right)
+    first[1].wait_recv()
+    here = ref.at[right, pl.ds(half, half)]
+    return [one, post.push(here, here, left)]
+
+
+def scatter_start(post, parts, halves, me):
+    right, left = ring(me)
+    far = ring(right)[0]
+    half = parts.shape[1] // 2
+    return [
+        post.push(parts.at[far, pl.ds(0, half)], halves.at[0], right),
+        post.push(parts.at[far, pl.ds(half, half)], halves.at[1], left),
+    ]
+
+
+def scatter_relay(post, parts, halves, box, me, first):
+    right, left = ring(me)
+    half = parts.shape[1] // 2
+    copies = []
+    for n, (peer, rows) in enumerate(((right, pl.ds(0, half)), (left, pl.ds(half, half)))):
+        first[n].wait_recv()
+        parts[peer, rows, :] = (parts[peer, rows, :].astype(F32) + halves[n].astype(F32)).astype(BF)
+        copies.append(post.push(parts.at[peer], box.at[n], peer))
+    return copies
+
+
+def scatter_total(parts, box, me, copies):
+    arrive(copies)
+    return parts[me].astype(F32) + box[0].astype(F32) + box[1].astype(F32)
+
+
 def fetch(pairs, sem):
     copies = [
         pltpu.make_async_copy(source, target, sem.at[n]) for n, (source, target) in enumerate(pairs)
@@ -128,14 +177,14 @@
 
 
 def front_kernel(
-    local, bias, cos_rows, sin_rows, gain1, gain2, q_gain, k_gain, router_t, routes, slot_of, keep,
+    local, bias, cos_rows, sin_rows, gain1, gain2, q_gain, k_gain, router_t, routes, slot_of, slot_back, keep,
     wq_hbm, wk_hbm, wv_hbm, wo_hbm,
     x_out, dy_out, an_out, resid_out, mixed_out, q_out, k_out, qh_out, kh_out, vh_out, ob_out,
     gates_out, send_out, send_dy_out, pick_out,
-    wq, wk, wv, wo, x_all, dy_all, parts, box, total, load_sem, send_sem, recv_sem,
+    wq, wk, wv, wo, x_all, dy_all, parts, halves, box, total, load_sem, send_sem, recv_sem,
 ):
-    me, peers = tensor_peers()
-    ready = greet("tensor", peers)
+    me = lax.axis_index("tensor")
+    ready = greet("tensor", ring(me))
     loads = fetch([(wq_hbm, wq), (wk_hbm, wk), (wv_hbm, wv), (wo_hbm, wo)], load_sem)
     blocks, tok, col = x_all.shape
     width = blocks * col
@@ -143,8 +192,8 @@
     dy_all[me] = local[:, col:]
     ready()
     post = Post("tensor", send_sem, recv_sem)
-    x_in = [post.push(x_all.at[me], x_all.at[me], peer) for peer in peers]
-    dy_in = [post.push(dy_all.at[me], dy_all.at[me], peer) for peer in peers]
+    x_in = gather_relay(post, x_all, me, gather_start(post, x_all, me))
+    dy_in = gather_start(post, dy_all, me)
     arrive(x_in)
     square = jnp.zeros((tok, 1), F32)
     for t in range(blocks):
@@ -167,6 +216,7 @@
     q_out[...] = project(wq)
     k_out[...] = project(wk)
     vh_out[...] = project(wv).astype(BF)
+    dy_in = gather_relay(post, dy_all, me, dy_in)
     head = q_gain.shape[1]
     scale = 1.0 / math.sqrt(head)
     for h in range(col // head):
@@ -179,12 +229,10 @@
         ob_out[:, lanes] = dot(probs, vh_out[:, lanes]).astype(BF)
     for t in range(blocks):
         parts[t] = dot(ob_out[...], wo[:, t * col : (t + 1) * col]).astype(BF)
-    arrive([post.push(parts.at[peer], box.at[d], peer) for d, peer in enumerate(peers)])
-    summed = parts[me].astype(F32)
-    for d in range(blocks - 1):
-        summed = summed + box[d].astype(F32)
-    total[me] = summed.astype(BF)
-    arrive([post.push(total.at[me], total.at[me], peer) for peer in peers])
+    first = scatter_start(post, parts, halves, me)
+    moved = scatter_relay(post, parts, halves, box, me, first)
+    total[me] = scatter_total(parts, box, me, moved).astype(BF)
+    arrive(gather_relay(post, total, me, gather_start(post, total, me)))
     square = jnp.zeros((tok, 1), F32)
     for t in range(blocks):
         value = x_all[t].astype(F32) + total[t].astype(F32)
@@ -207,14 +255,16 @@
     slots = send_out.shape[0]
     slot = lax.broadcasted_iota(jnp.int32, (slots, tok), 0)
     pick = jnp.zeros((slots, tok), F32)
+    pick_back = jnp.zeros((slots, tok), F32)
     weight = jnp.zeros((slots, tok), F32)
     for k in range(top):
         gate = grown[k] / whole
         gates_out[k : k + 1, :] = gate
         hot = slot_of[k : k + 1, :] == slot
         pick = jnp.where(hot, 1.0, pick)
+        pick_back = jnp.where(slot_back[k : k + 1, :] == slot, 1.0, pick_back)
         weight = jnp.where(hot, gate * keep[k : k + 1, :], weight)
-    pick_out[...] = pick.T.astype(BF)
+    pick_out[...] = pick_back.T.astype(BF)
     pick = pick.astype(BF)
     for t in range(blocks):
         send_out[:, t * col : (t + 1) * col] = dot(pick, mixed_out[t]).astype(BF)
@@ -235,7 +285,7 @@
 
 
 def front_call(local, bias, cos_rows, sin_rows, gain1, gain2, q_gain, k_gain, router_t, routes,
-               slot_of, keep, weights, slots):
+               slot_of, slot_back, keep, weights, slots):
     tok, both = local.shape
     col = both // 2
     blocks = gain1.shape[0]
@@ -253,31 +303,31 @@
             shape((tok, col), BF), shape((top, tok), F32), shape((slots, width + 128), BF),
             shape((slots, width), BF), shape((tok, slots), BF),
         ),
-        in_specs=[vmem] * 12 + [pl.BlockSpec(memory_space=pl.ANY)] * 4,
+        in_specs=[vmem] * 13 + [pl.BlockSpec(memory_space=pl.ANY)] * 4,
         out_specs=(vmem,) * 15,
         scratch_shapes=[
             pltpu.VMEM((width, col), BF), pltpu.VMEM((width, col), BF), pltpu.VMEM((width, col), BF),
             pltpu.VMEM((col, width), BF),
             pltpu.VMEM(tiles, BF), pltpu.VMEM(tiles, BF), pltpu.VMEM(tiles, BF),
-            pltpu.VMEM((blocks - 1, tok, col), BF), pltpu.VMEM(tiles, BF),
+            pltpu.VMEM((2, tok // 2, col), BF), pltpu.VMEM((2, tok, col), BF), pltpu.VMEM(tiles, BF),
             pltpu.SemaphoreType.DMA((4,)),
-            pltpu.SemaphoreType.DMA((12,)), pltpu.SemaphoreType.DMA((12,)),
+            pltpu.SemaphoreType.DMA((16,)), pltpu.SemaphoreType.DMA((16,)),
         ],
         compiler_params=pltpu.CompilerParams(
             collective_id=1, has_side_effects=True, vmem_limit_bytes=56 * 1024 * 1024
         ),
         name="front",
     )(local, bias, cos_rows, sin_rows, gain1, gain2, q_gain, k_gain, router_t, routes, slot_of,
-      keep, *weights)
+      slot_back, keep, *weights)
 
 
 def back_kernel(
-    pick_t, ret, slot_of, keep, gates, routes, bias, cos_rows, sin_rows, gain1, gain2, q_gain,
+    pick_t, ret_early, ret_late, slot_of, keep, gates, routes, bias, cos_rows, sin_rows, gain1, gain2, q_gain,
     k_gain, router, resid, dy_all, x_all, mixed, qh, kh, vh, ob,
     q_hbm, k_hbm, an_hbm, wq_hbm, wk_hbm, wv_hbm, wo_hbm,
     grads, dx_out, small_out,
     q_raw, k_raw, an, wq, wk, wv, wo, parts, box, total, dm, dr, d_qkv, d_att,
-    dg_mine, dg_box, note, load_sem, send_sem, recv_sem,
+    halves, dg_mine, dg_box, note, load_sem, send_sem, recv_sem,
 ):
     me, peers = tensor_peers()
     ready = greet("tensor", peers)
@@ -289,24 +339,26 @@
     blocks, tok, col = parts.shape
     width = blocks * col
     post = Post("tensor", send_sem, recv_sem)
-    for t in range(blocks):
-        parts[t] = dot(pick_t[...], ret[:, t * col : (t + 1) * col]).astype(BF)
+    early = ret_early.shape[0]
+    for t in range(blocks):
+        lanes = slice(t * col, (t + 1) * col)
+        parts[t] = (
+            dot(pick_t[:, :early], ret_early[:, lanes]) + dot(pick_t[:, early:], ret_late[:, lanes])
+        ).astype(BF)
     ready()
-    part_in = [post.push(parts.at[peer], box.at[d], peer) for d, peer in enumerate(peers)]
-    slots = ret.shape[0]
-    dgate = row_sum(ret[:, width : width + 128].astype(F32))
-    slot = lax.broadcasted_iota(jnp.int32, (slots, tok), 0)
+    first = scatter_start(post, parts, halves.at[pl.ds(0, 2)], me)
     top = routes.shape[0]
-    for k in range(top):
-        hot = slot_of[k : k + 1, :] == slot
-        dg_mine[k : k + 1, :] = jnp.sum(jnp.where(hot, dgate, 0.0), axis=0, keepdims=True)
+    for n, (ret, base) in enumerate(((ret_early, 0), (ret_late, early))):
+        dgate = row_sum(ret[:, width : width + 128].astype(F32))
+        slot = lax.broadcasted_iota(jnp.int32, (ret.shape[0], tok), 0) + base
+        for k in range(top):
+            hot = slot_of[k : k + 1, :] == slot
+            found = jnp.sum(jnp.where(hot, dgate, 0.0), axis=0, keepdims=True)
+            dg_mine[k : k + 1, :] = dg_mine[k : k + 1, :] + found if n else found
     dg_in = [post.push(dg_mine, dg_box.at[d], peer) for d, peer in enumerate(peers)]
-    arrive(part_in)
-    summed = parts[me].astype(F32)
-    for d in range(blocks - 1):
-        summed = summed + box[d].astype(F32)
-    total[me] = summed.astype(BF)
-    total_in = [post.push(total.at[me], total.at[me], peer) for peer in peers]
+    moved = scatter_relay(post, parts, halves.at[pl.ds(0, 2)], box.at[pl.ds(0, 2)], me, first)
+    total[me] = scatter_total(parts, box.at[pl.ds(0, 2)], me, moved).astype(BF)
+    total_first = gather_start(post, total, me)
 
     arrive(dg_in)
     d_gates = dg_mine[...]
@@ -328,7 +380,7 @@
         dm[t] = dot(d_logits, router[rows, :], 1, 1)
         square = square + row_sum(resid[t] * resid[t])
     r2 = inverse_rms(square, width)
-    arrive(total_in)
+    arrive(gather_relay(post, total, me, total_first))
     cross = jnp.zeros((tok, 1), F32)
     for t in range(blocks):
         dm[t] = dm[t] + total[t].astype(F32)
@@ -384,20 +436,22 @@
             + dot(d_qkv[:, col : 2 * col], wk[rows, :], 1, 1)
             + dot(d_qkv[:, 2 * col : 3 * col], wv[rows, :], 1, 1)
         ).astype(BF)
-    again = [post.push(parts.at[peer], box.at[blocks - 1 + d], peer) for d, peer in enumerate(peers)]
+    halves_again, box_again = halves.at[pl.ds(2, 2)], box.at[pl.ds(2, 2)]
+    first = scatter_start(post, parts, halves_again, me)
     for t in range(blocks):
         rows = slice(t * col, (t + 1) * col)
         grads[rows, : 3 * col] = dot(an[t].T, d_qkv[...]).astype(BF)
+        if t == 1:
+            moved = scatter_relay(post, parts, halves_again, box_again, me, first)
+    for t in range(blocks):
+        rows = slice(t * col, (t + 1) * col)
         grads[rows, 3 * col : 4 * col] = dot(dr[t].T, ob[...]).astype(BF)
     square = jnp.zeros((tok, 1), F32)
     for t in range(blocks):
         value = x_all[t].astype(F32)
         square = square + row_sum(value * value)
     r1 = inverse_rms(square, width)
-    arrive(again)
-    d_an = parts[me].astype(F32)
-    for d in range(blocks - 1):
-        d_an = d_an + box[blocks - 1 + d].astype(F32)
+    d_an = scatter_total(parts, box_again, me, moved)
     x_mine = x_all[me].astype(F32)
     grown = gain1[pl.ds(me, 1), :] * d_an
     mean_part = row_sum(x_mine * grown)
@@ -419,7 +473,7 @@
     post.finish()
 
 
-def back_call(pick_t, ret, slot_of, keep, gates, routes, bias, cos_rows, sin_rows, gain1, gain2,
+def back_call(pick_t, ret_early, ret_late, slot_of, keep, gates, routes, bias, cos_rows, sin_rows, gain1, gain2,
               q_gain, k_gain, router, resid, dy_all, x_all, mixed, qh, kh, vh, ob, q_raw, k_raw,
               an, weights):
     blocks, tok, col = x_all.shape
@@ -428,21 +482,22 @@
     shape = jax.ShapeDtypeStruct
     vmem = pl.BlockSpec(memory_space=pltpu.VMEM)
     top = routes.shape[0]
-    count = 5 * (blocks - 1)
+    count = 12 + 2 * (blocks - 1)
     return pl.pallas_call(
         back_kernel,
         out_shape=(
             shape((width, 4 * col + 128), BF), shape((tok, col), BF), shape((16, col), F32),
         ),
-        in_specs=[vmem] * 22 + [pl.BlockSpec(memory_space=pl.ANY)] * 7,
+        in_specs=[vmem] * 23 + [pl.BlockSpec(memory_space=pl.ANY)] * 7,
         out_specs=(vmem,) * 3,
         scratch_shapes=[
             pltpu.VMEM((tok, col), F32), pltpu.VMEM((tok, col), F32), pltpu.VMEM(tiles, BF),
             pltpu.VMEM((width, col), BF), pltpu.VMEM((width, col), BF), pltpu.VMEM((width, col), BF),
             pltpu.VMEM((col, width), BF),
-            pltpu.VMEM(tiles, BF), pltpu.VMEM((2 * (blocks - 1), tok, col), BF),
+            pltpu.VMEM(tiles, BF), pltpu.VMEM((4, tok, col), BF),
             pltpu.VMEM(tiles, BF), pltpu.VMEM(tiles, F32), pltpu.VMEM(tiles, BF),
             pltpu.VMEM((tok, 3 * col), BF), pltpu.VMEM((tok, col), BF),
+            pltpu.VMEM((4, tok // 2, col), BF),
             pltpu.VMEM((top, tok), F32), pltpu.VMEM((blocks - 1, top, tok), F32),
             pltpu.VMEM((blocks, 16, col), F32),
             pltpu.SemaphoreType.DMA((7,)),
@@ -451,29 +506,34 @@
         compiler_params=pltpu.CompilerParams(
             collective_id=2, has_side_effects=True, vmem_limit_bytes=60 * 1024 * 1024
         ),
+        cost_estimate=pl.CostEstimate(
+            flops=20000000000, bytes_accessed=1, transcendentals=0
+        ),
         name="back",
-    )(pick_t, ret, slot_of, keep, gates, routes, bias, cos_rows, sin_rows, gain1, gain2, q_gain,
+    )(pick_t, ret_early, ret_late, slot_of, keep, gates, routes, bias, cos_rows, sin_rows, gain1, gain2, q_gain,
       k_gain, router, resid, dy_all, x_all, mixed, qh, kh, vh, ob, q_raw, k_raw, an, *weights)
 
 
-def expert_kernel(side, per, rows_ref, grads_ref, w_ref, *rest):
+def expert_kernel(side, per, early, rows_ref, grads_ref, w_ref, *rest):
     if side:
-        y_in, dx_in = rest[:2]
-        rest = rest[2:]
-    y_ref, dx_ref, grad_ref, rows, rows_t, dys, dys_t, y_acc, dx_acc, gate_of, dgate = rest
+        y_rest, dx_rest, *rest = rest
+        y_ref, dx_ref, *rest = rest
+    else:
+        y_ref, dx_ref, y_rest, dx_rest, *rest = rest
+    grad_ref, rows, rows_t, dys, dys_t, y_acc, dx_acc, gate_of, dgate = rest
     step = pl.program_id(0)
-    count = rows.shape[0]
+    count, width = rows.shape
     both = rows_ref.shape[0]
-
-    def selector(shape, row_dim):
-        place = lax.broadcasted_iota(jnp.int32, shape, row_dim)
-        source = lax.broadcasted_iota(jnp.int32, shape, 1 - row_dim)
-        return (place + (place // per + side) * per == source).astype(F32).astype(BF)
+    late = per - early
+
+    def selector(shape, source_of):
+        place = lax.broadcasted_iota(jnp.int32, shape, 0)
+        source = lax.broadcasted_iota(jnp.int32, shape, 1)
+        return (source_of(place) == source).astype(F32).astype(BF)
 
     @pl.when(step == 0)
     def _():
-        pick = selector((count, both), 0)
-        width = rows.shape[1]
+        pick = selector((count, both), lambda p: p + (p // per + side) * per)
         rows[...] = dot(pick, rows_ref[:, :width]).astype(BF)
         gate_of[...] = row_sum(dot(pick, rows_ref[:, width:]))
         dy_rows = dot(pick, grads_ref[...])
@@ -503,42 +563,57 @@
 
     @pl.when(step == pl.num_programs(0) - 1)
     def _():
-        spread = selector((both, count), 1)
-        width = rows.shape[1]
         first = dgate[...].astype(BF).astype(F32)
         lane = lax.broadcasted_iota(jnp.int32, (count, 128), 1)
         facts = jnp.where(lane == 0, first, jnp.where(lane == 1, dgate[...] - first, 0.0))
-        y_all = dot(spread, (y_acc[...] * gate_of[...]).astype(BF)).astype(BF)
-        dx_all = dot(spread, dx_acc[...].astype(BF)).astype(BF)
-        facts = dot(spread, facts.astype(BF)).astype(BF)
+        facts = facts.astype(BF)
+        y_rows = (y_acc[...] * gate_of[...]).astype(BF)
+        dx_rows = dx_acc[...].astype(BF)
         if side:
-            y_all = y_all + y_in[...]
-            dx_all = dx_all + dx_in[:, :width]
-            facts = facts + dx_in[:, width:]
-        y_ref[...] = y_all
-        dx_ref[:, :width] = dx_all
-        dx_ref[:, width:] = facts
-
-
-def expert_call(side, per, rows, grads, weights, earlier):
+            chunk = per + late
+            here = selector(
+                (y_ref.shape[0], count),
+                lambda p: jnp.where(p % chunk < late, -1, p // chunk * per + p % chunk - late),
+            )
+            there = selector(
+                (y_ref.shape[0], y_rest.shape[0]),
+                lambda p: jnp.where(p % chunk < late, p // chunk * late + p % chunk, -1),
+            )
+            y_ref[...] = (dot(here, y_rows) + dot(there, y_rest[...])).astype(BF)
+            dx_ref[:, :width] = (dot(here, dx_rows) + dot(there, dx_rest[:, :width])).astype(BF)
+            dx_ref[:, width:] = (dot(here, facts) + dot(there, dx_rest[:, width:])).astype(BF)
+        else:
+            soon = selector((y_ref.shape[0], count), lambda p: p // early * per + p % early)
+            later = selector(
+                (y_rest.shape[0], count), lambda p: p // late * per + early + p % late
+            )
+            for pick, y_out, dx_out in ((soon, y_ref, dx_ref), (later, y_rest, dx_rest)):
+                y_out[...] = dot(pick, y_rows).astype(BF)
+                dx_out[:, :width] = dot(pick, dx_rows).astype(BF)
+                dx_out[:, width:] = dot(pick, facts).astype(BF)
+
+
+def expert_call(side, per, early, rows, grads, weights, rest):
     quarters, _, width, hidden = weights.shape
     both = rows.shape[0]
     count = both // 2
-    whole = pl.BlockSpec((both, width), lambda q: (0, 0), pipeline_mode=pl.Buffered(1))
-    wider = pl.BlockSpec((both, width + 128), lambda q: (0, 0), pipeline_mode=pl.Buffered(1))
+    groups = count // per
+    shape = jax.ShapeDtypeStruct
+
+    def whole(value):
+        return pl.BlockSpec(value.shape, lambda q: (0, 0), pipeline_mode=pl.Buffered(1))
+
+    def pair(size):
+        return [shape((groups * size, width), BF), shape((groups * size, width + 128), BF)]
+
     block = pl.BlockSpec((1, 3, width, hidden), lambda q: (q, 0, 0, 0))
-    flops = 2 * 9 * count * width * hidden * quarters
-    moved = 2 * (2 * weights.size + 4 * rows.size)
+    outs = pair(2 * per - early) if side else pair(early) + pair(per - early)
     return pl.pallas_call(
-        functools.partial(expert_kernel, side, per),
+        functools.partial(expert_kernel, side, per, early),
         grid=(quarters,),
-        out_shape=(
-            jax.ShapeDtypeStruct((both, width), BF),
-            jax.ShapeDtypeStruct((both, width + 128), BF),
-            jax.ShapeDtypeStruct(weights.shape, BF),
-        ),
-        in_specs=[wider, whole, block] + [whole, wider][: len(earlier)],
-        out_specs=(whole, wider, block),
+        out_shape=tuple(outs) + (shape(weights.shape, BF),),
+        in_specs=[whole(rows), whole(grads), block] + [whole(value) for value in rest],
+        out_specs=tuple(whole(value) for value in outs) + (block,),
         scratch_shapes=[
             pltpu.VMEM((count, width), BF),
             pltpu.VMEM((width, count), BF),
@@ -550,11 +625,9 @@
             pltpu.VMEM((count, 1), F32),
         ],
         compiler_params=pltpu.CompilerParams(vmem_limit_bytes=60 * 1024 * 1024),
-        cost_estimate=pl.CostEstimate(
-            flops=flops, bytes_accessed=moved, transcendentals=count * hidden * quarters
-        ),
+        cost_estimate=COSTE if side else COST,
         name=f"expert{side}",
-    )(rows, grads, weights, *earlier)
+    )(rows, grads, weights, *rest)
 
 
 def plane():
@@ -729,7 +802,14 @@
     kept = slot_global < capacity
     keep_mask = kept.astype(F32)
     here = kept & (ranks % tensor_count == tensor_id)
-    slot_of = jnp.where(here, routes_t * per + ranks // tensor_count, -1)
+    place = ranks // tensor_count
+    slot_of = jnp.where(here, routes_t * per + place, -1)
+    early = per // 8 * 8
+    side, owner = routes_t % local_experts, routes_t // local_experts
+    ahead = owner * early + place
+    behind = groups * early + owner * (2 * per - early)
+    behind = behind + jnp.where(side == 0, place - early, per - early + place)
+    slot_back = jnp.where(here, jnp.where((side == 0) & (place < early), ahead, behind), -1)
 
     seq_ids, positions = sequence_layout(seq_lengths[0], tok_count)
     bias = jnp.where(seq_ids[:, None] == seq_ids[None, :], 0.0, mask_fill)
@@ -746,27 +826,34 @@
         send_dy, pick_t,
     ) = front_call(
         local, bias, cos_rows, sin_rows, gain1, gain2, *head_gains, router.T, routes_t, slot_of,
-        keep_mask, weights, slots,
+        slot_back, keep_mask, weights, slots,
     )
     recv_rows = exchange(send_rows.reshape(groups, -1, width + 128), "expert")
     recv_dy = exchange(send_dy.reshape(groups, -1, width), "expert")
-    earlier = ()
-    expert_grads = []
-    for e in range(local_experts):
-        *earlier, partial = expert_call(
-            e, per, recv_rows.reshape(slots, -1), recv_dy.reshape(slots, -1), w_all[e], earlier
-        )
-        expert_grads.append(lax.psum_scatter(partial, "tensor", scatter_dimension=0, tiled=False))
-    out_rows, d_rows = earlier
-    ret_rows = exchange(d_rows.reshape(groups, -1, width + 128), "expert")
-    ret_rows, out_rows = lax.optimization_barrier((ret_rows, out_rows))
-    ret_out = exchange(out_rows.reshape(groups, -1, width), "expert")
+    recv_rows = recv_rows.reshape(slots, -1)
+    recv_dy = recv_dy.reshape(slots, -1)
+    def homeward(value):
+        return exchange(value.reshape(groups, -1, value.shape[1]), "expert").reshape(value.shape)
+
+    y_early, d_early, *rest, partial = expert_call(0, per, early, recv_rows, recv_dy, w_all[0], ())
+    grad_first = lax.psum_scatter(partial, "tensor", scatter_dimension=0, tiled=False)
+    ret_early = homeward(d_early)
+    ret_early, y_early, later_rows = lax.optimization_barrier((ret_early, y_early, recv_rows))
+    out_early = homeward(y_early)
+    y_late, d_late, partial = expert_call(1, per, early, later_rows, recv_dy, w_all[1], rest)
+    grad_second = lax.psum_scatter(partial, "tensor", scatter_dimension=0, tiled=False)
+
+    ret_late = homeward(d_late)
+    ret_late, y_late = lax.optimization_barrier((ret_late, y_late))
+    out_late = homeward(y_late)
     grads, dx_slice, small = back_call(
-        pick_t, ret_rows.reshape(slots, -1), slot_of, keep_mask, gates, routes_t, bias, cos_rows,
+        pick_t, ret_early, ret_late, slot_back, keep_mask, gates, routes_t, bias, cos_rows,
         sin_rows, gain1, gain2, *head_gains, router, resid, dy_all, x_all, mixed, qh, kh, vh,
         attended, q_raw, k_raw, normed, weights,
     )
-    moe_part = dot(pick_t, ret_out.reshape(slots, -1)).astype(BF)
+    out_late, small = lax.optimization_barrier((out_late, small))
+    moe_part = dot(pick_t[:, : out_early.shape[0]], out_early)
+    moe_part = (moe_part + dot(pick_t[:, out_early.shape[0] :], out_late)).astype(BF)
     moe_got = exchange(column_blocks(moe_part, tensor_count), "tensor")
     moe_slice = jnp.sum(moe_got.astype(F32), axis=0)
     resid_slice = lax.dynamic_index_in_dim(resid, tensor_id, 0, False)
@@ -781,7 +868,7 @@
     small = jnp.sum(back[:, :, 2 * col_count :].astype(F32), axis=0)[:, : 9 * col_count // move_rows]
     small = small.reshape(-1)
     back = dot(by_rank, back.reshape(tok_count, -1)[:, : 2 * col_count], 0, 0).astype(BF)
-    expert_grad = jnp.transpose(jnp.stack(expert_grads).astype(F32), (0, 2, 1, 3))
+    expert_grad = jnp.transpose(jnp.stack([grad_first, grad_second]).astype(F32), (0, 2, 1, 3))
     wide = [summed[:, n * col_count : (n + 1) * col_count] for n in range(4)]
     gain_at = 2 * width + tok_count
     head = q_gain.shape[0]

time: 664 us -> 600 us (0.904); the launches traced: 653 us -> 596 us
  Pallas kernels: 347 us -> 310 us
  blocking collectives: 186 us -> 155 us
  starting transfers between devices: 19.8 us -> 27 us
    all_to_all x4, blocking collectives: 186 us -> 155 us  [exchange(): return lax.all_to_all(value, axis, split_axis=0, concat_axis=0, tiled=True)]
    all_gather x2, waiting for transfers between devices: 26.1 us -> 8.88 us  [body(): lax.all_gather(w_stored[e], 'tensor', axis=0)]
    all_to_all x3 -> x5, waiting for transfers between devices: 0.9 us -> 17.6 us  [exchange(): return lax.all_to_all(value, axis, split_axis=0, concat_axis=0, tiled=True)]
    pallas_call x1, Pallas kernels: 109 us -> 92.5 us  [front_call(): pl.pallas_call(front_kernel, out_shape=(shape(tiles, BF), shape(tiles, BF...]
    pallas_call x1, Pallas kernels: 90.1 us -> 74.3 us  [back_call(): pl.pallas_call(back_kernel, out_shape=(shape((width, 4 * col + 128), BF),...]
    all_to_all x3 -> x5, starting transfers between devices: 19.7 us -> 26.8 us  [exchange(): return lax.all_to_all(value, axis, split_axis=0, concat_axis=0, tiled=True)]
  transfers between devices with their start and end apart: 7 -> 9, of which waited for: 2 -> 3; matrix products, arithmetic and copies ran while one was open for 6% -> 8% of each run, Pallas kernels for 48% -> 52%
where the time goes in v3:
time: 600 us; the launch traced here: 596 us
  Pallas kernels  310 us (52%)
  blocking collectives  155 us (26%)
  other arithmetic  34.6 us (6%)
  waiting for transfers between devices  27.2 us (5%)
  starting transfers between devices  27 us (4%)
  local copies, waits for them, and re-layouts  19.9 us (3%)
  between operations  14.5 us (2%)
  matrix products  7.93 us (1%)
    all_to_all x4, blocking collectives, exchange(): return lax.all_to_all(value, axis, split_axis=0, concat_axis=0, tiled=True)  155 us
    pallas_call x1, Pallas kernels, front_call(): pl.pallas_call(front_kernel, out_shape=(shape(tiles, BF), shape(tiles, BF...  92.5 us
    pallas_call x1, Pallas kernels, reduce_call(): pl.pallas_call(reduce_kernel, out_shape=jax.ShapeDtypeStruct(part.shape,...  82.3 us
    pallas_call x1, Pallas kernels, back_call(): pl.pallas_call(back_kernel, out_shape=(shape((width, 4 * col + 128), BF),...  74.3 us
    pallas_call x2, Pallas kernels, expert_call(): pl.pallas_call(functools.partial(expert_kernel, side, per, early), grid=(...  61.2 us
    all_to_all x5, starting transfers between devices, exchange(): return lax.all_to_all(value, axis, split_axis=0, concat_axis=0, tiled=True)  26.8 us
    all_to_all x5, waiting for transfers between devices, exchange(): return lax.all_to_all(value, axis, split_axis=0, concat_axis=0, tiled=True)  17.6 us
  transfers between devices with their start and end apart: 9, of which 3 were waited for; matrix products, arithmetic and copies ran while one was open for 8% of the time, Pallas kernels for 52%

profile of v3, /device:TPU:1, one launch (start us, length us, event | category | flops | bytes accessed | tf_op | source)
XLA Modules:
  0.0 596.2 jit_solution(4698907426032688716)
XLA Ops:
  7.2 6.0 fusion.30
  14.8 1.2 fusion.1
  15.9 9.7 %all-to-all-start = ((bf16[32,8,1152]{2,1,0:T(8,128)(2,1)}), bf16[32,8,1152]{2,1,0:T(8,128)(2,1)S(1)}, u32[]{:S(2)}, u32[]{:S(2)}) async-start(bf16[32,8,1152]{2,1,0:T(8,128)(2,1)} %fusion.1), calls=%async_computation | async-start | bytes 1179648 | tf_op jit(solution)/shard_map/all_to_all | solution.py:46
  28.5 3.7 convert_reduce_fusion
  40.3 1.1 convolution_convert_fusion.3.local
  41.4 92.5 %front.1 = (bf16[4,256,512]{2,1,0:T(8,128)(2,1)}, bf16[4,256,512]{2,1,0:T(8,128)(2,1)}, bf16[4,256,512]{2,1,0:T(8,128)(2,1)}, f32[4,256,512]{2,1,0:T(8,128)}, bf...) custom-call(bf16[256,1024]{1,0:T(8,128)(2,1)} %convolution_convert_f, ...), custom_call_target="tpu_custom_call" | custom-call | tf_op jit(solution)/shard_map/front/pallas_call | solution.py:297
  133.8 48.7 %all_to_all.45 = bf16[32,24,2048]{2,1,0:T(8,128)(2,1)} all-to-all(bf16[32,24,2048]{2,1,0:T(8,128)(2,1)} %bitcast.75), channel_id=1, replica_groups=mesh['expert'=32,'tensor'=4] {'expert'}, dimensions={0} | all-to-all | bytes 6291456 | tf_op jit(solution)/shard_map/all_to_all | solution.py:46
  182.5 46.2 %all_to_all.46 = bf16[32,24,2176]{2,1,0:T(8,128)(2,1)} all-to-all(bf16[32,24,2176]{2,1,0:T(8,128)(2,1)S(1)} %bitcast.74), channel_id=1, replica_groups=mesh['expert'=32,'tensor'=4] {'expert'}, dimensions={0} | all-to-all | bytes 6684672 | tf_op jit(solution)/shard_map/all_to_all | solution.py:46
  228.7 29.6 %expert0.1 = (bf16[256,2048]{1,0:T(8,128)(2,1)}, bf16[256,2176]{1,0:T(8,128)(2,1)}, bf16[128,2048]{1,0:T(8,128)(2,1)}, bf16[128,2176]{1,0:T(8,128)(2,1)}, bf16[4,3,2048,256]{3,2,1,0:T(8,128)(2,1)}) custom-call(bf16[768,2176]{1,0:T(8,128)(2,1)} %bitcast.66, bf16[768,2048]{1,0:T(8,128)(2,1)} %bitcast.68, ...), custom_call_target="tpu_custom_call" | custom-call | flops 1 | bytes 1 | tf_op jit(solution)/shard_map/expert0/pallas_call | solution.py:611
  258.3 1.2 copy-done.2
  259.5 22.3 %all_to_all.47 = bf16[32,8,2176]{2,1,0:T(8,128)(2,1)} all-to-all(bf16[32,8,2176]{2,1,0:T(8,128)(2,1)S(1)} %bitcast.81), channel_id=1, replica_groups=mesh['expert'=32,'tensor'=4] {'expert'}, dimensions={0} | all-to-all | bytes 2228224 | tf_op jit(solution)/shard_map/all_to_all | solution.py:46
  281.9 8.9 %all-gather.5.cloned.1.call-done.w_ref = bf16[4,3,2048,256]{3,2,1,0:T(8,128)(2,1)} async-done(((bf16[1,3,2048,256]{3,2,1,0:T(8,128)(2,1)}), bf16[4,3,2048,256]{3,2,1,0:T(8,128)(2,1)}) %all-gather.5.cloned.1.call-update) | async-done | bytes 12582928 | tf_op jit(solution)/shard_map/all_gather | solution.py:770
  290.7 31.6 %expert1.1 = (bf16[512,2048]{1,0:T(8,128)(2,1)}, bf16[512,2176]{1,0:T(8,128)(2,1)}, bf16[4,3,2048,256]{3,2,1,0:T(8,128)(2,1)}) custom-call(bf16[768,2176]{1,0:T(8,128)(2,1)} %bitcast.67, bf16[768,2048]{1,0:T(8,128)(2,1)} %bitcast.69, bf16[4,3,2048,256]{3,2,1,0:T(8,128)(2,1)} %all-gather.5.cloned.1.call-done.w_ref, ...), custom_call_target="tpu_custom_call" | custom-call | flops 20000000000 | bytes 1 | tf_op jit(solution)/shard_map/expert1/pallas_call | solution.py:611
  322.4 1.6 copy-done.1
  324.0 37.8 %all_to_all.48 = bf16[32,16,2176]{2,1,0:T(8,128)(2,1)} all-to-all(bf16[32,16,2176]{2,1,0:T(8,128)(2,1)S(1)} %bitcast.78), channel_id=1, replica_groups=mesh['expert'=32,'tensor'=4] {'expert'}, dimensions={0} | all-to-all | bytes 4456448 | tf_op jit(solution)/shard_map/all_to_all | solution.py:46
  361.8 4.0 all-to-all-start.4
  365.8 17.0 %all-to-all-done.4 = bf16[32,8,2048]{2,1,0:T(8,128)(2,1)S(1)} async-done(((bf16[32,8,2048]{2,1,0:T(8,128)(2,1)}), bf16[32,8,2048]{2,1,0:T(8,128)(2,1)S(1)}, u32[]{:S(2)}, u32[]{:S(2)}) %all-to-all-start.4) | async-done | bytes 1048608 | tf_op jit(solution)/shard_map/all_to_all | solution.py:46
  382.8 4.1 all-to-all-start.6
  386.9 2.7 fusion.3
  389.6 74.3 %back.1 = (bf16[2048,2176]{1,0:T(8,128)(2,1)}, bf16[256,512]{1,0:T(8,128)(2,1)}, f32[16,512]{1,0:T(8,128)}) custom-call(bf16[256,768]{1,0:T(8,128)(2,1)} %get-tuple-element.46.pick_t, bf16[256,2176]{1,0:T(8,128)(2,1)} %bitcast.80, bf16[512,2176]{1,0:T(8,128)(2,1)} %bitcast.77, s32[8,256]{1,0:T(8,128)} %get-tuple-element.100.slot_back.slot_of, ...), custom_call_target="tpu_custom_call" | custom-call | flops 20000000000 | bytes 1 | tf_op jit(solution)/shard_map/back/pallas_call | solution.py:486
  463.9 2.3 fusion
  466.3 1.1 pad_maximum_fusion
  467.4 3.5 all-to-all-start.7
  470.9 82.3 %reduce.7 = bf16[128,16,2176]{2,1,0:T(8,128)(2,1)} custom-call(bf16[128,16,2176]{2,1,0:T(8,128)(2,1)} %bitcast.70), custom_call_target="tpu_custom_call" | custom-call | tf_op jit(solution)/shard_map/reduce/pallas_call | solution.py:723
  553.5 1.1 fusion.10
  555.1 1.0 pad_maximum_fusion.1
  556.1 5.5 all-to-all-start.8
  561.6 9.4 %fusion.29 = (bf16[2048,512]{1,0:T(8,128)(2,1)}, f32[2048,512]{1,0:T(8,128)}, f32[2048,512]{1,0:T(8,128)}, f32[2048,512]{1,0:T(8,128)}) fusion(bf16[2048,2176]{1,0:T(8,128)(2,1)} %bitcast.64), kind=kLoop, calls=%fused_computation.92 | loop fusion | flops 3145728 | bytes 23068672 | tf_op jit(solution)/shard_map/slice | solution.py:872
  571.0 1.1 slice.108
  573.1 2.9 copy.53
  576.0 2.5 convert_bitcast_fusion.1
  581.0 8.4 %convert_bitcast_fusion = f32[2,2048,3,256]{3,1,2,0:T(8,128)} fusion(bf16[1,3,2048,256]{3,2,1,0:T(8,128)(2,1)} %reduce-scatter.5.cloned.1.call-done, bf16[1,3,2048,256]{3,2,1,0:T(8,128)(2,1)} %reduce-scatter.3.cloned.1.call-done), kind=kLoop, calls=%fused_computation.1 | loop fusion | flops 6291456 | bytes 18874368 | tf_op jit(solution)/shard_map/transpose | solution.py:871
  (98 shorter events, 16.5 us)
Async XLA Ops:
  7.2 221.5 %all-gather.3.cloned.1.call-start = ((), (), s32[]{:S(2)}) async-start(), calls=%async_computation.11 | async-start | bytes 15728640 | tf_op jit(solution)/shard_map/all_gather | solution.py:770
  13.2 0.8 copy-start.7
  13.2 1.0 copy-start.12
  13.2 1.1 copy-start.4
  13.2 1.1 copy-start.5
  13.2 277.5 %all-gather.5.cloned.1.call-start = ((), (), s32[]{:S(2)}) async-start(), calls=%async_computation.12 | async-start | bytes 15728640 | tf_op jit(solution)/shard_map/all_gather | solution.py:770
  13.3 12.5 %copy-start.10 = (bf16[2048]{0:T(1024)(128)(2,1)S(1)}, bf16[2048]{0:T(1024)(128)(2,1)}, u32[]{:S(2)}) copy-start(bf16[2048]{0:T(1024)(128)(2,1)} %param.22) | copy-start | bytes 12292
  13.3 13.1 %copy-start.11 = (bf16[2048]{0:T(1024)(128)(2,1)S(1)}, bf16[2048]{0:T(1024)(128)(2,1)}, u32[]{:S(2)}) copy-start(bf16[2048]{0:T(1024)(128)(2,1)} %param.29) | copy-start | bytes 12292
  13.3 13.7 %copy-start.13 = (s32[1,3]{1,0:T(1,128)S(1)}, s32[1,3]{1,0:T(1,128)}, u32[]{:S(2)}) copy-start(s32[1,3]{1,0:T(1,128)} %param.18) | copy-start | bytes 40
  13.3 14.4 %copy-start.9 = (s32[1,2048]{1,0:T(1,128)S(1)}, s32[1,2048]{1,0:T(1,128)}, u32[]{:S(2)}) copy-start(s32[1,2048]{1,0:T(1,128)} %param.21) | copy-start | bytes 24580
  13.3 19.0 %copy-start.6 = (bf16[2048,64]{0,1:T(8,128)(2,1)S(1)}, bf16[2048,64]{0,1:T(8,128)(2,1)}, u32[]{:S(2)}) copy-start(bf16[2048,64]{0,1:T(8,128)(2,1)} %param.30) | copy-start | bytes 786436
  15.9 20.1 %copy-start.14 = (bf16[128]{0:T(256)(128)(2,1)S(1)}, bf16[128]{0:T(256)(128)(2,1)}, u32[]{:S(2)}) copy-start(bf16[128]{0:T(256)(128)(2,1)} %param.27) | copy-start | bytes 772
  15.9 20.1 %copy-start.15 = (bf16[128]{0:T(256)(128)(2,1)S(1)}, bf16[128]{0:T(256)(128)(2,1)}, u32[]{:S(2)}) copy-start(bf16[128]{0:T(256)(128)(2,1)} %param.26) | copy-start | bytes 772
  15.9 22.0 %all-to-all-start = ((bf16[32,8,1152]{2,1,0:T(8,128)(2,1)}), bf16[32,8,1152]{2,1,0:T(8,128)(2,1)S(1)}, u32[]{:S(2)}, u32[]{:S(2)}) async-start(bf16[32,8,1152]{2,1,0:T(8,128)(2,1)} %fusion.1), calls=%async_computation | async-start | bytes 1179648 | tf_op jit(solution)/shard_map/all_to_all | solution.py:46
  25.7 555.3 %reduce-scatter.3.cloned.1.call-start = ((), (), s32[]{:S(2)}) async-start(), calls=%async_computation.13 | async-start | bytes 15728640 | tf_op jit(solution)/shard_map/reduce_scatter | solution.py:839
  133.8 48.7 %copy-start = (bf16[768,2176]{1,0:T(8,128)(2,1)S(1)}, bf16[768,2176]{1,0:T(8,128)(2,1)}, u32[]{:S(2)}) copy-start(bf16[768,2176]{1,0:T(8,128)(2,1)} %get-tuple-element.47) | copy-start | bytes 10027012
  258.3 1.3 copy-start.2
  258.3 322.7 %reduce-scatter.5.cloned.1.call-start = ((), (), s32[]{:S(2)}) async-start(), calls=%async_computation.14 | async-start | bytes 15728640 | tf_op jit(solution)/shard_map/reduce_scatter | solution.py:844
  322.4 1.6 copy-start.1
  361.8 21.0 %all-to-all-start.4 = ((bf16[32,8,2048]{2,1,0:T(8,128)(2,1)}), bf16[32,8,2048]{2,1,0:T(8,128)(2,1)S(1)}, u32[]{:S(2)}, u32[]{:S(2)}) async-start(bf16[32,8,2048]{2,1,0:T(8,128)(2,1)} %bitcast.82), calls=%async_computation.4 | async-start | bytes 2097152 | tf_op jit(solution)/shard_map/all_to_all | solution.py:46
  382.8 81.1 %all-to-all-start.6 = ((bf16[32,16,2048]{2,1,0:T(8,128)(2,1)}), bf16[32,16,2048]{2,1,0:T(8,128)(2,1)S(1)}, u32[]{:S(2)}, u32[]{:S(2)}) async-start(bf16[32,16,2048]{2,1,0:T(8,128)(2,1)} %bitcast.79), calls=%async_computation.6 | async-start | bytes 4194304 | tf_op jit(solution)/shard_map/all_to_all | solution.py:46
  389.6 74.3 %copy-start.3 = (bf16[256,768]{1,0:T(8,128)(2,1)S(1)}, bf16[256,768]{1,0:T(8,128)(2,1)}, u32[]{:S(2)}) copy-start(bf16[256,768]{1,0:T(8,128)(2,1)} %get-tuple-element.46.pick_t) | copy-start | bytes 1179652
  467.4 86.0 %all-to-all-start.7 = ((bf16[4,256,512]{2,1,0:T(8,128)(2,1)}), bf16[4,256,512]{2,1,0:T(8,128)(2,1)S(1)}, u32[]{:S(2)}, u32[]{:S(2)}) async-start(bf16[4,256,512]{2,1,0:T(8,128)(2,1)} %pad_maximum_fusion), calls=%async_computation.7 | async-start | bytes 2097152 | tf_op jit(solution)/shard_map/all_to_all | solution.py:46
  470.9 82.3 %copy-start.8 = (f32[16,512]{1,0:T(8,128)S(1)}, f32[16,512]{1,0:T(8,128)}, u32[]{:S(2)}) copy-start(f32[16,512]{1,0:T(8,128)} %get-tuple-element.74) | copy-start | bytes 98308
  470.9 83.7 %copy-start.16 = (bf16[256,512]{1,0:T(8,128)(2,1)S(1)}, bf16[256,512]{1,0:T(8,128)(2,1)}, u32[]{:S(2)}) copy-start(bf16[256,512]{1,0:T(8,128)(2,1)} %get-tuple-element.73) | copy-start | bytes 786436
  556.1 22.5 %all-to-all-start.8 = ((bf16[32,8,1664]{2,1,0:T(8,128)(2,1)}), bf16[32,8,1664]{2,1,0:T(8,128)(2,1)S(1)}, u32[]{:S(2)}, u32[]{:S(2)}) async-start(bf16[32,8,1664]{2,1,0:T(8,128)(2,1)} %pad_maximum_fusion.1), calls=%async_computation.8 | async-start | bytes 1703936 | tf_op jit(solution)/shard_map/all_to_all | solution.py:46
Sparse Core Ops, SparseCore 0:
  13.3 155.5 all-gather.2
  171.1 119.5 all-gather.4
  293.8 123.2 reduce-scatter.2
  419.4 135.0 reduce-scatter.4

commit v4 on v3

--- a/solution.py
+++ b/solution.py
@@ -32,7 +32,6 @@
 
 BF = jnp.bfloat16
 F32 = jnp.float32
-COSTE = pl.CostEstimate(flops=20000000000, bytes_accessed=1, transcendentals=0)
 COST = pl.CostEstimate(flops=1, bytes_accessed=1, transcendentals=0)
 
 
@@ -179,9 +178,9 @@
 def front_kernel(
     local, bias, cos_rows, sin_rows, gain1, gain2, q_gain, k_gain, router_t, routes, slot_of, slot_back, keep,
     wq_hbm, wk_hbm, wv_hbm, wo_hbm,
-    x_out, dy_out, an_out, resid_out, mixed_out, q_out, k_out, qh_out, kh_out, vh_out, ob_out,
-    gates_out, send_out, send_dy_out, pick_out,
-    wq, wk, wv, wo, x_all, dy_all, parts, halves, box, total, load_sem, send_sem, recv_sem,
+    x_out, dy_out, resid_out, mixed_out, q_out, k_out, qh_out, kh_out, vh_out, ob_out,
+    gates_out, send_out, send_dy_out, pick_out, pick_y_out,
+    wq, wk, wv, wo, x_all, dy_all, an, parts, halves, box, total, load_sem, send_sem, recv_sem,
 ):
     me = lax.axis_index("tensor")
     ready = greet("tensor", ring(me))
@@ -201,16 +200,16 @@
         square = square + row_sum(value * value)
     r1 = inverse_rms(square, width)
     for t in range(blocks):
-        an_out[t] = (x_all[t].astype(F32) * r1 * gain1[t : t + 1, :]).astype(BF)
+        an[t] = (x_all[t].astype(F32) * r1 * gain1[t : t + 1, :]).astype(BF)
     x_out[...] = x_all[...]
 
     for copy in loads:
         copy.wait()
 
     def project(weight):
-        value = dot(an_out[0], weight[0:col, :])
+        value = dot(an[0], weight[0:col, :])
         for t in range(1, blocks):
-            value = value + dot(an_out[t], weight[t * col : (t + 1) * col, :])
+            value = value + dot(an[t], weight[t * col : (t + 1) * col, :])
         return value
 
     q_out[...] = project(wq)
@@ -265,6 +264,7 @@
         pick_back = jnp.where(slot_back[k : k + 1, :] == slot, 1.0, pick_back)
         weight = jnp.where(hot, gate * keep[k : k + 1, :], weight)
     pick_out[...] = pick_back.T.astype(BF)
+    pick_y_out[...] = pick.T.astype(BF)
     pick = pick.astype(BF)
     for t in range(blocks):
         send_out[:, t * col : (t + 1) * col] = dot(pick, mixed_out[t]).astype(BF)
@@ -297,18 +297,18 @@
     return pl.pallas_call(
         front_kernel,
         out_shape=(
-            shape(tiles, BF), shape(tiles, BF), shape(tiles, BF), shape(tiles, F32),
+            shape(tiles, BF), shape(tiles, BF), shape(tiles, F32),
             shape(tiles, BF), shape((tok, col), F32), shape((tok, col), F32),
             shape((tok, col), BF), shape((tok, col), BF), shape((tok, col), BF),
             shape((tok, col), BF), shape((top, tok), F32), shape((slots, width + 128), BF),
-            shape((slots, width), BF), shape((tok, slots), BF),
+            shape((slots, width), BF), shape((tok, slots), BF), shape((tok, slots), BF),
         ),
         in_specs=[vmem] * 13 + [pl.BlockSpec(memory_space=pl.ANY)] * 4,
         out_specs=(vmem,) * 15,
         scratch_shapes=[
             pltpu.VMEM((width, col), BF), pltpu.VMEM((width, col), BF), pltpu.VMEM((width, col), BF),
             pltpu.VMEM((col, width), BF),
-            pltpu.VMEM(tiles, BF), pltpu.VMEM(tiles, BF), pltpu.VMEM(tiles, BF),
+            pltpu.VMEM(tiles, BF), pltpu.VMEM(tiles, BF), pltpu.VMEM(tiles, BF), pltpu.VMEM(tiles, BF),
             pltpu.VMEM((2, tok // 2, col), BF), pltpu.VMEM((2, tok, col), BF), pltpu.VMEM(tiles, BF),
             pltpu.SemaphoreType.DMA((4,)),
             pltpu.SemaphoreType.DMA((16,)), pltpu.SemaphoreType.DMA((16,)),
@@ -322,20 +322,16 @@
 
 
 def back_kernel(
-    pick_t, ret_early, ret_late, slot_of, keep, gates, routes, bias, cos_rows, sin_rows, gain1, gain2, q_gain,
-    k_gain, router, resid, dy_all, x_all, mixed, qh, kh, vh, ob,
-    q_hbm, k_hbm, an_hbm, wq_hbm, wk_hbm, wv_hbm, wo_hbm,
-    grads, dx_out, small_out,
-    q_raw, k_raw, an, wq, wk, wv, wo, parts, box, total, dm, dr, d_qkv, d_att,
-    halves, dg_mine, dg_box, note, load_sem, send_sem, recv_sem,
+    pick_t, ret_early, ret_late, slot_of, keep, gates, routes, bias, cos_rows, sin_rows, gain2,
+    q_gain, k_gain, router, resid, dy_all, mixed, qh, kh, vh,
+    q_hbm, k_hbm, wo_hbm,
+    d_qkv, dr, d_mine, router_out, small_out,
+    q_raw, k_raw, wo, parts, halves, box, total, dm, d_att, dg_mine, dg_box,
+    load_sem, send_sem, recv_sem,
 ):
     me, peers = tensor_peers()
     ready = greet("tensor", peers)
-    loads = fetch(
-        [(wo_hbm, wo), (q_hbm, q_raw), (k_hbm, k_raw), (wq_hbm, wq), (wk_hbm, wk), (wv_hbm, wv),
-         (an_hbm, an)],
-        load_sem,
-    )
+    loads = fetch([(wo_hbm, wo), (q_hbm, q_raw), (k_hbm, k_raw)], load_sem)
     blocks, tok, col = parts.shape
     width = blocks * col
     post = Post("tensor", send_sem, recv_sem)
@@ -346,7 +342,7 @@
             dot(pick_t[:, :early], ret_early[:, lanes]) + dot(pick_t[:, early:], ret_late[:, lanes])
         ).astype(BF)
     ready()
-    first = scatter_start(post, parts, halves.at[pl.ds(0, 2)], me)
+    first = scatter_start(post, parts, halves, me)
     top = routes.shape[0]
     for n, (ret, base) in enumerate(((ret_early, 0), (ret_late, early))):
         dgate = row_sum(ret[:, width : width + 128].astype(F32))
@@ -356,8 +352,8 @@
             found = jnp.sum(jnp.where(hot, dgate, 0.0), axis=0, keepdims=True)
             dg_mine[k : k + 1, :] = dg_mine[k : k + 1, :] + found if n else found
     dg_in = [post.push(dg_mine, dg_box.at[d], peer) for d, peer in enumerate(peers)]
-    moved = scatter_relay(post, parts, halves.at[pl.ds(0, 2)], box.at[pl.ds(0, 2)], me, first)
-    total[me] = scatter_total(parts, box.at[pl.ds(0, 2)], me, moved).astype(BF)
+    moved = scatter_relay(post, parts, halves, box, me, first)
+    total[me] = scatter_total(parts, box, me, moved).astype(BF)
     total_first = gather_start(post, total, me)
 
     arrive(dg_in)
@@ -376,22 +372,27 @@
     square = jnp.zeros((tok, 1), F32)
     for t in range(blocks):
         rows = slice(t * col, (t + 1) * col)
-        grads[rows, 4 * col :] = dot(mixed[t].T, d_logits).astype(BF)
         dm[t] = dot(d_logits, router[rows, :], 1, 1)
         square = square + row_sum(resid[t] * resid[t])
     r2 = inverse_rms(square, width)
-    arrive(gather_relay(post, total, me, total_first))
+    total_moved = gather_relay(post, total, me, total_first)
+    for t in range(blocks):
+        rows = slice(t * col, (t + 1) * col)
+        router_out[rows, :] = dot(mixed[t].T, d_logits).astype(BF)
+    arrive(total_moved)
     cross = jnp.zeros((tok, 1), F32)
     for t in range(blocks):
         dm[t] = dm[t] + total[t].astype(F32)
         cross = cross + row_sum(resid[t] * gain2[t : t + 1, :] * dm[t])
     cross = cross * (1.0 / width) * r2 * r2 * r2
+    small_out[...] = jnp.zeros_like(small_out)
     for t in range(blocks):
         d_mixed = dm[t]
-        small_out[4 + t : 5 + t, :] = jnp.sum(d_mixed * resid[t] * r2, axis=0, keepdims=True)
+        small_out[t : t + 1, :] = jnp.sum(d_mixed * resid[t] * r2, axis=0, keepdims=True)
         d_resid = dy_all[t].astype(F32) + r2 * gain2[t : t + 1, :] * d_mixed - resid[t] * cross
         dm[t] = d_resid
         dr[t] = d_resid.astype(BF)
+    d_mine[...] = dm[me]
     for copy in loads:
         copy.wait()
     value = dot(dr[0], wo[:, 0:col], 1, 1)
@@ -428,90 +429,45 @@
         d_k, part = unturn(dot(d_scores.T.astype(BF), qh[:, lanes]) * scale, k_raw[:, lanes], k_gain)
         k_part = k_part + part
         d_qkv[:, col + h * head : col + (h + 1) * head] = d_k
+    small_out[blocks : blocks + 1, :head] = q_part
+    small_out[blocks : blocks + 1, head : 2 * head] = k_part
     post.finish()
-    for t in range(blocks):
-        rows = slice(t * col, (t + 1) * col)
-        parts[t] = (
-            dot(d_qkv[:, 0:col], wq[rows, :], 1, 1)
-            + dot(d_qkv[:, col : 2 * col], wk[rows, :], 1, 1)
-            + dot(d_qkv[:, 2 * col : 3 * col], wv[rows, :], 1, 1)
-        ).astype(BF)
-    halves_again, box_again = halves.at[pl.ds(2, 2)], box.at[pl.ds(2, 2)]
-    first = scatter_start(post, parts, halves_again, me)
-    for t in range(blocks):
-        rows = slice(t * col, (t + 1) * col)
-        grads[rows, : 3 * col] = dot(an[t].T, d_qkv[...]).astype(BF)
-        if t == 1:
-            moved = scatter_relay(post, parts, halves_again, box_again, me, first)
-    for t in range(blocks):
-        rows = slice(t * col, (t + 1) * col)
-        grads[rows, 3 * col : 4 * col] = dot(dr[t].T, ob[...]).astype(BF)
-    square = jnp.zeros((tok, 1), F32)
-    for t in range(blocks):
-        value = x_all[t].astype(F32)
-        square = square + row_sum(value * value)
-    r1 = inverse_rms(square, width)
-    d_an = scatter_total(parts, box_again, me, moved)
-    x_mine = x_all[me].astype(F32)
-    grown = gain1[pl.ds(me, 1), :] * d_an
-    mean_part = row_sum(x_mine * grown)
-    note[me, 0:8, :] = jnp.broadcast_to(
-        jnp.sum(d_an * x_mine * r1, axis=0, keepdims=True), (8, col)
-    )
-    note[me, 8:16, 0:tok] = jnp.broadcast_to(mean_part, (tok, 128)).T[0:8, :]
-    note[me, 8:16, tok : tok + head] = jnp.broadcast_to(q_part, (8, head))
-    note[me, 8:16, tok + head : tok + 2 * head] = jnp.broadcast_to(k_part, (8, head))
-    arrive([post.push(note.at[me], note.at[me], peer) for peer in peers])
-    facts = note[0, 8:16, :]
-    for t in range(1, blocks):
-        facts = facts + note[t, 8:16, :]
-    for t in range(blocks):
-        small_out[t : t + 1, :] = note[t, 0:1, :]
-    small_out[8:16, :] = facts
-    mean = jnp.broadcast_to(facts[0:1, 0:tok], (128, tok)).T[:, 0:1] * (1.0 / width)
-    dx_out[...] = (dm[me] + r1 * grown - x_mine * (r1 * r1 * r1 * mean)).astype(BF)
-    post.finish()
-
-
-def back_call(pick_t, ret_early, ret_late, slot_of, keep, gates, routes, bias, cos_rows, sin_rows, gain1, gain2,
-              q_gain, k_gain, router, resid, dy_all, x_all, mixed, qh, kh, vh, ob, q_raw, k_raw,
-              an, weights):
-    blocks, tok, col = x_all.shape
+
+
+def back_call(pick_t, ret_early, ret_late, slot_of, keep, gates, routes, bias, cos_rows, sin_rows,
+              gain2, q_gain, k_gain, router, resid, dy_all, mixed, qh, kh, vh, q_raw, k_raw, wo):
+    blocks, tok, col = dy_all.shape
     width = blocks * col
     tiles = (blocks, tok, col)
     shape = jax.ShapeDtypeStruct
     vmem = pl.BlockSpec(memory_space=pltpu.VMEM)
     top = routes.shape[0]
-    count = 12 + 2 * (blocks - 1)
+    count = 8 + blocks - 1
     return pl.pallas_call(
         back_kernel,
         out_shape=(
-            shape((width, 4 * col + 128), BF), shape((tok, col), BF), shape((16, col), F32),
+            shape((tok, 3 * col), BF), shape(tiles, BF), shape((tok, col), F32),
+            shape((width, 128), BF), shape((8, col), F32),
         ),
-        in_specs=[vmem] * 23 + [pl.BlockSpec(memory_space=pl.ANY)] * 7,
-        out_specs=(vmem,) * 3,
+        in_specs=[vmem] * 20 + [pl.BlockSpec(memory_space=pl.ANY)] * 3,
+        out_specs=(vmem,) * 5,
         scratch_shapes=[
-            pltpu.VMEM((tok, col), F32), pltpu.VMEM((tok, col), F32), pltpu.VMEM(tiles, BF),
-            pltpu.VMEM((width, col), BF), pltpu.VMEM((width, col), BF), pltpu.VMEM((width, col), BF),
-            pltpu.VMEM((col, width), BF),
-            pltpu.VMEM(tiles, BF), pltpu.VMEM((4, tok, col), BF),
-            pltpu.VMEM(tiles, BF), pltpu.VMEM(tiles, F32), pltpu.VMEM(tiles, BF),
-            pltpu.VMEM((tok, 3 * col), BF), pltpu.VMEM((tok, col), BF),
-            pltpu.VMEM((4, tok // 2, col), BF),
+            pltpu.VMEM((tok, col), F32), pltpu.VMEM((tok, col), F32), pltpu.VMEM((col, width), BF),
+            pltpu.VMEM(tiles, BF), pltpu.VMEM((2, tok // 2, col), BF), pltpu.VMEM((2, tok, col), BF),
+            pltpu.VMEM(tiles, BF), pltpu.VMEM(tiles, F32), pltpu.VMEM((tok, col), BF),
             pltpu.VMEM((top, tok), F32), pltpu.VMEM((blocks - 1, top, tok), F32),
-            pltpu.VMEM((blocks, 16, col), F32),
-            pltpu.SemaphoreType.DMA((7,)),
+            pltpu.SemaphoreType.DMA((3,)),
             pltpu.SemaphoreType.DMA((count,)), pltpu.SemaphoreType.DMA((count,)),
         ],
         compiler_params=pltpu.CompilerParams(
-            collective_id=2, has_side_effects=True, vmem_limit_bytes=60 * 1024 * 1024
+            collective_id=2, has_side_effects=True, vmem_limit_bytes=48 * 1024 * 1024
         ),
         cost_estimate=pl.CostEstimate(
-            flops=20000000000, bytes_accessed=1, transcendentals=0
+            flops=20_000_000_000, bytes_accessed=1, transcendentals=0
         ),
         name="back",
-    )(pick_t, ret_early, ret_late, slot_of, keep, gates, routes, bias, cos_rows, sin_rows, gain1, gain2, q_gain,
-      k_gain, router, resid, dy_all, x_all, mixed, qh, kh, vh, ob, q_raw, k_raw, an, *weights)
+    )(pick_t, ret_early, ret_late, slot_of, keep, gates, routes, bias, cos_rows, sin_rows, gain2,
+      q_gain, k_gain, router, resid, dy_all, mixed, qh, kh, vh, q_raw, k_raw, wo)
 
 
 def expert_kernel(side, per, early, rows_ref, grads_ref, w_ref, *rest):
@@ -519,7 +475,7 @@
         y_rest, dx_rest, *rest = rest
         y_ref, dx_ref, *rest = rest
     else:
-        y_ref, dx_ref, y_rest, dx_rest, *rest = rest
+        dx_ref, y_rest, dx_rest, *rest = rest
     grad_ref, rows, rows_t, dys, dys_t, y_acc, dx_acc, gate_of, dgate = rest
     step = pl.program_id(0)
     count, width = rows.shape
@@ -570,25 +526,33 @@
         y_rows = (y_acc[...] * gate_of[...]).astype(BF)
         dx_rows = dx_acc[...].astype(BF)
         if side:
+            here = selector(
+                (y_ref.shape[0], count),
+                lambda p: jnp.where(p % (2 * per) < per, -1, p // (2 * per) * per + p % (2 * per) - per),
+            )
+            there = selector(
+                (y_ref.shape[0], count),
+                lambda p: jnp.where(p % (2 * per) < per, p // (2 * per) * per + p % (2 * per), -1),
+            )
+            y_ref[...] = (dot(here, y_rows) + dot(there, y_rest[...])).astype(BF)
             chunk = per + late
             here = selector(
-                (y_ref.shape[0], count),
+                (dx_ref.shape[0], count),
                 lambda p: jnp.where(p % chunk < late, -1, p // chunk * per + p % chunk - late),
             )
             there = selector(
-                (y_ref.shape[0], y_rest.shape[0]),
+                (dx_ref.shape[0], dx_rest.shape[0]),
                 lambda p: jnp.where(p % chunk < late, p // chunk * late + p % chunk, -1),
             )
-            y_ref[...] = (dot(here, y_rows) + dot(there, y_rest[...])).astype(BF)
             dx_ref[:, :width] = (dot(here, dx_rows) + dot(there, dx_rest[:, :width])).astype(BF)
             dx_ref[:, width:] = (dot(here, facts) + dot(there, dx_rest[:, width:])).astype(BF)
         else:
-            soon = selector((y_ref.shape[0], count), lambda p: p // early * per + p % early)
+            y_rest[...] = y_rows
+            soon = selector((dx_ref.shape[0], count), lambda p: p // early * per + p % early)
             later = selector(
-                (y_rest.shape[0], count), lambda p: p // late * per + early + p % late
+                (dx_rest.shape[0], count), lambda p: p // late * per + early + p % late
             )
-            for pick, y_out, dx_out in ((soon, y_ref, dx_ref), (later, y_rest, dx_rest)):
-                y_out[...] = dot(pick, y_rows).astype(BF)
+            for pick, dx_out in ((soon, dx_ref), (later, dx_rest)):
                 dx_out[:, :width] = dot(pick, dx_rows).astype(BF)
                 dx_out[:, width:] = dot(pick, facts).astype(BF)
 
@@ -603,11 +567,17 @@
     def whole(value):
         return pl.BlockSpec(value.shape, lambda q: (0, 0), pipeline_mode=pl.Buffered(1))
 
-    def pair(size):
-        return [shape((groups * size, width), BF), shape((groups * size, width + 128), BF)]
+    def plain(size):
+        return shape((groups * size, width), BF)
+
+    def wider(size):
+        return shape((groups * size, width + 128), BF)
 
     block = pl.BlockSpec((1, 3, width, hidden), lambda q: (q, 0, 0, 0))
-    outs = pair(2 * per - early) if side else pair(early) + pair(per - early)
+    if side:
+        outs = [plain(2 * per), wider(2 * per - early)]
+    else:
+        outs = [wider(early), plain(per), wider(per - early)]
     return pl.pallas_call(
         functools.partial(expert_kernel, side, per, early),
         grid=(quarters,),
@@ -625,7 +595,7 @@
             pltpu.VMEM((count, 1), F32),
         ],
         compiler_params=pltpu.CompilerParams(vmem_limit_bytes=60 * 1024 * 1024),
-        cost_estimate=COSTE if side else COST,
+        cost_estimate=COST,
         name=f"expert{side}",
     )(rows, grads, weights, *rest)
 
@@ -643,98 +613,198 @@
 
 ORDERS = ((1, 3, 2, 4), (3, 2, 4, 1), (2, 4, 1, 3), (4, 1, 3, 2))
 
-def reduce_kernel(part, out, buf, box, got, load_sem, out_sem, send_sem, recv_sem):
+def reduce_kernel(
+    d_qkv, dr, d_mine, router_part, small_in, x_all, gain1, ob, pick_y, ret_y,
+    resid_hbm, wq_hbm, wk_hbm, wv_hbm,
+    wide_out, dx_out, out_out, small_out,
+    wq, wk, wv, resid, parts, y_parts, halves, box_x, note, buf, box, got,
+    load_sem, out_sem, x_send, x_recv, send_sem, recv_sem,
+):
+    me, peers = tensor_peers()
     dims = plane()
     barrier = pltpu.get_barrier_semaphore()
-    for _, partner in dims:
-        pl.semaphore_signal(barrier, inc=1, device_id={"expert": partner}, device_id_type=MESH)
-    load = pltpu.make_async_copy(part, buf, load_sem)
-    load.start()
-    pl.semaphore_wait(barrier, len(dims))
-    load.wait()
+    for axis, others in (("tensor", peers), ("expert", [partner for _, partner in dims])):
+        for other in others:
+            pl.semaphore_signal(barrier, inc=1, device_id={axis: other}, device_id_type=MESH)
+    loads = fetch(
+        [(wq_hbm, wq), (wk_hbm, wk), (wv_hbm, wv), (resid_hbm.at[me], resid)], load_sem
+    )
+    blocks, tok, col = x_all.shape
+    width = blocks * col
+    head = col // blocks
     core = dims[0][0]
-    sends = []
-
-    def push(slot, source, target, partner):
-        copy = pltpu.make_async_remote_copy(
-            src_ref=source, dst_ref=target, send_sem=send_sem.at[slot], recv_sem=recv_sem.at[slot],
-            device_id={"expert": partner}, device_id_type=MESH)
-        copy.start()
-        sends.append(copy)
-        return copy
-
-    def add(target, target_at, place, first, count):
+    square = jnp.zeros((tok, 1), F32)
+    for t in range(blocks):
+        value = x_all[t].astype(F32)
+        square = square + row_sum(value * value)
+    r1 = inverse_rms(square, width)
+    for copy in loads:
+        copy.wait()
+    for t in range(blocks):
+        rows = slice(t * col, (t + 1) * col)
+        parts[t] = (
+            dot(d_qkv[:, 0:col], wq[rows, :], 1, 1)
+            + dot(d_qkv[:, col : 2 * col], wk[rows, :], 1, 1)
+            + dot(d_qkv[:, 2 * col : 3 * col], wv[rows, :], 1, 1)
+        ).astype(BF)
+    pl.semaphore_wait(barrier, len(peers) + len(dims))
+    post_x = Post("tensor", x_send, x_recv)
+    post = Post("expert", send_sem, recv_sem)
+    x_halves, x_box = halves.at[pl.ds(0, 2)], box_x.at[pl.ds(0, 2)]
+    y_halves, y_box = halves.at[pl.ds(2, 2)], box_x.at[pl.ds(2, 2)]
+    x_first = scatter_start(post_x, parts, x_halves, me)
+
+    chunks = buf.shape[0] // blocks
+    rows_chunk = buf.shape[1]
+
+    def products(t):
+        here = pl.ds(t * chunks, chunks)
+        normed = (x_all[t].astype(F32) * r1 * gain1[pl.ds(t, 1), :]).T.astype(BF)
+        for n in range(3):
+            lanes = slice(n * col, (n + 1) * col)
+            value = dot(normed, d_qkv[:, lanes]).astype(BF)
+            buf[here, :, lanes] = value.reshape(chunks, rows_chunk, col)
+        value = dot(dr[t].T, ob[...]).astype(BF)
+        buf[here, :, 3 * col : 4 * col] = value.reshape(chunks, rows_chunk, col)
+        value = router_part[pl.ds(t * col, col), :]
+        buf[here, :, 4 * col :] = value.reshape(chunks, rows_chunk, value.shape[1])
+
+    def add(target, place, first, count):
         def one(i, _):
             total = buf[place + i].astype(F32) + box[first + i].astype(F32)
-            target[target_at + i] = total.astype(BF)
+            target[place + i] = total.astype(BF)
             return 0
+
         lax.fori_loop(0, count, one, 0)
 
     copies = []
-    for s in range(4):
-        copies.append(push(s, buf.at[pl.ds((1 - core) * 64 + s * 16, 16)], box.at[pl.ds(31 * s, 16)], dims[0][1]))
+    for n in range(2):
+        products(2 * (1 - core) + n)
+        for s in range(2 * n, 2 * n + 2):
+            source = buf.at[pl.ds((1 - core) * 64 + s * 16, 16)]
+            copies.append(post.push(source, box.at[pl.ds(31 * s, 16)], dims[0][1]))
+    x_moved = scatter_relay(post_x, parts, x_halves, x_box, me, x_first)
+    for n in range(2):
+        products(2 * core + n)
     place = [core * 64 + s * 16 for s in range(4)]
+    size, first = 16, 0
+
+    def halve(k):
+        for s in range(4):
+            copies[s].wait_recv()
+            add(buf, place[s], 31 * s + first, size)
+            bit, partner = dims[ORDERS[s][k]]
+            half = size // 2
+            copies[s] = post.push(
+                buf.at[pl.ds(place[s] + (1 - bit) * half, half)],
+                box.at[pl.ds(31 * s + first + size, half)],
+                partner,
+            )
+            place[s] = place[s] + bit * half
+
+    halve(0)
+    first, size = first + size, size // 2
+
+    for t in range(blocks):
+        y_parts[t] = dot(pick_y[...], ret_y[:, t * col : (t + 1) * col]).astype(BF)
+    y_first = scatter_start(post_x, y_parts, y_halves, me)
+    d_an = scatter_total(parts, x_box, me, x_moved)
+    x_mine = x_all[me].astype(F32)
+    grown = gain1[pl.ds(me, 1), :] * d_an
+    mean_part = row_sum(x_mine * grown)
+    note[me, 0:8, :] = jnp.broadcast_to(
+        jnp.sum(d_an * x_mine * r1, axis=0, keepdims=True), (8, col)
+    )
+    note[me, 8:16, 0:tok] = jnp.broadcast_to(mean_part, (tok, 128)).T[0:8, :]
+    note[me, 8:16, tok:] = jnp.broadcast_to(small_in[blocks : blocks + 1, : 2 * head], (8, 2 * head))
+    note_in = [post_x.push(note.at[me], note.at[me], peer) for peer in peers]
+
+    halve(1)
+    first, size = first + size, size // 2
+    y_moved = scatter_relay(post_x, y_parts, y_halves, y_box, me, y_first)
+    halve(2)
+    first, size = first + size, size // 2
+    halve(3)
+    first, size = first + size, size // 2
     for s in range(4):
         copies[s].wait_recv()
-        add(buf, place[s], place[s], 31 * s, 16)
-        bit, partner = dims[ORDERS[s][0]]
-        copies[s] = push(4 + s, buf.at[pl.ds(place[s] + (1 - bit) * 8, 8)], box.at[pl.ds(31 * s + 16, 8)], partner)
-        place[s] = place[s] + bit * 8
-    size, first = 8, 16
-    for k in range(1, 5):
-        for s in range(4):
-            copies[s].wait_recv()
-            if k < 4:
-                add(buf, place[s], place[s], 31 * s + first, size)
-                bit, partner = dims[ORDERS[s][k]]
-                half = size // 2
-                copies[s] = push(4 * (k + 1) + s, buf.at[pl.ds(place[s] + (1 - bit) * half, half)],
-                                 box.at[pl.ds(31 * s + first + size, half)], partner)
-                place[s] = place[s] + bit * half
-            else:
-                add(got, place[s], place[s], 31 * s + first, 1)
-                bit, partner = dims[ORDERS[s][3]]
-                here = got.at[pl.ds(place[s], 1)]
-                copies[s] = push(20 + s, here, here, partner)
-        first, size = first + size, size // 2
+        add(got, place[s], 31 * s + first, 1)
+        here = got.at[pl.ds(place[s], 1)]
+        copies[s] = post.push(here, here, dims[ORDERS[s][3]][1])
+
+    arrive(note_in)
+    facts = note[0, 8:16, :]
+    for t in range(1, blocks):
+        facts = facts + note[t, 8:16, :]
+    for t in range(blocks):
+        small_out[t : t + 1, :] = note[t, 0:1, :]
+        small_out[blocks + t : blocks + t + 1, :] = small_in[t : t + 1, :]
+    small_out[2 * blocks :, :] = facts
+    mean = jnp.broadcast_to(facts[0:1, 0:tok], (128, tok)).T[:, 0:1] * (1.0 / width)
+    dx_out[...] = (d_mine[...] + r1 * grown - x_mine * (r1 * r1 * r1 * mean)).astype(BF)
+
     size = 1
+    stores = []
     for k in range(3, -1, -1):
         for s in range(4):
             copies[s].wait_recv()
             bit, _ = dims[ORDERS[s][k]]
             place[s] = place[s] - bit * size
-            if k:
-                _, partner = dims[ORDERS[s][k - 1]]
-            else:
-                partner = dims[0][1]
+            partner = dims[ORDERS[s][k - 1]][1] if k else dims[0][1]
             here = got.at[pl.ds(place[s], 2 * size)]
-            copies[s] = push(20 + 4 * (4 - k) + s, here, here, partner)
+            copies[s] = post.push(here, here, partner)
+            if not k:
+                stores.append(
+                    pltpu.make_async_copy(here, wide_out.at[pl.ds(place[s], 16)], out_sem.at[s])
+                )
+                stores[-1].start()
         size *= 2
+        if k == 2:
+            out_out[...] = (resid[...] + scatter_total(y_parts, y_box, me, y_moved)).astype(BF)
     for s in range(4):
         copies[s].wait_recv()
-    store = pltpu.make_async_copy(got, out, out_sem)
-    store.start()
-    for copy in sends:
-        copy.wait_send()
-    store.wait()
-
-def reduce_call(part):
-    chunks, rows, cols = part.shape
+        there = pl.ds((1 - core) * 64 + s * 16, 16)
+        stores.append(pltpu.make_async_copy(got.at[there], wide_out.at[there], out_sem.at[4 + s]))
+        stores[-1].start()
+    post.finish()
+    post_x.finish()
+    for store in stores:
+        store.wait()
+
+
+def reduce_call(d_qkv, dr, d_mine, router_part, small, x_all, gain1, ob, pick_y, ret_y, resid,
+                weights):
+    blocks, tok, col = x_all.shape
+    width = blocks * col
+    tiles = (blocks, tok, col)
+    wide = (128, 16, 4 * col + 128)
+    shape = jax.ShapeDtypeStruct
+    vmem = pl.BlockSpec(memory_space=pltpu.VMEM)
+    hbm = pl.BlockSpec(memory_space=pl.ANY)
+    count = 8 + blocks - 1
     return pl.pallas_call(
         reduce_kernel,
-        out_shape=jax.ShapeDtypeStruct(part.shape, BF),
-        in_specs=[pl.BlockSpec(memory_space=pl.ANY)],
-        out_specs=pl.BlockSpec(memory_space=pl.ANY),
+        out_shape=(
+            shape(wide, BF), shape((tok, col), BF), shape((tok, col), BF), shape((16, col), F32),
+        ),
+        in_specs=[vmem] * 10 + [hbm] * 4,
+        out_specs=(hbm, vmem, vmem, vmem),
         scratch_shapes=[
-            pltpu.VMEM(part.shape, BF),
-            pltpu.VMEM((124, rows, cols), BF),
-            pltpu.VMEM(part.shape, BF),
-            pltpu.SemaphoreType.DMA, pltpu.SemaphoreType.DMA,
+            pltpu.VMEM((width, col), BF), pltpu.VMEM((width, col), BF), pltpu.VMEM((width, col), BF),
+            pltpu.VMEM((tok, col), F32), pltpu.VMEM(tiles, BF), pltpu.VMEM(tiles, BF),
+            pltpu.VMEM((4, tok // 2, col), BF), pltpu.VMEM((4, tok, col), BF),
+            pltpu.VMEM((blocks, 16, col), F32),
+            pltpu.VMEM(wide, BF), pltpu.VMEM((124,) + wide[1:], BF), pltpu.VMEM(wide, BF),
+            pltpu.SemaphoreType.DMA((4,)), pltpu.SemaphoreType.DMA((8,)),
+            pltpu.SemaphoreType.DMA((count,)), pltpu.SemaphoreType.DMA((count,)),
             pltpu.SemaphoreType.DMA((40,)), pltpu.SemaphoreType.DMA((40,)),
         ],
-        compiler_params=pltpu.CompilerParams(collective_id=3, has_side_effects=True, vmem_limit_bytes=48*1024*1024),
+        compiler_params=pltpu.CompilerParams(
+            collective_id=3, has_side_effects=True, vmem_limit_bytes=60 * 1024 * 1024
+        ),
+        cost_estimate=COST,
         name="reduce",
-    )(part)
+    )(d_qkv, dr, d_mine, router_part, small, x_all, gain1, ob, pick_y, ret_y, resid, *weights)
 
 
 def body(
@@ -767,7 +837,7 @@
     local_experts = expert_w.shape[0]
 
     w_stored = jnp.transpose(expert_w, (0, 2, 1, 3))
-    w_all = [lax.all_gather(w_stored[e], "tensor", axis=0) for e in range(local_experts)]
+    w_first = lax.all_gather(w_stored[0], "tensor", axis=0)
 
     routes_t = routes.T
     order_t = pair_order[0].reshape(tok_count, top_count).T
@@ -787,6 +857,8 @@
     inner = jnp.broadcast_to((dest_index % tok_count).astype(BF)[:, None], (tok_count, 64))
     facts = jnp.broadcast_to(counts.astype(BF)[None, :], (tok_count, expert_count))
     outgoing = dot(by_rank, jnp.concatenate([tokens, out_grad, inner, facts], axis=1)).astype(BF)
+    outgoing, w_stored = lax.optimization_barrier((outgoing, w_stored))
+    w_second = lax.all_gather(w_stored[1], "tensor", axis=0)
     got = exchange(outgoing.reshape(groups, move_rows, -1), "expert")
     all_counts = got[:, 0, 2 * col_count + 64 :].astype(jnp.int32)
     lower = jnp.arange(groups, dtype=jnp.int32) < group_id
@@ -822,8 +894,8 @@
     router = jnp.pad(w_router, ((0, 0), (0, 128 - expert_count)))
     weights = (w_query, w_key, w_value, w_output)
     (
-        x_all, dy_all, normed, resid, mixed, q_raw, k_raw, qh, kh, vh, attended, gates, send_rows,
-        send_dy, pick_t,
+        x_all, dy_all, resid, mixed, q_raw, k_raw, qh, kh, vh, attended, gates, send_rows,
+        send_dy, pick_t, pick_y,
     ) = front_call(
         local, bias, cos_rows, sin_rows, gain1, gain2, *head_gains, router.T, routes_t, slot_of,
         slot_back, keep_mask, weights, slots,
@@ -835,30 +907,25 @@
     def homeward(value):
         return exchange(value.reshape(groups, -1, value.shape[1]), "expert").reshape(value.shape)
 
-    y_early, d_early, *rest, partial = expert_call(0, per, early, recv_rows, recv_dy, w_all[0], ())
+    d_early, *rest, partial = expert_call(0, per, early, recv_rows, recv_dy, w_first, ())
     grad_first = lax.psum_scatter(partial, "tensor", scatter_dimension=0, tiled=False)
     ret_early = homeward(d_early)
-    ret_early, y_early, later_rows = lax.optimization_barrier((ret_early, y_early, recv_rows))
-    out_early = homeward(y_early)
-    y_late, d_late, partial = expert_call(1, per, early, later_rows, recv_dy, w_all[1], rest)
+    ret_early, later_rows = lax.optimization_barrier((ret_early, recv_rows))
+    y_rows, d_late, partial = expert_call(1, per, early, later_rows, recv_dy, w_second, rest)
     grad_second = lax.psum_scatter(partial, "tensor", scatter_dimension=0, tiled=False)
-
     ret_late = homeward(d_late)
-    ret_late, y_late = lax.optimization_barrier((ret_late, y_late))
-    out_late = homeward(y_late)
-    grads, dx_slice, small = back_call(
+    ret_late, y_rows = lax.optimization_barrier((ret_late, y_rows))
+    ret_y = homeward(y_rows)
+    d_qkv, dr, d_mine, router_part, small = back_call(
         pick_t, ret_early, ret_late, slot_back, keep_mask, gates, routes_t, bias, cos_rows,
-        sin_rows, gain1, gain2, *head_gains, router, resid, dy_all, x_all, mixed, qh, kh, vh,
-        attended, q_raw, k_raw, normed, weights,
+        sin_rows, gain2, *head_gains, router, resid, dy_all, mixed, qh, kh, vh, q_raw, k_raw,
+        w_output,
     )
-    out_late, small = lax.optimization_barrier((out_late, small))
-    moe_part = dot(pick_t[:, : out_early.shape[0]], out_early)
-    moe_part = (moe_part + dot(pick_t[:, out_early.shape[0] :], out_late)).astype(BF)
-    moe_got = exchange(column_blocks(moe_part, tensor_count), "tensor")
-    moe_slice = jnp.sum(moe_got.astype(F32), axis=0)
-    resid_slice = lax.dynamic_index_in_dim(resid, tensor_id, 0, False)
-    out_slice = (resid_slice + moe_slice).astype(BF)
-    summed = reduce_call(grads.reshape(4 * groups, -1, grads.shape[1])).reshape(grads.shape)
+    summed, dx_slice, out_slice, small = reduce_call(
+        d_qkv, dr, d_mine, router_part, small, x_all, gain1, attended, pick_y, ret_y, resid,
+        weights[:3],
+    )
+    summed = summed.reshape(width, -1)
 
     going = dot(put, jnp.concatenate([out_slice, dx_slice], axis=1), 0, 0).astype(BF)
     small = small[:9].astype(BF).reshape(move_rows, -1)

time: 600 us -> 577 us (0.962)
  Pallas kernels: 310 us -> 296 us
  starting transfers between devices: 27 us -> 20.3 us
  local copies, waits for them, and re-layouts: 19.9 us -> 26.1 us
    reduce_scatter x2, waiting for transfers between devices: 0.01 us -> 17.5 us  [body(): lax.psum_scatter(partial, 'tensor', scatter_dimension=0, tiled=False)]
    all_to_all x5 -> x3, waiting for transfers between devices: 17.6 us -> 1.19 us  [exchange(): return lax.all_to_all(value, axis, split_axis=0, concat_axis=0, tiled=True)]
    pallas_call x2, Pallas kernels: 157 us -> 141 us  [the longest x1 87.3 us: reduce_call(): pl.pallas_call(reduce_kernel, out_shape=(shape(wide, BF), shape((tok, col...]
    all_to_all x5 -> x3, starting transfers between devices: 26.8 us -> 20.1 us  [exchange(): return lax.all_to_all(value, axis, split_axis=0, concat_axis=0, tiled=True)]
  transfers between devices with their start and end apart: 9 -> 7, of which waited for: 3 -> 3; matrix products, arithmetic and copies ran while one was open for 8% -> 7% of each run, Pallas kernels for 52% -> 52%
where the time goes in v4:
time: 577 us; the launch traced here: 573 us
  Pallas kernels  296 us (51%)
  blocking collectives  154 us (27%)
  other arithmetic  32.5 us (6%)
  local copies, waits for them, and re-layouts  26.1 us (5%)
  waiting for transfers between devices  25.6 us (4%)
  starting transfers between devices  20.3 us (4%)
  between operations  14.5 us (3%)
    all_to_all x4, blocking collectives, exchange(): return lax.all_to_all(value, axis, split_axis=0, concat_axis=0, tiled=True)  154 us
    pallas_call x1, Pallas kernels, front_call(): pl.pallas_call(front_kernel, out_shape=(shape(tiles, BF), shape(tiles, BF...  92.2 us
    pallas_call x1, Pallas kernels, reduce_call(): pl.pallas_call(reduce_kernel, out_shape=(shape(wide, BF), shape((tok, col...  87.3 us
    pallas_call x2, Pallas kernels, expert_call(): pl.pallas_call(functools.partial(expert_kernel, side, per, early), grid=(...  63 us
    pallas_call x1, Pallas kernels, back_call(): pl.pallas_call(back_kernel, out_shape=(shape((tok, 3 * col), BF), shape(t...  53.3 us
    all_to_all x3, starting transfers between devices, exchange(): return lax.all_to_all(value, axis, split_axis=0, concat_axis=0, tiled=True)  20.1 us
    reduce_scatter x2, waiting for transfers between devices, body(): lax.psum_scatter(partial, 'tensor', scatter_dimension=0, tiled=False)  17.5 us
    unnamed x76, local copies, waits for them, and re-layouts  11.6 us
  transfers between devices with their start and end apart: 7, of which 3 were waited for; matrix products, arithmetic and copies ran while one was open for 7% of the time, Pallas kernels for 52%

profile of v4, /device:TPU:1, one launch (start us, length us, event | category | flops | bytes accessed | tf_op | source)
XLA Modules:
  0.0 572.8 jit_solution(1799992924133699165)
XLA Ops:
  7.2 3.8 slice.84
  12.5 1.2 convolution_convert_fusion
  13.7 3.8 slice.65
  17.5 9.7 %all-to-all-start = ((bf16[32,8,1152]{2,1,0:T(8,128)(2,1)}), bf16[32,8,1152]{2,1,0:T(8,128)(2,1)S(1)}, u32[]{:S(2)}, u32[]{:S(2)}) async-start(bf16[32,8,1152]{2,1,0:T(8,128)(2,1)} %bitcast.2), calls=%async_computation | async-start | bytes 1179648 | tf_op jit(solution)/shard_map/all_to_all | solution.py:45
  30.1 4.0 convert_reduce_fusion
  34.5 1.0 copy.50.router_t
  38.3 1.2 all-to-all-done
  41.8 1.1 convolution_convert_fusion.3.local
  42.9 92.2 %front.1 = (bf16[4,256,512]{2,1,0:T(8,128)(2,1)}, bf16[4,256,512]{2,1,0:T(8,128)(2,1)}, f32[4,256,512]{2,1,0:T(8,128)}, bf16[4,256,512]{2,1,0:T(8,128)(2,1)}, f3...) custom-call(bf16[256,1024]{1,0:T(8,128)(2,1)} %convolution_convert_f, ...), custom_call_target="tpu_custom_call" | custom-call | tf_op jit(solution)/shard_map/front/pallas_call | solution.py:297
  135.1 48.1 %all_to_all.35 = bf16[32,24,2048]{2,1,0:T(8,128)(2,1)} all-to-all(bf16[32,24,2048]{2,1,0:T(8,128)(2,1)} %bitcast.60), channel_id=1, replica_groups=mesh['expert'=32,'tensor'=4] {'expert'}, dimensions={0} | all-to-all | bytes 6291456 | tf_op jit(solution)/shard_map/all_to_all | solution.py:45
  183.2 45.9 %all_to_all.36 = bf16[32,24,2176]{2,1,0:T(8,128)(2,1)} all-to-all(bf16[32,24,2176]{2,1,0:T(8,128)(2,1)S(1)} %bitcast.58), channel_id=1, replica_groups=mesh['expert'=32,'tensor'=4] {'expert'}, dimensions={0} | all-to-all | bytes 6684672 | tf_op jit(solution)/shard_map/all_to_all | solution.py:45
  229.1 28.9 %expert0.1 = (bf16[256,2176]{1,0:T(8,128)(2,1)}, bf16[384,2048]{1,0:T(8,128)(2,1)}, bf16[128,2176]{1,0:T(8,128)(2,1)}, bf16[4,3,2048,256]{3,2,1,0:T(8,128)(2,1)}) custom-call(bf16[768,2176]{1,0:T(8,128)(2,1)} %bitcast.49, bf16[768,2048]{1,0:T(8,128)(2,1)} %bitcast.51, bf16[4,3,2048,256]{3,2,1,0:T(8,128)(2,1)} %all-gather.3.cloned.1.call-done.w_ref), custom_call_target="tpu_custom_call" | custom-call | flops 1 | bytes 1 | tf_op jit(solution)/shard_map/expert0/pallas_call | solution.py:581
  258.1 1.2 copy-done.24
  259.3 22.3 %all_to_all.37 = bf16[32,8,2176]{2,1,0:T(8,128)(2,1)} all-to-all(bf16[32,8,2176]{2,1,0:T(8,128)(2,1)S(1)} %bitcast.65), channel_id=1, replica_groups=mesh['expert'=32,'tensor'=4] {'expert'}, dimensions={0} | all-to-all | bytes 2228224 | tf_op jit(solution)/shard_map/all_to_all | solution.py:45
  281.6 6.9 %all-gather.5.cloned.1.call-done.w_ref = bf16[4,3,2048,256]{3,2,1,0:T(8,128)(2,1)} async-done(((bf16[1,3,2048,256]{3,2,1,0:T(8,128)(2,1)}), bf16[4,3,2048,256]{3,2,1,0:T(8,128)(2,1)}) %all-gather.5.cloned.1.call-update) | async-done | bytes 12582928 | tf_op jit(solution)/shard_map/all_gather | solution.py:861
  288.5 34.1 %expert1.1 = (bf16[768,2048]{1,0:T(8,128)(2,1)}, bf16[512,2176]{1,0:T(8,128)(2,1)}, bf16[4,3,2048,256]{3,2,1,0:T(8,128)(2,1)}) custom-call(bf16[768,2176]{1,0:T(8,128)(2,1)} %bitcast.50, bf16[768,2048]{1,0:T(8,128)(2,1)} %bitcast.52, bf16[4,3,2048,256]{3,2,1,0:T(8,128)(2,1)} %all-gather.5.cloned.1.call-done.w_ref, ...), custom_call_target="tpu_custom_call" | custom-call | flops 1 | bytes 1 | tf_op jit(solution)/shard_map/expert1/pallas_call | solution.py:581
  322.6 1.6 copy-done.23
  324.3 37.8 %all_to_all.38 = bf16[32,16,2176]{2,1,0:T(8,128)(2,1)} all-to-all(bf16[32,16,2176]{2,1,0:T(8,128)(2,1)S(1)} %bitcast.63), channel_id=1, replica_groups=mesh['expert'=32,'tensor'=4] {'expert'}, dimensions={0} | all-to-all | bytes 4456448 | tf_op jit(solution)/shard_map/all_to_all | solution.py:45
  362.2 5.1 all-to-all-start.5
  367.5 53.3 %back.1 = (bf16[256,1536]{1,0:T(8,128)(2,1)S(1)}, bf16[4,256,512]{2,1,0:T(8,128)(2,1)S(1)}, f32[256,512]{1,0:T(8,128)S(1)}, bf16[2048,128]{1,0:T(8,128)(2,1)S(1)}, f32[8,512]{1,0:T(8,128)S(1)}) custom-call(bf16[256,768]{1,0:T(8,128)(2,1)S(1)} %copy-done.17, bf16[256,2176]{1,0:T(8,128)(2,1)} %bitcast.64, bf16[512,2176]{1,0:T(8,128)(2,1)} %bitcast.62, ...), custom_call_target="tpu_custom_call" | custom-call | flops 20000000000 | bytes 1 | tf_op jit(solution)/shard_map/back/pallas_call | solution.py:446
  420.8 1.0 copy-done
  421.8 0.9 copy-done.2
  424.9 87.3 %reduce.7 = (bf16[128,16,2176]{2,1,0:T(8,128)(2,1)}, bf16[256,512]{1,0:T(8,128)(2,1)}, bf16[256,512]{1,0:T(8,128)(2,1)}, f32[16,512]{1,0:T(8,128)}) custom-call(bf16[256,1536]{1,0:T(8,128)(2,1)} %copy-done.2, bf16[4,256,512]{2,1,0:T(8,128)(2,1)} %copy-done, f32[256,512]{1,0:T(8,128)} %copy-done.5, bf16[2048,128]{1,0:T(8,128)(2,1)} %copy-done.6, ...), custom_call_target="tpu_custom_call" | custom-call | flops 1 | bytes 1 | tf_op jit(solution)/shard_map/reduce/pallas_call | solution.py:785
  513.0 1.4 fusion
  514.4 1.0 pad_maximum_fusion
  515.4 5.3 all-to-all-start.6
  520.7 9.4 %fusion.22 = (bf16[2048,512]{1,0:T(8,128)(2,1)}, f32[2048,512]{1,0:T(8,128)}, f32[2048,512]{1,0:T(8,128)}, f32[2048,512]{1,0:T(8,128)}) fusion(bf16[2048,2176]{1,0:T(8,128)(2,1)} %bitcast.53), kind=kLoop, calls=%fused_computation.77 | loop fusion | flops 3145728 | bytes 23068672 | tf_op jit(solution)/shard_map/slice | solution.py:939
  530.1 1.1 slice.99
  532.2 3.0 copy.53
  535.2 2.5 convert_bitcast_fusion.1
  540.2 17.5 %reduce-scatter.5.cloned.1.call-done = bf16[1,3,2048,256]{3,2,1,0:T(8,128)(2,1)} async-done(((bf16[4,3,2048,256]{3,2,1,0:T(8,128)(2,1)}), bf16[1,3,2048,256]{3,2,1,0:T(8,128)(2,1)}) %reduce-scatter.5.cloned.1.call-update) | async-done | bytes 3145744 | tf_op jit(solution)/shard_map/reduce_scatter | solution.py:915
  557.6 8.4 %convert_bitcast_fusion = f32[2,2048,3,256]{3,1,2,0:T(8,128)} fusion(bf16[1,3,2048,256]{3,2,1,0:T(8,128)(2,1)} %reduce-scatter.5.cloned.1.call-done, bf16[1,3,2048,256]{3,2,1,0:T(8,128)(2,1)} %reduce-scatter.3.cloned.1.call-done), kind=kLoop, calls=%fused_computation.1 | loop fusion | flops 6291456 | bytes 18874368 | tf_op jit(solution)/shard_map/transpose | solution.py:938
  (125 shorter events, 16.5 us)
Async XLA Ops:
  7.2 221.9 %all-gather.3.cloned.1.call-start = ((), (), s32[]{:S(2)}) async-start(), calls=%async_computation.9 | async-start | bytes 15728640 | tf_op jit(solution)/shard_map/all_gather | solution.py:840
  11.0 277.5 %all-gather.5.cloned.1.call-start = ((), (), s32[]{:S(2)}) async-start(), calls=%async_computation.10 | async-start | bytes 15728640 | tf_op jit(solution)/shard_map/all_gather | solution.py:861
  17.4 9.9 %copy-start.29 = (bf16[2048]{0:T(1024)(128)(2,1)S(1)}, bf16[2048]{0:T(1024)(128)(2,1)}, u32[]{:S(2)}) copy-start(bf16[2048]{0:T(1024)(128)(2,1)} %param.22) | copy-start | bytes 12292
  17.4 10.5 %copy-start.30 = (bf16[2048]{0:T(1024)(128)(2,1)S(1)}, bf16[2048]{0:T(1024)(128)(2,1)}, u32[]{:S(2)}) copy-start(bf16[2048]{0:T(1024)(128)(2,1)} %param.29) | copy-start | bytes 12292
  17.4 11.1 %copy-start.32 = (s32[1,3]{1,0:T(1,128)S(1)}, s32[1,3]{1,0:T(1,128)}, u32[]{:S(2)}) copy-start(s32[1,3]{1,0:T(1,128)} %param.18) | copy-start | bytes 40
  17.4 11.8 %copy-start.28 = (s32[1,2048]{1,0:T(1,128)S(1)}, s32[1,2048]{1,0:T(1,128)}, u32[]{:S(2)}) copy-start(s32[1,2048]{1,0:T(1,128)} %param.21) | copy-start | bytes 24580
  17.4 16.6 %copy-start.27 = (bf16[2048,64]{0,1:T(8,128)(2,1)S(1)}, bf16[2048,64]{0,1:T(8,128)(2,1)}, u32[]{:S(2)}) copy-start(bf16[2048,64]{0,1:T(8,128)(2,1)} %param.30) | copy-start | bytes 786436
  17.5 19.5 %copy-start.33 = (bf16[128]{0:T(256)(128)(2,1)S(1)}, bf16[128]{0:T(256)(128)(2,1)}, u32[]{:S(2)}) copy-start(bf16[128]{0:T(256)(128)(2,1)} %param.27) | copy-start | bytes 772
  17.5 19.5 %copy-start.34 = (bf16[128]{0:T(256)(128)(2,1)S(1)}, bf16[128]{0:T(256)(128)(2,1)}, u32[]{:S(2)}) copy-start(bf16[128]{0:T(256)(128)(2,1)} %param.26) | copy-start | bytes 772
  17.5 22.0 %all-to-all-start = ((bf16[32,8,1152]{2,1,0:T(8,128)(2,1)}), bf16[32,8,1152]{2,1,0:T(8,128)(2,1)S(1)}, u32[]{:S(2)}, u32[]{:S(2)}) async-start(bf16[32,8,1152]{2,1,0:T(8,128)(2,1)} %bitcast.2), calls=%async_computation | async-start | bytes 1179648 | tf_op jit(solution)/shard_map/all_to_all | solution.py:45
  27.2 512.9 %reduce-scatter.3.cloned.1.call-start = ((), (), s32[]{:S(2)}) async-start(), calls=%async_computation.11 | async-start | bytes 15728640 | tf_op jit(solution)/shard_map/reduce_scatter | solution.py:911
  135.1 48.1 %copy-start.22 = (bf16[768,2176]{1,0:T(8,128)(2,1)S(1)}, bf16[768,2176]{1,0:T(8,128)(2,1)}, u32[]{:S(2)}) copy-start(bf16[768,2176]{1,0:T(8,128)(2,1)} %get-tuple-element.51) | copy-start | bytes 10027012
  258.1 299.6 %reduce-scatter.5.cloned.1.call-start = ((), (), s32[]{:S(2)}) async-start(), calls=%async_computation.12 | async-start | bytes 15728640 | tf_op jit(solution)/shard_map/reduce_scatter | solution.py:915
  322.6 1.7 copy-start.23
  362.1 5.3 copy-start.1
  362.1 5.3 copy-start.3
  362.1 5.3 copy-start.4
  362.1 5.3 copy-start.8
  362.1 5.3 copy-start.9
  362.1 5.3 copy-start.10
  362.1 5.3 copy-start.11
  362.1 5.3 copy-start.13
  362.1 5.3 copy-start.14
  362.2 5.3 copy-start.15
  362.2 5.3 copy-start.16
  362.2 5.3 copy-start.17
  362.2 5.3 copy-start.18
  362.2 5.3 copy-start.19
  362.2 5.3 copy-start.20
  362.2 5.3 copy-start.21
  362.2 62.6 %all-to-all-start.5 = ((bf16[32,24,2048]{2,1,0:T(8,128)(2,1)}), bf16[32,24,2048]{2,1,0:T(8,128)(2,1)}, u32[]{:S(2)}, u32[]{:S(2)}) async-start(bf16[32,24,2048]{2,1,0:T(8,128)(2,1)} %bitcast.59), calls=%async_computation.5 | async-start | bytes 6291456 | tf_op jit(solution)/shard_map/all_to_all | solution.py:45
  515.4 22.3 %all-to-all-start.6 = ((bf16[32,8,1664]{2,1,0:T(8,128)(2,1)}), bf16[32,8,1664]{2,1,0:T(8,128)(2,1)S(1)}, u32[]{:S(2)}, u32[]{:S(2)}) async-start(bf16[32,8,1664]{2,1,0:T(8,128)(2,1)} %pad_maximum_fusion), calls=%async_computation.6 | async-start | bytes 1703936 | tf_op jit(solution)/shard_map/all_to_all | solution.py:45
  (10 other events, 8.9 us)
Sparse Core Ops, SparseCore 0:
  11.1 155.4 all-gather.2
  168.9 119.5 all-gather.4
  291.5 132.6 reduce-scatter.2
  426.6 131.0 reduce-scatter.4

commit v5 on v4

--- a/solution.py
+++ b/solution.py
@@ -32,6 +32,7 @@
 
 BF = jnp.bfloat16
 F32 = jnp.float32
+SHADOW = pl.CostEstimate(flops=40_000_000_000, bytes_accessed=1, transcendentals=0)
 COST = pl.CostEstimate(flops=1, bytes_accessed=1, transcendentals=0)
 
 
@@ -176,10 +177,10 @@
 
 
 def front_kernel(
-    local, bias, cos_rows, sin_rows, gain1, gain2, q_gain, k_gain, router_t, routes, slot_of, slot_back, keep,
+    local, bias, cos_rows, sin_rows, gain1, gain2, q_gain, k_gain, router_t, routes, slot_of, keep,
     wq_hbm, wk_hbm, wv_hbm, wo_hbm,
     x_out, dy_out, resid_out, mixed_out, q_out, k_out, qh_out, kh_out, vh_out, ob_out,
-    gates_out, send_out, send_dy_out, pick_out, pick_y_out,
+    gates_out, send_out, pick_out,
     wq, wk, wv, wo, x_all, dy_all, an, parts, halves, box, total, load_sem, send_sem, recv_sem,
 ):
     me = lax.axis_index("tensor")
@@ -254,17 +255,14 @@
     slots = send_out.shape[0]
     slot = lax.broadcasted_iota(jnp.int32, (slots, tok), 0)
     pick = jnp.zeros((slots, tok), F32)
-    pick_back = jnp.zeros((slots, tok), F32)
     weight = jnp.zeros((slots, tok), F32)
     for k in range(top):
         gate = grown[k] / whole
         gates_out[k : k + 1, :] = gate
         hot = slot_of[k : k + 1, :] == slot
         pick = jnp.where(hot, 1.0, pick)
-        pick_back = jnp.where(slot_back[k : k + 1, :] == slot, 1.0, pick_back)
         weight = jnp.where(hot, gate * keep[k : k + 1, :], weight)
-    pick_out[...] = pick_back.T.astype(BF)
-    pick_y_out[...] = pick.T.astype(BF)
+    pick_out[...] = pick.T.astype(BF)
     pick = pick.astype(BF)
     for t in range(blocks):
         send_out[:, t * col : (t + 1) * col] = dot(pick, mixed_out[t]).astype(BF)
@@ -276,16 +274,17 @@
     facts = jnp.zeros((slots, 128), F32)
     for n, piece in enumerate((first, second, third)):
         facts = jnp.where(lane == n, piece.astype(F32), facts)
-    send_out[:, width:] = facts.astype(BF)
+    send_out[:, width : width + 128] = facts.astype(BF)
     arrive(dy_in)
     dy_out[...] = dy_all[...]
     for t in range(blocks):
-        send_dy_out[:, t * col : (t + 1) * col] = dot(pick, dy_all[t]).astype(BF)
+        lanes = slice(width + 128 + t * col, width + 128 + (t + 1) * col)
+        send_out[:, lanes] = dot(pick, dy_all[t]).astype(BF)
     post.finish()
 
 
 def front_call(local, bias, cos_rows, sin_rows, gain1, gain2, q_gain, k_gain, router_t, routes,
-               slot_of, slot_back, keep, weights, slots):
+               slot_of, keep, weights, slots):
     tok, both = local.shape
     col = both // 2
     blocks = gain1.shape[0]
@@ -300,11 +299,11 @@
             shape(tiles, BF), shape(tiles, BF), shape(tiles, F32),
             shape(tiles, BF), shape((tok, col), F32), shape((tok, col), F32),
             shape((tok, col), BF), shape((tok, col), BF), shape((tok, col), BF),
-            shape((tok, col), BF), shape((top, tok), F32), shape((slots, width + 128), BF),
-            shape((slots, width), BF), shape((tok, slots), BF), shape((tok, slots), BF),
+            shape((tok, col), BF), shape((top, tok), F32), shape((slots, 2 * width + 128), BF),
+            shape((tok, slots), BF),
         ),
-        in_specs=[vmem] * 13 + [pl.BlockSpec(memory_space=pl.ANY)] * 4,
-        out_specs=(vmem,) * 15,
+        in_specs=[vmem] * 12 + [pl.BlockSpec(memory_space=pl.ANY)] * 4,
+        out_specs=(vmem,) * 13,
         scratch_shapes=[
             pltpu.VMEM((width, col), BF), pltpu.VMEM((width, col), BF), pltpu.VMEM((width, col), BF),
             pltpu.VMEM((col, width), BF),
@@ -318,11 +317,11 @@
         ),
         name="front",
     )(local, bias, cos_rows, sin_rows, gain1, gain2, q_gain, k_gain, router_t, routes, slot_of,
-      slot_back, keep, *weights)
+      keep, *weights)
 
 
 def back_kernel(
-    pick_t, ret_early, ret_late, slot_of, keep, gates, routes, bias, cos_rows, sin_rows, gain2,
+    pick_t, ret, slot_of, keep, gates, routes, bias, cos_rows, sin_rows, gain2,
     q_gain, k_gain, router, resid, dy_all, mixed, qh, kh, vh,
     q_hbm, k_hbm, wo_hbm,
     d_qkv, dr, d_mine, router_out, small_out,
@@ -335,22 +334,16 @@
     blocks, tok, col = parts.shape
     width = blocks * col
     post = Post("tensor", send_sem, recv_sem)
-    early = ret_early.shape[0]
-    for t in range(blocks):
-        lanes = slice(t * col, (t + 1) * col)
-        parts[t] = (
-            dot(pick_t[:, :early], ret_early[:, lanes]) + dot(pick_t[:, early:], ret_late[:, lanes])
-        ).astype(BF)
+    for t in range(blocks):
+        parts[t] = dot(pick_t[...], ret[:, t * col : (t + 1) * col]).astype(BF)
     ready()
     first = scatter_start(post, parts, halves, me)
     top = routes.shape[0]
-    for n, (ret, base) in enumerate(((ret_early, 0), (ret_late, early))):
-        dgate = row_sum(ret[:, width : width + 128].astype(F32))
-        slot = lax.broadcasted_iota(jnp.int32, (ret.shape[0], tok), 0) + base
-        for k in range(top):
-            hot = slot_of[k : k + 1, :] == slot
-            found = jnp.sum(jnp.where(hot, dgate, 0.0), axis=0, keepdims=True)
-            dg_mine[k : k + 1, :] = dg_mine[k : k + 1, :] + found if n else found
+    dgate = row_sum(ret[:, width:].astype(F32))
+    slot = lax.broadcasted_iota(jnp.int32, (ret.shape[0], tok), 0)
+    for k in range(top):
+        hot = slot_of[k : k + 1, :] == slot
+        dg_mine[k : k + 1, :] = jnp.sum(jnp.where(hot, dgate, 0.0), axis=0, keepdims=True)
     dg_in = [post.push(dg_mine, dg_box.at[d], peer) for d, peer in enumerate(peers)]
     moved = scatter_relay(post, parts, halves, box, me, first)
     total[me] = scatter_total(parts, box, me, moved).astype(BF)
@@ -434,7 +427,7 @@
     post.finish()
 
 
-def back_call(pick_t, ret_early, ret_late, slot_of, keep, gates, routes, bias, cos_rows, sin_rows,
+def back_call(pick_t, ret, slot_of, keep, gates, routes, bias, cos_rows, sin_rows,
               gain2, q_gain, k_gain, router, resid, dy_all, mixed, qh, kh, vh, q_raw, k_raw, wo):
     blocks, tok, col = dy_all.shape
     width = blocks * col
@@ -449,7 +442,7 @@
             shape((tok, 3 * col), BF), shape(tiles, BF), shape((tok, col), F32),
             shape((width, 128), BF), shape((8, col), F32),
         ),
-        in_specs=[vmem] * 20 + [pl.BlockSpec(memory_space=pl.ANY)] * 3,
+        in_specs=[vmem] * 19 + [pl.BlockSpec(memory_space=pl.ANY)] * 3,
         out_specs=(vmem,) * 5,
         scratch_shapes=[
             pltpu.VMEM((tok, col), F32), pltpu.VMEM((tok, col), F32), pltpu.VMEM((col, width), BF),
@@ -466,36 +459,200 @@
             flops=20_000_000_000, bytes_accessed=1, transcendentals=0
         ),
         name="back",
-    )(pick_t, ret_early, ret_late, slot_of, keep, gates, routes, bias, cos_rows, sin_rows, gain2,
+    )(pick_t, ret, slot_of, keep, gates, routes, bias, cos_rows, sin_rows, gain2,
       q_gain, k_gain, router, resid, dy_all, mixed, qh, kh, vh, q_raw, k_raw, wo)
 
 
-def expert_kernel(side, per, early, rows_ref, grads_ref, w_ref, *rest):
-    if side:
-        y_rest, dx_rest, *rest = rest
-        y_ref, dx_ref, *rest = rest
-    else:
-        dx_ref, y_rest, dx_rest, *rest = rest
-    grad_ref, rows, rows_t, dys, dys_t, y_acc, dx_acc, gate_of, dgate = rest
+def octet():
+    me = lax.axis_index("expert")
+    core = me % 2
+    return me - core, core, lax.axis_index("tensor")
+
+
+def octet_others(base, core, rank):
+    count = lax.axis_size("tensor")
+    others = [{"expert": base + core, "tensor": (rank + d) % count} for d in range(1, count)]
+    return others + [
+        {"expert": base + 1 - core, "tensor": (rank + d) % count} for d in range(count)
+    ]
+
+
+def meet(others):
+    barrier = pltpu.get_barrier_semaphore()
+    for other in others:
+        pl.semaphore_signal(barrier, inc=1, device_id=other, device_id_type=MESH)
+    return lambda: pl.semaphore_wait(barrier, len(others))
+
+
+def remote(source, target, send_sem, recv_sem, device):
+    return pltpu.make_async_remote_copy(
+        src_ref=source, dst_ref=target, send_sem=send_sem, recv_sem=recv_sem, device_id=device,
+        device_id_type=MESH,
+    )
+
+
+def weights_kernel(w, out, local_sem, send_sem, recv_sem, pass_send, pass_recv):
+    base, core, rank = octet()
+    ready = meet(octet_others(base, core, rank))
+    ranks = out.shape[0]
+    half = out.shape[2] // 2
+    sibling = {"expert": base + 1 - core, "tensor": rank}
+
+    def part(ref, index, side):
+        return ref.at[index, :, pl.ds(side * half, half), :]
+
+    ready()
+    sends = []
+    for s in range(2):
+        for k in range(2):
+            target = 2 * core + s
+            here = (target == rank) & (core == k)
+            source, place = part(w, s, k), part(out, rank, k)
+            local = pltpu.make_async_copy(source, place, local_sem)
+            away = remote(
+                source, place, send_sem.at[2 * s + k], recv_sem.at[rank],
+                {"expert": base + k, "tensor": target},
+            )
+            pl.when(here)(local.start)
+            pl.when(jnp.logical_not(here))(away.start)
+            sends.append((here, away))
+    passed = []
+    for d in (0, 1, 3, 2):
+        quarter = (rank + d) % ranks
+        mine = part(out, quarter, core)
+        arrival = remote(mine, mine, send_sem.at[0], recv_sem.at[quarter], sibling)
+        here = (rank // 2 == core) & (d == 0)
+        pl.when(here)(pltpu.make_async_copy(part(w, 0, 0), mine, local_sem).wait)
+        pl.when(jnp.logical_not(here))(arrival.wait_recv)
+        passed.append(remote(mine, mine, pass_send.at[d], pass_recv.at[d], sibling))
+        passed[-1].start()
+    for copy in passed:
+        copy.wait()
+    for here, away in sends:
+        pl.when(jnp.logical_not(here))(away.wait_send)
+
+
+def weights_call(w):
+    _, three, width, hidden = w.shape
+    hbm = pl.BlockSpec(memory_space=pl.ANY)
+    sems = pltpu.SemaphoreType.DMA((4,))
+    return pl.pallas_call(
+        weights_kernel,
+        out_shape=jax.ShapeDtypeStruct((4, three, width, hidden), BF),
+        in_specs=[hbm],
+        out_specs=hbm,
+        scratch_shapes=[pltpu.SemaphoreType.DMA, sems, sems, sems, sems],
+        compiler_params=pltpu.CompilerParams(collective_id=4, has_side_effects=True),
+        cost_estimate=SHADOW,
+        name="weights",
+    )(w)
+
+
+def home_kernel(grads, out, far_out, own, got, load_sem, local_sem, swap_send, swap_recv, send_sem, recv_sem):
+    base, core, rank = octet()
+    ready = meet(octet_others(base, core, rank))
+    ranks, three, half, hidden = own.shape
+    sibling = {"expert": base + 1 - core, "tensor": rank}
+    order = (1, 3, 0, 2)
+    loads, swaps = [], []
+    for d in order:
+        quarter = (rank + d) % ranks
+        source = grads.at[quarter, :, pl.ds(core * half, half), :]
+        loads.append(pltpu.make_async_copy(source, own.at[d], load_sem.at[d]))
+        loads[-1].start()
+    ready()
+    for d in order:
+        quarter = (rank + d) % ranks
+        source = grads.at[quarter, :, pl.ds((1 - core) * half, half), :]
+        swaps.append(remote(source, got.at[d], swap_send.at[d], swap_recv.at[d], sibling))
+        swaps[-1].start()
+    owner = rank // 2
+    side = rank - 2 * owner
+    rows = 64
+    place = out.at[side, :, pl.ds(core * half, half), :]
+    stays = owner == core
+    sends = []
+    for n, d in enumerate(order):
+        loads[n].wait()
+        swaps[n].wait_recv()
+
+        def one(i, _, d=d):
+            c, at = i // (half // rows), i % (half // rows) * rows
+            here = pl.ds(pl.multiple_of(at, rows), rows)
+            value = own[d, c, here, :].astype(F32) + got[d, c, here, :].astype(F32)
+            own[d, c, here, :] = value.astype(BF)
+            return 0
+
+        lax.fori_loop(0, three * (half // rows), one, 0)
+        if d == 2:
+            far = pltpu.make_async_copy(own.at[d], far_out, load_sem.at[d])
+            far.start()
+            continue
+        away = remote(
+            own.at[d], place, send_sem.at[d], recv_sem.at[2 * side + core],
+            {"expert": base + owner, "tensor": (rank + d) % ranks},
+        )
+        if d:
+            away.start()
+        else:
+            kept = pltpu.make_async_copy(own.at[d], place, local_sem)
+            pl.when(stays)(kept.start)
+            pl.when(jnp.logical_not(stays))(away.start)
+        sends.append((d, away))
+    for s in range(2):
+        for k in range(2):
+            off = (2 * core + s - rank) % ranks
+            mine = out.at[s, :, pl.ds(k * half, half), :]
+            arrival = remote(own.at[0], mine, send_sem.at[0], recv_sem.at[2 * s + k], sibling)
+            own_chip = off == 0
+            comes = (off != 2) & jnp.logical_not(own_chip & (core == k))
+            pl.when(comes)(arrival.wait_recv)
+    pl.when(stays)(kept.wait)
+    for d, away in sends:
+        if d:
+            away.wait_send()
+        else:
+            pl.when(jnp.logical_not(stays))(away.wait_send)
+    for swap in swaps:
+        swap.wait_send()
+    far.wait()
+
+
+def home_call(grads):
+    ranks, three, width, hidden = grads.shape
+    hbm = pl.BlockSpec(memory_space=pl.ANY)
+    sems = pltpu.SemaphoreType.DMA((4,))
+    halves = pltpu.VMEM((ranks, three, width // 2, hidden), BF)
+    shape = jax.ShapeDtypeStruct
+    return pl.pallas_call(
+        home_kernel,
+        out_shape=(
+            shape((2, three, width, hidden), BF), shape((three, width // 2, hidden), BF),
+        ),
+        in_specs=[hbm],
+        out_specs=(hbm, hbm),
+        scratch_shapes=[
+            halves, halves, sems, pltpu.SemaphoreType.DMA, sems, sems, sems, sems,
+        ],
+        compiler_params=pltpu.CompilerParams(
+            collective_id=5, has_side_effects=True, vmem_limit_bytes=24 * 1024 * 1024
+        ),
+        cost_estimate=SHADOW,
+        name="home",
+    )(grads)
+
+
+def expert_kernel(rows_ref, w_ref, y_ref, dx_ref, grad_ref, rows_t, dys_t, y_acc, dx_acc, gate_of, dgate):
     step = pl.program_id(0)
-    count, width = rows.shape
-    both = rows_ref.shape[0]
-    late = per - early
-
-    def selector(shape, source_of):
-        place = lax.broadcasted_iota(jnp.int32, shape, 0)
-        source = lax.broadcasted_iota(jnp.int32, shape, 1)
-        return (source_of(place) == source).astype(F32).astype(BF)
+    width = y_acc.shape[1]
+    rows = rows_ref.at[:, :width]
+    dys = rows_ref.at[:, width + 128 :]
 
     @pl.when(step == 0)
     def _():
-        pick = selector((count, both), lambda p: p + (p // per + side) * per)
-        rows[...] = dot(pick, rows_ref[:, :width]).astype(BF)
-        gate_of[...] = row_sum(dot(pick, rows_ref[:, width:]))
-        dy_rows = dot(pick, grads_ref[...])
-        dys[...] = dy_rows.astype(BF)
+        gate_of[...] = row_sum(rows_ref[:, width : width + 128].astype(F32))
         rows_t[...] = rows[...].T
-        dys_t[...] = (dy_rows * gate_of[...]).astype(BF).T
+        dys_t[...] = (dys[...].astype(F32) * gate_of[...]).astype(BF).T
         dgate[...] = jnp.zeros_like(dgate)
         y_acc[...] = jnp.zeros_like(y_acc)
         dx_acc[...] = jnp.zeros_like(dx_acc)
@@ -520,84 +677,41 @@
     @pl.when(step == pl.num_programs(0) - 1)
     def _():
         first = dgate[...].astype(BF).astype(F32)
-        lane = lax.broadcasted_iota(jnp.int32, (count, 128), 1)
+        lane = lax.broadcasted_iota(jnp.int32, (y_ref.shape[0], 128), 1)
         facts = jnp.where(lane == 0, first, jnp.where(lane == 1, dgate[...] - first, 0.0))
-        facts = facts.astype(BF)
-        y_rows = (y_acc[...] * gate_of[...]).astype(BF)
-        dx_rows = dx_acc[...].astype(BF)
-        if side:
-            here = selector(
-                (y_ref.shape[0], count),
-                lambda p: jnp.where(p % (2 * per) < per, -1, p // (2 * per) * per + p % (2 * per) - per),
-            )
-            there = selector(
-                (y_ref.shape[0], count),
-                lambda p: jnp.where(p % (2 * per) < per, p // (2 * per) * per + p % (2 * per), -1),
-            )
-            y_ref[...] = (dot(here, y_rows) + dot(there, y_rest[...])).astype(BF)
-            chunk = per + late
-            here = selector(
-                (dx_ref.shape[0], count),
-                lambda p: jnp.where(p % chunk < late, -1, p // chunk * per + p % chunk - late),
-            )
-            there = selector(
-                (dx_ref.shape[0], dx_rest.shape[0]),
-                lambda p: jnp.where(p % chunk < late, p // chunk * late + p % chunk, -1),
-            )
-            dx_ref[:, :width] = (dot(here, dx_rows) + dot(there, dx_rest[:, :width])).astype(BF)
-            dx_ref[:, width:] = (dot(here, facts) + dot(there, dx_rest[:, width:])).astype(BF)
-        else:
-            y_rest[...] = y_rows
-            soon = selector((dx_ref.shape[0], count), lambda p: p // early * per + p % early)
-            later = selector(
-                (dx_rest.shape[0], count), lambda p: p // late * per + early + p % late
-            )
-            for pick, dx_out in ((soon, dx_ref), (later, dx_rest)):
-                dx_out[:, :width] = dot(pick, dx_rows).astype(BF)
-                dx_out[:, width:] = dot(pick, facts).astype(BF)
-
-
-def expert_call(side, per, early, rows, grads, weights, rest):
+        y_ref[...] = (y_acc[...] * gate_of[...]).astype(BF)
+        dx_ref[:, :width] = dx_acc[...].astype(BF)
+        dx_ref[:, width:] = facts.astype(BF)
+
+
+def expert_call(rows, weights):
     quarters, _, width, hidden = weights.shape
-    both = rows.shape[0]
-    count = both // 2
-    groups = count // per
+    count = rows.shape[0]
     shape = jax.ShapeDtypeStruct
 
     def whole(value):
         return pl.BlockSpec(value.shape, lambda q: (0, 0), pipeline_mode=pl.Buffered(1))
 
-    def plain(size):
-        return shape((groups * size, width), BF)
-
-    def wider(size):
-        return shape((groups * size, width + 128), BF)
-
     block = pl.BlockSpec((1, 3, width, hidden), lambda q: (q, 0, 0, 0))
-    if side:
-        outs = [plain(2 * per), wider(2 * per - early)]
-    else:
-        outs = [wider(early), plain(per), wider(per - early)]
+    outs = [shape((count, width), BF), shape((count, width + 128), BF)]
     return pl.pallas_call(
-        functools.partial(expert_kernel, side, per, early),
+        expert_kernel,
         grid=(quarters,),
         out_shape=tuple(outs) + (shape(weights.shape, BF),),
-        in_specs=[whole(rows), whole(grads), block] + [whole(value) for value in rest],
+        in_specs=[whole(rows), block],
         out_specs=tuple(whole(value) for value in outs) + (block,),
         scratch_shapes=[
-            pltpu.VMEM((count, width), BF),
             pltpu.VMEM((width, count), BF),
-            pltpu.VMEM((count, width), BF),
             pltpu.VMEM((width, count), BF),
             pltpu.VMEM((count, width), F32),
             pltpu.VMEM((count, width), F32),
             pltpu.VMEM((count, 1), F32),
             pltpu.VMEM((count, 1), F32),
         ],
-        compiler_params=pltpu.CompilerParams(vmem_limit_bytes=60 * 1024 * 1024),
+        compiler_params=pltpu.CompilerParams(vmem_limit_bytes=62 * 1024 * 1024),
         cost_estimate=COST,
-        name=f"expert{side}",
-    )(rows, grads, weights, *rest)
+        name="expert",
+    )(rows, weights)
 
 
 def plane():
@@ -615,24 +729,21 @@
 
 def reduce_kernel(
     d_qkv, dr, d_mine, router_part, small_in, x_all, gain1, ob, pick_y, ret_y,
-    resid_hbm, wq_hbm, wk_hbm, wv_hbm,
-    wide_out, dx_out, out_out, small_out,
+    far_hbm, resid_hbm, wq_hbm, wk_hbm, wv_hbm,
+    wide_out, dx_out, out_out, small_out, far_out,
     wq, wk, wv, resid, parts, y_parts, halves, box_x, note, buf, box, got,
-    load_sem, out_sem, x_send, x_recv, send_sem, recv_sem,
+    load_sem, out_sem, x_send, x_recv, send_sem, recv_sem, far_send, far_recv,
 ):
     me, peers = tensor_peers()
     dims = plane()
-    barrier = pltpu.get_barrier_semaphore()
-    for axis, others in (("tensor", peers), ("expert", [partner for _, partner in dims])):
-        for other in others:
-            pl.semaphore_signal(barrier, inc=1, device_id={axis: other}, device_id_type=MESH)
+    base, core, _ = octet()
+    ready = meet(octet_others(base, core, me) + [{"expert": partner} for _, partner in dims[1:]])
     loads = fetch(
         [(wq_hbm, wq), (wk_hbm, wk), (wv_hbm, wv), (resid_hbm.at[me], resid)], load_sem
     )
     blocks, tok, col = x_all.shape
     width = blocks * col
     head = col // blocks
-    core = dims[0][0]
     square = jnp.zeros((tok, 1), F32)
     for t in range(blocks):
         value = x_all[t].astype(F32)
@@ -647,12 +758,26 @@
             + dot(d_qkv[:, col : 2 * col], wk[rows, :], 1, 1)
             + dot(d_qkv[:, 2 * col : 3 * col], wv[rows, :], 1, 1)
         ).astype(BF)
-    pl.semaphore_wait(barrier, len(peers) + len(dims))
+    ready()
     post_x = Post("tensor", x_send, x_recv)
     post = Post("expert", send_sem, recv_sem)
     x_halves, x_box = halves.at[pl.ds(0, 2)], box_x.at[pl.ds(0, 2)]
     y_halves, y_box = halves.at[pl.ds(2, 2)], box_x.at[pl.ds(2, 2)]
     x_first = scatter_start(post_x, parts, x_halves, me)
+
+    half = far_hbm.shape[1]
+    owner = me // 2
+
+    def far_copy(n, side, device):
+        return remote(
+            far_hbm.at[n], far_out.at[n, pl.ds(side * half, half), :],
+            far_send.at[n], far_recv.at[n, side], device,
+        )
+
+    far_copies = [
+        far_copy(n, core, {"expert": base + owner, "tensor": (me + 2) % blocks}) for n in range(3)
+    ]
+    far_copies[0].start()
 
     chunks = buf.shape[0] // blocks
     rows_chunk = buf.shape[1]
@@ -684,6 +809,7 @@
             source = buf.at[pl.ds((1 - core) * 64 + s * 16, 16)]
             copies.append(post.push(source, box.at[pl.ds(31 * s, 16)], dims[0][1]))
     x_moved = scatter_relay(post_x, parts, x_halves, x_box, me, x_first)
+    far_copies[1].start()
     for n in range(2):
         products(2 * core + n)
     place = [core * 64 + s * 16 for s in range(4)]
@@ -722,6 +848,7 @@
     halve(1)
     first, size = first + size, size // 2
     y_moved = scatter_relay(post_x, y_parts, y_halves, y_box, me, y_first)
+    far_copies[2].start()
     halve(2)
     first, size = first + size, size // 2
     halve(3)
@@ -770,9 +897,14 @@
     post_x.finish()
     for store in stores:
         store.wait()
-
-
-def reduce_call(d_qkv, dr, d_mine, router_part, small, x_all, gain1, ob, pick_y, ret_y, resid,
+    comes = (me + 2) % blocks // 2 == core
+    for n in range(3):
+        for side in range(2):
+            pl.when(comes)(far_copy(n, side, {"expert": base + core, "tensor": (me + 2) % blocks}).wait_recv)
+        far_copies[n].wait_send()
+
+
+def reduce_call(d_qkv, dr, d_mine, router_part, small, x_all, gain1, ob, pick_y, ret_y, far, resid,
                 weights):
     blocks, tok, col = x_all.shape
     width = blocks * col
@@ -786,9 +918,10 @@
         reduce_kernel,
         out_shape=(
             shape(wide, BF), shape((tok, col), BF), shape((tok, col), BF), shape((16, col), F32),
+            shape((far.shape[0], 2 * far.shape[1], far.shape[2]), BF),
         ),
-        in_specs=[vmem] * 10 + [hbm] * 4,
-        out_specs=(hbm, vmem, vmem, vmem),
+        in_specs=[vmem] * 10 + [hbm] * 5,
+        out_specs=(hbm, vmem, vmem, vmem, hbm),
         scratch_shapes=[
             pltpu.VMEM((width, col), BF), pltpu.VMEM((width, col), BF), pltpu.VMEM((width, col), BF),
             pltpu.VMEM((tok, col), F32), pltpu.VMEM(tiles, BF), pltpu.VMEM(tiles, BF),
@@ -798,13 +931,14 @@
             pltpu.SemaphoreType.DMA((4,)), pltpu.SemaphoreType.DMA((8,)),
             pltpu.SemaphoreType.DMA((count,)), pltpu.SemaphoreType.DMA((count,)),
             pltpu.SemaphoreType.DMA((40,)), pltpu.SemaphoreType.DMA((40,)),
+            pltpu.SemaphoreType.DMA((3,)), pltpu.SemaphoreType.DMA((3, 2)),
         ],
         compiler_params=pltpu.CompilerParams(
             collective_id=3, has_side_effects=True, vmem_limit_bytes=60 * 1024 * 1024
         ),
         cost_estimate=COST,
         name="reduce",
-    )(d_qkv, dr, d_mine, router_part, small, x_all, gain1, ob, pick_y, ret_y, resid, *weights)
+    )(d_qkv, dr, d_mine, router_part, small, x_all, gain1, ob, pick_y, ret_y, far, resid, *weights)
 
 
 def body(
@@ -837,7 +971,6 @@
     local_experts = expert_w.shape[0]
 
     w_stored = jnp.transpose(expert_w, (0, 2, 1, 3))
-    w_first = lax.all_gather(w_stored[0], "tensor", axis=0)
 
     routes_t = routes.T
     order_t = pair_order[0].reshape(tok_count, top_count).T
@@ -857,8 +990,6 @@
     inner = jnp.broadcast_to((dest_index % tok_count).astype(BF)[:, None], (tok_count, 64))
     facts = jnp.broadcast_to(counts.astype(BF)[None, :], (tok_count, expert_count))
     outgoing = dot(by_rank, jnp.concatenate([tokens, out_grad, inner, facts], axis=1)).astype(BF)
-    outgoing, w_stored = lax.optimization_barrier((outgoing, w_stored))
-    w_second = lax.all_gather(w_stored[1], "tensor", axis=0)
     got = exchange(outgoing.reshape(groups, move_rows, -1), "expert")
     all_counts = got[:, 0, 2 * col_count + 64 :].astype(jnp.int32)
     lower = jnp.arange(groups, dtype=jnp.int32) < group_id
@@ -868,20 +999,14 @@
     local = dot(put, got.reshape(tok_count, -1)[:, : 2 * col_count]).astype(BF)
     capacity = 5 * tok_count * groups * top_count // (4 * expert_count)
     most_rows = 3 * tok_count * top_count // (2 * expert_count)
-    per = most_rows // tensor_count
-    slots = expert_count * per
+    per = most_rows // 2
+    slots = groups * per
     slot_global = jnp.sum(jnp.where(route_hot, offsets[None, :, None], 0), axis=1) + ranks
     kept = slot_global < capacity
     keep_mask = kept.astype(F32)
-    here = kept & (ranks % tensor_count == tensor_id)
-    place = ranks // tensor_count
-    slot_of = jnp.where(here, routes_t * per + place, -1)
-    early = per // 8 * 8
-    side, owner = routes_t % local_experts, routes_t // local_experts
-    ahead = owner * early + place
-    behind = groups * early + owner * (2 * per - early)
-    behind = behind + jnp.where(side == 0, place - early, per - early + place)
-    slot_back = jnp.where(here, jnp.where((side == 0) & (place < early), ahead, behind), -1)
+    here = kept & (routes_t % tensor_count == tensor_id)
+    owner = routes_t // tensor_count * 2 + ranks % 2
+    slot_of = jnp.where(here, owner * per + ranks // 2, -1)
 
     seq_ids, positions = sequence_layout(seq_lengths[0], tok_count)
     bias = jnp.where(seq_ids[:, None] == seq_ids[None, :], 0.0, mask_fill)
@@ -894,35 +1019,28 @@
     router = jnp.pad(w_router, ((0, 0), (0, 128 - expert_count)))
     weights = (w_query, w_key, w_value, w_output)
     (
-        x_all, dy_all, resid, mixed, q_raw, k_raw, qh, kh, vh, attended, gates, send_rows,
-        send_dy, pick_t, pick_y,
+        x_all, dy_all, resid, mixed, q_raw, k_raw, qh, kh, vh, attended, gates, send_rows, pick_t,
     ) = front_call(
         local, bias, cos_rows, sin_rows, gain1, gain2, *head_gains, router.T, routes_t, slot_of,
-        slot_back, keep_mask, weights, slots,
+        keep_mask, weights, slots,
     )
-    recv_rows = exchange(send_rows.reshape(groups, -1, width + 128), "expert")
-    recv_dy = exchange(send_dy.reshape(groups, -1, width), "expert")
-    recv_rows = recv_rows.reshape(slots, -1)
-    recv_dy = recv_dy.reshape(slots, -1)
     def homeward(value):
         return exchange(value.reshape(groups, -1, value.shape[1]), "expert").reshape(value.shape)
 
-    d_early, *rest, partial = expert_call(0, per, early, recv_rows, recv_dy, w_first, ())
-    grad_first = lax.psum_scatter(partial, "tensor", scatter_dimension=0, tiled=False)
-    ret_early = homeward(d_early)
-    ret_early, later_rows = lax.optimization_barrier((ret_early, recv_rows))
-    y_rows, d_late, partial = expert_call(1, per, early, later_rows, recv_dy, w_second, rest)
-    grad_second = lax.psum_scatter(partial, "tensor", scatter_dimension=0, tiled=False)
-    ret_late = homeward(d_late)
-    ret_late, y_rows = lax.optimization_barrier((ret_late, y_rows))
+    send_rows, w_stored = lax.optimization_barrier((send_rows, w_stored))
+    recv_rows = homeward(send_rows)
+    y_rows, d_rows, partial = expert_call(recv_rows, weights_call(w_stored))
+    ret_rows = homeward(d_rows)
+    near, far = home_call(partial)
+    ret_rows, near, far, y_rows = lax.optimization_barrier((ret_rows, near, far, y_rows))
     ret_y = homeward(y_rows)
     d_qkv, dr, d_mine, router_part, small = back_call(
-        pick_t, ret_early, ret_late, slot_back, keep_mask, gates, routes_t, bias, cos_rows,
+        pick_t, ret_rows, slot_of, keep_mask, gates, routes_t, bias, cos_rows,
         sin_rows, gain2, *head_gains, router, resid, dy_all, mixed, qh, kh, vh, q_raw, k_raw,
         w_output,
     )
-    summed, dx_slice, out_slice, small = reduce_call(
-        d_qkv, dr, d_mine, router_part, small, x_all, gain1, attended, pick_y, ret_y, resid,
+    summed, dx_slice, out_slice, small, far = reduce_call(
+        d_qkv, dr, d_mine, router_part, small, x_all, gain1, attended, pick_t, ret_y, far, resid,
         weights[:3],
     )
     summed = summed.reshape(width, -1)
@@ -935,7 +1053,10 @@
     small = jnp.sum(back[:, :, 2 * col_count :].astype(F32), axis=0)[:, : 9 * col_count // move_rows]
     small = small.reshape(-1)
     back = dot(by_rank, back.reshape(tok_count, -1)[:, : 2 * col_count], 0, 0).astype(BF)
-    expert_grad = jnp.transpose(jnp.stack([grad_first, grad_second]).astype(F32), (0, 2, 1, 3))
+    opposite = (tensor_id + 2) % tensor_count - 2 * (group_id % 2)
+    is_far = jnp.arange(local_experts) == opposite
+    expert_grad = jnp.where(is_far[:, None, None, None], far[None], near).astype(F32)
+    expert_grad = jnp.transpose(expert_grad, (0, 2, 1, 3))
     wide = [summed[:, n * col_count : (n + 1) * col_count] for n in range(4)]
     gain_at = 2 * width + tok_count
     head = q_gain.shape[0]

time: 577 us -> 480 us (0.83)
  blocking collectives: 154 us -> 0 us
  Pallas kernels: 296 us -> 346 us
  starting transfers between devices: 20.3 us -> 59.5 us
  waiting for transfers between devices: 25.6 us -> 1.92 us
  between operations: 14.5 us -> 1.45 us
    all_to_all x4 -> x0, blocking collectives: 154 us -> none  [exchange(): return lax.all_to_all(value, axis, split_axis=0, concat_axis=0, tiled=True)]
    pallas_call x2 -> x3, Pallas kernels: 63 us -> 165 us  [the longest x1 80 us: weights_call(): pl.pallas_call(weights_kernel, out_shape=jax.ShapeDtypeStruct((4, three,...]
    pallas_call x1, Pallas kernels: 92.2 us -> 52.1 us  [front_call(): pl.pallas_call(front_kernel, out_shape=(shape(tiles, BF), shape(tiles, BF...]
    all_to_all x3 -> x5, starting transfers between devices: 20.1 us -> 59.5 us  [exchange(): return lax.all_to_all(value, axis, split_axis=0, concat_axis=0, tiled=True)]
    pallas_call x1, Pallas kernels: 53.3 us -> 32.2 us  [back_call(): pl.pallas_call(back_kernel, out_shape=(shape((tok, 3 * col), BF), shape(t...]
    reduce_scatter x2 -> x0, waiting for transfers between devices: 17.5 us -> none  [body(): lax.psum_scatter(partial, 'tensor', scatter_dimension=0, tiled=False)]
    pallas_call x1, Pallas kernels: 87.3 us -> 96.9 us  [reduce_call(): pl.pallas_call(reduce_kernel, out_shape=(shape(wide, BF), shape((tok, col...]
    slice x2 -> x0, local copies, waits for them, and re-layouts: 7.51 us -> none  [the longest x1 3.76 us: body(): w_first = lax.all_gather(w_stored[0], 'tensor', axis=0)]
  transfers between devices with their start and end apart: 7 -> 5, of which waited for: 3 -> 2; matrix products, arithmetic and copies ran while one was open for 7% -> 6% of each run, Pallas kernels for 52% -> 33%
where the time goes in v5:
time: 480 us; the launch traced here: 476 us
  Pallas kernels  346 us (72%)
  starting transfers between devices  59.5 us (12%)
  other arithmetic  37 us (8%)
  local copies, waits for them, and re-layouts  27.2 us (6%)
    pallas_call x1, Pallas kernels, reduce_call(): pl.pallas_call(reduce_kernel, out_shape=(shape(wide, BF), shape((tok, col...  96.9 us
    pallas_call x1, Pallas kernels, weights_call(): pl.pallas_call(weights_kernel, out_shape=jax.ShapeDtypeStruct((4, three,...  80 us
    all_to_all x5, starting transfers between devices, exchange(): return lax.all_to_all(value, axis, split_axis=0, concat_axis=0, tiled=True)  59.5 us
    pallas_call x1, Pallas kernels, front_call(): pl.pallas_call(front_kernel, out_shape=(shape(tiles, BF), shape(tiles, BF...  52.1 us
    pallas_call x1, Pallas kernels, home_call(): pl.pallas_call(home_kernel, out_shape=(shape((2, three, width, hidden), B...  43.1 us
    pallas_call x1, Pallas kernels, expert_call(): pl.pallas_call(expert_kernel, grid=(quarters,), out_shape=tuple(outs) + (...  42.1 us
    pallas_call x1, Pallas kernels, back_call(): pl.pallas_call(back_kernel, out_shape=(shape((tok, 3 * col), BF), shape(t...  32.2 us
    unnamed x70, local copies, waits for them, and re-layouts  18.6 us
  transfers between devices with their start and end apart: 5, of which 2 were waited for; matrix products, arithmetic and copies ran while one was open for 6% of the time, Pallas kernels for 33%

profile of v5, /device:TPU:1, one launch (start us, length us, event | category | flops | bytes accessed | tf_op | source)
XLA Modules:
  0.0 476.4 jit_solution(4258041936798129587)
XLA Ops:
  3.3 1.2 concatenate.15
  4.6 1.2 fusion
  5.7 9.6 %all-to-all-start = ((bf16[32,8,1152]{2,1,0:T(8,128)(2,1)}), bf16[32,8,1152]{2,1,0:T(8,128)(2,1)S(1)}, u32[]{:S(2)}, u32[]{:S(2)}) async-start(bf16[32,8,1152]{2,1,0:T(8,128)(2,1)} %fusion), calls=%async_computation | async-start | bytes 1179648 | tf_op jit(solution)/shard_map/all_to_all | solution.py:46
  17.7 1.3 reshape.194.gain1
  19.0 1.3 reshape.196.gain2
  20.8 1.4 reduce.6
  22.3 3.6 convert_reduce_fusion
  26.4 1.0 copy.45.router_t
  32.4 1.1 convolution_convert_fusion.3.local
  33.5 52.1 %front.1 = (bf16[4,256,512]{2,1,0:T(8,128)(2,1)}, bf16[4,256,512]{2,1,0:T(8,128)(2,1)}, f32[4,256,512]{2,1,0:T(8,128)}, bf16[4,256,512]{2,1,0:T(8,128)(2,1)}, f3...) custom-call(bf16[256,1024]{1,0:T(8,128)(2,1)} %convolution_convert_f, ...), custom_call_target="tpu_custom_call" | custom-call | tf_op jit(solution)/shard_map/front/pallas_call | solution.py:296
  85.6 12.8 %all-to-all-start.1 = ((bf16[32,24,4224]{2,1,0:T(8,128)(2,1)}), bf16[32,24,4224]{2,1,0:T(8,128)(2,1)}, u32[]{:S(2)}, u32[]{:S(2)}) async-start(bf16[32,24,4224]{2,1,0:T(8,128)(2,1)} %bitcast.47), calls=%async_computation.1 | async-start | bytes 12976128 | tf_op jit(solution)/shard_map/all_to_all | solution.py:46
  98.4 80.0 %weights.1.w_ref = bf16[4,3,2048,256]{3,2,1,0:T(8,128)(2,1)} custom-call(bf16[2,3,2048,256]{3,2,1,0:T(8,128)(2,1)} %bitcast.62), custom_call_target="tpu_custom_call" | custom-call | flops 40000000000 | bytes 1 | tf_op jit(solution)/shard_map/weights/pallas_call | solution.py:539
  178.8 42.1 %expert.1 = (bf16[768,2048]{1,0:T(8,128)(2,1)}, bf16[768,2176]{1,0:T(8,128)(2,1)}, bf16[4,3,2048,256]{3,2,1,0:T(8,128)(2,1)}) custom-call(bf16[768,4224]{1,0:T(8,128)(2,1)} %bitcast.13.rows_ref, bf16[4,3,2048,256]{3,2,1,0:T(8,128)(2,1)} %weights.1.w_ref), custom_call_target="tpu_custom_call" | custom-call | flops 1 | bytes 1 | tf_op jit(solution)/shard_map/expert/pallas_call | solution.py:697
  220.9 21.0 %all-to-all-start.2 = ((bf16[32,24,2176]{2,1,0:T(8,128)(2,1)}), bf16[32,24,2176]{2,1,0:T(8,128)(2,1)}, u32[]{:S(2)}, u32[]{:S(2)}) async-start(bf16[32,24,2176]{2,1,0:T(8,128)(2,1)} %bitcast.49), calls=%async_computation.2 | async-start | bytes 6684672 | tf_op jit(solution)/shard_map/all_to_all | solution.py:46
  241.9 4.6 copy-done.18
  246.5 43.1 %home.1 = (bf16[2,3,2048,256]{3,2,1,0:T(8,128)(2,1)S(1)}, bf16[3,1024,256]{2,1,0:T(8,128)(2,1)S(1)}) custom-call(bf16[4,3,2048,256]{3,2,1,0:T(8,128)(2,1)S(1)} %copy-done.18), custom_call_target="tpu_custom_call" | custom-call | flops 40000000000 | bytes 1 | tf_op jit(solution)/shard_map/home/pallas_call | solution.py:627
  289.6 2.7 copy-done
  292.3 1.1 copy-done.1
  293.6 9.1 %all-to-all-start.3 = ((bf16[32,24,2048]{2,1,0:T(8,128)(2,1)}), bf16[32,24,2048]{2,1,0:T(8,128)(2,1)}, u32[]{:S(2)}, u32[]{:S(2)}) async-start(bf16[32,24,2048]{2,1,0:T(8,128)(2,1)} %bitcast.50), calls=%async_computation.3 | async-start | bytes 6291456 | tf_op jit(solution)/shard_map/all_to_all | solution.py:46
  302.9 0.9 copy-done.22
  303.8 0.9 copy-done.23
  304.8 32.2 %back.1 = (bf16[256,1536]{1,0:T(8,128)(2,1)S(1)}, bf16[4,256,512]{2,1,0:T(8,128)(2,1)S(1)}, f32[256,512]{1,0:T(8,128)S(1)}, bf16[2048,128]{1,0:T(8,128)(2,1)S(1)}, f32[8,512]{1,0:T(8,128)S(1)}) custom-call(bf16[256,768]{1,0:T(8,128)(2,1)S(1)} %copy-done.9, bf16[768,2176]{1,0:T(8,128)(2,1)} %bitcast.15.ret, s32[8,256]{1,0:T(8,128)S(1)} %copy-done.14, ...), custom_call_target="tpu_custom_call" | custom-call | flops 20000000000 | bytes 1 | tf_op jit(solution)/shard_map/back/pallas_call | solution.py:439
  337.0 1.0 copy-done.2
  341.0 1.5 all-to-all-done.3
  342.5 96.9 %reduce.7 = (bf16[128,16,2176]{2,1,0:T(8,128)(2,1)}, bf16[256,512]{1,0:T(8,128)(2,1)}, bf16[256,512]{1,0:T(8,128)(2,1)}, f32[16,512]{1,0:T(8,128)}, bf16[3,2048,256]{2,1,0:T(8,128)(2,1)}) custom-call(bf16[256,1536]{1,0:T(8,128)(2,1)} %copy-done.4, bf16[4,256,512]{2,1,0:T(8,128)(2,1)} %copy-done.2, f32[256,512]{1,0:T(8,128)} %copy-done.7, ...), custom_call_target="tpu_custom_call" | custom-call | flops 1 | bytes 1 | tf_op jit(solution)/shard_map/reduce/pallas_call | solution.py:917
  439.4 1.1 slice.90
  440.5 9.5 %fusion.29 = (bf16[2048,512]{1,0:T(8,128)(2,1)}, f32[2048,512]{1,0:T(8,128)}, f32[2048,512]{1,0:T(8,128)}, f32[2048,512]{1,0:T(8,128)}) fusion(bf16[2048,2176]{1,0:T(8,128)(2,1)} %bitcast.46), kind=kLoop, calls=%fused_computation.83 | loop fusion | flops 3145728 | bytes 23068672 | tf_op jit(solution)/shard_map/slice | solution.py:1060
  450.4 1.0 pad_maximum_fusion
  451.5 7.0 %all-to-all-start.4 = ((bf16[32,8,1664]{2,1,0:T(8,128)(2,1)}), bf16[32,8,1664]{2,1,0:T(8,128)(2,1)S(1)}, u32[]{:S(2)}, u32[]{:S(2)}) async-start(bf16[32,8,1664]{2,1,0:T(8,128)(2,1)} %pad_maximum_fusion), calls=%async_computation.4 | async-start | bytes 1703936 | tf_op jit(solution)/shard_map/all_to_all | solution.py:46
  459.5 2.9 copy.48
  462.4 2.5 convert_bitcast_fusion.1
  465.3 8.4 %convert_bitcast_fusion = f32[2,2048,3,256]{3,1,2,0:T(8,128)} fusion(bf16[2,3,2048,256]{3,2,1,0:T(8,128)(2,1)} %copy-done, pred[2]{0:T(512)(128)(4,1)S(1)} %iota_compare_fusion.8, bf16[3,2048,256]{2,1,0:T(8,128)(2,1)S(1)} %copy-done.25), kind=kLoop, calls=%fused_computation.1 | loop fusion | flops 6291456 | bytes 22020098 | tf_op jit(solution)/shard_map/transpose | solution.py:1059
  (107 shorter events, 18.9 us)
Async XLA Ops:
  0.6 25.3 %copy-start.26 = (bf16[2048,64]{0,1:T(8,128)(2,1)S(1)}, bf16[2048,64]{0,1:T(8,128)(2,1)}, u32[]{:S(2)}) copy-start(bf16[2048,64]{0,1:T(8,128)(2,1)} %param.30) | copy-start | bytes 786436
  3.3 25.5 %copy-start.28 = (bf16[128]{0:T(256)(128)(2,1)S(1)}, bf16[128]{0:T(256)(128)(2,1)}, u32[]{:S(2)}) copy-start(bf16[128]{0:T(256)(128)(2,1)} %param.27) | copy-start | bytes 772
  3.3 25.4 %copy-start.29 = (bf16[128]{0:T(256)(128)(2,1)S(1)}, bf16[128]{0:T(256)(128)(2,1)}, u32[]{:S(2)}) copy-start(bf16[128]{0:T(256)(128)(2,1)} %param.26) | copy-start | bytes 772
  3.3 27.0 %copy-start.10 = (s32[256,8]{0,1:T(8,128)S(1)}, s32[256,8]{0,1:T(8,128)}, u32[]{:S(2)}) copy-start(s32[256,8]{0,1:T(8,128)} %param.20) | copy-start | bytes 24580
  5.7 24.3 %all-to-all-start = ((bf16[32,8,1152]{2,1,0:T(8,128)(2,1)}), bf16[32,8,1152]{2,1,0:T(8,128)(2,1)S(1)}, u32[]{:S(2)}, u32[]{:S(2)}) async-start(bf16[32,8,1152]{2,1,0:T(8,128)(2,1)} %fusion), calls=%async_computation | async-start | bytes 1179648 | tf_op jit(solution)/shard_map/all_to_all | solution.py:46
  85.6 93.2 %all-to-all-start.1 = ((bf16[32,24,4224]{2,1,0:T(8,128)(2,1)}), bf16[32,24,4224]{2,1,0:T(8,128)(2,1)}, u32[]{:S(2)}, u32[]{:S(2)}) async-start(bf16[32,24,4224]{2,1,0:T(8,128)(2,1)} %bitcast.47), calls=%async_computation.1 | async-start | bytes 12976128 | tf_op jit(solution)/shard_map/all_to_all | solution.py:46
  220.9 72.6 %all-to-all-start.2 = ((bf16[32,24,2176]{2,1,0:T(8,128)(2,1)}), bf16[32,24,2176]{2,1,0:T(8,128)(2,1)}, u32[]{:S(2)}, u32[]{:S(2)}) async-start(bf16[32,24,2176]{2,1,0:T(8,128)(2,1)} %bitcast.49), calls=%async_computation.2 | async-start | bytes 6684672 | tf_op jit(solution)/shard_map/all_to_all | solution.py:46
  241.9 4.6 copy-start.18
  289.6 2.7 copy-start
  292.3 1.1 copy-start.1
  293.4 9.3 %copy-start.3 = (f32[256,256]{1,0:T(8,128)S(1)}, f32[256,256]{1,0:T(8,128)}, u32[]{:S(2)}) copy-start(f32[256,256]{1,0:T(8,128)} %compare_select_fusion.bias) | copy-start | bytes 786436
  293.4 9.3 %copy-start.5 = (f32[256,128]{1,0:T(8,128)S(1)}, f32[256,128]{1,0:T(8,128)}, u32[]{:S(2)}) copy-start(f32[256,128]{1,0:T(8,128)} %get-tuple-element.99.cos_rows) | copy-start | bytes 393220
  293.4 9.3 %copy-start.6 = (f32[256,128]{1,0:T(8,128)S(1)}, f32[256,128]{1,0:T(8,128)}, u32[]{:S(2)}) copy-start(f32[256,128]{1,0:T(8,128)} %get-tuple-element.100.sin_rows) | copy-start | bytes 393220
  293.4 9.3 %copy-start.9 = (bf16[256,768]{1,0:T(8,128)(2,1)S(1)}, bf16[256,768]{1,0:T(8,128)(2,1)}, u32[]{:S(2)}) copy-start(bf16[256,768]{1,0:T(8,128)(2,1)} %get-tuple-element.46.pick_t.pick_y) | copy-start | bytes 1179652
  293.4 9.3 %copy-start.11 = (s32[256,8]{0,1:T(8,128)S(1)}, s32[256,8]{0,1:T(8,128)}, u32[]{:S(2)}) copy-start(s32[256,8]{0,1:T(8,128)} %param.20) | copy-start | bytes 24580
  293.5 9.3 %copy-start.12 = (f32[4,512]{1,0:T(4,128)S(1)}, f32[4,512]{1,0:T(4,128)}, u32[]{:S(2)}) copy-start(f32[4,512]{1,0:T(4,128)} %reshape.196.gain2) | copy-start | bytes 24580
  293.5 9.3 %copy-start.13 = (f32[8,256]{1,0:T(8,128)S(1)}, f32[8,256]{1,0:T(8,128)}, u32[]{:S(2)}) copy-start(f32[8,256]{1,0:T(8,128)} %get-tuple-element.82.keep) | copy-start | bytes 24580
  293.5 9.3 %copy-start.14 = (s32[8,256]{1,0:T(8,128)S(1)}, s32[8,256]{1,0:T(8,128)}, u32[]{:S(2)}) copy-start(s32[8,256]{1,0:T(8,128)} %fusion.17.slot_of) | copy-start | bytes 24580
  293.5 9.3 %copy-start.16 = (f32[1,128]{1,0:T(1,128)S(1)}, f32[1,128]{1,0:T(1,128)}, u32[]{:S(2)}) copy-start(f32[1,128]{1,0:T(1,128)} %get-tuple-element.101.k_gain) | copy-start | bytes 1540
  293.5 9.3 %copy-start.17 = (f32[1,128]{1,0:T(1,128)S(1)}, f32[1,128]{1,0:T(1,128)}, u32[]{:S(2)}) copy-start(f32[1,128]{1,0:T(1,128)} %get-tuple-element.102.q_gain) | copy-start | bytes 1540
  293.5 9.3 %copy-start.19 = (f32[256,512]{1,0:T(8,128)S(1)}, f32[256,512]{1,0:T(8,128)}, u32[]{:S(2)}) copy-start(f32[256,512]{1,0:T(8,128)} %get-tuple-element.63.q_hbm) | copy-start | bytes 1572868
  293.5 9.3 %copy-start.20 = (f32[256,512]{1,0:T(8,128)S(1)}, f32[256,512]{1,0:T(8,128)}, u32[]{:S(2)}) copy-start(f32[256,512]{1,0:T(8,128)} %get-tuple-element.64.k_hbm) | copy-start | bytes 1572868
  293.5 9.3 %copy-start.21 = (bf16[256,512]{1,0:T(8,128)(2,1)S(1)}, bf16[256,512]{1,0:T(8,128)(2,1)}, u32[]{:S(2)}) copy-start(bf16[256,512]{1,0:T(8,128)(2,1)} %get-tuple-element.60.qh) | copy-start | bytes 786436
  293.5 9.3 %copy-start.24 = (f32[8,256]{1,0:T(8,128)S(1)}, f32[8,256]{1,0:T(8,128)}, u32[]{:S(2)}) copy-start(f32[8,256]{1,0:T(8,128)} %get-tuple-element.56.gates) | copy-start | bytes 24580
  293.6 48.9 %all-to-all-start.3 = ((bf16[32,24,2048]{2,1,0:T(8,128)(2,1)}), bf16[32,24,2048]{2,1,0:T(8,128)(2,1)}, u32[]{:S(2)}, u32[]{:S(2)}) async-start(bf16[32,24,2048]{2,1,0:T(8,128)(2,1)} %bitcast.50), calls=%async_computation.3 | async-start | bytes 6291456 | tf_op jit(solution)/shard_map/all_to_all | solution.py:46
  302.9 1.0 copy-start.22
  337.0 1.0 copy-start.2
  440.4 9.5 %copy-start.27 = (f32[16,512]{1,0:T(8,128)S(1)}, f32[16,512]{1,0:T(8,128)}, u32[]{:S(2)}) copy-start(f32[16,512]{1,0:T(8,128)} %get-tuple-element.76) | copy-start | bytes 98308
  440.5 9.6 %copy-start.30 = (bf16[256,512]{1,0:T(8,128)(2,1)S(1)}, bf16[256,512]{1,0:T(8,128)(2,1)}, u32[]{:S(2)}) copy-start(bf16[256,512]{1,0:T(8,128)(2,1)} %get-tuple-element.75) | copy-start | bytes 786436
  440.5 9.6 %copy-start.31 = (bf16[256,512]{1,0:T(8,128)(2,1)S(1)}, bf16[256,512]{1,0:T(8,128)(2,1)}, u32[]{:S(2)}) copy-start(bf16[256,512]{1,0:T(8,128)(2,1)} %get-tuple-element.74) | copy-start | bytes 786436
  451.5 22.3 %all-to-all-start.4 = ((bf16[32,8,1664]{2,1,0:T(8,128)(2,1)}), bf16[32,8,1664]{2,1,0:T(8,128)(2,1)S(1)}, u32[]{:S(2)}, u32[]{:S(2)}) async-start(bf16[32,8,1664]{2,1,0:T(8,128)(2,1)} %pad_maximum_fusion), calls=%async_computation.4 | async-start | bytes 1703936 | tf_op jit(solution)/shard_map/all_to_all | solution.py:46
  462.4 2.9 copy-start.25
  (5 other events, 4.0 us)

commit v6 on v5

--- a/solution.py
+++ b/solution.py
@@ -176,25 +176,73 @@
     return grown / row_sum(grown)
 
 
+def select_slots(slot_of, slots):
+    top, tok = slot_of.shape
+    slot = lax.broadcasted_iota(jnp.int32, (slots, tok), 0)
+    pick = jnp.zeros((slots, tok), F32)
+    for k in range(top):
+        pick = jnp.where(slot_of[k : k + 1, :] == slot, 1.0, pick)
+    return pick
+
+
+def pre_kernel(local, slot_of, x_out, dy_out, send_out, x_all, dy_all, send_sem, recv_sem):
+    me = lax.axis_index("tensor")
+    ready = greet("tensor", ring(me))
+    blocks, _, col = x_all.shape
+    x_all[me] = local[:, :col]
+    dy_all[me] = local[:, col:]
+    ready()
+    post = Post("tensor", send_sem, recv_sem)
+    dy_in = gather_start(post, dy_all, me)
+    x_in = gather_start(post, x_all, me)
+    pick = select_slots(slot_of, send_out.shape[0]).astype(BF)
+    dy_in = gather_relay(post, dy_all, me, dy_in)
+    x_in = gather_relay(post, x_all, me, x_in)
+    arrive(dy_in)
+    dy_out[...] = dy_all[...]
+    for t in range(blocks):
+        send_out[:, t * col : (t + 1) * col] = dot(pick, dy_all[t]).astype(BF)
+    arrive(x_in)
+    x_out[...] = x_all[...]
+    post.finish()
+
+
+def pre_call(local, slot_of, blocks, slots):
+    tok, both = local.shape
+    col = both // 2
+    tiles = (blocks, tok, col)
+    shape = jax.ShapeDtypeStruct
+    vmem = pl.BlockSpec(memory_space=pltpu.VMEM)
+    return pl.pallas_call(
+        pre_kernel,
+        out_shape=(shape(tiles, BF), shape(tiles, BF), shape((slots, col * blocks), BF)),
+        in_specs=[vmem] * 2,
+        out_specs=(vmem,) * 3,
+        scratch_shapes=[
+            pltpu.VMEM(tiles, BF), pltpu.VMEM(tiles, BF),
+            pltpu.SemaphoreType.DMA((8,)), pltpu.SemaphoreType.DMA((8,)),
+        ],
+        compiler_params=pltpu.CompilerParams(
+            collective_id=6, has_side_effects=True, vmem_limit_bytes=48 * 1024 * 1024
+        ),
+        cost_estimate=COST,
+        name="pre",
+    )(local, slot_of)
+
+
 def front_kernel(
-    local, bias, cos_rows, sin_rows, gain1, gain2, q_gain, k_gain, router_t, routes, slot_of, keep,
+    x_all, bias, cos_rows, sin_rows, gain1, gain2, q_gain, k_gain, router_t, routes, slot_of, keep,
     wq_hbm, wk_hbm, wv_hbm, wo_hbm,
-    x_out, dy_out, resid_out, mixed_out, q_out, k_out, qh_out, kh_out, vh_out, ob_out,
+    resid_out, mixed_out, q_out, k_out, qh_out, kh_out, vh_out, ob_out,
     gates_out, send_out, pick_out,
-    wq, wk, wv, wo, x_all, dy_all, an, parts, halves, box, total, load_sem, send_sem, recv_sem,
+    wq, wk, wv, wo, an, parts, halves, box, total, load_sem, send_sem, recv_sem,
 ):
     me = lax.axis_index("tensor")
     ready = greet("tensor", ring(me))
     loads = fetch([(wq_hbm, wq), (wk_hbm, wk), (wv_hbm, wv), (wo_hbm, wo)], load_sem)
     blocks, tok, col = x_all.shape
     width = blocks * col
-    x_all[me] = local[:, :col]
-    dy_all[me] = local[:, col:]
-    ready()
     post = Post("tensor", send_sem, recv_sem)
-    x_in = gather_relay(post, x_all, me, gather_start(post, x_all, me))
-    dy_in = gather_start(post, dy_all, me)
-    arrive(x_in)
     square = jnp.zeros((tok, 1), F32)
     for t in range(blocks):
         value = x_all[t].astype(F32)
@@ -202,7 +250,6 @@
     r1 = inverse_rms(square, width)
     for t in range(blocks):
         an[t] = (x_all[t].astype(F32) * r1 * gain1[t : t + 1, :]).astype(BF)
-    x_out[...] = x_all[...]
 
     for copy in loads:
         copy.wait()
@@ -216,7 +263,6 @@
     q_out[...] = project(wq)
     k_out[...] = project(wk)
     vh_out[...] = project(wv).astype(BF)
-    dy_in = gather_relay(post, dy_all, me, dy_in)
     head = q_gain.shape[1]
     scale = 1.0 / math.sqrt(head)
     for h in range(col // head):
@@ -229,6 +275,7 @@
         ob_out[:, lanes] = dot(probs, vh_out[:, lanes]).astype(BF)
     for t in range(blocks):
         parts[t] = dot(ob_out[...], wo[:, t * col : (t + 1) * col]).astype(BF)
+    ready()
     first = scatter_start(post, parts, halves, me)
     moved = scatter_relay(post, parts, halves, box, me, first)
     total[me] = scatter_total(parts, box, me, moved).astype(BF)
@@ -274,49 +321,41 @@
     facts = jnp.zeros((slots, 128), F32)
     for n, piece in enumerate((first, second, third)):
         facts = jnp.where(lane == n, piece.astype(F32), facts)
-    send_out[:, width : width + 128] = facts.astype(BF)
-    arrive(dy_in)
-    dy_out[...] = dy_all[...]
-    for t in range(blocks):
-        lanes = slice(width + 128 + t * col, width + 128 + (t + 1) * col)
-        send_out[:, lanes] = dot(pick, dy_all[t]).astype(BF)
+    send_out[:, width:] = facts.astype(BF)
     post.finish()
 
 
-def front_call(local, bias, cos_rows, sin_rows, gain1, gain2, q_gain, k_gain, router_t, routes,
+def front_call(x_all, bias, cos_rows, sin_rows, gain1, gain2, q_gain, k_gain, router_t, routes,
                slot_of, keep, weights, slots):
-    tok, both = local.shape
-    col = both // 2
-    blocks = gain1.shape[0]
+    blocks, tok, col = tiles = x_all.shape
     width = col * blocks
     shape = jax.ShapeDtypeStruct
     vmem = pl.BlockSpec(memory_space=pltpu.VMEM)
-    tiles = (blocks, tok, col)
     top = routes.shape[0]
     return pl.pallas_call(
         front_kernel,
         out_shape=(
-            shape(tiles, BF), shape(tiles, BF), shape(tiles, F32),
-            shape(tiles, BF), shape((tok, col), F32), shape((tok, col), F32),
+            shape(tiles, F32), shape(tiles, BF), shape((tok, col), F32), shape((tok, col), F32),
             shape((tok, col), BF), shape((tok, col), BF), shape((tok, col), BF),
-            shape((tok, col), BF), shape((top, tok), F32), shape((slots, 2 * width + 128), BF),
+            shape((tok, col), BF), shape((top, tok), F32), shape((slots, width + 128), BF),
             shape((tok, slots), BF),
         ),
         in_specs=[vmem] * 12 + [pl.BlockSpec(memory_space=pl.ANY)] * 4,
-        out_specs=(vmem,) * 13,
+        out_specs=(vmem,) * 11,
         scratch_shapes=[
             pltpu.VMEM((width, col), BF), pltpu.VMEM((width, col), BF), pltpu.VMEM((width, col), BF),
             pltpu.VMEM((col, width), BF),
-            pltpu.VMEM(tiles, BF), pltpu.VMEM(tiles, BF), pltpu.VMEM(tiles, BF), pltpu.VMEM(tiles, BF),
+            pltpu.VMEM(tiles, BF), pltpu.VMEM(tiles, BF),
             pltpu.VMEM((2, tok // 2, col), BF), pltpu.VMEM((2, tok, col), BF), pltpu.VMEM(tiles, BF),
             pltpu.SemaphoreType.DMA((4,)),
-            pltpu.SemaphoreType.DMA((16,)), pltpu.SemaphoreType.DMA((16,)),
+            pltpu.SemaphoreType.DMA((8,)), pltpu.SemaphoreType.DMA((8,)),
         ],
         compiler_params=pltpu.CompilerParams(
             collective_id=1, has_side_effects=True, vmem_limit_bytes=56 * 1024 * 1024
         ),
+        cost_estimate=SHADOW,
         name="front",
-    )(local, bias, cos_rows, sin_rows, gain1, gain2, q_gain, k_gain, router_t, routes, slot_of,
+    )(x_all, bias, cos_rows, sin_rows, gain1, gain2, q_gain, k_gain, router_t, routes, slot_of,
       keep, *weights)
 
 
@@ -491,7 +530,7 @@
     )
 
 
-def weights_kernel(w, out, local_sem, send_sem, recv_sem, pass_send, pass_recv):
+def weights_kernel(w, first, second, out, local_sem, near_sem, send_sem, recv_sem, pass_send, pass_recv):
     base, core, rank = octet()
     ready = meet(octet_others(base, core, rank))
     ranks = out.shape[0]
@@ -501,23 +540,33 @@
     def part(ref, index, side):
         return ref.at[index, :, pl.ds(side * half, half), :]
 
+    offsets = (3 - 2 * core, 1 + 2 * core)
+    kept = []
+    for n, source in enumerate((first, second)):
+        place = part(out, (rank + offsets[n]) % ranks, core)
+        kept.append(pltpu.make_async_copy(source, place, near_sem.at[n]))
+        kept[-1].start()
     ready()
+    side = rank % 2
+    target = 2 * core + side
     sends = []
-    for s in range(2):
-        for k in range(2):
-            target = 2 * core + s
-            here = (target == rank) & (core == k)
-            source, place = part(w, s, k), part(out, rank, k)
-            local = pltpu.make_async_copy(source, place, local_sem)
-            away = remote(
-                source, place, send_sem.at[2 * s + k], recv_sem.at[rank],
-                {"expert": base + k, "tensor": target},
-            )
-            pl.when(here)(local.start)
-            pl.when(jnp.logical_not(here))(away.start)
-            sends.append((here, away))
+    for k in range(2):
+        here = (target == rank) & (core == k)
+        source, place = part(w, side, k), part(out, rank, k)
+        local = pltpu.make_async_copy(source, place, local_sem)
+        away = remote(
+            source, place, send_sem.at[k], recv_sem.at[rank], {"expert": base + k, "tensor": target}
+        )
+        pl.when(here)(local.start)
+        pl.when(jnp.logical_not(here))(away.start)
+        sends.append((here, away))
     passed = []
-    for d in (0, 1, 3, 2):
+    for n, source in enumerate((first, second)):
+        d = offsets[n]
+        place = part(out, (rank + d) % ranks, core)
+        passed.append(remote(source, place, pass_send.at[d], pass_recv.at[d], sibling))
+        passed[-1].start()
+    for d in (0, 2):
         quarter = (rank + d) % ranks
         mine = part(out, quarter, core)
         arrival = remote(mine, mine, send_sem.at[0], recv_sem.at[quarter], sibling)
@@ -527,25 +576,53 @@
         passed.append(remote(mine, mine, pass_send.at[d], pass_recv.at[d], sibling))
         passed[-1].start()
     for copy in passed:
-        copy.wait()
+        copy.wait_send()
+    for d in range(ranks):
+        theirs = part(out, (rank + d) % ranks, 1 - core)
+        remote(theirs, theirs, pass_send.at[d], pass_recv.at[d], sibling).wait_recv()
     for here, away in sends:
         pl.when(jnp.logical_not(here))(away.wait_send)
-
-
-def weights_call(w):
+    for copy in kept:
+        copy.wait()
+
+
+def weights_call(w, first, second):
     _, three, width, hidden = w.shape
     hbm = pl.BlockSpec(memory_space=pl.ANY)
-    sems = pltpu.SemaphoreType.DMA((4,))
+    pairs, sems = pltpu.SemaphoreType.DMA((2,)), pltpu.SemaphoreType.DMA((4,))
     return pl.pallas_call(
         weights_kernel,
         out_shape=jax.ShapeDtypeStruct((4, three, width, hidden), BF),
-        in_specs=[hbm],
+        in_specs=[hbm] * 3,
         out_specs=hbm,
-        scratch_shapes=[pltpu.SemaphoreType.DMA, sems, sems, sems, sems],
-        compiler_params=pltpu.CompilerParams(collective_id=4, has_side_effects=True),
+        scratch_shapes=[pltpu.SemaphoreType.DMA, pairs, pairs, sems, sems, sems],
+        compiler_params=pltpu.CompilerParams(
+            collective_id=4, has_side_effects=True, vmem_limit_bytes=60 * 1024 * 1024
+        ),
         cost_estimate=SHADOW,
         name="weights",
-    )(w)
+    )(w, first, second)
+
+
+def near_weights(w):
+    ranks = lax.axis_size("tensor")
+    places = lax.axis_size("expert")
+    half = w.shape[2] // 2
+    core, rank = lax.axis_index("expert") % 2, lax.axis_index("tensor")
+    side = 1 - rank % 2
+    leftward = jnp.where(2 * core + side == (rank + 1) % ranks, 0, 1)
+    come = []
+    for turn_over in range(2):
+        pairs = []
+        for place in range(places):
+            for t in range(ranks):
+                target = 2 * (place % 2) + 1 - t % 2
+                to_core = (0 if target == (t + 1) % ranks else 1) ^ turn_over
+                pairs.append((place * ranks + t, (place - place % 2 + to_core) * ranks + target))
+        to_core = jnp.where(turn_over == 0, leftward, 1 - leftward)
+        piece = lax.dynamic_slice(w, (side, 0, to_core * half, 0), (1,) + w.shape[1:2] + (half,) + w.shape[3:])
+        come.append(lax.ppermute(piece[0], ("expert", "tensor"), pairs))
+    return come
 
 
 def home_kernel(grads, out, far_out, own, got, load_sem, local_sem, swap_send, swap_recv, send_sem, recv_sem):
@@ -635,22 +712,21 @@
             halves, halves, sems, pltpu.SemaphoreType.DMA, sems, sems, sems, sems,
         ],
         compiler_params=pltpu.CompilerParams(
-            collective_id=5, has_side_effects=True, vmem_limit_bytes=24 * 1024 * 1024
+            collective_id=5, has_side_effects=True, vmem_limit_bytes=60 * 1024 * 1024
         ),
         cost_estimate=SHADOW,
         name="home",
     )(grads)
 
 
-def expert_kernel(rows_ref, w_ref, y_ref, dx_ref, grad_ref, rows_t, dys_t, y_acc, dx_acc, gate_of, dgate):
+def expert_kernel(rows_ref, dys, w_ref, y_ref, dx_ref, grad_ref, rows_t, dys_t, y_acc, dx_acc, gate_of, dgate):
     step = pl.program_id(0)
     width = y_acc.shape[1]
     rows = rows_ref.at[:, :width]
-    dys = rows_ref.at[:, width + 128 :]
 
     @pl.when(step == 0)
     def _():
-        gate_of[...] = row_sum(rows_ref[:, width : width + 128].astype(F32))
+        gate_of[...] = row_sum(rows_ref[:, width:].astype(F32))
         rows_t[...] = rows[...].T
         dys_t[...] = (dys[...].astype(F32) * gate_of[...]).astype(BF).T
         dgate[...] = jnp.zeros_like(dgate)
@@ -684,7 +760,7 @@
         dx_ref[:, width:] = facts.astype(BF)
 
 
-def expert_call(rows, weights):
+def expert_call(rows, dys, weights):
     quarters, _, width, hidden = weights.shape
     count = rows.shape[0]
     shape = jax.ShapeDtypeStruct
@@ -698,7 +774,7 @@
         expert_kernel,
         grid=(quarters,),
         out_shape=tuple(outs) + (shape(weights.shape, BF),),
-        in_specs=[whole(rows), block],
+        in_specs=[whole(rows), whole(dys), block],
         out_specs=tuple(whole(value) for value in outs) + (block,),
         scratch_shapes=[
             pltpu.VMEM((width, count), BF),
@@ -711,7 +787,7 @@
         compiler_params=pltpu.CompilerParams(vmem_limit_bytes=62 * 1024 * 1024),
         cost_estimate=COST,
         name="expert",
-    )(rows, weights)
+    )(rows, dys, weights)
 
 
 def plane():
@@ -730,7 +806,7 @@
 def reduce_kernel(
     d_qkv, dr, d_mine, router_part, small_in, x_all, gain1, ob, pick_y, ret_y,
     far_hbm, resid_hbm, wq_hbm, wk_hbm, wv_hbm,
-    wide_out, dx_out, out_out, small_out, far_out,
+    q_out, k_out, v_out, router_out, o_out, dx_out, out_out, small_out, far_out,
     wq, wk, wv, resid, parts, y_parts, halves, box_x, note, buf, box, got,
     load_sem, out_sem, x_send, x_recv, send_sem, recv_sem, far_send, far_recv,
 ):
@@ -749,36 +825,10 @@
         value = x_all[t].astype(F32)
         square = square + row_sum(value * value)
     r1 = inverse_rms(square, width)
-    for copy in loads:
-        copy.wait()
-    for t in range(blocks):
-        rows = slice(t * col, (t + 1) * col)
-        parts[t] = (
-            dot(d_qkv[:, 0:col], wq[rows, :], 1, 1)
-            + dot(d_qkv[:, col : 2 * col], wk[rows, :], 1, 1)
-            + dot(d_qkv[:, 2 * col : 3 * col], wv[rows, :], 1, 1)
-        ).astype(BF)
-    ready()
     post_x = Post("tensor", x_send, x_recv)
     post = Post("expert", send_sem, recv_sem)
     x_halves, x_box = halves.at[pl.ds(0, 2)], box_x.at[pl.ds(0, 2)]
     y_halves, y_box = halves.at[pl.ds(2, 2)], box_x.at[pl.ds(2, 2)]
-    x_first = scatter_start(post_x, parts, x_halves, me)
-
-    half = far_hbm.shape[1]
-    owner = me // 2
-
-    def far_copy(n, side, device):
-        return remote(
-            far_hbm.at[n], far_out.at[n, pl.ds(side * half, half), :],
-            far_send.at[n], far_recv.at[n, side], device,
-        )
-
-    far_copies = [
-        far_copy(n, core, {"expert": base + owner, "tensor": (me + 2) % blocks}) for n in range(3)
-    ]
-    far_copies[0].start()
-
     chunks = buf.shape[0] // blocks
     rows_chunk = buf.shape[1]
 
@@ -802,16 +852,40 @@
 
         lax.fori_loop(0, count, one, 0)
 
+    half = far_hbm.shape[1]
+    owner = me // 2
+
+    def far_copy(n, side, device):
+        return remote(
+            far_hbm.at[n], far_out.at[n, pl.ds(side * half, half), :],
+            far_send.at[n], far_recv.at[n, side], device,
+        )
+
+    far_copies = [
+        far_copy(n, core, {"expert": base + owner, "tensor": (me + 2) % blocks}) for n in range(3)
+    ]
     copies = []
+    ready()
     for n in range(2):
         products(2 * (1 - core) + n)
         for s in range(2 * n, 2 * n + 2):
             source = buf.at[pl.ds((1 - core) * 64 + s * 16, 16)]
             copies.append(post.push(source, box.at[pl.ds(31 * s, 16)], dims[0][1]))
+    for copy in loads:
+        copy.wait()
+    for t in range(blocks):
+        rows = slice(t * col, (t + 1) * col)
+        parts[t] = (
+            dot(d_qkv[:, 0:col], wq[rows, :], 1, 1)
+            + dot(d_qkv[:, col : 2 * col], wk[rows, :], 1, 1)
+            + dot(d_qkv[:, 2 * col : 3 * col], wv[rows, :], 1, 1)
+        ).astype(BF)
+    x_first = scatter_start(post_x, parts, x_halves, me)
+    far_copies[0].start()
+    for n in range(2):
+        products(2 * core + n)
     x_moved = scatter_relay(post_x, parts, x_halves, x_box, me, x_first)
     far_copies[1].start()
-    for n in range(2):
-        products(2 * core + n)
     place = [core * 64 + s * 16 for s in range(4)]
     size, first = 16, 0
 
@@ -872,6 +946,21 @@
 
     size = 1
     stores = []
+
+    def keep(n, at):
+        here = pl.ds(at, 16)
+        outs = (q_out, k_out, v_out, None, router_out)
+        for m, target in enumerate(outs):
+            lanes = pl.ds(m * col, target.shape[2] if m != 3 else col)
+            if m == 3:
+                turned = got[here, :, lanes].reshape(16 * rows_chunk, col).T
+                o_out[:, pl.ds(pl.multiple_of(at * rows_chunk, 128), 16 * rows_chunk)] = turned
+                continue
+            stores.append(
+                pltpu.make_async_copy(got.at[here, :, lanes], target.at[here], out_sem.at[n, m])
+            )
+            stores[-1].start()
+
     for k in range(3, -1, -1):
         for s in range(4):
             copies[s].wait_recv()
@@ -881,18 +970,13 @@
             here = got.at[pl.ds(place[s], 2 * size)]
             copies[s] = post.push(here, here, partner)
             if not k:
-                stores.append(
-                    pltpu.make_async_copy(here, wide_out.at[pl.ds(place[s], 16)], out_sem.at[s])
-                )
-                stores[-1].start()
+                keep(s, place[s])
         size *= 2
         if k == 2:
             out_out[...] = (resid[...] + scatter_total(y_parts, y_box, me, y_moved)).astype(BF)
     for s in range(4):
         copies[s].wait_recv()
-        there = pl.ds((1 - core) * 64 + s * 16, 16)
-        stores.append(pltpu.make_async_copy(got.at[there], wide_out.at[there], out_sem.at[4 + s]))
-        stores[-1].start()
+        keep(4 + s, (1 - core) * 64 + s * 16)
     post.finish()
     post_x.finish()
     for store in stores:
@@ -917,18 +1001,20 @@
     return pl.pallas_call(
         reduce_kernel,
         out_shape=(
-            shape(wide, BF), shape((tok, col), BF), shape((tok, col), BF), shape((16, col), F32),
+            shape(wide[:2] + (col,), BF), shape(wide[:2] + (col,), BF), shape(wide[:2] + (col,), BF),
+            shape(wide[:2] + (128,), BF), shape((col, width), BF),
+            shape((tok, col), BF), shape((tok, col), BF), shape((16, col), F32),
             shape((far.shape[0], 2 * far.shape[1], far.shape[2]), BF),
         ),
         in_specs=[vmem] * 10 + [hbm] * 5,
-        out_specs=(hbm, vmem, vmem, vmem, hbm),
+        out_specs=(hbm,) * 4 + (vmem,) * 4 + (hbm,),
         scratch_shapes=[
             pltpu.VMEM((width, col), BF), pltpu.VMEM((width, col), BF), pltpu.VMEM((width, col), BF),
             pltpu.VMEM((tok, col), F32), pltpu.VMEM(tiles, BF), pltpu.VMEM(tiles, BF),
             pltpu.VMEM((4, tok // 2, col), BF), pltpu.VMEM((4, tok, col), BF),
             pltpu.VMEM((blocks, 16, col), F32),
             pltpu.VMEM(wide, BF), pltpu.VMEM((124,) + wide[1:], BF), pltpu.VMEM(wide, BF),
-            pltpu.SemaphoreType.DMA((4,)), pltpu.SemaphoreType.DMA((8,)),
+            pltpu.SemaphoreType.DMA((4,)), pltpu.SemaphoreType.DMA((8, 5)),
             pltpu.SemaphoreType.DMA((count,)), pltpu.SemaphoreType.DMA((count,)),
             pltpu.SemaphoreType.DMA((40,)), pltpu.SemaphoreType.DMA((40,)),
             pltpu.SemaphoreType.DMA((3,)), pltpu.SemaphoreType.DMA((3, 2)),
@@ -971,6 +1057,7 @@
     local_experts = expert_w.shape[0]
 
     w_stored = jnp.transpose(expert_w, (0, 2, 1, 3))
+    w_near = near_weights(w_stored)
 
     routes_t = routes.T
     order_t = pair_order[0].reshape(tok_count, top_count).T
@@ -1018,18 +1105,21 @@
     head_gains = (q_gain.astype(F32)[None], k_gain.astype(F32)[None])
     router = jnp.pad(w_router, ((0, 0), (0, 128 - expert_count)))
     weights = (w_query, w_key, w_value, w_output)
+    def homeward(value):
+        return exchange(value.reshape(groups, -1, value.shape[1]), "expert").reshape(value.shape)
+
+    x_all, dy_all, send_dy = pre_call(local, slot_of, tensor_count, slots)
+    send_dy, x_all = lax.optimization_barrier((send_dy, x_all))
+    recv_dy = homeward(send_dy)
     (
-        x_all, dy_all, resid, mixed, q_raw, k_raw, qh, kh, vh, attended, gates, send_rows, pick_t,
+        resid, mixed, q_raw, k_raw, qh, kh, vh, attended, gates, send_rows, pick_t,
     ) = front_call(
-        local, bias, cos_rows, sin_rows, gain1, gain2, *head_gains, router.T, routes_t, slot_of,
+        x_all, bias, cos_rows, sin_rows, gain1, gain2, *head_gains, router.T, routes_t, slot_of,
         keep_mask, weights, slots,
     )
-    def homeward(value):
-        return exchange(value.reshape(groups, -1, value.shape[1]), "expert").reshape(value.shape)
-
-    send_rows, w_stored = lax.optimization_barrier((send_rows, w_stored))
+    send_rows, w_stored, recv_dy = lax.optimization_barrier((send_rows, w_stored, recv_dy))
     recv_rows = homeward(send_rows)
-    y_rows, d_rows, partial = expert_call(recv_rows, weights_call(w_stored))
+    y_rows, d_rows, partial = expert_call(recv_rows, recv_dy, weights_call(w_stored, *w_near))
     ret_rows = homeward(d_rows)
     near, far = home_call(partial)
     ret_rows, near, far, y_rows = lax.optimization_barrier((ret_rows, near, far, y_rows))
@@ -1039,11 +1129,10 @@
         sin_rows, gain2, *head_gains, router, resid, dy_all, mixed, qh, kh, vh, q_raw, k_raw,
         w_output,
     )
-    summed, dx_slice, out_slice, small, far = reduce_call(
+    *wide, router_sum, out_proj, dx_slice, out_slice, small, far = reduce_call(
         d_qkv, dr, d_mine, router_part, small, x_all, gain1, attended, pick_t, ret_y, far, resid,
         weights[:3],
     )
-    summed = summed.reshape(width, -1)
 
     going = dot(put, jnp.concatenate([out_slice, dx_slice], axis=1), 0, 0).astype(BF)
     small = small[:9].astype(BF).reshape(move_rows, -1)
@@ -1057,7 +1146,7 @@
     is_far = jnp.arange(local_experts) == opposite
     expert_grad = jnp.where(is_far[:, None, None, None], far[None], near).astype(F32)
     expert_grad = jnp.transpose(expert_grad, (0, 2, 1, 3))
-    wide = [summed[:, n * col_count : (n + 1) * col_count] for n in range(4)]
+    wide = [value.reshape(width, -1) for value in wide]
     gain_at = 2 * width + tok_count
     head = q_gain.shape[0]
     return (
@@ -1069,9 +1158,9 @@
         wide[2].astype(F32),
         small[gain_at : gain_at + head],
         small[gain_at + head : gain_at + 2 * head],
-        wide[3].T.astype(F32),
+        out_proj.astype(F32),
         small[width : 2 * width],
-        summed[:, width : width + expert_count].astype(F32),
+        router_sum.reshape(width, -1)[:, :expert_count].astype(F32),
         expert_grad,
     )
 

time: 480 us -> 568 us (1.18)
  Pallas kernels: 346 us -> 449 us
  starting transfers between devices: 59.5 us -> 50.9 us
  local copies, waits for them, and re-layouts: 27.2 us -> 19.1 us
    pallas_call x1, Pallas kernels: 80 us -> 150 us  [weights_call(): pl.pallas_call(weights_kernel, out_shape=jax.ShapeDtypeStruct((4, three,...]
    pallas_call x2 -> x3, Pallas kernels: 149 us -> 180 us  [the longest x1 99.4 us: reduce_call(): pl.pallas_call(reduce_kernel, out_shape=(shape(wide[:2] + (col,), BF), sh...]
    all_to_all x5 -> x6, starting transfers between devices: 59.5 us -> 47.8 us  [exchange(): return lax.all_to_all(value, axis, split_axis=0, concat_axis=0, tiled=True)]
    unnamed x70 -> x89, local copies, waits for them, and re-layouts: 18.6 us -> 8.41 us
    slice x1 -> x0, other arithmetic: 9.45 us -> none  [body(): wide = [summed[:, n * col_count:(n + 1) * col_count] for n in range(4)]]
    convert_element_type x2 -> x5, other arithmetic: 3.37 us -> 11.8 us  [the longest x1 2.86 us: body(): wide[1].astype(F32)]
  transfers between devices with their start and end apart: 5 -> 8, of which waited for: 2 -> 2; matrix products, arithmetic and copies ran while one was open for 6% -> 6% of each run, Pallas kernels for 33% -> 55%
where the time goes in v6:
time: 568 us; the launch traced here: 561 us
  Pallas kernels  449 us (79%)
  starting transfers between devices  50.9 us (9%)
  other arithmetic  32.6 us (6%)
  local copies, waits for them, and re-layouts  19.1 us (3%)
    pallas_call x1, Pallas kernels, weights_call(): pl.pallas_call(weights_kernel, out_shape=jax.ShapeDtypeStruct((4, three,...  150 us
    pallas_call x1, Pallas kernels, reduce_call(): pl.pallas_call(reduce_kernel, out_shape=(shape(wide[:2] + (col,), BF), sh...  99.4 us
    all_to_all x6, starting transfers between devices, exchange(): return lax.all_to_all(value, axis, split_axis=0, concat_axis=0, tiled=True)  47.8 us
    pallas_call x1, Pallas kernels, home_call(): pl.pallas_call(home_kernel, out_shape=(shape((2, three, width, hidden), B...  44.1 us
    pallas_call x1, Pallas kernels, expert_call(): pl.pallas_call(expert_kernel, grid=(quarters,), out_shape=tuple(outs) + (...  42.1 us
    pallas_call x1, Pallas kernels, pre_call(): pl.pallas_call(pre_kernel, out_shape=(shape(tiles, BF), shape(tiles, BF),...  41.7 us
    pallas_call x1, Pallas kernels, front_call(): pl.pallas_call(front_kernel, out_shape=(shape(tiles, F32), shape(tiles, B...  38.5 us
    pallas_call x1, Pallas kernels, back_call(): pl.pallas_call(back_kernel, out_shape=(shape((tok, 3 * col), BF), shape(t...  33.6 us
  transfers between devices with their start and end apart: 8, of which 2 were waited for; matrix products, arithmetic and copies ran while one was open for 6% of the time, Pallas kernels for 55%

profile of v6, /device:TPU:1, one launch (start us, length us, event | category | flops | bytes accessed | tf_op | source)
XLA Modules:
  0.0 561.0 jit_solution(6584000969982478495)
XLA Ops:
  3.3 1.2 concatenate.15
  4.5 1.2 fusion
  5.7 9.6 %all-to-all-start = ((bf16[32,8,1152]{2,1,0:T(8,128)(2,1)}), bf16[32,8,1152]{2,1,0:T(8,128)(2,1)S(1)}, u32[]{:S(2)}, u32[]{:S(2)}) async-start(bf16[32,8,1152]{2,1,0:T(8,128)(2,1)} %fusion), calls=%async_computation | async-start | bytes 1179648 | tf_op jit(solution)/shard_map/all_to_all | solution.py:46
  15.4 3.8 dynamic-slice_bitcast_fusion
  19.2 2.6 collective-permute-start.1
  25.3 3.4 convert_reduce_fusion
  33.9 1.0 copy.42.router_t
  34.9 41.7 %pre.1 = (bf16[4,256,512]{2,1,0:T(8,128)(2,1)S(1)}, bf16[4,256,512]{2,1,0:T(8,128)(2,1)S(1)}, bf16[768,2048]{1,0:T(8,128)(2,1)}) custom-call(bf16[256,1024]{1,0:T(8,128)(2,1)S(1)} %convolution_convert_fusion.3.local, s32[8,256]{1,0:T(8,128)S(1)} %fusion.17.slot_of), custom_call_target="tpu_custom_call" | custom-call | flops 1 | bytes 1 | tf_op jit(solution)/shard_map/pre/pallas_call | solution.py:216
  77.6 1.0 copy-done.18
  78.6 8.0 %all-to-all-start.1 = ((bf16[32,24,2048]{2,1,0:T(8,128)(2,1)}), bf16[32,24,2048]{2,1,0:T(8,128)(2,1)}, u32[]{:S(2)}, u32[]{:S(2)}) async-start(bf16[32,24,2048]{2,1,0:T(8,128)(2,1)} %bitcast.12), calls=%async_computation.1 | async-start | bytes 6291456 | tf_op jit(solution)/shard_map/all_to_all | solution.py:46
  86.6 38.5 %front.1 = (f32[4,256,512]{2,1,0:T(8,128)}, bf16[4,256,512]{2,1,0:T(8,128)(2,1)}, f32[256,512]{1,0:T(8,128)}, f32[256,512]{1,0:T(8,128)}, bf16[256,512]{1,0:T(8,...) custom-call(bf16[4,256,512]{2,1,0:T(8,128)(2,1)} %copy-done, ...), custom_call_target="tpu_custom_call" | custom-call | flops 40000000000 | bytes 1 | tf_op jit(solution)/shard_map/front/pallas_call | solution.py:335
  125.1 1.2 all-to-all-done.1
  126.2 7.9 %all-to-all-start.2 = ((bf16[32,24,2176]{2,1,0:T(8,128)(2,1)}), bf16[32,24,2176]{2,1,0:T(8,128)(2,1)}, u32[]{:S(2)}, u32[]{:S(2)}) async-start(bf16[32,24,2176]{2,1,0:T(8,128)(2,1)} %bitcast.65), calls=%async_computation.2 | async-start | bytes 6684672 | tf_op jit(solution)/shard_map/all_to_all | solution.py:46
  134.2 150.0 %weights.1.w_ref = bf16[4,3,2048,256]{3,2,1,0:T(8,128)(2,1)} custom-call(bf16[2,3,2048,256]{3,2,1,0:T(8,128)(2,1)} %bitcast.69, bf16[3,1024,256]{2,1,0:T(8,128)(2,1)} %collective-permute-done.first, bf16[3,1024,256]{2,1,0:T(8,128)(2,1)} %collective-permute-done.1.second), custom_call_target="tpu_custom_call" | custom-call | flops 40000000000 | bytes 1 | tf_op jit(solution)/shard_map/weights/pallas_call | solution.py:593
  284.2 42.1 %expert.1 = (bf16[768,2048]{1,0:T(8,128)(2,1)}, bf16[768,2176]{1,0:T(8,128)(2,1)}, bf16[4,3,2048,256]{3,2,1,0:T(8,128)(2,1)}) custom-call(bf16[768,2176]{1,0:T(8,128)(2,1)} %bitcast.15.rows_ref, bf16[768,2048]{1,0:T(8,128)(2,1)} %bitcast.13.dys, bf16[4,3,2048,256]{3,2,1,0:T(8,128)(2,1)} %weights.1.w_ref), custom_call_target="tpu_custom_call" | custom-call | flops 1 | bytes 1 | tf_op jit(solution)/shard_map/expert/pallas_call | solution.py:773
  326.3 7.5 %all-to-all-start.3 = ((bf16[32,24,2176]{2,1,0:T(8,128)(2,1)}), bf16[32,24,2176]{2,1,0:T(8,128)(2,1)}, u32[]{:S(2)}, u32[]{:S(2)}) async-start(bf16[32,24,2176]{2,1,0:T(8,128)(2,1)} %bitcast.66), calls=%async_computation.3 | async-start | bytes 6684672 | tf_op jit(solution)/shard_map/all_to_all | solution.py:46
  333.8 44.1 %home.1 = (bf16[2,3,2048,256]{3,2,1,0:T(8,128)(2,1)}, bf16[3,1024,256]{2,1,0:T(8,128)(2,1)}) custom-call(bf16[4,3,2048,256]{3,2,1,0:T(8,128)(2,1)} %get-tuple-element.64.grads), custom_call_target="tpu_custom_call" | custom-call | flops 40000000000 | bytes 1 | tf_op jit(solution)/shard_map/home/pallas_call | solution.py:704
  378.1 9.4 %all-to-all-start.4 = ((bf16[32,24,2048]{2,1,0:T(8,128)(2,1)}), bf16[32,24,2048]{2,1,0:T(8,128)(2,1)}, u32[]{:S(2)}, u32[]{:S(2)}) async-start(bf16[32,24,2048]{2,1,0:T(8,128)(2,1)} %bitcast.67), calls=%async_computation.4 | async-start | bytes 6291456 | tf_op jit(solution)/shard_map/all_to_all | solution.py:46
  387.7 33.6 %back.1 = (bf16[256,1536]{1,0:T(8,128)(2,1)S(1)}, bf16[4,256,512]{2,1,0:T(8,128)(2,1)S(1)}, f32[256,512]{1,0:T(8,128)S(1)}, bf16[2048,128]{1,0:T(8,128)(2,1)S(1)}, f32[8,512]{1,0:T(8,128)S(1)}) custom-call(bf16[256,768]{1,0:T(8,128)(2,1)S(1)} %copy-done.5, bf16[768,2176]{1,0:T(8,128)(2,1)} %bitcast.21.ret, s32[8,256]{1,0:T(8,128)S(1)} %copy-done.12, ...), custom_call_target="tpu_custom_call" | custom-call | flops 20000000000 | bytes 1 | tf_op jit(solution)/shard_map/back/pallas_call | solution.py:478
  425.4 1.9 all-to-all-done.4
  427.3 99.4 %reduce.7 = (bf16[128,16,512]{2,1,0:T(8,128)(2,1)}, bf16[128,16,512]{2,1,0:T(8,128)(2,1)}, bf16[128,16,512]{2,1,0:T(8,128)(2,1)}, bf16[128,16,128]{2,1,0:T(8,128...) custom-call(bf16[256,1536]{1,0:T(8,128)(2,1)} %copy-done.2, ...), custom_call_target="tpu_custom_call" | custom-call | flops 1 | bytes 1 | tf_op jit(solution)/shard_map/reduce/pallas_call | solution.py:1001
  527.6 1.4 copy.44
  529.9 1.4 fusion.1
  531.3 1.0 pad_maximum_fusion
  532.3 5.3 all-to-all-start.5
  537.6 2.7 bitcast_convert_fusion.2
  540.4 2.9 bitcast_convert_fusion.1
  543.2 2.9 bitcast_convert_fusion
  546.2 2.5 convert_element_type.122
  548.8 7.6 %convert_bitcast_fusion = f32[2,2048,3,256]{3,1,2,0:T(8,128)} fusion(bf16[2,3,2048,256]{3,2,1,0:T(8,128)(2,1)S(1)} %bitcast.64, pred[2]{0:T(512)(128)(4,1)S(1)} %iota_compare_fusion.8, bf16[3,2048,256]{2,1,0:T(8,128)(2,1)} %get-tuple-element.94), kind=kLoop, calls=%fused_computation.1 | loop fusion | flops 6291456 | bytes 22020098 | tf_op jit(solution)/shard_map/transpose | solution.py:1148
  556.3 1.0 convert_reduce_fusion.1
  558.5 1.4 convolution_convert_fusion.1
  (136 shorter events, 20.1 us)
Async XLA Ops:
  5.7 26.2 %all-to-all-start = ((bf16[32,8,1152]{2,1,0:T(8,128)(2,1)}), bf16[32,8,1152]{2,1,0:T(8,128)(2,1)S(1)}, u32[]{:S(2)}, u32[]{:S(2)}) async-start(bf16[32,8,1152]{2,1,0:T(8,128)(2,1)} %fusion), calls=%async_computation | async-start | bytes 1179648 | tf_op jit(solution)/shard_map/all_to_all | solution.py:46
  15.4 13.3 %copy-start.29 = (bf16[2048,64]{0,1:T(8,128)(2,1)S(1)}, bf16[2048,64]{0,1:T(8,128)(2,1)}, u32[]{:S(2)}) copy-start(bf16[2048,64]{0,1:T(8,128)(2,1)} %param.30) | copy-start | bytes 786436
  15.4 13.6 %copy-start.38 = (bf16[128]{0:T(256)(128)(2,1)S(1)}, bf16[128]{0:T(256)(128)(2,1)}, u32[]{:S(2)}) copy-start(bf16[128]{0:T(256)(128)(2,1)} %param.27) | copy-start | bytes 772
  15.4 13.6 %copy-start.39 = (bf16[128]{0:T(256)(128)(2,1)S(1)}, bf16[128]{0:T(256)(128)(2,1)}, u32[]{:S(2)}) copy-start(bf16[128]{0:T(256)(128)(2,1)} %param.26) | copy-start | bytes 772
  19.2 115.0 %collective-permute-start.1 = (bf16[3,1024,256]{2,1,0:T(8,128)(2,1)}, bf16[3,1024,256]{2,1,0:T(8,128)(2,1)}, u32[]{:S(2)}, u32[]{:S(2)}) collective-permute-start(bf16[3,1024,256]{2,1,0:T(8,128)(2,1)} %get-tuple-element.100), channel_id=1, source_target_pairs={{0,5},{1,0},{2,1},{3,4},{4,3},{5,6},{6,7},{7,2},{8,13},{9,8},{10,9... | collective-permute-start | bytes 4718600 | tf_op jit(solution)/shard_map/ppermute | solution.py:624
  21.8 112.4 %collective-permute-start = (bf16[3,1024,256]{2,1,0:T(8,128)(2,1)}, bf16[3,1024,256]{2,1,0:T(8,128)(2,1)}, u32[]{:S(2)}, u32[]{:S(2)}) collective-permute-start(bf16[3,1024,256]{2,1,0:T(8,128)(2,1)} %get-tuple-element.101), channel_id=1, source_target_pairs={{0,1},{1,4},{2,5},{3,0},{4,7},{5,2},{6,3},{7,6},{8,9},{9,12},{10,1... | collective-permute-start | bytes 4718600 | tf_op jit(solution)/shard_map/ppermute | solution.py:624
  32.9 45.7 %copy-start.11 = (s32[8,256]{1,0:T(8,128)}, s32[8,256]{1,0:T(8,128)S(1)}, u32[]{:S(2)}) copy-start(s32[8,256]{1,0:T(8,128)S(1)} %fusion.17.slot_of) | copy-start | bytes 24580
  33.6 45.0 %copy-start.33 = (s32[256]{0:T(256)}, s32[256]{0:T(256)S(1)}, u32[]{:S(2)}) copy-start(s32[256]{0:T(256)S(1)} %reshape.209) | copy-start | bytes 3076
  78.6 47.7 %all-to-all-start.1 = ((bf16[32,24,2048]{2,1,0:T(8,128)(2,1)}), bf16[32,24,2048]{2,1,0:T(8,128)(2,1)}, u32[]{:S(2)}, u32[]{:S(2)}) async-start(bf16[32,24,2048]{2,1,0:T(8,128)(2,1)} %bitcast.12), calls=%async_computation.1 | async-start | bytes 6291456 | tf_op jit(solution)/shard_map/all_to_all | solution.py:46
  126.2 157.9 %all-to-all-start.2 = ((bf16[32,24,2176]{2,1,0:T(8,128)(2,1)}), bf16[32,24,2176]{2,1,0:T(8,128)(2,1)}, u32[]{:S(2)}, u32[]{:S(2)}) async-start(bf16[32,24,2176]{2,1,0:T(8,128)(2,1)} %bitcast.65), calls=%async_computation.2 | async-start | bytes 6684672 | tf_op jit(solution)/shard_map/all_to_all | solution.py:46
  326.3 51.6 %all-to-all-start.3 = ((bf16[32,24,2176]{2,1,0:T(8,128)(2,1)}), bf16[32,24,2176]{2,1,0:T(8,128)(2,1)}, u32[]{:S(2)}, u32[]{:S(2)}) async-start(bf16[32,24,2176]{2,1,0:T(8,128)(2,1)} %bitcast.66), calls=%async_computation.3 | async-start | bytes 6684672 | tf_op jit(solution)/shard_map/all_to_all | solution.py:46
  377.9 9.6 %copy-start.5 = (bf16[256,768]{1,0:T(8,128)(2,1)S(1)}, bf16[256,768]{1,0:T(8,128)(2,1)}, u32[]{:S(2)}) copy-start(bf16[256,768]{1,0:T(8,128)(2,1)} %get-tuple-element.57.pick_t.pick_y) | copy-start | bytes 1179652
  377.9 9.6 %copy-start.6 = (f32[256,256]{1,0:T(8,128)S(1)}, f32[256,256]{1,0:T(8,128)}, u32[]{:S(2)}) copy-start(f32[256,256]{1,0:T(8,128)} %compare_select_fusion.bias) | copy-start | bytes 786436
  377.9 9.6 %copy-start.7 = (f32[256,128]{1,0:T(8,128)S(1)}, f32[256,128]{1,0:T(8,128)}, u32[]{:S(2)}) copy-start(f32[256,128]{1,0:T(8,128)} %get-tuple-element.113.cos_rows) | copy-start | bytes 393220
  377.9 9.6 %copy-start.8 = (f32[256,128]{1,0:T(8,128)S(1)}, f32[256,128]{1,0:T(8,128)}, u32[]{:S(2)}) copy-start(f32[256,128]{1,0:T(8,128)} %get-tuple-element.114.sin_rows) | copy-start | bytes 393220
  377.9 9.6 %copy-start.10 = (s32[256,8]{0,1:T(8,128)S(1)}, s32[256,8]{0,1:T(8,128)}, u32[]{:S(2)}) copy-start(s32[256,8]{0,1:T(8,128)} %param.20) | copy-start | bytes 24580
  378.0 9.6 %copy-start.12 = (s32[8,256]{1,0:T(8,128)S(1)}, s32[8,256]{1,0:T(8,128)}, u32[]{:S(2)}) copy-start(s32[8,256]{1,0:T(8,128)} %copy-done.11) | copy-start | bytes 24580
  378.0 9.6 %copy-start.14 = (f32[4,512]{1,0:T(4,128)S(1)}, f32[4,512]{1,0:T(4,128)}, u32[]{:S(2)}) copy-start(f32[4,512]{1,0:T(4,128)} %reshape.214.gain2) | copy-start | bytes 24580
  378.0 9.6 %copy-start.15 = (f32[8,256]{1,0:T(8,128)S(1)}, f32[8,256]{1,0:T(8,128)}, u32[]{:S(2)}) copy-start(f32[8,256]{1,0:T(8,128)} %get-tuple-element.98.keep) | copy-start | bytes 24580
  378.0 9.6 %copy-start.16 = (f32[1,128]{1,0:T(1,128)S(1)}, f32[1,128]{1,0:T(1,128)}, u32[]{:S(2)}) copy-start(f32[1,128]{1,0:T(1,128)} %get-tuple-element.115.k_gain) | copy-start | bytes 1540
  378.0 9.6 %copy-start.17 = (f32[1,128]{1,0:T(1,128)S(1)}, f32[1,128]{1,0:T(1,128)}, u32[]{:S(2)}) copy-start(f32[1,128]{1,0:T(1,128)} %get-tuple-element.116.q_gain) | copy-start | bytes 1540
  378.0 9.6 %copy-start.19 = (f32[256,512]{1,0:T(8,128)S(1)}, f32[256,512]{1,0:T(8,128)}, u32[]{:S(2)}) copy-start(f32[256,512]{1,0:T(8,128)} %get-tuple-element.76.q_hbm) | copy-start | bytes 1572868
  378.0 9.6 %copy-start.20 = (f32[256,512]{1,0:T(8,128)S(1)}, f32[256,512]{1,0:T(8,128)}, u32[]{:S(2)}) copy-start(f32[256,512]{1,0:T(8,128)} %get-tuple-element.77.k_hbm) | copy-start | bytes 1572868
  378.0 9.6 %copy-start.21 = (bf16[256,512]{1,0:T(8,128)(2,1)S(1)}, bf16[256,512]{1,0:T(8,128)(2,1)}, u32[]{:S(2)}) copy-start(bf16[256,512]{1,0:T(8,128)(2,1)} %get-tuple-element.73.qh) | copy-start | bytes 786436
  378.0 9.6 %copy-start.22 = (bf16[256,512]{1,0:T(8,128)(2,1)S(1)}, bf16[256,512]{1,0:T(8,128)(2,1)}, u32[]{:S(2)}) copy-start(bf16[256,512]{1,0:T(8,128)(2,1)} %get-tuple-element.74.kh) | copy-start | bytes 786436
  378.1 9.6 %copy-start.23 = (bf16[256,512]{1,0:T(8,128)(2,1)S(1)}, bf16[256,512]{1,0:T(8,128)(2,1)}, u32[]{:S(2)}) copy-start(bf16[256,512]{1,0:T(8,128)(2,1)} %get-tuple-element.75.vh) | copy-start | bytes 786436
  378.1 9.6 %copy-start.24 = (f32[8,256]{1,0:T(8,128)S(1)}, f32[8,256]{1,0:T(8,128)}, u32[]{:S(2)}) copy-start(f32[8,256]{1,0:T(8,128)} %get-tuple-element.69.gates) | copy-start | bytes 24580
  378.1 49.3 %all-to-all-start.4 = ((bf16[32,24,2048]{2,1,0:T(8,128)(2,1)}), bf16[32,24,2048]{2,1,0:T(8,128)(2,1)}, u32[]{:S(2)}, u32[]{:S(2)}) async-start(bf16[32,24,2048]{2,1,0:T(8,128)(2,1)} %bitcast.67), calls=%async_computation.4 | async-start | bytes 6291456 | tf_op jit(solution)/shard_map/all_to_all | solution.py:46
  427.3 102.5 %copy-start.34 = (s32[256]{0:T(256)S(1)}, s32[256]{0:T(256)}, u32[]{:S(2)}) copy-start(s32[256]{0:T(256)} %copy-done.33) | copy-start | bytes 3076
  527.6 9.9 %copy-start.28 = (bf16[128,16,512]{2,1,0:T(8,128)(2,1)S(1)}, bf16[128,16,512]{2,1,0:T(8,128)(2,1)}, u32[]{:S(2)}) copy-start(bf16[128,16,512]{2,1,0:T(8,128)(2,1)} %get-tuple-element.89) | copy-start | bytes 6291460
  532.3 24.0 %all-to-all-start.5 = ((bf16[32,8,1664]{2,1,0:T(8,128)(2,1)}), bf16[32,8,1664]{2,1,0:T(8,128)(2,1)}, u32[]{:S(2)}, u32[]{:S(2)}) async-start(bf16[32,8,1664]{2,1,0:T(8,128)(2,1)} %pad_maximum_fusion), calls=%async_computation.5 | async-start | bytes 1703936 | tf_op jit(solution)/shard_map/all_to_all | solution.py:46
  548.7 9.8 %copy-start.31 = (s32[256]{0:T(256)S(1)}, s32[256]{0:T(256)}, u32[]{:S(2)}) copy-start(s32[256]{0:T(256)} %copy-done.30) | copy-start | bytes 3076
  (18 other events, 70.3 us)

commit v7 on v6

--- a/solution.py
+++ b/solution.py
@@ -530,99 +530,118 @@
     )
 
 
-def weights_kernel(w, first, second, out, local_sem, near_sem, send_sem, recv_sem, pass_send, pass_recv):
+def weights_kernel(
+    w, first, out, near, own, load_sem, near_sem, send_sem, recv_sem, pass_send, pass_recv
+):
     base, core, rank = octet()
     ready = meet(octet_others(base, core, rank))
     ranks = out.shape[0]
     half = out.shape[2] // 2
     sibling = {"expert": base + 1 - core, "tensor": rank}
-
-    def part(ref, index, side):
-        return ref.at[index, :, pl.ds(side * half, half), :]
-
-    offsets = (3 - 2 * core, 1 + 2 * core)
-    kept = []
-    for n, source in enumerate((first, second)):
-        place = part(out, (rank + offsets[n]) % ranks, core)
-        kept.append(pltpu.make_async_copy(source, place, near_sem.at[n]))
-        kept[-1].start()
-    ready()
     side = rank % 2
     target = 2 * core + side
+    own_chip = target == rank
+
+    def part(ref, index, which):
+        return ref.at[index, :, pl.ds(which * half, half), :]
+
+    mine = 1 - (rank // 2 + core) % 2
+    loads = fetch([(first, near)], load_sem)
+    own_loads, own_stores = [], []
+    for k in range(2):
+        own_loads.append(pltpu.make_async_copy(part(w, side, k), own.at[k], load_sem.at[2 + k]))
+        own_stores.append(pltpu.make_async_copy(own.at[k], part(out, rank, k), near_sem.at[2 + k]))
+        pl.when(own_chip)(own_loads[k].start)
+    ready()
     sends = []
     for k in range(2):
-        here = (target == rank) & (core == k)
-        source, place = part(w, side, k), part(out, rank, k)
-        local = pltpu.make_async_copy(source, place, local_sem)
-        away = remote(
-            source, place, send_sem.at[k], recv_sem.at[rank], {"expert": base + k, "tensor": target}
+        device = {"expert": base + mine * (1 - core) + (1 - mine) * k, "tensor": target}
+        arrives = recv_sem.at[1 - mine, mine * k]
+        sends.append(remote(part(w, side, k), part(out, rank, k), send_sem.at[k], arrives, device))
+        sends[k].start()
+    other = 1 - side
+    beside = 2 * core + other
+    to_core = 1 - ((beside - rank) % ranks - 1) // 2
+    sends.append(
+        remote(
+            part(w, other, to_core), part(out, rank, to_core), send_sem.at[2], recv_sem.at[1, 1],
+            {"expert": base + to_core, "tensor": beside},
         )
-        pl.when(here)(local.start)
-        pl.when(jnp.logical_not(here))(away.start)
-        sends.append((here, away))
-    passed = []
-    for n, source in enumerate((first, second)):
-        d = offsets[n]
-        place = part(out, (rank + d) % ranks, core)
-        passed.append(remote(source, place, pass_send.at[d], pass_recv.at[d], sibling))
-        passed[-1].start()
-    for d in (0, 2):
-        quarter = (rank + d) % ranks
-        mine = part(out, quarter, core)
-        arrival = remote(mine, mine, send_sem.at[0], recv_sem.at[quarter], sibling)
-        here = (rank // 2 == core) & (d == 0)
-        pl.when(here)(pltpu.make_async_copy(part(w, 0, 0), mine, local_sem).wait)
-        pl.when(jnp.logical_not(here))(arrival.wait_recv)
-        passed.append(remote(mine, mine, pass_send.at[d], pass_recv.at[d], sibling))
-        passed[-1].start()
-    for copy in passed:
-        copy.wait_send()
-    for d in range(ranks):
+    )
+    sends[2].start()
+    come, coming = 3 - 2 * core, 1 + 2 * core
+    place = part(out, (rank + come) % ranks, core)
+    loads[0].wait()
+    passed = [remote(near, place, pass_send.at[come], pass_recv.at[come], sibling)]
+    passed[0].start()
+    stores = [pltpu.make_async_copy(near, place, near_sem.at[0])]
+    stores[0].start()
+
+    @pl.when(own_chip)
+    def _():
+        for k in range(2):
+            own_loads[k].wait()
+            own_stores[k].start()
+
+    place = part(out, (rank + coming) % ranks, core)
+    remote(place, place, send_sem.at[2], recv_sem.at[1, 1], sibling).wait_recv()
+    passed.append(remote(place, place, pass_send.at[coming], pass_recv.at[coming], sibling))
+    passed[-1].start()
+    far = part(out, (rank + 2) % ranks, core)
+    remote(far, far, send_sem.at[0], recv_sem.at[1, 0], sibling).wait_recv()
+    passed.append(remote(far, far, pass_send.at[2], pass_recv.at[2], sibling))
+    passed[-1].start()
+    for k in range(2):
+        theirs = part(out, rank, k)
+        arrival = remote(theirs, theirs, send_sem.at[k], recv_sem.at[0, k], sibling)
+        pl.when(jnp.logical_not(own_chip))(arrival.wait_recv)
+        pl.when(own_chip)(own_stores[k].wait)
+    for d in range(1, ranks):
         theirs = part(out, (rank + d) % ranks, 1 - core)
         remote(theirs, theirs, pass_send.at[d], pass_recv.at[d], sibling).wait_recv()
-    for here, away in sends:
-        pl.when(jnp.logical_not(here))(away.wait_send)
-    for copy in kept:
+    for copy in passed + sends:
+        copy.wait_send()
+    for copy in stores:
         copy.wait()
 
 
-def weights_call(w, first, second):
+def weights_call(w, first):
     _, three, width, hidden = w.shape
     hbm = pl.BlockSpec(memory_space=pl.ANY)
-    pairs, sems = pltpu.SemaphoreType.DMA((2,)), pltpu.SemaphoreType.DMA((4,))
+    sems = pltpu.SemaphoreType.DMA((4,))
+    halves = pltpu.VMEM((2, three, width // 2, hidden), BF)
     return pl.pallas_call(
         weights_kernel,
         out_shape=jax.ShapeDtypeStruct((4, three, width, hidden), BF),
-        in_specs=[hbm] * 3,
+        in_specs=[hbm] * 2,
         out_specs=hbm,
-        scratch_shapes=[pltpu.SemaphoreType.DMA, pairs, pairs, sems, sems, sems],
+        scratch_shapes=[
+            pltpu.VMEM((three, width // 2, hidden), BF), halves, sems, sems,
+            pltpu.SemaphoreType.DMA((3,)),
+            pltpu.SemaphoreType.DMA((2, 2)), sems, sems,
+        ],
         compiler_params=pltpu.CompilerParams(
             collective_id=4, has_side_effects=True, vmem_limit_bytes=60 * 1024 * 1024
         ),
         cost_estimate=SHADOW,
         name="weights",
-    )(w, first, second)
+    )(w, first)
 
 
 def near_weights(w):
-    ranks = lax.axis_size("tensor")
-    places = lax.axis_size("expert")
+    ranks, places = lax.axis_size("tensor"), lax.axis_size("expert")
     half = w.shape[2] // 2
     core, rank = lax.axis_index("expert") % 2, lax.axis_index("tensor")
     side = 1 - rank % 2
     leftward = jnp.where(2 * core + side == (rank + 1) % ranks, 0, 1)
-    come = []
-    for turn_over in range(2):
-        pairs = []
-        for place in range(places):
-            for t in range(ranks):
-                target = 2 * (place % 2) + 1 - t % 2
-                to_core = (0 if target == (t + 1) % ranks else 1) ^ turn_over
-                pairs.append((place * ranks + t, (place - place % 2 + to_core) * ranks + target))
-        to_core = jnp.where(turn_over == 0, leftward, 1 - leftward)
-        piece = lax.dynamic_slice(w, (side, 0, to_core * half, 0), (1,) + w.shape[1:2] + (half,) + w.shape[3:])
-        come.append(lax.ppermute(piece[0], ("expert", "tensor"), pairs))
-    return come
+    piece = lax.dynamic_slice(w, (side, 0, leftward * half, 0), (1, w.shape[1], half, w.shape[3]))
+    pairs = []
+    for place in range(places):
+        for t in range(ranks):
+            target = 2 * (place % 2) + 1 - t % 2
+            to_core = 0 if target == (t + 1) % ranks else 1
+            pairs.append((place * ranks + t, (place - place % 2 + to_core) * ranks + target))
+    return lax.ppermute(piece[0], ("expert", "tensor"), pairs)
 
 
 def home_kernel(grads, out, far_out, own, got, load_sem, local_sem, swap_send, swap_recv, send_sem, recv_sem):
@@ -1119,7 +1138,7 @@
     )
     send_rows, w_stored, recv_dy = lax.optimization_barrier((send_rows, w_stored, recv_dy))
     recv_rows = homeward(send_rows)
-    y_rows, d_rows, partial = expert_call(recv_rows, recv_dy, weights_call(w_stored, *w_near))
+    y_rows, d_rows, partial = expert_call(recv_rows, recv_dy, weights_call(w_stored, w_near))
     ret_rows = homeward(d_rows)
     near, far = home_call(partial)
     ret_rows, near, far, y_rows = lax.optimization_barrier((ret_rows, near, far, y_rows))

time: 568 us -> 459 us (0.81)
  Pallas kernels: 449 us -> 340 us
    pallas_call x1, Pallas kernels: 150 us -> 62 us  [weights_call(): pl.pallas_call(weights_kernel, out_shape=jax.ShapeDtypeStruct((4, three,...]
    pallas_call x1, Pallas kernels: 41.7 us -> 25.6 us  [pre_call(): pl.pallas_call(pre_kernel, out_shape=(shape(tiles, BF), shape(tiles, BF),...]
  transfers between devices with their start and end apart: 8 -> 7, of which waited for: 2 -> 2; matrix products, arithmetic and copies ran while one was open for 6% -> 7% of each run, Pallas kernels for 55% -> 44%
where the time goes in v7:
time: 459 us; the launch traced here: 451 us
  Pallas kernels  340 us (74%)
  starting transfers between devices  50.4 us (11%)
  other arithmetic  32.6 us (7%)
  local copies, waits for them, and re-layouts  17.9 us (4%)
  waiting for transfers between devices  4.72 us (1%)
    pallas_call x1, Pallas kernels, reduce_call(): pl.pallas_call(reduce_kernel, out_shape=(shape(wide[:2] + (col,), BF), sh...  97.2 us
    pallas_call x1, Pallas kernels, weights_call(): pl.pallas_call(weights_kernel, out_shape=jax.ShapeDtypeStruct((4, three,...  62 us
    all_to_all x6, starting transfers between devices, exchange(): return lax.all_to_all(value, axis, split_axis=0, concat_axis=0, tiled=True)  47.9 us
    pallas_call x1, Pallas kernels, home_call(): pl.pallas_call(home_kernel, out_shape=(shape((2, three, width, hidden), B...  42.6 us
    pallas_call x1, Pallas kernels, expert_call(): pl.pallas_call(expert_kernel, grid=(quarters,), out_shape=tuple(outs) + (...  42.1 us
    pallas_call x1, Pallas kernels, front_call(): pl.pallas_call(front_kernel, out_shape=(shape(tiles, F32), shape(tiles, B...  38.2 us
    pallas_call x1, Pallas kernels, back_call(): pl.pallas_call(back_kernel, out_shape=(shape((tok, 3 * col), BF), shape(t...  32.3 us
    pallas_call x1, Pallas kernels, pre_call(): pl.pallas_call(pre_kernel, out_shape=(shape(tiles, BF), shape(tiles, BF),...  25.6 us
  transfers between devices with their start and end apart: 7, of which 2 were waited for; matrix products, arithmetic and copies ran while one was open for 7% of the time, Pallas kernels for 44%

profile of v7, /device:TPU:1, one launch (start us, length us, event | category | flops | bytes accessed | tf_op | source)
XLA Modules:
  0.0 451.5 jit_solution(17122763545974226831)
XLA Ops:
  3.3 1.2 concatenate.15
  4.6 1.2 fusion
  5.8 9.6 %all-to-all-start = ((bf16[32,8,1152]{2,1,0:T(8,128)(2,1)}), bf16[32,8,1152]{2,1,0:T(8,128)(2,1)S(1)}, u32[]{:S(2)}, u32[]{:S(2)}) async-start(bf16[32,8,1152]{2,1,0:T(8,128)(2,1)} %fusion), calls=%async_computation | async-start | bytes 1179648 | tf_op jit(solution)/shard_map/all_to_all | solution.py:46
  15.4 2.7 dynamic-slice_bitcast_fusion
  18.1 2.5 collective-permute-start
  23.5 3.4 convert_reduce_fusion
  32.1 1.0 copy.42.router_t
  33.1 25.6 %pre.1 = (bf16[4,256,512]{2,1,0:T(8,128)(2,1)S(1)}, bf16[4,256,512]{2,1,0:T(8,128)(2,1)S(1)}, bf16[768,2048]{1,0:T(8,128)(2,1)}) custom-call(bf16[256,1024]{1,0:T(8,128)(2,1)S(1)} %convolution_convert_fusion.3.local, s32[8,256]{1,0:T(8,128)S(1)} %fusion.17.slot_of), custom_call_target="tpu_custom_call" | custom-call | flops 1 | bytes 1 | tf_op jit(solution)/shard_map/pre/pallas_call | solution.py:216
  59.7 1.0 copy-done.18
  60.7 8.2 %all-to-all-start.1 = ((bf16[32,24,2048]{2,1,0:T(8,128)(2,1)}), bf16[32,24,2048]{2,1,0:T(8,128)(2,1)}, u32[]{:S(2)}, u32[]{:S(2)}) async-start(bf16[32,24,2048]{2,1,0:T(8,128)(2,1)} %bitcast.12), calls=%async_computation.1 | async-start | bytes 6291456 | tf_op jit(solution)/shard_map/all_to_all | solution.py:46
  68.8 38.2 %front.1 = (f32[4,256,512]{2,1,0:T(8,128)}, bf16[4,256,512]{2,1,0:T(8,128)(2,1)}, f32[256,512]{1,0:T(8,128)}, f32[256,512]{1,0:T(8,128)}, bf16[256,512]{1,0:T(8,...) custom-call(bf16[4,256,512]{2,1,0:T(8,128)(2,1)} %copy-done, ...), custom_call_target="tpu_custom_call" | custom-call | flops 40000000000 | bytes 1 | tf_op jit(solution)/shard_map/front/pallas_call | solution.py:335
  107.1 1.4 all-to-all-done.1
  108.5 7.9 %all-to-all-start.2 = ((bf16[32,24,2176]{2,1,0:T(8,128)(2,1)}), bf16[32,24,2176]{2,1,0:T(8,128)(2,1)}, u32[]{:S(2)}, u32[]{:S(2)}) async-start(bf16[32,24,2176]{2,1,0:T(8,128)(2,1)} %bitcast.61), calls=%async_computation.2 | async-start | bytes 6684672 | tf_op jit(solution)/shard_map/all_to_all | solution.py:46
  116.4 62.0 %weights.1.w_ref = bf16[4,3,2048,256]{3,2,1,0:T(8,128)(2,1)} custom-call(bf16[2,3,2048,256]{3,2,1,0:T(8,128)(2,1)} %bitcast.67, bf16[3,1024,256]{2,1,0:T(8,128)(2,1)} %collective-permute-done.first), custom_call_target="tpu_custom_call" | custom-call | flops 40000000000 | bytes 1 | tf_op jit(solution)/shard_map/weights/pallas_call | solution.py:613
  178.4 42.1 %expert.1 = (bf16[768,2048]{1,0:T(8,128)(2,1)}, bf16[768,2176]{1,0:T(8,128)(2,1)}, bf16[4,3,2048,256]{3,2,1,0:T(8,128)(2,1)}) custom-call(bf16[768,2176]{1,0:T(8,128)(2,1)} %bitcast.15.rows_ref, bf16[768,2048]{1,0:T(8,128)(2,1)} %bitcast.13.dys, bf16[4,3,2048,256]{3,2,1,0:T(8,128)(2,1)} %weights.1.w_ref), custom_call_target="tpu_custom_call" | custom-call | flops 1 | bytes 1 | tf_op jit(solution)/shard_map/expert/pallas_call | solution.py:792
  220.5 7.6 %all-to-all-start.3 = ((bf16[32,24,2176]{2,1,0:T(8,128)(2,1)}), bf16[32,24,2176]{2,1,0:T(8,128)(2,1)}, u32[]{:S(2)}, u32[]{:S(2)}) async-start(bf16[32,24,2176]{2,1,0:T(8,128)(2,1)} %bitcast.62), calls=%async_computation.3 | async-start | bytes 6684672 | tf_op jit(solution)/shard_map/all_to_all | solution.py:46
  228.2 42.6 %home.1 = (bf16[2,3,2048,256]{3,2,1,0:T(8,128)(2,1)}, bf16[3,1024,256]{2,1,0:T(8,128)(2,1)}) custom-call(bf16[4,3,2048,256]{3,2,1,0:T(8,128)(2,1)} %get-tuple-element.64.grads), custom_call_target="tpu_custom_call" | custom-call | flops 40000000000 | bytes 1 | tf_op jit(solution)/shard_map/home/pallas_call | solution.py:723
  270.9 8.8 %all-to-all-start.4 = ((bf16[32,24,2048]{2,1,0:T(8,128)(2,1)}), bf16[32,24,2048]{2,1,0:T(8,128)(2,1)}, u32[]{:S(2)}, u32[]{:S(2)}) async-start(bf16[32,24,2048]{2,1,0:T(8,128)(2,1)} %bitcast.63), calls=%async_computation.4 | async-start | bytes 6291456 | tf_op jit(solution)/shard_map/all_to_all | solution.py:46
  279.9 32.3 %back.1 = (bf16[256,1536]{1,0:T(8,128)(2,1)S(1)}, bf16[4,256,512]{2,1,0:T(8,128)(2,1)S(1)}, f32[256,512]{1,0:T(8,128)S(1)}, bf16[2048,128]{1,0:T(8,128)(2,1)S(1)}, f32[8,512]{1,0:T(8,128)S(1)}) custom-call(bf16[256,768]{1,0:T(8,128)(2,1)S(1)} %copy-done.5, bf16[768,2176]{1,0:T(8,128)(2,1)} %bitcast.19.ret, s32[8,256]{1,0:T(8,128)S(1)} %copy-done.12, ...), custom_call_target="tpu_custom_call" | custom-call | flops 20000000000 | bytes 1 | tf_op jit(solution)/shard_map/back/pallas_call | solution.py:478
  316.2 3.3 all-to-all-done.4
  319.5 97.2 %reduce.7 = (bf16[128,16,512]{2,1,0:T(8,128)(2,1)}, bf16[128,16,512]{2,1,0:T(8,128)(2,1)}, bf16[128,16,512]{2,1,0:T(8,128)(2,1)}, bf16[128,16,128]{2,1,0:T(8,128...) custom-call(bf16[256,1536]{1,0:T(8,128)(2,1)} %copy-done.2, ...), custom_call_target="tpu_custom_call" | custom-call | flops 1 | bytes 1 | tf_op jit(solution)/shard_map/reduce/pallas_call | solution.py:1020
  417.7 1.2 copy.44
  419.8 1.4 fusion.1
  421.2 1.0 pad_maximum_fusion
  422.2 5.8 %all-to-all-start.5 = ((bf16[32,8,1664]{2,1,0:T(8,128)(2,1)}), bf16[32,8,1664]{2,1,0:T(8,128)(2,1)}, u32[]{:S(2)}, u32[]{:S(2)}) async-start(bf16[32,8,1664]{2,1,0:T(8,128)(2,1)} %pad_maximum_fusion), calls=%async_computation.5 | async-start | bytes 1703936 | tf_op jit(solution)/shard_map/all_to_all | solution.py:46
  428.1 2.7 bitcast_convert_fusion.2
  430.8 2.9 bitcast_convert_fusion.1
  433.7 2.9 bitcast_convert_fusion
  436.7 2.5 convert_element_type.122
  439.2 7.6 %convert_bitcast_fusion = f32[2,2048,3,256]{3,1,2,0:T(8,128)} fusion(bf16[2,3,2048,256]{3,2,1,0:T(8,128)(2,1)S(1)} %bitcast.60, pred[2]{0:T(512)(128)(4,1)S(1)} %iota_compare_fusion.8, bf16[3,2048,256]{2,1,0:T(8,128)(2,1)} %get-tuple-element.94), kind=kLoop, calls=%fused_computation.1 | loop fusion | flops 6291456 | bytes 22020098 | tf_op jit(solution)/shard_map/transpose | solution.py:1167
  446.8 1.0 convert_reduce_fusion.1
  449.0 1.4 convolution_convert_fusion.1
  (134 shorter events, 19.7 us)
Async XLA Ops:
  3.3 17.3 %copy-start.9 = (s32[256,8]{0,1:T(8,128)S(1)}, s32[256,8]{0,1:T(8,128)}, u32[]{:S(2)}) copy-start(s32[256,8]{0,1:T(8,128)} %param.20) | copy-start | bytes 24580
  3.3 17.3 %copy-start.37 = (s32[1,3]{1,0:T(1,128)S(1)}, s32[1,3]{1,0:T(1,128)}, u32[]{:S(2)}) copy-start(s32[1,3]{1,0:T(1,128)} %param.18) | copy-start | bytes 40
  3.3 17.6 %copy-start.35 = (bf16[2048]{0:T(1024)(128)(2,1)S(1)}, bf16[2048]{0:T(1024)(128)(2,1)}, u32[]{:S(2)}) copy-start(bf16[2048]{0:T(1024)(128)(2,1)} %param.22) | copy-start | bytes 12292
  3.3 18.2 %copy-start.36 = (bf16[2048]{0:T(1024)(128)(2,1)S(1)}, bf16[2048]{0:T(1024)(128)(2,1)}, u32[]{:S(2)}) copy-start(bf16[2048]{0:T(1024)(128)(2,1)} %param.29) | copy-start | bytes 12292
  3.3 19.3 %copy-start.32 = (s32[1,2048]{1,0:T(1,128)S(1)}, s32[1,2048]{1,0:T(1,128)}, u32[]{:S(2)}) copy-start(s32[1,2048]{1,0:T(1,128)} %param.21) | copy-start | bytes 24580
  4.6 22.3 %copy-start.29 = (bf16[2048,64]{0,1:T(8,128)(2,1)S(1)}, bf16[2048,64]{0,1:T(8,128)(2,1)}, u32[]{:S(2)}) copy-start(bf16[2048,64]{0,1:T(8,128)(2,1)} %param.30) | copy-start | bytes 786436
  4.6 22.6 %copy-start.38 = (bf16[128]{0:T(256)(128)(2,1)S(1)}, bf16[128]{0:T(256)(128)(2,1)}, u32[]{:S(2)}) copy-start(bf16[128]{0:T(256)(128)(2,1)} %param.27) | copy-start | bytes 772
  4.6 22.6 %copy-start.39 = (bf16[128]{0:T(256)(128)(2,1)S(1)}, bf16[128]{0:T(256)(128)(2,1)}, u32[]{:S(2)}) copy-start(bf16[128]{0:T(256)(128)(2,1)} %param.26) | copy-start | bytes 772
  5.8 24.3 %all-to-all-start = ((bf16[32,8,1152]{2,1,0:T(8,128)(2,1)}), bf16[32,8,1152]{2,1,0:T(8,128)(2,1)S(1)}, u32[]{:S(2)}, u32[]{:S(2)}) async-start(bf16[32,8,1152]{2,1,0:T(8,128)(2,1)} %fusion), calls=%async_computation | async-start | bytes 1179648 | tf_op jit(solution)/shard_map/all_to_all | solution.py:46
  18.1 98.3 %collective-permute-start = (bf16[3,1024,256]{2,1,0:T(8,128)(2,1)}, bf16[3,1024,256]{2,1,0:T(8,128)(2,1)}, u32[]{:S(2)}, u32[]{:S(2)}) collective-permute-start(bf16[3,1024,256]{2,1,0:T(8,128)(2,1)} %dynamic-slice_bitcast_fusion), channel_id=1, source_target_pairs={{0,1},{1,4},{2,5},{3,0},{4,7},{5,2},{6,3},{7,6},{8,9},{9,12},{10,1... | collective-permute-start | bytes 4718600 | tf_op jit(solution)/shard_map/ppermute | solution.py:644
  31.1 29.6 %copy-start.11 = (s32[8,256]{1,0:T(8,128)}, s32[8,256]{1,0:T(8,128)S(1)}, u32[]{:S(2)}) copy-start(s32[8,256]{1,0:T(8,128)S(1)} %fusion.17.slot_of) | copy-start | bytes 24580
  31.8 28.9 %copy-start.33 = (s32[256]{0:T(256)}, s32[256]{0:T(256)S(1)}, u32[]{:S(2)}) copy-start(s32[256]{0:T(256)S(1)} %reshape.209) | copy-start | bytes 3076
  60.7 47.8 %all-to-all-start.1 = ((bf16[32,24,2048]{2,1,0:T(8,128)(2,1)}), bf16[32,24,2048]{2,1,0:T(8,128)(2,1)}, u32[]{:S(2)}, u32[]{:S(2)}) async-start(bf16[32,24,2048]{2,1,0:T(8,128)(2,1)} %bitcast.12), calls=%async_computation.1 | async-start | bytes 6291456 | tf_op jit(solution)/shard_map/all_to_all | solution.py:46
  108.5 69.9 %all-to-all-start.2 = ((bf16[32,24,2176]{2,1,0:T(8,128)(2,1)}), bf16[32,24,2176]{2,1,0:T(8,128)(2,1)}, u32[]{:S(2)}, u32[]{:S(2)}) async-start(bf16[32,24,2176]{2,1,0:T(8,128)(2,1)} %bitcast.61), calls=%async_computation.2 | async-start | bytes 6684672 | tf_op jit(solution)/shard_map/all_to_all | solution.py:46
  220.5 50.4 %all-to-all-start.3 = ((bf16[32,24,2176]{2,1,0:T(8,128)(2,1)}), bf16[32,24,2176]{2,1,0:T(8,128)(2,1)}, u32[]{:S(2)}, u32[]{:S(2)}) async-start(bf16[32,24,2176]{2,1,0:T(8,128)(2,1)} %bitcast.62), calls=%async_computation.3 | async-start | bytes 6684672 | tf_op jit(solution)/shard_map/all_to_all | solution.py:46
  270.7 9.0 %copy-start.5 = (bf16[256,768]{1,0:T(8,128)(2,1)S(1)}, bf16[256,768]{1,0:T(8,128)(2,1)}, u32[]{:S(2)}) copy-start(bf16[256,768]{1,0:T(8,128)(2,1)} %get-tuple-element.57.pick_t.pick_y) | copy-start | bytes 1179652
  270.7 9.0 %copy-start.6 = (f32[256,256]{1,0:T(8,128)S(1)}, f32[256,256]{1,0:T(8,128)}, u32[]{:S(2)}) copy-start(f32[256,256]{1,0:T(8,128)} %compare_select_fusion.bias) | copy-start | bytes 786436
  270.8 9.0 %copy-start.7 = (f32[256,128]{1,0:T(8,128)S(1)}, f32[256,128]{1,0:T(8,128)}, u32[]{:S(2)}) copy-start(f32[256,128]{1,0:T(8,128)} %get-tuple-element.111.cos_rows) | copy-start | bytes 393220
  270.8 9.0 %copy-start.8 = (f32[256,128]{1,0:T(8,128)S(1)}, f32[256,128]{1,0:T(8,128)}, u32[]{:S(2)}) copy-start(f32[256,128]{1,0:T(8,128)} %get-tuple-element.112.sin_rows) | copy-start | bytes 393220
  270.8 9.0 %copy-start.10 = (s32[256,8]{0,1:T(8,128)S(1)}, s32[256,8]{0,1:T(8,128)}, u32[]{:S(2)}) copy-start(s32[256,8]{0,1:T(8,128)} %param.20) | copy-start | bytes 24580
  270.8 9.0 %copy-start.12 = (s32[8,256]{1,0:T(8,128)S(1)}, s32[8,256]{1,0:T(8,128)}, u32[]{:S(2)}) copy-start(s32[8,256]{1,0:T(8,128)} %copy-done.11) | copy-start | bytes 24580
  270.8 9.0 %copy-start.14 = (f32[4,512]{1,0:T(4,128)S(1)}, f32[4,512]{1,0:T(4,128)}, u32[]{:S(2)}) copy-start(f32[4,512]{1,0:T(4,128)} %reshape.214.gain2) | copy-start | bytes 24580
  270.8 9.0 %copy-start.15 = (f32[8,256]{1,0:T(8,128)S(1)}, f32[8,256]{1,0:T(8,128)}, u32[]{:S(2)}) copy-start(f32[8,256]{1,0:T(8,128)} %get-tuple-element.98.keep) | copy-start | bytes 24580
  270.8 9.0 %copy-start.16 = (f32[1,128]{1,0:T(1,128)S(1)}, f32[1,128]{1,0:T(1,128)}, u32[]{:S(2)}) copy-start(f32[1,128]{1,0:T(1,128)} %get-tuple-element.113.k_gain) | copy-start | bytes 1540
  270.8 9.0 %copy-start.17 = (f32[1,128]{1,0:T(1,128)S(1)}, f32[1,128]{1,0:T(1,128)}, u32[]{:S(2)}) copy-start(f32[1,128]{1,0:T(1,128)} %get-tuple-element.114.q_gain) | copy-start | bytes 1540
  270.8 9.0 %copy-start.19 = (f32[256,512]{1,0:T(8,128)S(1)}, f32[256,512]{1,0:T(8,128)}, u32[]{:S(2)}) copy-start(f32[256,512]{1,0:T(8,128)} %get-tuple-element.76.q_hbm) | copy-start | bytes 1572868
  270.9 9.0 %copy-start.20 = (f32[256,512]{1,0:T(8,128)S(1)}, f32[256,512]{1,0:T(8,128)}, u32[]{:S(2)}) copy-start(f32[256,512]{1,0:T(8,128)} %get-tuple-element.77.k_hbm) | copy-start | bytes 1572868
  270.9 48.6 %all-to-all-start.4 = ((bf16[32,24,2048]{2,1,0:T(8,128)(2,1)}), bf16[32,24,2048]{2,1,0:T(8,128)(2,1)}, u32[]{:S(2)}, u32[]{:S(2)}) async-start(bf16[32,24,2048]{2,1,0:T(8,128)(2,1)} %bitcast.63), calls=%async_computation.4 | async-start | bytes 6291456 | tf_op jit(solution)/shard_map/all_to_all | solution.py:46
  319.5 100.3 %copy-start.34 = (s32[256]{0:T(256)S(1)}, s32[256]{0:T(256)}, u32[]{:S(2)}) copy-start(s32[256]{0:T(256)} %copy-done.33) | copy-start | bytes 3076
  416.7 11.4 %copy-start.28 = (bf16[128,16,512]{2,1,0:T(8,128)(2,1)S(1)}, bf16[128,16,512]{2,1,0:T(8,128)(2,1)}, u32[]{:S(2)}) copy-start(bf16[128,16,512]{2,1,0:T(8,128)(2,1)} %get-tuple-element.89) | copy-start | bytes 6291460
  422.2 24.6 %all-to-all-start.5 = ((bf16[32,8,1664]{2,1,0:T(8,128)(2,1)}), bf16[32,8,1664]{2,1,0:T(8,128)(2,1)}, u32[]{:S(2)}, u32[]{:S(2)}) async-start(bf16[32,8,1664]{2,1,0:T(8,128)(2,1)} %pad_maximum_fusion), calls=%async_computation.5 | async-start | bytes 1703936 | tf_op jit(solution)/shard_map/all_to_all | solution.py:46
  439.2 9.8 %copy-start.31 = (s32[256]{0:T(256)S(1)}, s32[256]{0:T(256)}, u32[]{:S(2)}) copy-start(s32[256]{0:T(256)} %copy-done.30) | copy-start | bytes 3076
  (17 other events, 67.9 us)

commit v8 on v7

--- a/solution.py
+++ b/solution.py
@@ -531,7 +531,7 @@
 
 
 def weights_kernel(
-    w, first, out, near, own, load_sem, near_sem, send_sem, recv_sem, pass_send, pass_recv
+    w, first, second, out, near, own, load_sem, near_sem, send_sem, recv_sem, pass_send, pass_recv
 ):
     base, core, rank = octet()
     ready = meet(octet_others(base, core, rank))
@@ -546,7 +546,7 @@
         return ref.at[index, :, pl.ds(which * half, half), :]
 
     mine = 1 - (rank // 2 + core) % 2
-    loads = fetch([(first, near)], load_sem)
+    loads = fetch([(first, near.at[0]), (second, near.at[1])], load_sem)
     own_loads, own_stores = [], []
     for k in range(2):
         own_loads.append(pltpu.make_async_copy(part(w, side, k), own.at[k], load_sem.at[2 + k]))
@@ -559,23 +559,16 @@
         arrives = recv_sem.at[1 - mine, mine * k]
         sends.append(remote(part(w, side, k), part(out, rank, k), send_sem.at[k], arrives, device))
         sends[k].start()
-    other = 1 - side
-    beside = 2 * core + other
-    to_core = 1 - ((beside - rank) % ranks - 1) // 2
-    sends.append(
-        remote(
-            part(w, other, to_core), part(out, rank, to_core), send_sem.at[2], recv_sem.at[1, 1],
-            {"expert": base + to_core, "tensor": beside},
-        )
-    )
-    sends[2].start()
-    come, coming = 3 - 2 * core, 1 + 2 * core
-    place = part(out, (rank + come) % ranks, core)
-    loads[0].wait()
-    passed = [remote(near, place, pass_send.at[come], pass_recv.at[come], sibling)]
-    passed[0].start()
-    stores = [pltpu.make_async_copy(near, place, near_sem.at[0])]
-    stores[0].start()
+    offsets = (3 - 2 * core, 1 + 2 * core)
+    stores, passed = [], []
+    for n in range(2):
+        d = offsets[n]
+        place = part(out, (rank + d) % ranks, core)
+        loads[n].wait()
+        passed.append(remote(near.at[n], place, pass_send.at[d], pass_recv.at[d], sibling))
+        passed[-1].start()
+        stores.append(pltpu.make_async_copy(near.at[n], place, near_sem.at[n]))
+        stores[-1].start()
 
     @pl.when(own_chip)
     def _():
@@ -583,10 +576,6 @@
             own_loads[k].wait()
             own_stores[k].start()
 
-    place = part(out, (rank + coming) % ranks, core)
-    remote(place, place, send_sem.at[2], recv_sem.at[1, 1], sibling).wait_recv()
-    passed.append(remote(place, place, pass_send.at[coming], pass_recv.at[coming], sibling))
-    passed[-1].start()
     far = part(out, (rank + 2) % ranks, core)
     remote(far, far, send_sem.at[0], recv_sem.at[1, 0], sibling).wait_recv()
     passed.append(remote(far, far, pass_send.at[2], pass_recv.at[2], sibling))
@@ -605,7 +594,7 @@
         copy.wait()
 
 
-def weights_call(w, first):
+def weights_call(w, first, second):
     _, three, width, hidden = w.shape
     hbm = pl.BlockSpec(memory_space=pl.ANY)
     sems = pltpu.SemaphoreType.DMA((4,))
@@ -613,11 +602,10 @@
     return pl.pallas_call(
         weights_kernel,
         out_shape=jax.ShapeDtypeStruct((4, three, width, hidden), BF),
-        in_specs=[hbm] * 2,
+        in_specs=[hbm] * 3,
         out_specs=hbm,
         scratch_shapes=[
-            pltpu.VMEM((three, width // 2, hidden), BF), halves, sems, sems,
-            pltpu.SemaphoreType.DMA((3,)),
+            halves, halves, sems, sems, pltpu.SemaphoreType.DMA((2,)),
             pltpu.SemaphoreType.DMA((2, 2)), sems, sems,
         ],
         compiler_params=pltpu.CompilerParams(
@@ -625,22 +613,22 @@
         ),
         cost_estimate=SHADOW,
         name="weights",
-    )(w, first)
-
-
-def near_weights(w):
+    )(w, first, second)
+
+
+def near_weights(w, turn_over):
     ranks, places = lax.axis_size("tensor"), lax.axis_size("expert")
     half = w.shape[2] // 2
     core, rank = lax.axis_index("expert") % 2, lax.axis_index("tensor")
     side = 1 - rank % 2
-    leftward = jnp.where(2 * core + side == (rank + 1) % ranks, 0, 1)
-    piece = lax.dynamic_slice(w, (side, 0, leftward * half, 0), (1, w.shape[1], half, w.shape[3]))
+    to_core = jnp.where(2 * core + side == (rank + 1) % ranks, turn_over, 1 - turn_over)
+    piece = lax.dynamic_slice(w, (side, 0, to_core * half, 0), (1, w.shape[1], half, w.shape[3]))
     pairs = []
     for place in range(places):
         for t in range(ranks):
             target = 2 * (place % 2) + 1 - t % 2
-            to_core = 0 if target == (t + 1) % ranks else 1
-            pairs.append((place * ranks + t, (place - place % 2 + to_core) * ranks + target))
+            core_of = (0 if target == (t + 1) % ranks else 1) ^ turn_over
+            pairs.append((place * ranks + t, (place - place % 2 + core_of) * ranks + target))
     return lax.ppermute(piece[0], ("expert", "tensor"), pairs)
 
 
@@ -946,11 +934,13 @@
     first, size = first + size, size // 2
     halve(3)
     first, size = first + size, size // 2
+    shared = [[] for _ in range(4)]
     for s in range(4):
         copies[s].wait_recv()
         add(got, place[s], 31 * s + first, 1)
         here = got.at[pl.ds(place[s], 1)]
         copies[s] = post.push(here, here, dims[ORDERS[s][3]][1])
+        shared[s].append(post.push(here, here, dims[0][1]))
 
     arrive(note_in)
     facts = note[0, 8:16, :]
@@ -984,17 +974,19 @@
         for s in range(4):
             copies[s].wait_recv()
             bit, _ = dims[ORDERS[s][k]]
+            come = got.at[pl.ds(place[s] + (1 - 2 * bit) * size, size)]
             place[s] = place[s] - bit * size
-            partner = dims[ORDERS[s][k - 1]][1] if k else dims[0][1]
-            here = got.at[pl.ds(place[s], 2 * size)]
-            copies[s] = post.push(here, here, partner)
+            if k:
+                here = got.at[pl.ds(place[s], 2 * size)]
+                copies[s] = post.push(here, here, dims[ORDERS[s][k - 1]][1])
+            shared[s].append(post.push(come, come, dims[0][1]))
             if not k:
                 keep(s, place[s])
         size *= 2
         if k == 2:
             out_out[...] = (resid[...] + scatter_total(y_parts, y_box, me, y_moved)).astype(BF)
     for s in range(4):
-        copies[s].wait_recv()
+        arrive(shared[s])
         keep(4 + s, (1 - core) * 64 + s * 16)
     post.finish()
     post_x.finish()
@@ -1035,7 +1027,7 @@
             pltpu.VMEM(wide, BF), pltpu.VMEM((124,) + wide[1:], BF), pltpu.VMEM(wide, BF),
             pltpu.SemaphoreType.DMA((4,)), pltpu.SemaphoreType.DMA((8, 5)),
             pltpu.SemaphoreType.DMA((count,)), pltpu.SemaphoreType.DMA((count,)),
-            pltpu.SemaphoreType.DMA((40,)), pltpu.SemaphoreType.DMA((40,)),
+            pltpu.SemaphoreType.DMA((56,)), pltpu.SemaphoreType.DMA((56,)),
             pltpu.SemaphoreType.DMA((3,)), pltpu.SemaphoreType.DMA((3, 2)),
         ],
         compiler_params=pltpu.CompilerParams(
@@ -1076,7 +1068,7 @@
     local_experts = expert_w.shape[0]
 
     w_stored = jnp.transpose(expert_w, (0, 2, 1, 3))
-    w_near = near_weights(w_stored)
+    w_first = near_weights(w_stored, 0)
 
     routes_t = routes.T
     order_t = pair_order[0].reshape(tok_count, top_count).T
@@ -1128,7 +1120,8 @@
         return exchange(value.reshape(groups, -1, value.shape[1]), "expert").reshape(value.shape)
 
     x_all, dy_all, send_dy = pre_call(local, slot_of, tensor_count, slots)
-    send_dy, x_all = lax.optimization_barrier((send_dy, x_all))
+    send_dy, x_all, w_stored = lax.optimization_barrier((send_dy, x_all, w_stored))
+    w_second = near_weights(w_stored, 1)
     recv_dy = homeward(send_dy)
     (
         resid, mixed, q_raw, k_raw, qh, kh, vh, attended, gates, send_rows, pick_t,
@@ -1138,7 +1131,7 @@
     )
     send_rows, w_stored, recv_dy = lax.optimization_barrier((send_rows, w_stored, recv_dy))
     recv_rows = homeward(send_rows)
-    y_rows, d_rows, partial = expert_call(recv_rows, recv_dy, weights_call(w_stored, w_near))
+    y_rows, d_rows, partial = expert_call(recv_rows, recv_dy, weights_call(w_stored, w_first, w_second))
     ret_rows = homeward(d_rows)
     near, far = home_call(partial)
     ret_rows, near, far, y_rows = lax.optimization_barrier((ret_rows, near, far, y_rows))

time: 459 us -> 452 us (0.985)
  Pallas kernels: 340 us -> 334 us
    pallas_call x1, Pallas kernels: 62 us -> 42.5 us  [weights_call(): pl.pallas_call(weights_kernel, out_shape=jax.ShapeDtypeStruct((4, three,...]
    pallas_call x1, Pallas kernels: 38.2 us -> 47.7 us  [front_call(): pl.pallas_call(front_kernel, out_shape=(shape(tiles, F32), shape(tiles, B...]
  transfers between devices with their start and end apart: 7 -> 8, of which waited for: 2 -> 1; matrix products, arithmetic and copies ran while one was open for 7% -> 8% of each run, Pallas kernels for 44% -> 43%
where the time goes in v8:
time: 452 us; the launch traced here: 445 us
  Pallas kernels  334 us (74%)
  starting transfers between devices  50.5 us (11%)
  other arithmetic  32.6 us (7%)
  local copies, waits for them, and re-layouts  20.6 us (5%)
    pallas_call x1, Pallas kernels, reduce_call(): pl.pallas_call(reduce_kernel, out_shape=(shape(wide[:2] + (col,), BF), sh...  98.8 us
    pallas_call x1, Pallas kernels, front_call(): pl.pallas_call(front_kernel, out_shape=(shape(tiles, F32), shape(tiles, B...  47.7 us
    all_to_all x6, starting transfers between devices, exchange(): return lax.all_to_all(value, axis, split_axis=0, concat_axis=0, tiled=True)  46.3 us
    pallas_call x1, Pallas kernels, home_call(): pl.pallas_call(home_kernel, out_shape=(shape((2, three, width, hidden), B...  42.9 us
    pallas_call x1, Pallas kernels, weights_call(): pl.pallas_call(weights_kernel, out_shape=jax.ShapeDtypeStruct((4, three,...  42.5 us
    pallas_call x1, Pallas kernels, expert_call(): pl.pallas_call(expert_kernel, grid=(quarters,), out_shape=tuple(outs) + (...  42.1 us
    pallas_call x1, Pallas kernels, back_call(): pl.pallas_call(back_kernel, out_shape=(shape((tok, 3 * col), BF), shape(t...  34.4 us
    pallas_call x1, Pallas kernels, pre_call(): pl.pallas_call(pre_kernel, out_shape=(shape(tiles, BF), shape(tiles, BF),...  25.6 us
  transfers between devices with their start and end apart: 8, of which 1 were waited for; matrix products, arithmetic and copies ran while one was open for 8% of the time, Pallas kernels for 43%

profile of v8, /device:TPU:1, one launch (start us, length us, event | category | flops | bytes accessed | tf_op | source)
XLA Modules:
  0.0 444.8 jit_solution(10394093577948060575)
XLA Ops:
  3.3 1.2 concatenate.15
  4.6 1.2 fusion
  5.7 9.6 %all-to-all-start = ((bf16[32,8,1152]{2,1,0:T(8,128)(2,1)}), bf16[32,8,1152]{2,1,0:T(8,128)(2,1)S(1)}, u32[]{:S(2)}, u32[]{:S(2)}) async-start(bf16[32,8,1152]{2,1,0:T(8,128)(2,1)} %fusion), calls=%async_computation | async-start | bytes 1179648 | tf_op jit(solution)/shard_map/all_to_all | solution.py:46
  15.4 2.7 dynamic-slice_bitcast_fusion.1
  18.1 2.5 collective-permute-start
  23.5 3.4 convert_reduce_fusion
  27.3 1.0 copy.42.router_t
  33.1 25.6 %pre.1 = (bf16[4,256,512]{2,1,0:T(8,128)(2,1)S(1)}, bf16[4,256,512]{2,1,0:T(8,128)(2,1)S(1)}, bf16[768,2048]{1,0:T(8,128)(2,1)}) custom-call(bf16[256,1024]{1,0:T(8,128)(2,1)S(1)} %convolution_convert_fusion.3.local, s32[8,256]{1,0:T(8,128)S(1)} %fusion.17.slot_of), custom_call_target="tpu_custom_call" | custom-call | flops 1 | bytes 1 | tf_op jit(solution)/shard_map/pre/pallas_call | solution.py:216
  60.7 7.7 %all-to-all-start.1 = ((bf16[32,24,2048]{2,1,0:T(8,128)(2,1)}), bf16[32,24,2048]{2,1,0:T(8,128)(2,1)}, u32[]{:S(2)}, u32[]{:S(2)}) async-start(bf16[32,24,2048]{2,1,0:T(8,128)(2,1)} %bitcast.12), calls=%async_computation.1 | async-start | bytes 6291456 | tf_op jit(solution)/shard_map/all_to_all | solution.py:46
  68.3 2.7 dynamic-slice_bitcast_fusion
  71.0 1.7 collective-permute-start.1
  72.7 47.7 %front.1 = (f32[4,256,512]{2,1,0:T(8,128)}, bf16[4,256,512]{2,1,0:T(8,128)(2,1)}, f32[256,512]{1,0:T(8,128)}, f32[256,512]{1,0:T(8,128)}, bf16[256,512]{1,0:T(8,...) custom-call(bf16[4,256,512]{2,1,0:T(8,128)(2,1)} %copy-done, ...), custom_call_target="tpu_custom_call" | custom-call | flops 40000000000 | bytes 1 | tf_op jit(solution)/shard_map/front/pallas_call | solution.py:335
  120.4 8.5 %all-to-all-start.2 = ((bf16[32,24,2176]{2,1,0:T(8,128)(2,1)}), bf16[32,24,2176]{2,1,0:T(8,128)(2,1)}, u32[]{:S(2)}, u32[]{:S(2)}) async-start(bf16[32,24,2176]{2,1,0:T(8,128)(2,1)} %bitcast.63), calls=%async_computation.2 | async-start | bytes 6684672 | tf_op jit(solution)/shard_map/all_to_all | solution.py:46
  128.9 42.5 %weights.1.w_ref = bf16[4,3,2048,256]{3,2,1,0:T(8,128)(2,1)} custom-call(bf16[2,3,2048,256]{3,2,1,0:T(8,128)(2,1)} %bitcast.68, bf16[3,1024,256]{2,1,0:T(8,128)(2,1)} %collective-permute-done.first, bf16[3,1024,256]{2,1,0:T(8,128)(2,1)} %collective-permute-done.1.second), custom_call_target="tpu_custom_call" | custom-call | flops 40000000000 | bytes 1 | tf_op jit(solution)/shard_map/weights/pallas_call | solution.py:602
  171.5 42.1 %expert.1 = (bf16[768,2048]{1,0:T(8,128)(2,1)}, bf16[768,2176]{1,0:T(8,128)(2,1)}, bf16[4,3,2048,256]{3,2,1,0:T(8,128)(2,1)}) custom-call(bf16[768,2176]{1,0:T(8,128)(2,1)} %bitcast.15.rows_ref, bf16[768,2048]{1,0:T(8,128)(2,1)} %bitcast.13.dys, bf16[4,3,2048,256]{3,2,1,0:T(8,128)(2,1)} %weights.1.w_ref), custom_call_target="tpu_custom_call" | custom-call | flops 1 | bytes 1 | tf_op jit(solution)/shard_map/expert/pallas_call | solution.py:780
  213.6 7.4 %all-to-all-start.3 = ((bf16[32,24,2176]{2,1,0:T(8,128)(2,1)}), bf16[32,24,2176]{2,1,0:T(8,128)(2,1)}, u32[]{:S(2)}, u32[]{:S(2)}) async-start(bf16[32,24,2176]{2,1,0:T(8,128)(2,1)} %bitcast.64), calls=%async_computation.3 | async-start | bytes 6684672 | tf_op jit(solution)/shard_map/all_to_all | solution.py:46
  221.0 42.9 %home.1 = (bf16[2,3,2048,256]{3,2,1,0:T(8,128)(2,1)}, bf16[3,1024,256]{2,1,0:T(8,128)(2,1)}) custom-call(bf16[4,3,2048,256]{3,2,1,0:T(8,128)(2,1)} %get-tuple-element.66.grads), custom_call_target="tpu_custom_call" | custom-call | flops 40000000000 | bytes 1 | tf_op jit(solution)/shard_map/home/pallas_call | solution.py:711
  264.1 8.7 %all-to-all-start.4 = ((bf16[32,24,2048]{2,1,0:T(8,128)(2,1)}), bf16[32,24,2048]{2,1,0:T(8,128)(2,1)}, u32[]{:S(2)}, u32[]{:S(2)}) async-start(bf16[32,24,2048]{2,1,0:T(8,128)(2,1)} %bitcast.65), calls=%async_computation.4 | async-start | bytes 6291456 | tf_op jit(solution)/shard_map/all_to_all | solution.py:46
  273.0 34.4 %back.1 = (bf16[256,1536]{1,0:T(8,128)(2,1)S(1)}, bf16[4,256,512]{2,1,0:T(8,128)(2,1)S(1)}, f32[256,512]{1,0:T(8,128)S(1)}, bf16[2048,128]{1,0:T(8,128)(2,1)S(1)}, f32[8,512]{1,0:T(8,128)S(1)}) custom-call(bf16[256,768]{1,0:T(8,128)(2,1)S(1)} %copy-done.5, bf16[768,2176]{1,0:T(8,128)(2,1)} %bitcast.20.ret, s32[8,256]{1,0:T(8,128)S(1)} %copy-done.12, ...), custom_call_target="tpu_custom_call" | custom-call | flops 20000000000 | bytes 1 | tf_op jit(solution)/shard_map/back/pallas_call | solution.py:478
  311.4 1.2 all-to-all-done.4
  312.6 98.8 %reduce.7 = (bf16[128,16,512]{2,1,0:T(8,128)(2,1)}, bf16[128,16,512]{2,1,0:T(8,128)(2,1)}, bf16[128,16,512]{2,1,0:T(8,128)(2,1)}, bf16[128,16,128]{2,1,0:T(8,128...) custom-call(bf16[256,1536]{1,0:T(8,128)(2,1)} %copy-done.2, ...), custom_call_target="tpu_custom_call" | custom-call | flops 1 | bytes 1 | tf_op jit(solution)/shard_map/reduce/pallas_call | solution.py:1012
  412.3 1.4 copy.44
  414.5 1.4 fusion.1
  415.9 1.0 pad_maximum_fusion
  416.9 4.4 all-to-all-start.5
  421.4 2.7 bitcast_convert_fusion.2
  424.1 2.9 bitcast_convert_fusion.1
  427.0 2.9 bitcast_convert_fusion
  430.0 2.5 convert_element_type.122
  432.5 7.6 %convert_bitcast_fusion = f32[2,2048,3,256]{3,1,2,0:T(8,128)} fusion(bf16[2,3,2048,256]{3,2,1,0:T(8,128)(2,1)S(1)} %bitcast.62, pred[2]{0:T(512)(128)(4,1)S(1)} %iota_compare_fusion.8, bf16[3,2048,256]{2,1,0:T(8,128)(2,1)} %get-tuple-element.96), kind=kLoop, calls=%fused_computation.1 | loop fusion | flops 6291456 | bytes 22020098 | tf_op jit(solution)/shard_map/transpose | solution.py:1160
  440.1 1.0 convert_reduce_fusion.1
  442.3 1.4 convolution_convert_fusion.1
  (137 shorter events, 20.5 us)
Async XLA Ops:
  3.3 17.3 %copy-start.9 = (s32[256,8]{0,1:T(8,128)S(1)}, s32[256,8]{0,1:T(8,128)}, u32[]{:S(2)}) copy-start(s32[256,8]{0,1:T(8,128)} %param.20) | copy-start | bytes 24580
  3.3 17.3 %copy-start.37 = (s32[1,3]{1,0:T(1,128)S(1)}, s32[1,3]{1,0:T(1,128)}, u32[]{:S(2)}) copy-start(s32[1,3]{1,0:T(1,128)} %param.18) | copy-start | bytes 40
  3.3 17.6 %copy-start.35 = (bf16[2048]{0:T(1024)(128)(2,1)S(1)}, bf16[2048]{0:T(1024)(128)(2,1)}, u32[]{:S(2)}) copy-start(bf16[2048]{0:T(1024)(128)(2,1)} %param.22) | copy-start | bytes 12292
  3.3 18.2 %copy-start.36 = (bf16[2048]{0:T(1024)(128)(2,1)S(1)}, bf16[2048]{0:T(1024)(128)(2,1)}, u32[]{:S(2)}) copy-start(bf16[2048]{0:T(1024)(128)(2,1)} %param.29) | copy-start | bytes 12292
  4.5 18.1 %copy-start.32 = (s32[1,2048]{1,0:T(1,128)S(1)}, s32[1,2048]{1,0:T(1,128)}, u32[]{:S(2)}) copy-start(s32[1,2048]{1,0:T(1,128)} %param.21) | copy-start | bytes 24580
  4.6 22.3 %copy-start.29 = (bf16[2048,64]{0,1:T(8,128)(2,1)S(1)}, bf16[2048,64]{0,1:T(8,128)(2,1)}, u32[]{:S(2)}) copy-start(bf16[2048,64]{0,1:T(8,128)(2,1)} %param.30) | copy-start | bytes 786436
  5.7 25.3 %all-to-all-start = ((bf16[32,8,1152]{2,1,0:T(8,128)(2,1)}), bf16[32,8,1152]{2,1,0:T(8,128)(2,1)S(1)}, u32[]{:S(2)}, u32[]{:S(2)}) async-start(bf16[32,8,1152]{2,1,0:T(8,128)(2,1)} %fusion), calls=%async_computation | async-start | bytes 1179648 | tf_op jit(solution)/shard_map/all_to_all | solution.py:46
  18.1 11.7 %copy-start.38 = (bf16[128]{0:T(256)(128)(2,1)S(1)}, bf16[128]{0:T(256)(128)(2,1)}, u32[]{:S(2)}) copy-start(bf16[128]{0:T(256)(128)(2,1)} %param.27) | copy-start | bytes 772
  18.1 11.7 %copy-start.39 = (bf16[128]{0:T(256)(128)(2,1)S(1)}, bf16[128]{0:T(256)(128)(2,1)}, u32[]{:S(2)}) copy-start(bf16[128]{0:T(256)(128)(2,1)} %param.26) | copy-start | bytes 772
  18.1 110.9 %collective-permute-start = (bf16[3,1024,256]{2,1,0:T(8,128)(2,1)}, bf16[3,1024,256]{2,1,0:T(8,128)(2,1)}, u32[]{:S(2)}, u32[]{:S(2)}) collective-permute-start(bf16[3,1024,256]{2,1,0:T(8,128)(2,1)} %dynamic-slice_bitcast_fusion.1), channel_id=1, source_target_pairs={{0,1},{1,4},{2,5},{3,0},{4,7},{5,2},{6,3},{7,6},{8,9},{9,12},{10,1... | collective-permute-start | bytes 4718600 | tf_op jit(solution)/shard_map/ppermute | solution.py:632
  32.1 28.6 %copy-start.11 = (s32[8,256]{1,0:T(8,128)}, s32[8,256]{1,0:T(8,128)S(1)}, u32[]{:S(2)}) copy-start(s32[8,256]{1,0:T(8,128)S(1)} %fusion.17.slot_of) | copy-start | bytes 24580
  32.8 27.9 %copy-start.33 = (s32[256]{0:T(256)}, s32[256]{0:T(256)S(1)}, u32[]{:S(2)}) copy-start(s32[256]{0:T(256)S(1)} %reshape.209) | copy-start | bytes 3076
  60.7 59.8 %all-to-all-start.1 = ((bf16[32,24,2048]{2,1,0:T(8,128)(2,1)}), bf16[32,24,2048]{2,1,0:T(8,128)(2,1)}, u32[]{:S(2)}, u32[]{:S(2)}) async-start(bf16[32,24,2048]{2,1,0:T(8,128)(2,1)} %bitcast.12), calls=%async_computation.1 | async-start | bytes 6291456 | tf_op jit(solution)/shard_map/all_to_all | solution.py:46
  71.0 57.9 %collective-permute-start.1 = (bf16[3,1024,256]{2,1,0:T(8,128)(2,1)}, bf16[3,1024,256]{2,1,0:T(8,128)(2,1)}, u32[]{:S(2)}, u32[]{:S(2)}) collective-permute-start(bf16[3,1024,256]{2,1,0:T(8,128)(2,1)} %dynamic-slice_bitcast_fusion), channel_id=1, source_target_pairs={{0,5},{1,0},{2,1},{3,4},{4,3},{5,6},{6,7},{7,2},{8,13},{9,8},{10,9... | collective-permute-start | bytes 4718600 | tf_op jit(solution)/shard_map/ppermute | solution.py:632
  120.4 51.1 %all-to-all-start.2 = ((bf16[32,24,2176]{2,1,0:T(8,128)(2,1)}), bf16[32,24,2176]{2,1,0:T(8,128)(2,1)}, u32[]{:S(2)}, u32[]{:S(2)}) async-start(bf16[32,24,2176]{2,1,0:T(8,128)(2,1)} %bitcast.63), calls=%async_computation.2 | async-start | bytes 6684672 | tf_op jit(solution)/shard_map/all_to_all | solution.py:46
  213.6 50.3 %all-to-all-start.3 = ((bf16[32,24,2176]{2,1,0:T(8,128)(2,1)}), bf16[32,24,2176]{2,1,0:T(8,128)(2,1)}, u32[]{:S(2)}, u32[]{:S(2)}) async-start(bf16[32,24,2176]{2,1,0:T(8,128)(2,1)} %bitcast.64), calls=%async_computation.3 | async-start | bytes 6684672 | tf_op jit(solution)/shard_map/all_to_all | solution.py:46
  263.9 8.9 %copy-start.5 = (bf16[256,768]{1,0:T(8,128)(2,1)S(1)}, bf16[256,768]{1,0:T(8,128)(2,1)}, u32[]{:S(2)}) copy-start(bf16[256,768]{1,0:T(8,128)(2,1)} %get-tuple-element.58.pick_t.pick_y) | copy-start | bytes 1179652
  263.9 8.9 %copy-start.6 = (f32[256,256]{1,0:T(8,128)S(1)}, f32[256,256]{1,0:T(8,128)}, u32[]{:S(2)}) copy-start(f32[256,256]{1,0:T(8,128)} %compare_select_fusion.bias) | copy-start | bytes 786436
  263.9 8.9 %copy-start.7 = (f32[256,128]{1,0:T(8,128)S(1)}, f32[256,128]{1,0:T(8,128)}, u32[]{:S(2)}) copy-start(f32[256,128]{1,0:T(8,128)} %get-tuple-element.113.cos_rows) | copy-start | bytes 393220
  264.0 8.9 %copy-start.8 = (f32[256,128]{1,0:T(8,128)S(1)}, f32[256,128]{1,0:T(8,128)}, u32[]{:S(2)}) copy-start(f32[256,128]{1,0:T(8,128)} %get-tuple-element.114.sin_rows) | copy-start | bytes 393220
  264.0 8.9 %copy-start.10 = (s32[256,8]{0,1:T(8,128)S(1)}, s32[256,8]{0,1:T(8,128)}, u32[]{:S(2)}) copy-start(s32[256,8]{0,1:T(8,128)} %param.20) | copy-start | bytes 24580
  264.0 8.9 %copy-start.12 = (s32[8,256]{1,0:T(8,128)S(1)}, s32[8,256]{1,0:T(8,128)}, u32[]{:S(2)}) copy-start(s32[8,256]{1,0:T(8,128)} %copy-done.11) | copy-start | bytes 24580
  264.0 8.9 %copy-start.14 = (f32[4,512]{1,0:T(4,128)S(1)}, f32[4,512]{1,0:T(4,128)}, u32[]{:S(2)}) copy-start(f32[4,512]{1,0:T(4,128)} %reshape.214.gain2) | copy-start | bytes 24580
  264.0 8.9 %copy-start.15 = (f32[8,256]{1,0:T(8,128)S(1)}, f32[8,256]{1,0:T(8,128)}, u32[]{:S(2)}) copy-start(f32[8,256]{1,0:T(8,128)} %get-tuple-element.100.keep) | copy-start | bytes 24580
  264.0 8.9 %copy-start.16 = (f32[1,128]{1,0:T(1,128)S(1)}, f32[1,128]{1,0:T(1,128)}, u32[]{:S(2)}) copy-start(f32[1,128]{1,0:T(1,128)} %get-tuple-element.115.k_gain) | copy-start | bytes 1540
  264.0 8.9 %copy-start.17 = (f32[1,128]{1,0:T(1,128)S(1)}, f32[1,128]{1,0:T(1,128)}, u32[]{:S(2)}) copy-start(f32[1,128]{1,0:T(1,128)} %get-tuple-element.116.q_gain) | copy-start | bytes 1540
  264.0 8.9 %copy-start.19 = (f32[256,512]{1,0:T(8,128)S(1)}, f32[256,512]{1,0:T(8,128)}, u32[]{:S(2)}) copy-start(f32[256,512]{1,0:T(8,128)} %get-tuple-element.78.q_hbm) | copy-start | bytes 1572868
  264.1 48.5 %all-to-all-start.4 = ((bf16[32,24,2048]{2,1,0:T(8,128)(2,1)}), bf16[32,24,2048]{2,1,0:T(8,128)(2,1)}, u32[]{:S(2)}, u32[]{:S(2)}) async-start(bf16[32,24,2048]{2,1,0:T(8,128)(2,1)} %bitcast.65), calls=%async_computation.4 | async-start | bytes 6291456 | tf_op jit(solution)/shard_map/all_to_all | solution.py:46
  312.6 101.9 %copy-start.34 = (s32[256]{0:T(256)S(1)}, s32[256]{0:T(256)}, u32[]{:S(2)}) copy-start(s32[256]{0:T(256)} %copy-done.33) | copy-start | bytes 3076
  412.3 9.1 %copy-start.28 = (bf16[128,16,512]{2,1,0:T(8,128)(2,1)S(1)}, bf16[128,16,512]{2,1,0:T(8,128)(2,1)}, u32[]{:S(2)}) copy-start(bf16[128,16,512]{2,1,0:T(8,128)(2,1)} %get-tuple-element.91) | copy-start | bytes 6291460
  416.9 23.2 %all-to-all-start.5 = ((bf16[32,8,1664]{2,1,0:T(8,128)(2,1)}), bf16[32,8,1664]{2,1,0:T(8,128)(2,1)}, u32[]{:S(2)}, u32[]{:S(2)}) async-start(bf16[32,8,1664]{2,1,0:T(8,128)(2,1)} %pad_maximum_fusion), calls=%async_computation.5 | async-start | bytes 1703936 | tf_op jit(solution)/shard_map/all_to_all | solution.py:46
  432.5 9.8 %copy-start.31 = (s32[256]{0:T(256)S(1)}, s32[256]{0:T(256)}, u32[]{:S(2)}) copy-start(s32[256]{0:T(256)} %copy-done.30) | copy-start | bytes 3076
  (18 other events, 76.6 us)

commit v9 on v8

--- a/solution.py
+++ b/solution.py
@@ -223,7 +223,7 @@
             pltpu.SemaphoreType.DMA((8,)), pltpu.SemaphoreType.DMA((8,)),
         ],
         compiler_params=pltpu.CompilerParams(
-            collective_id=6, has_side_effects=True, vmem_limit_bytes=48 * 1024 * 1024
+            collective_id=6, has_side_effects=True, vmem_limit_bytes=63 * 1024 * 1024
         ),
         cost_estimate=COST,
         name="pre",
@@ -492,7 +492,7 @@
             pltpu.SemaphoreType.DMA((count,)), pltpu.SemaphoreType.DMA((count,)),
         ],
         compiler_params=pltpu.CompilerParams(
-            collective_id=2, has_side_effects=True, vmem_limit_bytes=48 * 1024 * 1024
+            collective_id=2, has_side_effects=True, vmem_limit_bytes=63 * 1024 * 1024
         ),
         cost_estimate=pl.CostEstimate(
             flops=20_000_000_000, bytes_accessed=1, transcendentals=0
@@ -813,7 +813,7 @@
 def reduce_kernel(
     d_qkv, dr, d_mine, router_part, small_in, x_all, gain1, ob, pick_y, ret_y,
     far_hbm, resid_hbm, wq_hbm, wk_hbm, wv_hbm,
-    q_out, k_out, v_out, router_out, o_out, dx_out, out_out, small_out, far_out,
+    q_out, k_out, v_out, o_out, dx_out, out_out, small_out, far_out,
     wq, wk, wv, resid, parts, y_parts, halves, box_x, note, buf, box, got,
     load_sem, out_sem, x_send, x_recv, send_sem, recv_sem, far_send, far_recv,
 ):
@@ -888,11 +888,9 @@
             + dot(d_qkv[:, 2 * col : 3 * col], wv[rows, :], 1, 1)
         ).astype(BF)
     x_first = scatter_start(post_x, parts, x_halves, me)
-    far_copies[0].start()
     for n in range(2):
         products(2 * core + n)
     x_moved = scatter_relay(post_x, parts, x_halves, x_box, me, x_first)
-    far_copies[1].start()
     place = [core * 64 + s * 16 for s in range(4)]
     size, first = 16, 0
 
@@ -927,12 +925,13 @@
     note_in = [post_x.push(note.at[me], note.at[me], peer) for peer in peers]
 
     halve(1)
+    far_copies[0].start()
     first, size = first + size, size // 2
     y_moved = scatter_relay(post_x, y_parts, y_halves, y_box, me, y_first)
-    far_copies[2].start()
     halve(2)
     first, size = first + size, size // 2
     halve(3)
+    far_copies[1].start()
     first, size = first + size, size // 2
     shared = [[] for _ in range(4)]
     for s in range(4):
@@ -958,17 +957,16 @@
 
     def keep(n, at):
         here = pl.ds(at, 16)
-        outs = (q_out, k_out, v_out, None, router_out)
-        for m, target in enumerate(outs):
-            lanes = pl.ds(m * col, target.shape[2] if m != 3 else col)
-            if m == 3:
-                turned = got[here, :, lanes].reshape(16 * rows_chunk, col).T
-                o_out[:, pl.ds(pl.multiple_of(at * rows_chunk, 128), 16 * rows_chunk)] = turned
-                continue
+        for m, target in enumerate((q_out, k_out, v_out)):
             stores.append(
-                pltpu.make_async_copy(got.at[here, :, lanes], target.at[here], out_sem.at[n, m])
+                pltpu.make_async_copy(
+                    got.at[here, :, pl.ds(m * col, col)], target.at[here], out_sem.at[n, m]
+                )
             )
             stores[-1].start()
+        count = 16 * rows_chunk
+        turned = got[here, :, 3 * col :].reshape(count, o_out.shape[0]).T
+        o_out[:, pl.ds(pl.multiple_of(at * rows_chunk, 128), count)] = turned
 
     for k in range(3, -1, -1):
         for s in range(4):
@@ -983,6 +981,8 @@
             if not k:
                 keep(s, place[s])
         size *= 2
+        if k == 3:
+            far_copies[2].start()
         if k == 2:
             out_out[...] = (resid[...] + scatter_total(y_parts, y_box, me, y_moved)).astype(BF)
     for s in range(4):
@@ -1013,19 +1013,19 @@
         reduce_kernel,
         out_shape=(
             shape(wide[:2] + (col,), BF), shape(wide[:2] + (col,), BF), shape(wide[:2] + (col,), BF),
-            shape(wide[:2] + (128,), BF), shape((col, width), BF),
+            shape((col + 128, width), BF),
             shape((tok, col), BF), shape((tok, col), BF), shape((16, col), F32),
             shape((far.shape[0], 2 * far.shape[1], far.shape[2]), BF),
         ),
         in_specs=[vmem] * 10 + [hbm] * 5,
-        out_specs=(hbm,) * 4 + (vmem,) * 4 + (hbm,),
+        out_specs=(hbm,) * 3 + (vmem,) * 4 + (hbm,),
         scratch_shapes=[
             pltpu.VMEM((width, col), BF), pltpu.VMEM((width, col), BF), pltpu.VMEM((width, col), BF),
             pltpu.VMEM((tok, col), F32), pltpu.VMEM(tiles, BF), pltpu.VMEM(tiles, BF),
             pltpu.VMEM((4, tok // 2, col), BF), pltpu.VMEM((4, tok, col), BF),
             pltpu.VMEM((blocks, 16, col), F32),
             pltpu.VMEM(wide, BF), pltpu.VMEM((124,) + wide[1:], BF), pltpu.VMEM(wide, BF),
-            pltpu.SemaphoreType.DMA((4,)), pltpu.SemaphoreType.DMA((8, 5)),
+            pltpu.SemaphoreType.DMA((4,)), pltpu.SemaphoreType.DMA((8, 3)),
             pltpu.SemaphoreType.DMA((count,)), pltpu.SemaphoreType.DMA((count,)),
             pltpu.SemaphoreType.DMA((56,)), pltpu.SemaphoreType.DMA((56,)),
             pltpu.SemaphoreType.DMA((3,)), pltpu.SemaphoreType.DMA((3, 2)),
@@ -1141,7 +1141,7 @@
         sin_rows, gain2, *head_gains, router, resid, dy_all, mixed, qh, kh, vh, q_raw, k_raw,
         w_output,
     )
-    *wide, router_sum, out_proj, dx_slice, out_slice, small, far = reduce_call(
+    *wide, turned, dx_slice, out_slice, small, far = reduce_call(
         d_qkv, dr, d_mine, router_part, small, x_all, gain1, attended, pick_t, ret_y, far, resid,
         weights[:3],
     )
@@ -1170,9 +1170,9 @@
         wide[2].astype(F32),
         small[gain_at : gain_at + head],
         small[gain_at + head : gain_at + 2 * head],
-        out_proj.astype(F32),
+        turned[:col_count].astype(F32),
         small[width : 2 * width],
-        router_sum.reshape(width, -1)[:, :expert_count].astype(F32),
+        turned[col_count : col_count + expert_count].astype(F32).T,
         expert_grad,
     )
 

time: 452 us -> 437 us (0.967)
  Pallas kernels: 334 us -> 316 us
    pallas_call x1, Pallas kernels: 98.8 us -> 81.4 us  [reduce_call(): pl.pallas_call(reduce_kernel, out_shape=(shape(wide[:2] + (col,), BF), sh...]
  transfers between devices with their start and end apart: 8 -> 8, of which waited for: 1 -> 1; matrix products, arithmetic and copies ran while one was open for 8% -> 8% of each run, Pallas kernels for 43% -> 45%
where the time goes in v9:
time: 437 us; the launch traced here: 430 us
  Pallas kernels  316 us (72%)
  starting transfers between devices  52.9 us (12%)
  other arithmetic  35.8 us (8%)
  local copies, waits for them, and re-layouts  16.5 us (4%)
    pallas_call x1, Pallas kernels, reduce_call(): pl.pallas_call(reduce_kernel, out_shape=(shape(wide[:2] + (col,), BF), sh...  81.4 us
    all_to_all x6, starting transfers between devices, exchange(): return lax.all_to_all(value, axis, split_axis=0, concat_axis=0, tiled=True)  48.2 us
    pallas_call x1, Pallas kernels, front_call(): pl.pallas_call(front_kernel, out_shape=(shape(tiles, F32), shape(tiles, B...  46.9 us
    pallas_call x1, Pallas kernels, home_call(): pl.pallas_call(home_kernel, out_shape=(shape((2, three, width, hidden), B...  42.8 us
    pallas_call x1, Pallas kernels, weights_call(): pl.pallas_call(weights_kernel, out_shape=jax.ShapeDtypeStruct((4, three,...  42.5 us
    pallas_call x1, Pallas kernels, expert_call(): pl.pallas_call(expert_kernel, grid=(quarters,), out_shape=tuple(outs) + (...  42.1 us
    pallas_call x1, Pallas kernels, back_call(): pl.pallas_call(back_kernel, out_shape=(shape((tok, 3 * col), BF), shape(t...  36.2 us
    pallas_call x1, Pallas kernels, pre_call(): pl.pallas_call(pre_kernel, out_shape=(shape(tiles, BF), shape(tiles, BF),...  23.8 us
  transfers between devices with their start and end apart: 8, of which 1 were waited for; matrix products, arithmetic and copies ran while one was open for 8% of the time, Pallas kernels for 45%

profile of v9, /device:TPU:1, one launch (start us, length us, event | category | flops | bytes accessed | tf_op | source)
XLA Modules:
  0.0 430.0 jit_solution(2805049803003536243)
XLA Ops:
  3.3 1.2 concatenate.15
  4.6 1.2 fusion
  5.7 9.6 %all-to-all-start = ((bf16[32,8,1152]{2,1,0:T(8,128)(2,1)}), bf16[32,8,1152]{2,1,0:T(8,128)(2,1)S(1)}, u32[]{:S(2)}, u32[]{:S(2)}) async-start(bf16[32,8,1152]{2,1,0:T(8,128)(2,1)} %fusion), calls=%async_computation | async-start | bytes 1179648 | tf_op jit(solution)/shard_map/all_to_all | solution.py:46
  15.4 2.7 dynamic-slice_bitcast_fusion.1
  18.1 2.5 collective-permute-start
  23.5 3.4 convert_reduce_fusion
  34.2 1.1 convolution_convert_fusion.3.local
  35.3 23.8 %pre.1 = (bf16[4,256,512]{2,1,0:T(8,128)(2,1)}, bf16[4,256,512]{2,1,0:T(8,128)(2,1)}, bf16[768,2048]{1,0:T(8,128)(2,1)}) custom-call(bf16[256,1024]{1,0:T(8,128)(2,1)} %convolution_convert_fusion.3.local, s32[8,256]{1,0:T(8,128)} %fusion.17.slot_of), custom_call_target="tpu_custom_call" | custom-call | flops 1 | bytes 1 | tf_op jit(solution)/shard_map/pre/pallas_call | solution.py:216
  59.0 7.7 %all-to-all-start.1 = ((bf16[32,24,2048]{2,1,0:T(8,128)(2,1)}), bf16[32,24,2048]{2,1,0:T(8,128)(2,1)S(1)}, u32[]{:S(2)}, u32[]{:S(2)}) async-start(bf16[32,24,2048]{2,1,0:T(8,128)(2,1)} %bitcast.64), calls=%async_computation.1 | async-start | bytes 6291456 | tf_op jit(solution)/shard_map/all_to_all | solution.py:46
  66.7 2.7 dynamic-slice_bitcast_fusion
  69.4 2.2 collective-permute-start.1
  71.6 46.9 %front.1 = (f32[4,256,512]{2,1,0:T(8,128)}, bf16[4,256,512]{2,1,0:T(8,128)(2,1)}, f32[256,512]{1,0:T(8,128)}, f32[256,512]{1,0:T(8,128)}, bf16[256,512]{1,0:T(8,...) custom-call(bf16[4,256,512]{2,1,0:T(8,128)(2,1)} %get-tuple-element., ...), custom_call_target="tpu_custom_call" | custom-call | flops 40000000000 | bytes 1 | tf_op jit(solution)/shard_map/front/pallas_call | solution.py:335
  118.5 1.7 copy-done
  120.2 8.7 %all-to-all-start.2 = ((bf16[32,24,2176]{2,1,0:T(8,128)(2,1)}), bf16[32,24,2176]{2,1,0:T(8,128)(2,1)}, u32[]{:S(2)}, u32[]{:S(2)}) async-start(bf16[32,24,2176]{2,1,0:T(8,128)(2,1)} %bitcast.61), calls=%async_computation.2 | async-start | bytes 6684672 | tf_op jit(solution)/shard_map/all_to_all | solution.py:46
  128.9 42.5 %weights.1.w_ref = bf16[4,3,2048,256]{3,2,1,0:T(8,128)(2,1)} custom-call(bf16[2,3,2048,256]{3,2,1,0:T(8,128)(2,1)} %bitcast.67, bf16[3,1024,256]{2,1,0:T(8,128)(2,1)} %collective-permute-done.first, bf16[3,1024,256]{2,1,0:T(8,128)(2,1)} %collective-permute-done.1.second), custom_call_target="tpu_custom_call" | custom-call | flops 40000000000 | bytes 1 | tf_op jit(solution)/shard_map/weights/pallas_call | solution.py:602
  171.5 42.1 %expert.1 = (bf16[768,2048]{1,0:T(8,128)(2,1)}, bf16[768,2176]{1,0:T(8,128)(2,1)}, bf16[4,3,2048,256]{3,2,1,0:T(8,128)(2,1)}) custom-call(bf16[768,2176]{1,0:T(8,128)(2,1)} %bitcast.15.rows_ref, bf16[768,2048]{1,0:T(8,128)(2,1)} %bitcast.57, bf16[4,3,2048,256]{3,2,1,0:T(8,128)(2,1)} %weights.1.w_ref), custom_call_target="tpu_custom_call" | custom-call | flops 1 | bytes 1 | tf_op jit(solution)/shard_map/expert/pallas_call | solution.py:780
  213.6 7.4 %all-to-all-start.3 = ((bf16[32,24,2176]{2,1,0:T(8,128)(2,1)}), bf16[32,24,2176]{2,1,0:T(8,128)(2,1)S(1)}, u32[]{:S(2)}, u32[]{:S(2)}) async-start(bf16[32,24,2176]{2,1,0:T(8,128)(2,1)} %bitcast.62), calls=%async_computation.3 | async-start | bytes 6684672 | tf_op jit(solution)/shard_map/all_to_all | solution.py:46
  220.9 42.8 %home.1 = (bf16[2,3,2048,256]{3,2,1,0:T(8,128)(2,1)}, bf16[3,1024,256]{2,1,0:T(8,128)(2,1)}) custom-call(bf16[4,3,2048,256]{3,2,1,0:T(8,128)(2,1)} %get-tuple-element.65.grads), custom_call_target="tpu_custom_call" | custom-call | flops 40000000000 | bytes 1 | tf_op jit(solution)/shard_map/home/pallas_call | solution.py:711
  263.8 1.7 copy-done.1
  265.5 8.7 %all-to-all-start.4 = ((bf16[32,24,2048]{2,1,0:T(8,128)(2,1)}), bf16[32,24,2048]{2,1,0:T(8,128)(2,1)}, u32[]{:S(2)}, u32[]{:S(2)}) async-start(bf16[32,24,2048]{2,1,0:T(8,128)(2,1)} %bitcast.63), calls=%async_computation.4 | async-start | bytes 6291456 | tf_op jit(solution)/shard_map/all_to_all | solution.py:46
  274.2 36.2 %back.1 = (bf16[256,1536]{1,0:T(8,128)(2,1)}, bf16[4,256,512]{2,1,0:T(8,128)(2,1)}, f32[256,512]{1,0:T(8,128)}, bf16[2048,128]{1,0:T(8,128)(2,1)}, f32[8,512]{1,0:T(8,128)}) custom-call(bf16[256,768]{1,0:T(8,128)(2,1)} %get-tuple-element.57.pick_t.pick_y, bf16[768,2176]{1,0:T(8,128)(2,1)} %bitcast.60, s32[8,256]{1,0:T(8,128)} %fusion.17.slot_of, ...), custom_call_target="tpu_custom_call" | custom-call | flops 20000000000 | bytes 1 | tf_op jit(solution)/shard_map/back/pallas_call | solution.py:478
  310.4 3.4 all-to-all-done.4
  313.8 81.4 %reduce.7 = (bf16[128,16,512]{2,1,0:T(8,128)(2,1)}, bf16[128,16,512]{2,1,0:T(8,128)(2,1)}, bf16[128,16,512]{2,1,0:T(8,128)(2,1)}, bf16[640,2048]{1,0:T(8,128)(2,...) custom-call(bf16[256,1536]{1,0:T(8,128)(2,1)} %get-tuple-element.79., ...), custom_call_target="tpu_custom_call" | custom-call | flops 1 | bytes 1 | tf_op jit(solution)/shard_map/reduce/pallas_call | solution.py:1012
  395.2 1.8 convert_bitcast_fusion.1
  397.0 4.2 slice_convert_fusion
  402.7 6.2 %all-to-all-start.5 = ((bf16[32,8,1664]{2,1,0:T(8,128)(2,1)}), bf16[32,8,1664]{2,1,0:T(8,128)(2,1)}, u32[]{:S(2)}, u32[]{:S(2)}) async-start(bf16[32,8,1664]{2,1,0:T(8,128)(2,1)} %pad_maximum_fusion), calls=%async_computation.5 | async-start | bytes 1703936 | tf_op jit(solution)/shard_map/all_to_all | solution.py:46
  409.0 2.9 bitcast_convert_fusion.2
  411.9 2.9 bitcast_convert_fusion.1
  414.8 2.7 bitcast_convert_fusion
  417.5 7.6 %convert_bitcast_fusion = f32[2,2048,3,256]{3,1,2,0:T(8,128)} fusion(bf16[2,3,2048,256]{3,2,1,0:T(8,128)(2,1)S(1)} %bitcast.59, pred[2]{0:T(512)(128)(4,1)S(1)} %iota_compare_fusion.8, bf16[3,2048,256]{2,1,0:T(8,128)(2,1)} %get-tuple-element.94), kind=kLoop, calls=%fused_computation.1 | loop fusion | flops 6291456 | bytes 22020098 | tf_op jit(solution)/shard_map/transpose | solution.py:1160
  425.1 1.0 convert_reduce_fusion.1
  427.3 1.4 convolution_convert_fusion.1
  (96 shorter events, 16.3 us)
Async XLA Ops:
  2.3 15.8 %copy-start.7 = (s32[256]{0:T(256)}, s32[256]{0:T(256)S(1)}, u32[]{:S(2)}) copy-start(s32[256]{0:T(256)S(1)} %convert_reduce_fusion.3) | copy-start | bytes 3076
  3.3 17.3 %copy-start.6 = (s32[256,8]{0,1:T(8,128)S(1)}, s32[256,8]{0,1:T(8,128)}, u32[]{:S(2)}) copy-start(s32[256,8]{0,1:T(8,128)} %param.20) | copy-start | bytes 24580
  3.3 17.3 %copy-start.15 = (s32[1,3]{1,0:T(1,128)S(1)}, s32[1,3]{1,0:T(1,128)}, u32[]{:S(2)}) copy-start(s32[1,3]{1,0:T(1,128)} %param.18) | copy-start | bytes 40
  3.3 17.6 %copy-start.13 = (bf16[2048]{0:T(1024)(128)(2,1)S(1)}, bf16[2048]{0:T(1024)(128)(2,1)}, u32[]{:S(2)}) copy-start(bf16[2048]{0:T(1024)(128)(2,1)} %param.22) | copy-start | bytes 12292
  3.3 18.2 %copy-start.14 = (bf16[2048]{0:T(1024)(128)(2,1)S(1)}, bf16[2048]{0:T(1024)(128)(2,1)}, u32[]{:S(2)}) copy-start(bf16[2048]{0:T(1024)(128)(2,1)} %param.29) | copy-start | bytes 12292
  4.5 18.0 %copy-start.10 = (s32[1,2048]{1,0:T(1,128)S(1)}, s32[1,2048]{1,0:T(1,128)}, u32[]{:S(2)}) copy-start(s32[1,2048]{1,0:T(1,128)} %param.21) | copy-start | bytes 24580
  4.6 22.3 %copy-start.5 = (bf16[2048,64]{0,1:T(8,128)(2,1)S(1)}, bf16[2048,64]{0,1:T(8,128)(2,1)}, u32[]{:S(2)}) copy-start(bf16[2048,64]{0,1:T(8,128)(2,1)} %param.30) | copy-start | bytes 786436
  5.7 26.1 %all-to-all-start = ((bf16[32,8,1152]{2,1,0:T(8,128)(2,1)}), bf16[32,8,1152]{2,1,0:T(8,128)(2,1)S(1)}, u32[]{:S(2)}, u32[]{:S(2)}) async-start(bf16[32,8,1152]{2,1,0:T(8,128)(2,1)} %fusion), calls=%async_computation | async-start | bytes 1179648 | tf_op jit(solution)/shard_map/all_to_all | solution.py:46
  18.1 12.5 %copy-start.16 = (bf16[128]{0:T(256)(128)(2,1)S(1)}, bf16[128]{0:T(256)(128)(2,1)}, u32[]{:S(2)}) copy-start(bf16[128]{0:T(256)(128)(2,1)} %param.27) | copy-start | bytes 772
  18.1 12.5 %copy-start.17 = (bf16[128]{0:T(256)(128)(2,1)S(1)}, bf16[128]{0:T(256)(128)(2,1)}, u32[]{:S(2)}) copy-start(bf16[128]{0:T(256)(128)(2,1)} %param.26) | copy-start | bytes 772
  18.1 110.8 %collective-permute-start = (bf16[3,1024,256]{2,1,0:T(8,128)(2,1)}, bf16[3,1024,256]{2,1,0:T(8,128)(2,1)}, u32[]{:S(2)}, u32[]{:S(2)}) collective-permute-start(bf16[3,1024,256]{2,1,0:T(8,128)(2,1)} %dynamic-slice_bitcast_fusion.1), channel_id=1, source_target_pairs={{0,1},{1,4},{2,5},{3,0},{4,7},{5,2},{6,3},{7,6},{8,9},{9,12},{10,1... | collective-permute-start | bytes 4718600 | tf_op jit(solution)/shard_map/ppermute | solution.py:632
  34.1 1.1 copy-start.11
  59.0 59.5 %all-to-all-start.1 = ((bf16[32,24,2048]{2,1,0:T(8,128)(2,1)}), bf16[32,24,2048]{2,1,0:T(8,128)(2,1)S(1)}, u32[]{:S(2)}, u32[]{:S(2)}) async-start(bf16[32,24,2048]{2,1,0:T(8,128)(2,1)} %bitcast.64), calls=%async_computation.1 | async-start | bytes 6291456 | tf_op jit(solution)/shard_map/all_to_all | solution.py:46
  69.4 59.5 %collective-permute-start.1 = (bf16[3,1024,256]{2,1,0:T(8,128)(2,1)}, bf16[3,1024,256]{2,1,0:T(8,128)(2,1)}, u32[]{:S(2)}, u32[]{:S(2)}) collective-permute-start(bf16[3,1024,256]{2,1,0:T(8,128)(2,1)} %dynamic-slice_bitcast_fusion), channel_id=1, source_target_pairs={{0,5},{1,0},{2,1},{3,4},{4,3},{5,6},{6,7},{7,2},{8,13},{9,8},{10,9... | collective-permute-start | bytes 4718600 | tf_op jit(solution)/shard_map/ppermute | solution.py:632
  118.5 1.7 copy-start
  120.2 51.3 %all-to-all-start.2 = ((bf16[32,24,2176]{2,1,0:T(8,128)(2,1)}), bf16[32,24,2176]{2,1,0:T(8,128)(2,1)}, u32[]{:S(2)}, u32[]{:S(2)}) async-start(bf16[32,24,2176]{2,1,0:T(8,128)(2,1)} %bitcast.61), calls=%async_computation.2 | async-start | bytes 6684672 | tf_op jit(solution)/shard_map/all_to_all | solution.py:46
  213.6 50.2 %all-to-all-start.3 = ((bf16[32,24,2176]{2,1,0:T(8,128)(2,1)}), bf16[32,24,2176]{2,1,0:T(8,128)(2,1)S(1)}, u32[]{:S(2)}, u32[]{:S(2)}) async-start(bf16[32,24,2176]{2,1,0:T(8,128)(2,1)} %bitcast.62), calls=%async_computation.3 | async-start | bytes 6684672 | tf_op jit(solution)/shard_map/all_to_all | solution.py:46
  263.8 1.7 copy-start.1
  265.5 48.3 %all-to-all-start.4 = ((bf16[32,24,2048]{2,1,0:T(8,128)(2,1)}), bf16[32,24,2048]{2,1,0:T(8,128)(2,1)}, u32[]{:S(2)}, u32[]{:S(2)}) async-start(bf16[32,24,2048]{2,1,0:T(8,128)(2,1)} %bitcast.63), calls=%async_computation.4 | async-start | bytes 6291456 | tf_op jit(solution)/shard_map/all_to_all | solution.py:46
  397.0 4.2 copy-start.9
  397.0 4.3 %copy-start.12 = (s32[256]{0:T(256)S(1)}, s32[256]{0:T(256)}, u32[]{:S(2)}) copy-start(s32[256]{0:T(256)} %copy-done.11) | copy-start | bytes 3076
  397.0 4.3 %copy-start.18 = (bf16[256,512]{1,0:T(8,128)(2,1)S(1)}, bf16[256,512]{1,0:T(8,128)(2,1)}, u32[]{:S(2)}) copy-start(bf16[256,512]{1,0:T(8,128)(2,1)} %get-tuple-element.88) | copy-start | bytes 786436
  397.0 4.3 %copy-start.19 = (bf16[256,512]{1,0:T(8,128)(2,1)S(1)}, bf16[256,512]{1,0:T(8,128)(2,1)}, u32[]{:S(2)}) copy-start(bf16[256,512]{1,0:T(8,128)(2,1)} %get-tuple-element.87) | copy-start | bytes 786436
  401.2 7.8 %copy-start.4 = (bf16[128,16,512]{2,1,0:T(8,128)(2,1)S(1)}, bf16[128,16,512]{2,1,0:T(8,128)(2,1)}, u32[]{:S(2)}) copy-start(bf16[128,16,512]{2,1,0:T(8,128)(2,1)} %get-tuple-element.90) | copy-start | bytes 6291460
  402.7 22.4 %all-to-all-start.5 = ((bf16[32,8,1664]{2,1,0:T(8,128)(2,1)}), bf16[32,8,1664]{2,1,0:T(8,128)(2,1)}, u32[]{:S(2)}, u32[]{:S(2)}) async-start(bf16[32,8,1664]{2,1,0:T(8,128)(2,1)} %pad_maximum_fusion), calls=%async_computation.5 | async-start | bytes 1703936 | tf_op jit(solution)/shard_map/all_to_all | solution.py:46
  409.0 2.9 copy-start.3
  409.0 8.5 %slice-start = ((s8[6291456]{0:T(1024)(128)(4,1)}), s8[4194304]{0:T(1024)(128)(4,1)S(1)}, s32[]{:S(2)}) async-start(s8[6291456]{0:T(1024)(128)(4,1)} %bitcast.58), calls=%async_computation.6 | async-start | bytes 8388608
  411.8 2.9 copy-start.2
  411.8 5.7 %slice-start.1 = ((s8[6291456]{0:T(1024)(128)(4,1)}), s8[2097152]{0:T(1024)(128)(4,1)S(1)}, s32[]{:S(2)}) async-start(s8[6291456]{0:T(1024)(128)(4,1)} %bitcast.58), calls=%async_computation.7 | async-start | bytes 4194304
  417.5 9.8 %copy-start.8 = (s32[256]{0:T(256)S(1)}, s32[256]{0:T(256)}, u32[]{:S(2)}) copy-start(s32[256]{0:T(256)} %copy-done.7) | copy-start | bytes 3076

commit v10 on v9

--- a/solution.py
+++ b/solution.py
@@ -351,7 +351,7 @@
             pltpu.SemaphoreType.DMA((8,)), pltpu.SemaphoreType.DMA((8,)),
         ],
         compiler_params=pltpu.CompilerParams(
-            collective_id=1, has_side_effects=True, vmem_limit_bytes=56 * 1024 * 1024
+            collective_id=1, has_side_effects=True, vmem_limit_bytes=63 * 1024 * 1024
         ),
         cost_estimate=SHADOW,
         name="front",
@@ -609,7 +609,7 @@
             pltpu.SemaphoreType.DMA((2, 2)), sems, sems,
         ],
         compiler_params=pltpu.CompilerParams(
-            collective_id=4, has_side_effects=True, vmem_limit_bytes=60 * 1024 * 1024
+            collective_id=4, has_side_effects=True, vmem_limit_bytes=63 * 1024 * 1024
         ),
         cost_estimate=SHADOW,
         name="weights",
@@ -719,7 +719,7 @@
             halves, halves, sems, pltpu.SemaphoreType.DMA, sems, sems, sems, sems,
         ],
         compiler_params=pltpu.CompilerParams(
-            collective_id=5, has_side_effects=True, vmem_limit_bytes=60 * 1024 * 1024
+            collective_id=5, has_side_effects=True, vmem_limit_bytes=63 * 1024 * 1024
         ),
         cost_estimate=SHADOW,
         name="home",
@@ -791,7 +791,7 @@
             pltpu.VMEM((count, 1), F32),
             pltpu.VMEM((count, 1), F32),
         ],
-        compiler_params=pltpu.CompilerParams(vmem_limit_bytes=62 * 1024 * 1024),
+        compiler_params=pltpu.CompilerParams(vmem_limit_bytes=63 * 1024 * 1024),
         cost_estimate=COST,
         name="expert",
     )(rows, dys, weights)
@@ -1031,7 +1031,7 @@
             pltpu.SemaphoreType.DMA((3,)), pltpu.SemaphoreType.DMA((3, 2)),
         ],
         compiler_params=pltpu.CompilerParams(
-            collective_id=3, has_side_effects=True, vmem_limit_bytes=60 * 1024 * 1024
+            collective_id=3, has_side_effects=True, vmem_limit_bytes=63 * 1024 * 1024
         ),
         cost_estimate=COST,
         name="reduce",

time: 437 us -> 434 us (level)
  no operation moved by 1% of the time
where the time goes in v10:
time: 434 us; the launch traced here: 427 us
  Pallas kernels  316 us (73%)
  starting transfers between devices  52.7 us (12%)
  other arithmetic  35.8 us (8%)
  local copies, waits for them, and re-layouts  13.2 us (3%)
    pallas_call x1, Pallas kernels, reduce_call(): pl.pallas_call(reduce_kernel, out_shape=(shape(wide[:2] + (col,), BF), sh...  81.4 us
    all_to_all x6, starting transfers between devices, exchange(): return lax.all_to_all(value, axis, split_axis=0, concat_axis=0, tiled=True)  48 us
    pallas_call x1, Pallas kernels, front_call(): pl.pallas_call(front_kernel, out_shape=(shape(tiles, F32), shape(tiles, B...  47.4 us
    pallas_call x1, Pallas kernels, home_call(): pl.pallas_call(home_kernel, out_shape=(shape((2, three, width, hidden), B...  42.9 us
    pallas_call x1, Pallas kernels, weights_call(): pl.pallas_call(weights_kernel, out_shape=jax.ShapeDtypeStruct((4, three,...  42.5 us
    pallas_call x1, Pallas kernels, expert_call(): pl.pallas_call(expert_kernel, grid=(quarters,), out_shape=tuple(outs) + (...  42.1 us
    pallas_call x1, Pallas kernels, back_call(): pl.pallas_call(back_kernel, out_shape=(shape((tok, 3 * col), BF), shape(t...  36 us
    pallas_call x1, Pallas kernels, pre_call(): pl.pallas_call(pre_kernel, out_shape=(shape(tiles, BF), shape(tiles, BF),...  23.8 us
  transfers between devices with their start and end apart: 8, of which 1 were waited for; matrix products, arithmetic and copies ran while one was open for 8% of the time, Pallas kernels for 45%

profile of v10, /device:TPU:1, one launch (start us, length us, event | category | flops | bytes accessed | tf_op | source)
XLA Modules:
  0.0 427.0 jit_solution(407336727980546806)
XLA Ops:
  3.3 1.2 concatenate.15
  4.6 1.2 fusion
  5.7 9.6 %all-to-all-start = ((bf16[32,8,1152]{2,1,0:T(8,128)(2,1)}), bf16[32,8,1152]{2,1,0:T(8,128)(2,1)S(1)}, u32[]{:S(2)}, u32[]{:S(2)}) async-start(bf16[32,8,1152]{2,1,0:T(8,128)(2,1)} %fusion), calls=%async_computation | async-start | bytes 1179648 | tf_op jit(solution)/shard_map/all_to_all | solution.py:46
  15.4 2.7 dynamic-slice_bitcast_fusion.1
  18.1 2.5 collective-permute-start
  23.5 3.4 convert_reduce_fusion
  28.2 1.0 copy.39.router_t
  34.2 1.1 convolution_convert_fusion.3.local
  35.3 23.8 %pre.1 = (bf16[4,256,512]{2,1,0:T(8,128)(2,1)}, bf16[4,256,512]{2,1,0:T(8,128)(2,1)}, bf16[768,2048]{1,0:T(8,128)(2,1)}) custom-call(bf16[256,1024]{1,0:T(8,128)(2,1)} %convolution_convert_fusion.3.local, s32[8,256]{1,0:T(8,128)} %fusion.17.slot_of), custom_call_target="tpu_custom_call" | custom-call | flops 1 | bytes 1 | tf_op jit(solution)/shard_map/pre/pallas_call | solution.py:216
  59.1 7.7 %all-to-all-start.1 = ((bf16[32,24,2048]{2,1,0:T(8,128)(2,1)}), bf16[32,24,2048]{2,1,0:T(8,128)(2,1)}, u32[]{:S(2)}, u32[]{:S(2)}) async-start(bf16[32,24,2048]{2,1,0:T(8,128)(2,1)} %bitcast.62), calls=%async_computation.1 | async-start | bytes 6291456 | tf_op jit(solution)/shard_map/all_to_all | solution.py:46
  66.8 2.7 dynamic-slice_bitcast_fusion
  69.5 2.2 collective-permute-start.1
  71.7 47.4 %front.1 = (f32[4,256,512]{2,1,0:T(8,128)}, bf16[4,256,512]{2,1,0:T(8,128)(2,1)}, f32[256,512]{1,0:T(8,128)}, f32[256,512]{1,0:T(8,128)}, bf16[256,512]{1,0:T(8,...) custom-call(bf16[4,256,512]{2,1,0:T(8,128)(2,1)} %get-tuple-element., ...), custom_call_target="tpu_custom_call" | custom-call | flops 40000000000 | bytes 1 | tf_op jit(solution)/shard_map/front/pallas_call | solution.py:335
  119.1 8.5 %all-to-all-start.2 = ((bf16[32,24,2176]{2,1,0:T(8,128)(2,1)}), bf16[32,24,2176]{2,1,0:T(8,128)(2,1)}, u32[]{:S(2)}, u32[]{:S(2)}) async-start(bf16[32,24,2176]{2,1,0:T(8,128)(2,1)} %bitcast.59), calls=%async_computation.2 | async-start | bytes 6684672 | tf_op jit(solution)/shard_map/all_to_all | solution.py:46
  127.6 42.5 %weights.1.w_ref = bf16[4,3,2048,256]{3,2,1,0:T(8,128)(2,1)} custom-call(bf16[2,3,2048,256]{3,2,1,0:T(8,128)(2,1)} %bitcast.65, bf16[3,1024,256]{2,1,0:T(8,128)(2,1)} %collective-permute-done.first, bf16[3,1024,256]{2,1,0:T(8,128)(2,1)} %collective-permute-done.1.second), custom_call_target="tpu_custom_call" | custom-call | flops 40000000000 | bytes 1 | tf_op jit(solution)/shard_map/weights/pallas_call | solution.py:602
  170.2 42.1 %expert.1 = (bf16[768,2048]{1,0:T(8,128)(2,1)}, bf16[768,2176]{1,0:T(8,128)(2,1)}, bf16[4,3,2048,256]{3,2,1,0:T(8,128)(2,1)}) custom-call(bf16[768,2176]{1,0:T(8,128)(2,1)} %bitcast.15.rows_ref, bf16[768,2048]{1,0:T(8,128)(2,1)} %bitcast.13.dys, bf16[4,3,2048,256]{3,2,1,0:T(8,128)(2,1)} %weights.1.w_ref), custom_call_target="tpu_custom_call" | custom-call | flops 1 | bytes 1 | tf_op jit(solution)/shard_map/expert/pallas_call | solution.py:780
  212.3 7.4 %all-to-all-start.3 = ((bf16[32,24,2176]{2,1,0:T(8,128)(2,1)}), bf16[32,24,2176]{2,1,0:T(8,128)(2,1)}, u32[]{:S(2)}, u32[]{:S(2)}) async-start(bf16[32,24,2176]{2,1,0:T(8,128)(2,1)} %bitcast.60), calls=%async_computation.3 | async-start | bytes 6684672 | tf_op jit(solution)/shard_map/all_to_all | solution.py:46
  219.7 42.9 %home.1 = (bf16[2,3,2048,256]{3,2,1,0:T(8,128)(2,1)}, bf16[3,1024,256]{2,1,0:T(8,128)(2,1)}) custom-call(bf16[4,3,2048,256]{3,2,1,0:T(8,128)(2,1)} %get-tuple-element.65.grads), custom_call_target="tpu_custom_call" | custom-call | flops 40000000000 | bytes 1 | tf_op jit(solution)/shard_map/home/pallas_call | solution.py:711
  262.6 8.6 %all-to-all-start.4 = ((bf16[32,24,2048]{2,1,0:T(8,128)(2,1)}), bf16[32,24,2048]{2,1,0:T(8,128)(2,1)}, u32[]{:S(2)}, u32[]{:S(2)}) async-start(bf16[32,24,2048]{2,1,0:T(8,128)(2,1)} %bitcast.61), calls=%async_computation.4 | async-start | bytes 6291456 | tf_op jit(solution)/shard_map/all_to_all | solution.py:46
  271.3 36.0 %back.1 = (bf16[256,1536]{1,0:T(8,128)(2,1)}, bf16[4,256,512]{2,1,0:T(8,128)(2,1)}, f32[256,512]{1,0:T(8,128)}, bf16[2048,128]{1,0:T(8,128)(2,1)}, f32[8,512]{1,0:T(8,128)}) custom-call(bf16[256,768]{1,0:T(8,128)(2,1)} %get-tuple-element.57.pick_t.pick_y, bf16[768,2176]{1,0:T(8,128)(2,1)} %bitcast.20.ret, s32[8,256]{1,0:T(8,128)} %fusion.17.slot_of, ...), custom_call_target="tpu_custom_call" | custom-call | flops 20000000000 | bytes 1 | tf_op jit(solution)/shard_map/back/pallas_call | solution.py:478
  307.3 3.5 all-to-all-done.4
  310.9 81.4 %reduce.7 = (bf16[128,16,512]{2,1,0:T(8,128)(2,1)}, bf16[128,16,512]{2,1,0:T(8,128)(2,1)}, bf16[128,16,512]{2,1,0:T(8,128)(2,1)}, bf16[640,2048]{1,0:T(8,128)(2,...) custom-call(bf16[256,1536]{1,0:T(8,128)(2,1)} %get-tuple-element.79., ...), custom_call_target="tpu_custom_call" | custom-call | flops 1 | bytes 1 | tf_op jit(solution)/shard_map/reduce/pallas_call | solution.py:1012
  392.3 1.8 convert_bitcast_fusion.1
  394.1 4.2 slice_convert_fusion
  398.8 1.0 pad_maximum_fusion
  399.8 6.1 %all-to-all-start.5 = ((bf16[32,8,1664]{2,1,0:T(8,128)(2,1)}), bf16[32,8,1664]{2,1,0:T(8,128)(2,1)}, u32[]{:S(2)}, u32[]{:S(2)}) async-start(bf16[32,8,1664]{2,1,0:T(8,128)(2,1)} %pad_maximum_fusion), calls=%async_computation.5 | async-start | bytes 1703936 | tf_op jit(solution)/shard_map/all_to_all | solution.py:46
  406.0 2.9 bitcast_convert_fusion.2
  408.9 2.9 bitcast_convert_fusion.1
  411.8 2.7 bitcast_convert_fusion
  414.5 7.6 %convert_bitcast_fusion = f32[2,2048,3,256]{3,1,2,0:T(8,128)} fusion(bf16[2,3,2048,256]{3,2,1,0:T(8,128)(2,1)S(1)} %bitcast.58, pred[2]{0:T(512)(128)(4,1)S(1)} %iota_compare_fusion.8, bf16[3,2048,256]{2,1,0:T(8,128)(2,1)} %get-tuple-element.94), kind=kLoop, calls=%fused_computation.1 | loop fusion | flops 6291456 | bytes 22020098 | tf_op jit(solution)/shard_map/transpose | solution.py:1160
  422.1 1.0 convert_reduce_fusion.1
  424.3 1.4 convolution_convert_fusion.1
  (92 shorter events, 14.3 us)
Async XLA Ops:
  2.3 15.8 %copy-start.5 = (s32[256]{0:T(256)}, s32[256]{0:T(256)S(1)}, u32[]{:S(2)}) copy-start(s32[256]{0:T(256)S(1)} %convert_reduce_fusion.3) | copy-start | bytes 3076
  3.3 17.3 %copy-start.4 = (s32[256,8]{0,1:T(8,128)S(1)}, s32[256,8]{0,1:T(8,128)}, u32[]{:S(2)}) copy-start(s32[256,8]{0,1:T(8,128)} %param.20) | copy-start | bytes 24580
  3.3 17.3 %copy-start.13 = (s32[1,3]{1,0:T(1,128)S(1)}, s32[1,3]{1,0:T(1,128)}, u32[]{:S(2)}) copy-start(s32[1,3]{1,0:T(1,128)} %param.18) | copy-start | bytes 40
  3.3 17.6 %copy-start.11 = (bf16[2048]{0:T(1024)(128)(2,1)S(1)}, bf16[2048]{0:T(1024)(128)(2,1)}, u32[]{:S(2)}) copy-start(bf16[2048]{0:T(1024)(128)(2,1)} %param.22) | copy-start | bytes 12292
  3.3 18.2 %copy-start.12 = (bf16[2048]{0:T(1024)(128)(2,1)S(1)}, bf16[2048]{0:T(1024)(128)(2,1)}, u32[]{:S(2)}) copy-start(bf16[2048]{0:T(1024)(128)(2,1)} %param.29) | copy-start | bytes 12292
  4.5 18.1 %copy-start.8 = (s32[1,2048]{1,0:T(1,128)S(1)}, s32[1,2048]{1,0:T(1,128)}, u32[]{:S(2)}) copy-start(s32[1,2048]{1,0:T(1,128)} %param.21) | copy-start | bytes 24580
  4.6 22.4 %copy-start.3 = (bf16[2048,64]{0,1:T(8,128)(2,1)S(1)}, bf16[2048,64]{0,1:T(8,128)(2,1)}, u32[]{:S(2)}) copy-start(bf16[2048,64]{0,1:T(8,128)(2,1)} %param.30) | copy-start | bytes 786436
  5.7 26.1 %all-to-all-start = ((bf16[32,8,1152]{2,1,0:T(8,128)(2,1)}), bf16[32,8,1152]{2,1,0:T(8,128)(2,1)S(1)}, u32[]{:S(2)}, u32[]{:S(2)}) async-start(bf16[32,8,1152]{2,1,0:T(8,128)(2,1)} %fusion), calls=%async_computation | async-start | bytes 1179648 | tf_op jit(solution)/shard_map/all_to_all | solution.py:46
  18.1 12.5 %copy-start.14 = (bf16[128]{0:T(256)(128)(2,1)S(1)}, bf16[128]{0:T(256)(128)(2,1)}, u32[]{:S(2)}) copy-start(bf16[128]{0:T(256)(128)(2,1)} %param.27) | copy-start | bytes 772
  18.1 12.5 %copy-start.15 = (bf16[128]{0:T(256)(128)(2,1)S(1)}, bf16[128]{0:T(256)(128)(2,1)}, u32[]{:S(2)}) copy-start(bf16[128]{0:T(256)(128)(2,1)} %param.26) | copy-start | bytes 772
  18.1 109.6 %collective-permute-start = (bf16[3,1024,256]{2,1,0:T(8,128)(2,1)}, bf16[3,1024,256]{2,1,0:T(8,128)(2,1)}, u32[]{:S(2)}, u32[]{:S(2)}) collective-permute-start(bf16[3,1024,256]{2,1,0:T(8,128)(2,1)} %dynamic-slice_bitcast_fusion.1), channel_id=1, source_target_pairs={{0,1},{1,4},{2,5},{3,0},{4,7},{5,2},{6,3},{7,6},{8,9},{9,12},{10,1... | collective-permute-start | bytes 4718600 | tf_op jit(solution)/shard_map/ppermute | solution.py:632
  34.2 1.1 copy-start.9
  59.1 60.0 %all-to-all-start.1 = ((bf16[32,24,2048]{2,1,0:T(8,128)(2,1)}), bf16[32,24,2048]{2,1,0:T(8,128)(2,1)}, u32[]{:S(2)}, u32[]{:S(2)}) async-start(bf16[32,24,2048]{2,1,0:T(8,128)(2,1)} %bitcast.62), calls=%async_computation.1 | async-start | bytes 6291456 | tf_op jit(solution)/shard_map/all_to_all | solution.py:46
  69.5 58.1 %collective-permute-start.1 = (bf16[3,1024,256]{2,1,0:T(8,128)(2,1)}, bf16[3,1024,256]{2,1,0:T(8,128)(2,1)}, u32[]{:S(2)}, u32[]{:S(2)}) collective-permute-start(bf16[3,1024,256]{2,1,0:T(8,128)(2,1)} %dynamic-slice_bitcast_fusion), channel_id=1, source_target_pairs={{0,5},{1,0},{2,1},{3,4},{4,3},{5,6},{6,7},{7,2},{8,13},{9,8},{10,9... | collective-permute-start | bytes 4718600 | tf_op jit(solution)/shard_map/ppermute | solution.py:632
  119.1 51.1 %all-to-all-start.2 = ((bf16[32,24,2176]{2,1,0:T(8,128)(2,1)}), bf16[32,24,2176]{2,1,0:T(8,128)(2,1)}, u32[]{:S(2)}, u32[]{:S(2)}) async-start(bf16[32,24,2176]{2,1,0:T(8,128)(2,1)} %bitcast.59), calls=%async_computation.2 | async-start | bytes 6684672 | tf_op jit(solution)/shard_map/all_to_all | solution.py:46
  212.3 50.3 %all-to-all-start.3 = ((bf16[32,24,2176]{2,1,0:T(8,128)(2,1)}), bf16[32,24,2176]{2,1,0:T(8,128)(2,1)}, u32[]{:S(2)}, u32[]{:S(2)}) async-start(bf16[32,24,2176]{2,1,0:T(8,128)(2,1)} %bitcast.60), calls=%async_computation.3 | async-start | bytes 6684672 | tf_op jit(solution)/shard_map/all_to_all | solution.py:46
  262.6 48.2 %all-to-all-start.4 = ((bf16[32,24,2048]{2,1,0:T(8,128)(2,1)}), bf16[32,24,2048]{2,1,0:T(8,128)(2,1)}, u32[]{:S(2)}, u32[]{:S(2)}) async-start(bf16[32,24,2048]{2,1,0:T(8,128)(2,1)} %bitcast.61), calls=%async_computation.4 | async-start | bytes 6291456 | tf_op jit(solution)/shard_map/all_to_all | solution.py:46
  394.1 4.2 copy-start.7
  394.1 4.3 %copy-start.10 = (s32[256]{0:T(256)S(1)}, s32[256]{0:T(256)}, u32[]{:S(2)}) copy-start(s32[256]{0:T(256)} %copy-done.9) | copy-start | bytes 3076
  394.1 4.3 %copy-start.16 = (bf16[256,512]{1,0:T(8,128)(2,1)S(1)}, bf16[256,512]{1,0:T(8,128)(2,1)}, u32[]{:S(2)}) copy-start(bf16[256,512]{1,0:T(8,128)(2,1)} %get-tuple-element.88) | copy-start | bytes 786436
  394.1 4.3 %copy-start.17 = (bf16[256,512]{1,0:T(8,128)(2,1)S(1)}, bf16[256,512]{1,0:T(8,128)(2,1)}, u32[]{:S(2)}) copy-start(bf16[256,512]{1,0:T(8,128)(2,1)} %get-tuple-element.87) | copy-start | bytes 786436
  398.3 7.7 %copy-start.2 = (bf16[128,16,512]{2,1,0:T(8,128)(2,1)S(1)}, bf16[128,16,512]{2,1,0:T(8,128)(2,1)}, u32[]{:S(2)}) copy-start(bf16[128,16,512]{2,1,0:T(8,128)(2,1)} %get-tuple-element.90) | copy-start | bytes 6291460
  399.8 22.3 %all-to-all-start.5 = ((bf16[32,8,1664]{2,1,0:T(8,128)(2,1)}), bf16[32,8,1664]{2,1,0:T(8,128)(2,1)}, u32[]{:S(2)}, u32[]{:S(2)}) async-start(bf16[32,8,1664]{2,1,0:T(8,128)(2,1)} %pad_maximum_fusion), calls=%async_computation.5 | async-start | bytes 1703936 | tf_op jit(solution)/shard_map/all_to_all | solution.py:46
  406.0 2.9 copy-start.1
  406.0 8.5 %slice-start = ((s8[6291456]{0:T(1024)(128)(4,1)}), s8[4194304]{0:T(1024)(128)(4,1)S(1)}, s32[]{:S(2)}) async-start(s8[6291456]{0:T(1024)(128)(4,1)} %bitcast.57), calls=%async_computation.6 | async-start | bytes 8388608
  408.9 2.9 copy-start
  408.9 5.7 %slice-start.1 = ((s8[6291456]{0:T(1024)(128)(4,1)}), s8[2097152]{0:T(1024)(128)(4,1)S(1)}, s32[]{:S(2)}) async-start(s8[6291456]{0:T(1024)(128)(4,1)} %bitcast.57), calls=%async_computation.7 | async-start | bytes 4194304
  414.5 9.8 %copy-start.6 = (s32[256]{0:T(256)S(1)}, s32[256]{0:T(256)}, u32[]{:S(2)}) copy-start(s32[256]{0:T(256)} %copy-done.5) | copy-start | bytes 3076

commit v11 on v10

--- a/solution.py
+++ b/solution.py
@@ -231,7 +231,7 @@
 
 
 def front_kernel(
-    x_all, bias, cos_rows, sin_rows, gain1, gain2, q_gain, k_gain, router_t, routes, slot_of, keep,
+    x_all, bias, cos_rows, sin_rows, gain1, gain2, q_gain, k_gain, router, routes, slot_of, keep,
     wq_hbm, wk_hbm, wv_hbm, wo_hbm,
     resid_out, mixed_out, q_out, k_out, qh_out, kh_out, vh_out, ob_out,
     gates_out, send_out, pick_out,
@@ -286,10 +286,10 @@
         resid_out[t] = value
         square = square + row_sum(value * value)
     r2 = inverse_rms(square, width)
-    logits = jnp.zeros((router_t.shape[0], tok), F32)
+    logits = jnp.zeros((router.shape[1], tok), F32)
     for t in range(blocks):
         mixed_out[t] = (resid_out[t] * r2 * gain2[t : t + 1, :]).astype(BF)
-        logits = logits + dot(router_t[:, t * col : (t + 1) * col], mixed_out[t], 1, 1)
+        logits = logits + dot(router[t * col : (t + 1) * col, :].T, mixed_out[t], 1, 1)
     expert = lax.broadcasted_iota(jnp.int32, logits.shape, 0)
     top = routes.shape[0]
     chosen = [
@@ -325,7 +325,7 @@
     post.finish()
 
 
-def front_call(x_all, bias, cos_rows, sin_rows, gain1, gain2, q_gain, k_gain, router_t, routes,
+def front_call(x_all, bias, cos_rows, sin_rows, gain1, gain2, q_gain, k_gain, router, routes,
                slot_of, keep, weights, slots):
     blocks, tok, col = tiles = x_all.shape
     width = col * blocks
@@ -355,7 +355,7 @@
         ),
         cost_estimate=SHADOW,
         name="front",
-    )(x_all, bias, cos_rows, sin_rows, gain1, gain2, q_gain, k_gain, router_t, routes, slot_of,
+    )(x_all, bias, cos_rows, sin_rows, gain1, gain2, q_gain, k_gain, router, routes, slot_of,
       keep, *weights)
 
 
@@ -813,7 +813,7 @@
 def reduce_kernel(
     d_qkv, dr, d_mine, router_part, small_in, x_all, gain1, ob, pick_y, ret_y,
     far_hbm, resid_hbm, wq_hbm, wk_hbm, wv_hbm,
-    q_out, k_out, v_out, o_out, dx_out, out_out, small_out, far_out,
+    q_out, k_out, v_out, o_out, router_out, dx_out, out_out, small_out, far_out,
     wq, wk, wv, resid, parts, y_parts, halves, box_x, note, buf, box, got,
     load_sem, out_sem, x_send, x_recv, send_sem, recv_sem, far_send, far_recv,
 ):
@@ -965,8 +965,9 @@
             )
             stores[-1].start()
         count = 16 * rows_chunk
-        turned = got[here, :, 3 * col :].reshape(count, o_out.shape[0]).T
-        o_out[:, pl.ds(pl.multiple_of(at * rows_chunk, 128), count)] = turned
+        there = pl.ds(pl.multiple_of(at * rows_chunk, 128), count)
+        o_out[:, there] = got[here, :, 3 * col : 4 * col].reshape(count, col).T
+        router_out[:, there] = got[here, :, 4 * col :].reshape(count, router_out.shape[0]).T
 
     for k in range(3, -1, -1):
         for s in range(4):
@@ -1013,12 +1014,12 @@
         reduce_kernel,
         out_shape=(
             shape(wide[:2] + (col,), BF), shape(wide[:2] + (col,), BF), shape(wide[:2] + (col,), BF),
-            shape((col + 128, width), BF),
+            shape((col, width), BF), shape((128, width), BF),
             shape((tok, col), BF), shape((tok, col), BF), shape((16, col), F32),
             shape((far.shape[0], 2 * far.shape[1], far.shape[2]), BF),
         ),
         in_specs=[vmem] * 10 + [hbm] * 5,
-        out_specs=(hbm,) * 3 + (vmem,) * 4 + (hbm,),
+        out_specs=(hbm,) * 3 + (vmem,) * 5 + (hbm,),
         scratch_shapes=[
             pltpu.VMEM((width, col), BF), pltpu.VMEM((width, col), BF), pltpu.VMEM((width, col), BF),
             pltpu.VMEM((tok, col), F32), pltpu.VMEM(tiles, BF), pltpu.VMEM(tiles, BF),
@@ -1126,7 +1127,7 @@
     (
         resid, mixed, q_raw, k_raw, qh, kh, vh, attended, gates, send_rows, pick_t,
     ) = front_call(
-        x_all, bias, cos_rows, sin_rows, gain1, gain2, *head_gains, router.T, routes_t, slot_of,
+        x_all, bias, cos_rows, sin_rows, gain1, gain2, *head_gains, router, routes_t, slot_of,
         keep_mask, weights, slots,
     )
     send_rows, w_stored, recv_dy = lax.optimization_barrier((send_rows, w_stored, recv_dy))
@@ -1141,7 +1142,7 @@
         sin_rows, gain2, *head_gains, router, resid, dy_all, mixed, qh, kh, vh, q_raw, k_raw,
         w_output,
     )
-    *wide, turned, dx_slice, out_slice, small, far = reduce_call(
+    *wide, out_proj, router_sum, dx_slice, out_slice, small, far = reduce_call(
         d_qkv, dr, d_mine, router_part, small, x_all, gain1, attended, pick_t, ret_y, far, resid,
         weights[:3],
     )
@@ -1170,9 +1171,9 @@
         wide[2].astype(F32),
         small[gain_at : gain_at + head],
         small[gain_at + head : gain_at + 2 * head],
-        turned[:col_count].astype(F32),
+        out_proj.astype(F32),
         small[width : 2 * width],
-        turned[col_count : col_count + expert_count].astype(F32).T,
+        router_sum[:expert_count].astype(F32).T,
         expert_grad,
     )
 

time: 434 us -> 434 us (level)
  transfers between devices with their start and end apart: 8 -> 8, of which waited for: 1 -> 1; matrix products, arithmetic and copies ran while one was open for 8% -> 9% of each run, Pallas kernels for 45% -> 45%
where the time goes in v11:
time: 434 us; the launch traced here: 426 us
  Pallas kernels  317 us (73%)
  starting transfers between devices  52.9 us (12%)
  other arithmetic  33.2 us (8%)
  local copies, waits for them, and re-layouts  13.1 us (3%)
  matrix products  5.03 us (1%)
    pallas_call x1, Pallas kernels, reduce_call(): pl.pallas_call(reduce_kernel, out_shape=(shape(wide[:2] + (col,), BF), sh...  81.4 us
    all_to_all x6, starting transfers between devices, exchange(): return lax.all_to_all(value, axis, split_axis=0, concat_axis=0, tiled=True)  47.9 us
    pallas_call x1, Pallas kernels, front_call(): pl.pallas_call(front_kernel, out_shape=(shape(tiles, F32), shape(tiles, B...  47.7 us
    pallas_call x1, Pallas kernels, home_call(): pl.pallas_call(home_kernel, out_shape=(shape((2, three, width, hidden), B...  42.9 us
    pallas_call x1, Pallas kernels, weights_call(): pl.pallas_call(weights_kernel, out_shape=jax.ShapeDtypeStruct((4, three,...  42.5 us
    pallas_call x1, Pallas kernels, expert_call(): pl.pallas_call(expert_kernel, grid=(quarters,), out_shape=tuple(outs) + (...  42.1 us
    pallas_call x1, Pallas kernels, back_call(): pl.pallas_call(back_kernel, out_shape=(shape((tok, 3 * col), BF), shape(t...  36.1 us
    pallas_call x1, Pallas kernels, pre_call(): pl.pallas_call(pre_kernel, out_shape=(shape(tiles, BF), shape(tiles, BF),...  24.6 us
  transfers between devices with their start and end apart: 8, of which 1 were waited for; matrix products, arithmetic and copies ran while one was open for 9% of the time, Pallas kernels for 45%

profile of v11, /device:TPU:1, one launch (start us, length us, event | category | flops | bytes accessed | tf_op | source)
XLA Modules:
  0.0 426.4 jit_solution(14429895559330773819)
XLA Ops:
  1.3 0.9 convert_reduce_fusion.3
  3.3 1.2 concatenate.15
  4.6 1.2 fusion
  5.7 9.7 %all-to-all-start = ((bf16[32,8,1152]{2,1,0:T(8,128)(2,1)}), bf16[32,8,1152]{2,1,0:T(8,128)(2,1)S(1)}, u32[]{:S(2)}, u32[]{:S(2)}) async-start(bf16[32,8,1152]{2,1,0:T(8,128)(2,1)} %fusion), calls=%async_computation | async-start | bytes 1179648 | tf_op jit(solution)/shard_map/all_to_all | solution.py:46
  15.5 2.7 dynamic-slice_bitcast_fusion.1
  18.2 2.5 collective-permute-start
  23.6 3.4 convert_reduce_fusion
  32.3 1.1 convolution_convert_fusion.3.local
  34.3 24.6 %pre.1 = (bf16[4,256,512]{2,1,0:T(8,128)(2,1)}, bf16[4,256,512]{2,1,0:T(8,128)(2,1)}, bf16[768,2048]{1,0:T(8,128)(2,1)}) custom-call(bf16[256,1024]{1,0:T(8,128)(2,1)} %convolution_convert_fusion.3.local, s32[8,256]{1,0:T(8,128)} %fusion.17.slot_of), custom_call_target="tpu_custom_call" | custom-call | flops 1 | bytes 1 | tf_op jit(solution)/shard_map/pre/pallas_call | solution.py:216
  59.0 7.5 %all-to-all-start.1 = ((bf16[32,24,2048]{2,1,0:T(8,128)(2,1)}), bf16[32,24,2048]{2,1,0:T(8,128)(2,1)}, u32[]{:S(2)}, u32[]{:S(2)}) async-start(bf16[32,24,2048]{2,1,0:T(8,128)(2,1)} %bitcast.60), calls=%async_computation.1 | async-start | bytes 6291456 | tf_op jit(solution)/shard_map/all_to_all | solution.py:46
  66.5 2.7 dynamic-slice_bitcast_fusion
  69.2 2.4 collective-permute-start.1
  71.6 47.7 %front.1 = (f32[4,256,512]{2,1,0:T(8,128)}, bf16[4,256,512]{2,1,0:T(8,128)(2,1)}, f32[256,512]{1,0:T(8,128)}, f32[256,512]{1,0:T(8,128)}, bf16[256,512]{1,0:T(8,...) custom-call(bf16[4,256,512]{2,1,0:T(8,128)(2,1)} %get-tuple-element., ...), custom_call_target="tpu_custom_call" | custom-call | flops 40000000000 | bytes 1 | tf_op jit(solution)/shard_map/front/pallas_call | solution.py:335
  119.4 8.6 %all-to-all-start.2 = ((bf16[32,24,2176]{2,1,0:T(8,128)(2,1)}), bf16[32,24,2176]{2,1,0:T(8,128)(2,1)}, u32[]{:S(2)}, u32[]{:S(2)}) async-start(bf16[32,24,2176]{2,1,0:T(8,128)(2,1)} %bitcast.57), calls=%async_computation.2 | async-start | bytes 6684672 | tf_op jit(solution)/shard_map/all_to_all | solution.py:46
  128.0 42.5 %weights.1.w_ref = bf16[4,3,2048,256]{3,2,1,0:T(8,128)(2,1)} custom-call(bf16[2,3,2048,256]{3,2,1,0:T(8,128)(2,1)} %bitcast.63, bf16[3,1024,256]{2,1,0:T(8,128)(2,1)} %collective-permute-done.first, bf16[3,1024,256]{2,1,0:T(8,128)(2,1)} %collective-permute-done.1.second), custom_call_target="tpu_custom_call" | custom-call | flops 40000000000 | bytes 1 | tf_op jit(solution)/shard_map/weights/pallas_call | solution.py:602
  170.5 42.1 %expert.1 = (bf16[768,2048]{1,0:T(8,128)(2,1)}, bf16[768,2176]{1,0:T(8,128)(2,1)}, bf16[4,3,2048,256]{3,2,1,0:T(8,128)(2,1)}) custom-call(bf16[768,2176]{1,0:T(8,128)(2,1)} %bitcast.14.rows_ref, bf16[768,2048]{1,0:T(8,128)(2,1)} %bitcast.12.dys, bf16[4,3,2048,256]{3,2,1,0:T(8,128)(2,1)} %weights.1.w_ref), custom_call_target="tpu_custom_call" | custom-call | flops 1 | bytes 1 | tf_op jit(solution)/shard_map/expert/pallas_call | solution.py:780
  212.7 7.4 %all-to-all-start.3 = ((bf16[32,24,2176]{2,1,0:T(8,128)(2,1)}), bf16[32,24,2176]{2,1,0:T(8,128)(2,1)}, u32[]{:S(2)}, u32[]{:S(2)}) async-start(bf16[32,24,2176]{2,1,0:T(8,128)(2,1)} %bitcast.58), calls=%async_computation.3 | async-start | bytes 6684672 | tf_op jit(solution)/shard_map/all_to_all | solution.py:46
  220.1 42.9 %home.1 = (bf16[2,3,2048,256]{3,2,1,0:T(8,128)(2,1)}, bf16[3,1024,256]{2,1,0:T(8,128)(2,1)}) custom-call(bf16[4,3,2048,256]{3,2,1,0:T(8,128)(2,1)} %get-tuple-element.66.grads), custom_call_target="tpu_custom_call" | custom-call | flops 40000000000 | bytes 1 | tf_op jit(solution)/shard_map/home/pallas_call | solution.py:711
  263.0 8.6 %all-to-all-start.4 = ((bf16[32,24,2048]{2,1,0:T(8,128)(2,1)}), bf16[32,24,2048]{2,1,0:T(8,128)(2,1)}, u32[]{:S(2)}, u32[]{:S(2)}) async-start(bf16[32,24,2048]{2,1,0:T(8,128)(2,1)} %bitcast.59), calls=%async_computation.4 | async-start | bytes 6291456 | tf_op jit(solution)/shard_map/all_to_all | solution.py:46
  271.6 36.1 %back.1 = (bf16[256,1536]{1,0:T(8,128)(2,1)}, bf16[4,256,512]{2,1,0:T(8,128)(2,1)}, f32[256,512]{1,0:T(8,128)}, bf16[2048,128]{1,0:T(8,128)(2,1)}, f32[8,512]{1,0:T(8,128)}) custom-call(bf16[256,768]{1,0:T(8,128)(2,1)} %get-tuple-element.58.pick_t.pick_y, bf16[768,2176]{1,0:T(8,128)(2,1)} %bitcast.19.ret, s32[8,256]{1,0:T(8,128)} %fusion.17.slot_of, ...), custom_call_target="tpu_custom_call" | custom-call | flops 20000000000 | bytes 1 | tf_op jit(solution)/shard_map/back/pallas_call | solution.py:478
  307.7 3.5 all-to-all-done.4
  311.2 81.4 %reduce.7 = (bf16[128,16,512]{2,1,0:T(8,128)(2,1)}, bf16[128,16,512]{2,1,0:T(8,128)(2,1)}, bf16[128,16,512]{2,1,0:T(8,128)(2,1)}, bf16[512,2048]{1,0:T(8,128)(2,...) custom-call(bf16[256,1536]{1,0:T(8,128)(2,1)} %get-tuple-element.80., ...), custom_call_target="tpu_custom_call" | custom-call | flops 1 | bytes 1 | tf_op jit(solution)/shard_map/reduce/pallas_call | solution.py:1013
  393.7 1.4 fusion.1
  395.1 1.0 pad_maximum_fusion
  396.1 6.2 %all-to-all-start.5 = ((bf16[32,8,1664]{2,1,0:T(8,128)(2,1)}), bf16[32,8,1664]{2,1,0:T(8,128)(2,1)}, u32[]{:S(2)}, u32[]{:S(2)}) async-start(bf16[32,8,1664]{2,1,0:T(8,128)(2,1)} %pad_maximum_fusion), calls=%async_computation.5 | async-start | bytes 1703936 | tf_op jit(solution)/shard_map/all_to_all | solution.py:46
  403.1 2.7 bitcast_convert_fusion.2
  405.8 2.9 bitcast_convert_fusion.1
  408.7 2.9 bitcast_convert_fusion
  411.7 2.5 convert_element_type.120
  414.2 7.6 %convert_bitcast_fusion = f32[2,2048,3,256]{3,1,2,0:T(8,128)} fusion(bf16[2,3,2048,256]{3,2,1,0:T(8,128)(2,1)S(1)} %bitcast.56, pred[2]{0:T(512)(128)(4,1)S(1)} %iota_compare_fusion.8, bf16[3,2048,256]{2,1,0:T(8,128)(2,1)} %get-tuple-element.96), kind=kLoop, calls=%fused_computation.1 | loop fusion | flops 6291456 | bytes 22020098 | tf_op jit(solution)/shard_map/transpose | solution.py:1161
  421.8 1.0 convert_reduce_fusion.1
  424.0 1.4 convolution_convert_fusion.1
  (89 shorter events, 14.8 us)
Async XLA Ops:
  2.3 15.9 %copy-start.7 = (s32[256]{0:T(256)}, s32[256]{0:T(256)S(1)}, u32[]{:S(2)}) copy-start(s32[256]{0:T(256)S(1)} %convert_reduce_fusion.3) | copy-start | bytes 3076
  3.3 17.4 %copy-start.6 = (s32[256,8]{0,1:T(8,128)S(1)}, s32[256,8]{0,1:T(8,128)}, u32[]{:S(2)}) copy-start(s32[256,8]{0,1:T(8,128)} %param.20) | copy-start | bytes 24580
  3.3 17.4 %copy-start.14 = (s32[1,3]{1,0:T(1,128)S(1)}, s32[1,3]{1,0:T(1,128)}, u32[]{:S(2)}) copy-start(s32[1,3]{1,0:T(1,128)} %param.18) | copy-start | bytes 40
  3.3 17.7 %copy-start.12 = (bf16[2048]{0:T(1024)(128)(2,1)S(1)}, bf16[2048]{0:T(1024)(128)(2,1)}, u32[]{:S(2)}) copy-start(bf16[2048]{0:T(1024)(128)(2,1)} %param.22) | copy-start | bytes 12292
  3.3 18.3 %copy-start.13 = (bf16[2048]{0:T(1024)(128)(2,1)S(1)}, bf16[2048]{0:T(1024)(128)(2,1)}, u32[]{:S(2)}) copy-start(bf16[2048]{0:T(1024)(128)(2,1)} %param.29) | copy-start | bytes 12292
  4.5 18.2 %copy-start.9 = (s32[1,2048]{1,0:T(1,128)S(1)}, s32[1,2048]{1,0:T(1,128)}, u32[]{:S(2)}) copy-start(s32[1,2048]{1,0:T(1,128)} %param.21) | copy-start | bytes 24580
  4.6 22.5 %copy-start.4 = (bf16[2048,64]{0,1:T(8,128)(2,1)S(1)}, bf16[2048,64]{0,1:T(8,128)(2,1)}, u32[]{:S(2)}) copy-start(bf16[2048,64]{0,1:T(8,128)(2,1)} %param.30) | copy-start | bytes 786436
  5.7 23.0 %copy-start.15 = (bf16[128]{0:T(256)(128)(2,1)S(1)}, bf16[128]{0:T(256)(128)(2,1)}, u32[]{:S(2)}) copy-start(bf16[128]{0:T(256)(128)(2,1)} %param.27) | copy-start | bytes 772
  5.7 23.0 %copy-start.16 = (bf16[128]{0:T(256)(128)(2,1)S(1)}, bf16[128]{0:T(256)(128)(2,1)}, u32[]{:S(2)}) copy-start(bf16[128]{0:T(256)(128)(2,1)} %param.26) | copy-start | bytes 772
  5.7 24.3 %all-to-all-start = ((bf16[32,8,1152]{2,1,0:T(8,128)(2,1)}), bf16[32,8,1152]{2,1,0:T(8,128)(2,1)S(1)}, u32[]{:S(2)}, u32[]{:S(2)}) async-start(bf16[32,8,1152]{2,1,0:T(8,128)(2,1)} %fusion), calls=%async_computation | async-start | bytes 1179648 | tf_op jit(solution)/shard_map/all_to_all | solution.py:46
  18.2 109.8 %collective-permute-start = (bf16[3,1024,256]{2,1,0:T(8,128)(2,1)}, bf16[3,1024,256]{2,1,0:T(8,128)(2,1)}, u32[]{:S(2)}, u32[]{:S(2)}) collective-permute-start(bf16[3,1024,256]{2,1,0:T(8,128)(2,1)} %dynamic-slice_bitcast_fusion.1), channel_id=1, source_target_pairs={{0,1},{1,4},{2,5},{3,0},{4,7},{5,2},{6,3},{7,6},{8,9},{9,12},{10,1... | collective-permute-start | bytes 4718600 | tf_op jit(solution)/shard_map/ppermute | solution.py:632
  32.3 1.1 copy-start.10
  59.0 60.4 %all-to-all-start.1 = ((bf16[32,24,2048]{2,1,0:T(8,128)(2,1)}), bf16[32,24,2048]{2,1,0:T(8,128)(2,1)}, u32[]{:S(2)}, u32[]{:S(2)}) async-start(bf16[32,24,2048]{2,1,0:T(8,128)(2,1)} %bitcast.60), calls=%async_computation.1 | async-start | bytes 6291456 | tf_op jit(solution)/shard_map/all_to_all | solution.py:46
  69.2 58.8 %collective-permute-start.1 = (bf16[3,1024,256]{2,1,0:T(8,128)(2,1)}, bf16[3,1024,256]{2,1,0:T(8,128)(2,1)}, u32[]{:S(2)}, u32[]{:S(2)}) collective-permute-start(bf16[3,1024,256]{2,1,0:T(8,128)(2,1)} %dynamic-slice_bitcast_fusion), channel_id=1, source_target_pairs={{0,5},{1,0},{2,1},{3,4},{4,3},{5,6},{6,7},{7,2},{8,13},{9,8},{10,9... | collective-permute-start | bytes 4718600 | tf_op jit(solution)/shard_map/ppermute | solution.py:632
  119.4 51.2 %all-to-all-start.2 = ((bf16[32,24,2176]{2,1,0:T(8,128)(2,1)}), bf16[32,24,2176]{2,1,0:T(8,128)(2,1)}, u32[]{:S(2)}, u32[]{:S(2)}) async-start(bf16[32,24,2176]{2,1,0:T(8,128)(2,1)} %bitcast.57), calls=%async_computation.2 | async-start | bytes 6684672 | tf_op jit(solution)/shard_map/all_to_all | solution.py:46
  212.7 50.3 %all-to-all-start.3 = ((bf16[32,24,2176]{2,1,0:T(8,128)(2,1)}), bf16[32,24,2176]{2,1,0:T(8,128)(2,1)}, u32[]{:S(2)}, u32[]{:S(2)}) async-start(bf16[32,24,2176]{2,1,0:T(8,128)(2,1)} %bitcast.58), calls=%async_computation.3 | async-start | bytes 6684672 | tf_op jit(solution)/shard_map/all_to_all | solution.py:46
  263.0 48.2 %all-to-all-start.4 = ((bf16[32,24,2048]{2,1,0:T(8,128)(2,1)}), bf16[32,24,2048]{2,1,0:T(8,128)(2,1)}, u32[]{:S(2)}, u32[]{:S(2)}) async-start(bf16[32,24,2048]{2,1,0:T(8,128)(2,1)} %bitcast.59), calls=%async_computation.4 | async-start | bytes 6291456 | tf_op jit(solution)/shard_map/all_to_all | solution.py:46
  311.2 82.5 %copy-start.11 = (s32[256]{0:T(256)S(1)}, s32[256]{0:T(256)}, u32[]{:S(2)}) copy-start(s32[256]{0:T(256)} %copy-done.10) | copy-start | bytes 3076
  392.6 9.6 %copy-start.5 = (bf16[128,2048]{1,0:T(8,128)(2,1)S(1)}, bf16[128,2048]{1,0:T(8,128)(2,1)}, u32[]{:S(2)}) copy-start(bf16[128,2048]{1,0:T(8,128)(2,1)} %get-tuple-element.95) | copy-start | bytes 1572868
  392.6 10.4 %copy-start.3 = (bf16[128,16,512]{2,1,0:T(8,128)(2,1)S(1)}, bf16[128,16,512]{2,1,0:T(8,128)(2,1)}, u32[]{:S(2)}) copy-start(bf16[128,16,512]{2,1,0:T(8,128)(2,1)} %get-tuple-element.91) | copy-start | bytes 6291460
  396.1 25.7 %all-to-all-start.5 = ((bf16[32,8,1664]{2,1,0:T(8,128)(2,1)}), bf16[32,8,1664]{2,1,0:T(8,128)(2,1)}, u32[]{:S(2)}, u32[]{:S(2)}) async-start(bf16[32,8,1664]{2,1,0:T(8,128)(2,1)} %pad_maximum_fusion), calls=%async_computation.5 | async-start | bytes 1703936 | tf_op jit(solution)/shard_map/all_to_all | solution.py:46
  403.1 2.7 copy-start.2
  405.8 2.9 copy-start.1
  405.8 8.4 %slice-start = ((s8[6291456]{0:T(1024)(128)(4,1)}), s8[4194304]{0:T(1024)(128)(4,1)S(1)}, s32[]{:S(2)}) async-start(s8[6291456]{0:T(1024)(128)(4,1)} %bitcast.55), calls=%async_computation.6 | async-start | bytes 8388608
  408.7 3.0 copy-start
  408.7 5.5 %slice-start.1 = ((s8[6291456]{0:T(1024)(128)(4,1)}), s8[2097152]{0:T(1024)(128)(4,1)S(1)}, s32[]{:S(2)}) async-start(s8[6291456]{0:T(1024)(128)(4,1)} %bitcast.55), calls=%async_computation.7 | async-start | bytes 4194304
  414.2 9.8 %copy-start.8 = (s32[256]{0:T(256)S(1)}, s32[256]{0:T(256)}, u32[]{:S(2)}) copy-start(s32[256]{0:T(256)} %copy-done.7) | copy-start | bytes 3076
